TPU v7x, 32 devices: a whole 2x2x4 slice. The times are simulated.
32 devices in a mesh: pert: 8 (over y, x, core), gx: 4 (over z).
Axes of the slice: x: 2, y: 2, z: 4, core: 2. Of those that a mesh axis runs over, the one named last changes fastest.
Arguments:
- pert_field: float32 [8, 3, 1024, 8, 1024], P('pert', None, 'gx'), may hold values from -6 to 6
- base_store: bfloat16 [8, 3, 1024, 8, 1024], P('pert', None, 'gx'), may hold values from -6 to 6
- section_owner: int32 [1], replicated, may hold values from 0 to 7
- pert_ids: int32 [8], P('pert'), may hold values from 0 to 63
- member_visc: float32 [64], replicated, may hold values from 0.05 to 0.5
Outputs:
- section_field: float32 [8, 3, 1024, 2, 1024], P('pert', None, 'gx')
All inputs are finite; a program needn't handle non-finite values.
Results may differ from a plain program's by a relative error of at most 0.0003.
Values may be sent and summed in bfloat16 or wider, within the bound.
No kernel may reach another device: no remote copies, remote signals or barrier semaphores. Data moves between devices by JAX's collectives and lax.ppermute only.
A program may use at most 320 MiB of HBM per device.

v0:
```python
import math

import jax
import jax.numpy as jnp
from jax import lax
from jax.sharding import PartitionSpec as P

first_weights = (0.75, -0.15, 1.0 / 60.0)
second_weights = (1.5, -0.15, 1.0 / 90.0)
centre_second = -49.0 / 18.0
section_step = 0.25


def extended(array, sides, width):
    for axis, dim in sides:
        size, length = (lax.axis_size(axis), array.shape[dim])
        up = [(i, (i + 1) % size) for i in range(size)]
        down = [(j, i) for i, j in up]
        last = lax.slice_in_dim(array, length - width, length, axis=dim)
        first = lax.slice_in_dim(array, 0, width, axis=dim)
        before = lax.ppermute(last, axis, up)
        after = lax.ppermute(first, axis, down)
        array = jnp.concatenate([before, array, after], axis=dim)
    return array


def broadcast(value, axis, source):
    kept = jnp.where(lax.axis_index(axis) == source, value, 0).astype(value.dtype)
    return lax.psum(kept, axis)


def first_across(values, axis_number):
    summed = jnp.zeros_like(values)
    for offset_cells, weight in zip((1, 2, 3), first_weights):
        summed = summed + weight * (
            jnp.roll(values, -offset_cells, axis_number)
            - jnp.roll(values, offset_cells, axis_number)
        )
    return summed


def second_across(values, axis_number):
    summed = centre_second * values
    for offset_cells, weight in zip((1, 2, 3), second_weights):
        summed = summed + weight * (
            jnp.roll(values, -offset_cells, axis_number)
            + jnp.roll(values, offset_cells, axis_number)
        )
    return summed


def first_depth(values, plane_count):
    summed = jnp.zeros_like(values[:, :, 3 : 3 + plane_count])
    for offset_cells, weight in zip((1, 2, 3), first_weights):
        summed = summed + weight * (
            values[:, :, 3 + offset_cells : 3 + offset_cells + plane_count]
            - values[:, :, 3 - offset_cells : 3 - offset_cells + plane_count]
        )
    return summed


def second_depth(values, plane_count):
    summed = centre_second * values[:, :, 3 : 3 + plane_count]
    for offset_cells, weight in zip((1, 2, 3), second_weights):
        summed = summed + weight * (
            values[:, :, 3 + offset_cells : 3 + offset_cells + plane_count]
            + values[:, :, 3 - offset_cells : 3 - offset_cells + plane_count]
        )
    return summed


def local_inverse(slab_width):
    counter = jnp.arange(1, slab_width + 1, dtype=jnp.int32)
    period = 2 * (slab_width + 1)
    product_index = counter[:, None] * counter[None, :] % period
    sine_angle = math.pi / (slab_width + 1)
    sine_basis = jnp.sin(sine_angle * product_index.astype(jnp.float32)) * math.sqrt(
        2.0 / (slab_width + 1)
    )
    eigenvalues = 1.0 + 2.0 / 3.0 * jnp.cos(sine_angle * counter.astype(jnp.float32))
    return jnp.dot(sine_basis / eigenvalues[None, :], sine_basis, precision=lax.Precision.HIGHEST)


def along_terms(pert_interior, base_interior, inverse):
    stacked_rims = jnp.concatenate([pert_interior, base_interior], 0)
    padded_rims = extended(stacked_rims, (("gx", 1),), 3)
    slab_width = pert_interior.shape[1]

    def shifted(offset_cells):
        return padded_rims[:, 3 + offset_cells : 3 + offset_cells + slab_width]

    compact_rhs = 7.0 / 9.0 * (shifted(1) - shifted(-1)) + 1.0 / 36.0 * (shifted(2) - shifted(-2))
    particular = jnp.einsum("ij,cjzy->cizy", inverse, compact_rhs, precision=lax.Precision.HIGHEST)
    padded_solve = extended(particular.astype(jnp.bfloat16), (("gx", 1),), 1).astype(
        particular.dtype
    )
    left_last = padded_solve[:, 0]
    right_first = padded_solve[:, slab_width + 1]
    coupling = inverse[0, 0] / 3.0
    coupling_gain = 1.0 / (1.0 - coupling * coupling)
    left_value = (left_last - coupling * particular[:, 0]) * coupling_gain
    right_value = (right_first - coupling * particular[:, slab_width - 1]) * coupling_gain
    correction = (
        inverse[:, 0][None, :, None, None] * left_value[:, None]
        + inverse[:, slab_width - 1][None, :, None, None] * right_value[:, None]
    )
    derivative = particular - correction / 3.0
    pert_curve = centre_second * shifted(0)[:3]
    for offset_cells, weight in zip((1, 2, 3), second_weights):
        pert_curve = pert_curve + weight * (shifted(offset_cells)[:3] + shifted(-offset_cells)[:3])
    return (derivative[:3], pert_curve, derivative[3:])


def per_device(pert_field, base_store, section_owner, pert_ids, member_visc):
    state_field = pert_field[0]
    plane_count = state_field.shape[2] - 6
    interior = state_field[:, :, 3 : 3 + plane_count]
    inverse = local_inverse(state_field.shape[1])
    member_count = member_visc.shape[0]
    member_pick = (pert_ids[0] == jnp.arange(member_count, dtype=jnp.int32)).astype(jnp.float32)
    viscosity = jnp.sum(member_pick * member_visc)
    owner_level = section_owner[0]
    levels_here = base_store.shape[0]
    owner_slot = owner_level % levels_here
    owner_root = owner_level // levels_here
    stored_tile = lax.dynamic_index_in_dim(base_store, owner_slot, 0, keepdims=False)
    base_field = broadcast(stored_tile, "pert", owner_root).astype(jnp.float32)
    base_interior = base_field[:, :, 3 : 3 + plane_count]
    pert_along, pert_curve, base_along = along_terms(interior, base_interior, inverse)
    base_across = first_across(base_interior, 3)
    base_depth = first_depth(base_field, plane_count)
    pert_across = first_across(interior, 3)
    pert_depth = first_depth(state_field, plane_count)
    laplacian = pert_curve + second_across(interior, 3) + second_depth(state_field, plane_count)
    advection = (
        base_interior[0] * pert_along
        + base_interior[1] * pert_across
        + base_interior[2] * pert_depth
    )
    stretching = interior[0] * base_along + interior[1] * base_across + interior[2] * base_depth
    updated = interior + section_step * (-advection - stretching + viscosity * laplacian)
    return updated[None]


def solution(mesh):
    placed = (
        P("pert", None, "gx", None, None),
        P("pert", None, "gx", None, None),
        P(),
        P("pert"),
        P(),
    )
    return jax.shard_map(
        per_device,
        mesh=mesh,
        in_specs=placed,
        out_specs=P("pert", None, "gx", None, None),
        check_vma=False,
    )
```

profile of v0, /device:TPU:0, one launch (start us, length us, event | category | flops | bytes accessed | tf_op | source)
XLA Modules:
  0.0 418.2 jit_solution(17584555150854972511)
XLA Ops:
  7.2 23.5 %fusion.8 = bf16[3,256,8,1024]{3,1,2,0:T(8,128)(2,1)} fusion(bf16[1,3,256,8,1024]{4,3,2,1,0:T(8,128)(2,1)} %param.6, pred[]{:T(512)S(6)} %eq.13), kind=kLoop, calls=%fused_computation.12 | loop fusion | flops 6291456 | bytes 25165824 | tf_op jit(solution)/shard_map/jit(_where)/select_n | solution.py:28
  30.8 22.0 %copy.20 = f32[1,3,256,8,1024]{4,2,3,1,0:T(8,128)S(1)} copy(f32[1,3,256,8,1024]{4,3,2,1,0:T(8,128)} %param.5) | data formatting | bytes 50331648 | tf_op args[0]
  52.8 3.7 slice.347
  56.5 2.6 fusion.47
  59.2 1.3 slice.357
  63.7 1.5 fusion.83
  65.2 1.5 fusion.81
  66.6 1.4 fusion.79
  68.1 2.8 slice_bitcast_fusion.2
  70.9 11.5 %fusion.82 = (f32[3,256,2,1021]{3,1,2,0:T(8,128)}, f32[3,256,2,1021]{3,1,2,0:T(8,128)}) fusion(f32[3,256,8,1024]{3,1,2,0:T(8,128)} %bitcast.43), kind=kLoop, calls=%fused_computation.120 | loop fusion | bytes 25092096 | tf_op jit(solution)/shard_map/jit(_roll_static)/slice | solution.py:36
  82.4 11.3 %fusion.80 = (f32[3,256,2,1022]{3,1,2,0:T(8,128)}, f32[3,256,2,1022]{3,1,2,0:T(8,128)}) fusion(f32[3,256,8,1024]{3,1,2,0:T(8,128)} %bitcast.44), kind=kLoop, calls=%fused_computation.118 | loop fusion | bytes 25116672 | tf_op jit(solution)/shard_map/jit(_roll_static)/slice | solution.py:36
  93.7 11.1 %fusion.78 = (f32[3,256,2,1023]{3,1,2,0:T(8,128)}, f32[3,256,2,1023]{3,1,2,0:T(8,128)}) fusion(f32[3,256,8,1024]{3,1,2,0:T(8,128)} %bitcast.45), kind=kLoop, calls=%fused_computation.116 | loop fusion | bytes 25141248 | tf_op jit(solution)/shard_map/jit(_roll_static)/slice | solution.py:36
  104.7 101.2 %all-reduce.2.cloned.1.call-done = bf16[3,256,8,1024]{3,1,2,0:T(8,128)(2,1)} async-done(((bf16[3,256,8,1024]{3,1,2,0:T(8,128)(2,1)}), bf16[3,256,8,1024]{3,1,2,0:T(8,128)(2,1)}) %all-reduce.2.cloned.1.call-update) | async-done | bytes 12582928 | tf_op jit(solution)/shard_map/psum | solution.py:29
  205.9 2.8 slice.349
  208.7 4.5 %pad_maximum_fusion.8 = (f32[6,3,2,1024]{3,1,2,0:T(4,128)}, f32[6,3,2,1024]{3,1,2,0:T(4,128)}) fusion(f32[3,256,2,1024]{3,1,2,0:T(8,128)S(1)} %slice.349, f32[3,256,2,1024]{3,1,2,0:T(8,128)} %slice.347), kind=kLoop, calls=%fused_computation.87 | loop fusion | flops 73728 | bytes 12877824 | tf_op jit(solution)/shard_map/slice | solution.py:20
  213.2 3.9 collective-permute-start
  217.1 8.8 %convert_element_type.24 = f32[3,256,8,1024]{3,1,2,0:T(8,128)} convert(bf16[3,256,8,1024]{3,1,2,0:T(8,128)(2,1)S(1)} %bitcast.48) | non-fusion elementwise | flops 6291456 | bytes 37748736 | tf_op jit(solution)/shard_map/convert_element_type | solution.py:127
  225.9 5.7 %slice_bitcast_fusion.5 = (f32[256,2,1024]{2,0,1:T(8,128)}, f32[256,2,1024]{2,0,1:T(8,128)}, f32[256,2,1024]{2,0,1:T(8,128)}) fusion(f32[3,256,8,1024]{3,1,2,0:T(8,128)} %convert_element_type.24), kind=kLoop, calls=%fused_computation.73 | loop fusion | bytes 12582912 | tf_op jit(solution)/shard_map/mul | solution.py:136
  231.6 1.3 fusion.88
  233.0 6.4 %fusion.89 = (f32[3,256,2,1023]{3,1,2,0:T(8,128)}, f32[3,256,2,1023]{3,1,2,0:T(8,128)}) fusion(bf16[3,256,8,1024]{3,1,2,0:T(8,128)(2,1)S(1)} %bitcast.48), kind=kLoop, calls=%fused_computation.127 | loop fusion | bytes 25141248 | tf_op jit(solution)/shard_map/jit(_roll_static)/slice | solution.py:37
  239.3 6.3 %fusion.87 = (f32[3,256,2,1022]{3,1,2,0:T(8,128)}, f32[3,256,2,1022]{3,1,2,0:T(8,128)}) fusion(bf16[3,256,8,1024]{3,1,2,0:T(8,128)(2,1)S(1)} %bitcast.48), kind=kLoop, calls=%fused_computation.125 | loop fusion | bytes 25116672 | tf_op jit(solution)/shard_map/jit(_roll_static)/slice | solution.py:37
  245.6 6.3 %fusion.85 = (f32[3,256,2,1021]{3,1,2,0:T(8,128)}, f32[3,256,2,1021]{3,1,2,0:T(8,128)}) fusion(bf16[3,256,8,1024]{3,1,2,0:T(8,128)(2,1)S(1)} %bitcast.48), kind=kLoop, calls=%fused_computation.123 | loop fusion | bytes 25092096 | tf_op jit(solution)/shard_map/jit(_roll_static)/slice | solution.py:37
  251.9 1.4 fusion.86
  253.3 14.4 %pad_maximum_fusion = (f32[6,259,2,1024]{3,1,2,0:T(8,128)}, f32[6,259,2,1024]{3,1,2,0:T(8,128)}) fusion(f32[6,3,2,1024]{3,1,2,0:T(4,128)S(1)} %collective-permute-done, f32[3,256,2,1024]{3,1,2,0:T(8,128)} %copy-done.1, f32[3,256,2,1024]{3,1,2,0:T(8,128)S(1)} %bitcast.50, f32[6,3,2,1024]{3,1,2,0:T(4,128)S(1)} %collective-permute-done.1), kind=kLoop, calls=%fused_computation.1 | loop fusion | flops 12730368 | bytes 38338560 | tf_op jit(solution)/shard_map/concatenate | solution.py:23
  267.7 37.4 %fusion.92 = (bf16[6,256,2,1024]{3,1,2,0:T(8,128)(2,1)}, f32[6,256,2,1024]{3,1,2,0:T(8,128)}) fusion(f32[256,256]{0,1:T(8,128)} %copy-done.2, f32[6,259,2,1024]{3,1,2,0:T(8,128)} %get-tuple-element.38, f32[6,259,2,1024]{3,1,2,0:T(8,128)} %get-tuple-element.37), kind=kOutput, calls=%fused_computation.130 | convolution fusion | flops 9682550784 | bytes 69468160 | tf_op jit(solution)/shard_map/ij,cjzy->cizy/dot_general | solution.py:93
  306.2 3.9 collective-permute-start.3
  310.0 2.5 fusion.84
  312.5 3.4 collective-permute-done.2
  315.9 1.3 fusion.69
  317.3 12.4 %multiply_subtract_fusion = f32[6,256,2,1024]{3,1,2,0:T(8,128)} fusion(f32[6,256,2,1024]{3,1,2,0:T(8,128)} %get-tuple-element.46, f32[6,2,1024]{2,1,0:T(2,128)S(1)} %get-tuple-element.47, f32[256]{0:T(256)S(1)} %bitcast.52, f32[6,2,1024]{2,1,0:T(2,128)S(1)} %get-tuple-element.48, f32[256]{0:T(256)S(1)} %bitcast.51), kind=kLoop, calls=%fused_computation.13 | loop fusion | flops 15728640 | bytes 25266176 | tf_op jit(solution)/shard_map/sub | solution.py:107
  329.7 73.8 %fusion.17 = f32[1,3,256,2,1024]{4,2,3,1,0:T(8,128)S(1)} fusion(f32[6,259,2,1024]{3,1,2,0:T(8,128)} %get-tuple-element.38, f32[6,259,2,1024]{3,1,2,0:T(8,128)} %get-tuple-element.37, f32[3,256,8,1024]{3,1,2,0:T(8,128)} %convert_element_type.24, f32[6,256,2,1024]{3,1,2,0:T(8,128)} %multiply_subtract_fusion, f32[3,256,2,1]{3,1,2,0:T(8,128)} %get-tuple-element.34, ...), kind=kLoop, calls=%fused_computation.23 | loop fusion | flops 141557760 | bytes 226492416 | tf_op jit(solution)/shard_map/broadcast_in_dim | solution.py:142
  403.5 7.6 %copy.9 = f32[1,3,256,2,1024]{4,3,2,1,0:T(2,128)} copy(f32[1,3,256,2,1024]{4,2,3,1,0:T(8,128)S(1)} %fusion.17) | data formatting | bytes 12582912 | tf_op jit(solution)/shard_map/broadcast_in_dim | solution.py:142
  (33 shorter events, 1.9 us)
Async XLA Ops:
  6.5 199.4 %all-reduce.2.cloned.1.call-start = ((), (), s32[]{:S(2)}) async-start(), calls=%async_computation | async-start | bytes 25165824 | tf_op jit(solution)/shard_map/psum | solution.py:29
  52.8 15.3 %copy-start = (f32[1,3,256,8,1024]{4,2,3,1,0:T(8,128)}, f32[1,3,256,8,1024]{4,2,3,1,0:T(8,128)S(1)}, u32[]{:S(2)}) copy-start(f32[1,3,256,8,1024]{4,2,3,1,0:T(8,128)S(1)} %copy.20) | copy-start | bytes 75497472
  52.8 10.2 %copy-start.3 = (f32[64]{0:T(128)S(1)}, f32[64]{0:T(128)}, u32[]{:S(2)}) copy-start(f32[64]{0:T(128)} %param.9) | copy-start | bytes 772
  59.2 4.5 %copy-start.2 = (f32[256,256]{0,1:T(8,128)}, f32[256,256]{0,1:T(8,128)S(1)}, u32[]{:S(2)}) copy-start(f32[256,256]{0,1:T(8,128)S(1)} %fusion.47) | copy-start | bytes 786436
  205.9 11.2 %slice-start = ((s8[12582912]{0:T(1024)(128)(4,1)}), s8[4194304]{0:T(1024)(128)(4,1)S(1)}, s32[]{:S(2)}) async-start(s8[12582912]{0:T(1024)(128)(4,1)} %bitcast.47), calls=%async_computation.1 | async-start | bytes 8388608
  205.9 11.2 %slice-start.1 = ((s8[12582912]{0:T(1024)(128)(4,1)}), s8[4194304]{0:T(1024)(128)(4,1)S(1)}, s32[]{:S(2)}) async-start(s8[12582912]{0:T(1024)(128)(4,1)} %bitcast.47), calls=%async_computation.2 | async-start | bytes 8388608
  208.7 4.5 %copy-start.1 = (f32[3,256,2,1024]{3,1,2,0:T(8,128)}, f32[3,256,2,1024]{3,1,2,0:T(8,128)S(1)}, u32[]{:S(2)}) copy-start(f32[3,256,2,1024]{3,1,2,0:T(8,128)S(1)} %slice.349) | copy-start | bytes 18874372
  208.7 8.4 %slice-start.2 = ((s8[12582912]{0:T(1024)(128)(4,1)}), s8[4194304]{0:T(1024)(128)(4,1)S(1)}, s32[]{:S(2)}) async-start(s8[12582912]{0:T(1024)(128)(4,1)} %bitcast.47), calls=%async_computation.3 | async-start | bytes 8388608
  213.2 40.1 %collective-permute-start = (f32[6,3,2,1024]{3,1,2,0:T(4,128)}, f32[6,3,2,1024]{3,1,2,0:T(4,128)S(1)}, u32[]{:S(2)}, u32[]{:S(2)}) collective-permute-start(f32[6,3,2,1024]{3,1,2,0:T(4,128)} %get-tuple-element.39), channel_id=1, source_target_pairs={{1,0},{2,1},{3,2},{0,3},{5,4},{6,5},{7,6},{4,7},{9,8},{10,9},{11,1... | collective-permute-start | bytes 442376 | tf_op jit(solution)/shard_map/ppermute | solution.py:22
  217.1 36.2 %collective-permute-start.1 = (f32[6,3,2,1024]{3,1,2,0:T(4,128)}, f32[6,3,2,1024]{3,1,2,0:T(4,128)S(1)}, u32[]{:S(2)}, u32[]{:S(2)}) collective-permute-start(f32[6,3,2,1024]{3,1,2,0:T(4,128)} %get-tuple-element.40), channel_id=1, source_target_pairs={{0,1},{1,2},{2,3},{3,0},{4,5},{5,6},{6,7},{7,4},{8,9},{9,10},{10,1... | collective-permute-start | bytes 442376 | tf_op jit(solution)/shard_map/ppermute | solution.py:21
  239.3 14.0 %slice-start.3 = ((s8[6291456]{0:T(1024)(128)(4,1)}), s8[4194304]{0:T(1024)(128)(4,1)S(1)}, s32[]{:S(2)}) async-start(s8[6291456]{0:T(1024)(128)(4,1)} %bitcast.49), calls=%async_computation.4 | async-start | bytes 8388608
  245.6 7.6 %slice-start.4 = ((s8[6291456]{0:T(1024)(128)(4,1)}), s8[2097152]{0:T(1024)(128)(4,1)S(1)}, s32[]{:S(2)}) async-start(s8[6291456]{0:T(1024)(128)(4,1)} %bitcast.49), calls=%async_computation.5 | async-start | bytes 4194304
  306.2 6.4 %collective-permute-start.3 = (bf16[6,1,2,1024]{3,1,2,0:T(2,128)(2,1)S(1)}, bf16[6,1,2,1024]{3,1,2,0:T(2,128)(2,1)S(1)}, u32[]{:S(2)}, u32[]{:S(2)}) collective-permute-start(bf16[6,1,2,1024]{3,1,2,0:T(2,128)(2,1)S(1)} %get-tuple-element.42), channel_id=1, source_target_pairs={{1,0},{2,1},{3,2},{0,3},{5,4},{6,5},{7,6},{4,7},{9,8},{10,9},{11,1... | collective-permute-start | bytes 73736 | tf_op jit(solution)/shard_map/ppermute | solution.py:22
  310.0 5.9 %collective-permute-start.2 = (bf16[6,1,2,1024]{3,1,2,0:T(2,128)(2,1)S(1)}, bf16[6,1,2,1024]{3,1,2,0:T(2,128)(2,1)S(1)}, u32[]{:S(2)}, u32[]{:S(2)}) collective-permute-start(bf16[6,1,2,1024]{3,1,2,0:T(2,128)(2,1)S(1)} %get-tuple-element.41), channel_id=1, source_target_pairs={{0,1},{1,2},{2,3},{3,0},{4,5},{5,6},{6,7},{7,4},{8,9},{9,10},{10,1... | collective-permute-start | bytes 73736 | tf_op jit(solution)/shard_map/ppermute | solution.py:21
Sparse Core Ops, SparseCore 0:
  30.9 174.9 all-reduce.1
where the time goes:
time: 424 us; the launch traced here: 418 us
  other arithmetic  139 us (33%)
  local copies, waits for them, and re-layouts  110 us (26%)
  waiting for transfers between devices  105 us (25%)
  matrix products  40 us (9%)
  between operations  16.9 us (4%)
  starting transfers between devices  7.74 us (2%)
    psum x1, waiting for transfers between devices, broadcast(): return lax.psum(kept, axis)  101 us
    broadcast_in_dim x1, other arithmetic, per_device(): return updated[None]  73.8 us
    slice x6, local copies, waits for them, and re-layouts, first_across(): jnp.roll(values, -offset_cells, axis_number)  38.2 us
    dot_general x1, matrix products, along_terms(): jnp.einsum('ij,cjzy->cizy', inverse, compact_rhs, precision=lax.Precision...  37.4 us
    slice x6, local copies, waits for them, and re-layouts, first_across(): jnp.roll(values, offset_cells, axis_number)  24.1 us
    select_n x1, other arithmetic, broadcast(): jnp.where(lax.axis_index(axis) == source, value, 0).astype(value.dtype)  23.5 us
    unnamed x20, local copies, waits for them, and re-layouts  22.1 us
    concatenate x1, other arithmetic, extended(): array = jnp.concatenate([before, array, after], axis=dim)  14.4 us
  transfers between devices with their start and end apart: 5, of which 2 were waited for; matrix products, arithmetic and copies ran while one was open for 26% of the time, Pallas kernels for 0%

commit v1 on v0

v1 whole, which is shorter than its diff:
```python
import functools

import jax
import jax.numpy as jnp
import numpy as np
from jax import lax
from jax.experimental import pallas as pl
from jax.experimental.pallas import tpu as pltpu
from jax.sharding import PartitionSpec as P

section_step = 0.25
reach = 16
code_scale = 4096.0
phases = 2
streams = ((0, 3), (1, 2))


def compact_kernel(length):
    wave = 2.0 * np.pi * np.arange(length) / length
    symbol = 14.0 / 9.0 * np.sin(wave) + 1.0 / 18.0 * np.sin(2.0 * wave)
    symbol = 1j * symbol / (1.0 + 2.0 / 3.0 * np.cos(wave))
    return np.real(np.fft.ifft(symbol))


def along_matrices(rows, length):
    kernel = compact_kernel(length)
    first = np.zeros((rows, rows + 2 * reach))
    second = np.zeros((rows, rows + 2 * reach))
    for i in range(rows):
        for k in range(-reach, reach + 1):
            first[i, i + reach + k] = kernel[-k % length]
        for k, weight in ((0, -980.0), (1, 270.0), (2, -27.0), (3, 2.0)):
            second[i, i + reach + k] = weight
            second[i, i + reach - k] = weight
    high = first.astype(jnp.bfloat16)
    low = (first - high.astype(np.float64)).astype(jnp.bfloat16)
    return high, low, second.astype(jnp.bfloat16)


first_taps = ((1, 45.0), (2, -9.0), (3, 1.0))
second_taps = ((0, -490.0), (1, 270.0), (2, -27.0), (3, 2.0))


def depth_matrix(rows, planes, fields):
    matrix = np.zeros((len(fields) * rows, rows * planes))
    for f, taps in enumerate(fields):
        for i in range(rows):
            for z, weight in taps:
                matrix[f * rows + i, i * planes + z] += weight
    return matrix.astype(jnp.bfloat16)


def first_at(z):
    return [(z + k, w) for k, w in first_taps] + [(z - k, -w) for k, w in first_taps]


def second_at(z):
    taps = [(z + k, w) for k, w in second_taps]
    return taps + [(z - k, w) for k, w in second_taps if k > 0]


def product(a, b):
    return jnp.dot(a, b, preferred_element_type=jnp.float32)


def split(values):
    high = values.astype(jnp.bfloat16)
    return high, (values - high.astype(jnp.float32)).astype(jnp.bfloat16)


def shifted_pairs(values):
    width = values.shape[-1]
    return [
        (pltpu.roll(values, width - k, 1), pltpu.roll(values, k, 1)) for k in (1, 2, 3)
    ]


def first_across(pairs):
    (u1, d1), (u2, d2), (u3, d3) = pairs
    return 0.75 * (u1 - d1) - 0.15 * (u2 - d2) + (1.0 / 60.0) * (u3 - d3)


def pack_kernel(weights, tile, coded):
    rows = coded.shape[2]
    mixed = product(weights[...], tile[0])
    for f in range(4):
        scale = code_scale if f < 2 else code_scale / 60.0
        part = jnp.round(mixed[f * rows : (f + 1) * rows] * scale)
        coded[0, f] = part.astype(jnp.int32).astype(jnp.int16)


def pack(tile, planes, x_rows):
    comps, deep, width = tile.shape
    slab = deep // planes
    ghost = [[t for t in first_at(z) if t[0] not in (3, 4)] for z in (3, 4)]
    weights = depth_matrix(x_rows, planes, [[(3, 1.0)], [(4, 1.0)]] + ghost)
    return pl.pallas_call(
        pack_kernel,
        out_shape=jax.ShapeDtypeStruct((comps, 4, slab, width), jnp.int16),
        grid=(comps, slab // x_rows),
        in_specs=[
            pl.BlockSpec(weights.shape, lambda c, i: (0, 0)),
            pl.BlockSpec((1, x_rows * planes, width), lambda c, i: (c, i, 0)),
        ],
        out_specs=pl.BlockSpec((1, 4, x_rows, width), lambda c, i: (c, 0, i, 0)),
        cost_estimate=pl.CostEstimate(
            flops=0, bytes_accessed=4 * comps * deep * width, transcendentals=0
        ),
    )(jnp.asarray(weights), tile)


def unpack_kernel(viscosity, weights, field, inner, depth, partial):
    rows = inner.shape[2]
    high, low = split(field[0])
    mixed = product(weights[...], high) + product(weights[...], low)
    gain = viscosity[0] * (section_step / 180.0)
    for p in range(2):
        value = mixed[p * rows : (p + 1) * rows]
        inner[0, p] = value
        depth[0, p] = mixed[(2 + p) * rows : (3 + p) * rows] * (1.0 / 60.0)
        partial[0, p] = value + gain * mixed[(4 + p) * rows : (5 + p) * rows]


def unpack(field, viscosity, planes, x_rows):
    comps, deep, width = field.shape
    slab = deep // planes
    fields = [[(3, 1.0)], [(4, 1.0)], first_at(3), first_at(4), second_at(3), second_at(4)]
    weights = depth_matrix(x_rows, planes, fields)
    shape = jax.ShapeDtypeStruct((comps, 2, slab, width), jnp.float32)
    spec = pl.BlockSpec((1, 2, x_rows, width), lambda c, i: (c, 0, i, 0))
    return pl.pallas_call(
        unpack_kernel,
        out_shape=(shape,) * 3,
        grid=(comps, slab // x_rows),
        in_specs=[
            pl.BlockSpec(memory_space=pltpu.SMEM),
            pl.BlockSpec(weights.shape, lambda c, i: (0, 0)),
            pl.BlockSpec((1, x_rows * planes, width), lambda c, i: (c, i, 0)),
        ],
        out_specs=(spec,) * 3,
        cost_estimate=pl.CostEstimate(
            flops=0, bytes_accessed=7 * comps * deep * width, transcendentals=0
        ),
    )(viscosity, jnp.asarray(weights), field)


def along_kernel(
    viscosity, m_top, m_low, inner, before, after, partial, along, across, sums, high_s, low_s, curve_s
):
    slab = inner.shape[2]
    rows = m_low.shape[0]

    def place(start, values):
        high, low = split(values)
        high_s[pl.ds(start, values.shape[0]), :] = high
        low_s[pl.ds(start, values.shape[0]), :] = low

    place(0, before[0, 0])
    place(reach + slab, after[0, 0])

    def fill(i, carry):
        start = pl.multiple_of(i * 32, 32)
        high, low = split(inner[0, 0, pl.ds(start, 32), :])
        at = pl.multiple_of(start + reach, 16)
        high_s[pl.ds(at, 32), :] = high
        low_s[pl.ds(at, 32), :] = low
        return carry

    lax.fori_loop(0, slab // 32, fill, 0)
    for b in range(slab // rows):
        window = pl.ds(b * rows, rows + 2 * reach)
        high, low = high_s[window, :], low_s[window, :]
        both = product(m_top[...], high) + product(m_top[...], low)
        along[0, 0, b * rows : (b + 1) * rows] = both[:rows] + product(m_low[...], high)
        curve_s[b * rows : (b + 1) * rows] = both[rows:]
    gain = viscosity[0] * section_step
    gain_along = viscosity[0] * (section_step / 180.0)

    def body(i, carry):
        at = pl.ds(pl.multiple_of(i * 16, 16), 16)
        pairs = shifted_pairs(inner[0, 0, at, :])
        across[0, 0, at, :] = first_across(pairs)
        (u1, d1), (u2, d2), (u3, d3) = pairs
        curve = 1.5 * (u1 + d1) - 0.15 * (u2 + d2) + (1.0 / 90.0) * (u3 + d3)
        sums[0, 0, at, :] = partial[0, 0, at, :] + gain * curve + gain_along * curve_s[at, :]
        return carry

    lax.fori_loop(0, slab // 16, body, 0)


def along_across(inner, before, after, partial, viscosity, length):
    comps, pair, slab, width = inner.shape
    rows = min(slab, 128)
    high, low, second = along_matrices(rows, length)
    top = np.concatenate([high, second], 0)
    shape = jax.ShapeDtypeStruct(inner.shape, jnp.float32)
    spec = pl.BlockSpec((1, 1, slab, width), lambda c, p: (c, p, 0, 0))
    rim = pl.BlockSpec((1, 1, reach, width), lambda c, p: (c, p, 0, 0))
    return pl.pallas_call(
        along_kernel,
        out_shape=(shape,) * 3,
        grid=(comps, pair),
        in_specs=[
            pl.BlockSpec(memory_space=pltpu.SMEM),
            pl.BlockSpec(top.shape, lambda c, p: (0, 0)),
            pl.BlockSpec(low.shape, lambda c, p: (0, 0)),
            spec,
            rim,
            rim,
            spec,
        ],
        out_specs=(spec,) * 3,
        scratch_shapes=[
            pltpu.VMEM((slab + 2 * reach, width), jnp.bfloat16),
            pltpu.VMEM((slab + 2 * reach, width), jnp.bfloat16),
            pltpu.VMEM((slab, width), jnp.float32),
        ],
        cost_estimate=pl.CostEstimate(
            flops=0, bytes_accessed=5 * 4 * inner.size, transcendentals=0
        ),
    )(viscosity, jnp.asarray(top), jnp.asarray(low), inner, before, after, partial)


def final_kernel(
    m_both, base, ghost, before, after, inner, along, across, depth, sums, out, base_s, slope_s
):
    step = pl.program_id(0)
    rows = inner.shape[2]
    slab = base.shape[2]
    inverse = 1.0 / code_scale

    def decoded(values):
        return values.astype(jnp.int32).astype(jnp.float32) * inverse

    @pl.when(step == 0)
    def _():
        for c in range(3):
            for p in range(2):
                base_s[c, p, 0:reach] = decoded(before[c, p]).astype(jnp.bfloat16)
                base_s[c, p, reach + slab :] = decoded(after[c, p]).astype(jnp.bfloat16)

                def fill(i, carry):
                    start = pl.multiple_of(i * 16, 16)
                    to = pl.multiple_of(start + reach, 16)
                    values = decoded(base[c, p, pl.ds(start, 16), :])
                    base_s[c, p, pl.ds(to, 16), :] = values.astype(jnp.bfloat16)
                    return carry

                lax.fori_loop(0, slab // 16, fill, 0)

    origin = pl.multiple_of(step * rows, 32)
    for c in range(3):
        for p in range(2):
            both = product(m_both[...], base_s[c, p, pl.ds(origin, rows + 2 * reach), :])
            slope_s[c, p] = both[:rows] + both[rows:]

    def body(i, carry):
        start = pl.multiple_of(i * 16, 16)
        at = pl.ds(start, 16)
        inside = pl.ds(pl.multiple_of(origin + reach + start, 16), 16)
        flow = [
            [base_s[c, p, inside, :].astype(jnp.float32) for p in range(2)] for c in range(3)
        ]
        for p in range(2):
            move = [inner[c, p, at, :] for c in range(3)]
            for c in range(3):
                dz = decoded(ghost[c, p, at, :])
                if p == 0:
                    dz = dz + 0.75 * flow[c][1]
                else:
                    dz = dz - 0.75 * flow[c][0]
                dy = first_across(shifted_pairs(flow[c][p]))
                total = flow[0][p] * along[c, p, at, :] + flow[1][p] * across[c, p, at, :]
                total = total + flow[2][p] * depth[c, p, at, :]
                total = total + move[0] * slope_s[c, p, at, :] + move[1] * dy + move[2] * dz
                out[0, c, at, p, :] = sums[c, p, at, :] - section_step * total
        return carry

    lax.fori_loop(0, rows // 16, body, 0)


def final(base, ghost, before, after, inner, along, across, depth, sums, length):
    comps, pair, slab, width = inner.shape
    rows = 32
    high, low, _ = along_matrices(rows, length)
    both = np.concatenate([high, low], 0)
    whole = pl.BlockSpec(base.shape, lambda i: (0, 0, 0, 0))
    rim = pl.BlockSpec(before.shape, lambda i: (0, 0, 0, 0))
    spec = pl.BlockSpec((comps, pair, rows, width), lambda i: (0, 0, i, 0))
    return pl.pallas_call(
        final_kernel,
        out_shape=jax.ShapeDtypeStruct((1, comps, slab, pair, width), jnp.float32),
        grid=(slab // rows,),
        in_specs=[pl.BlockSpec(both.shape, lambda i: (0, 0)), whole, spec, rim, rim] + [spec] * 5,
        out_specs=pl.BlockSpec((1, comps, rows, pair, width), lambda i: (0, 0, i, 0, 0)),
        scratch_shapes=[
            pltpu.VMEM((comps, pair, slab + 2 * reach, width), jnp.bfloat16),
            pltpu.VMEM((comps, pair, rows, width), jnp.float32),
        ],
        cost_estimate=pl.CostEstimate(
            flops=0, bytes_accessed=7 * 4 * inner.size, transcendentals=0
        ),
    )(jnp.asarray(both), base, ghost, before, after, inner, along, across, depth, sums)


def rims(array, axis_number):
    size = lax.axis_size("gx")
    length = array.shape[axis_number]
    up = [(i, (i + 1) % size) for i in range(size)]
    down = [(j, i) for i, j in up]
    last = lax.slice_in_dim(array, length - reach, length, axis=axis_number)
    first = lax.slice_in_dim(array, 0, reach, axis=axis_number)
    return lax.ppermute(last, "gx", up), lax.ppermute(first, "gx", down)


def swap(array, bit):
    return lax.ppermute(array, "pert", [(i, i ^ bit) for i in range(lax.axis_size("pert"))])


def spread(coded, root):
    me = lax.axis_index("pert")
    if lax.axis_size("pert") != 8:
        kept = jnp.where(me == root, coded, 0).astype(jnp.float32)
        return lax.psum(kept, "pert").astype(jnp.int16)
    comps, _, slab, width = coded.shape
    quarter = slab // 4
    core = me % 2
    is_root = me == root
    place = (me // 2) ^ (root // 2)
    at_a, at_b, at_c = place == 0, place == 1, place == 2

    def cut(which, fields):
        parts = [coded[:, f, q * quarter : (q + 1) * quarter] for f in fields for q in streams[which]]
        return jnp.stack(parts, 0)

    halves = [[cut(u, (0, 1)), cut(u, (2, 3))] for u in range(2)]
    mine = [jnp.where(core == 0, h[0], h[1]) for h in halves]
    theirs = [swap(jnp.where(core == 0, h[1], h[0]), 1) for h in halves]
    source = [jnp.where(is_root, mine[u], theirs[u]) for u in range(2)]
    sent_x = [[], []]
    sent_y = [[], []]
    for s in range(phases + 1):
        for u in range(2):
            k = min(s, phases - 1)
            one, two = source[u][k], source[u][phases + k]
            if s == phases:
                one, two = two, one
            if s > 0:
                one = jnp.where(at_a, one, sent_y[u][s - 1])
                two = jnp.where(at_a, two, sent_x[u][s - 1])
            sent_x[u].append(swap(one, 2))
            sent_y[u].append(swap(two, 4))
    pieces = {}
    for u in range(2):
        X, Y, S = sent_x[u], sent_y[u], source[u]
        parts = []
        for h in range(2):
            P1, P2 = (X, Y) if h == 0 else (Y, X)
            near, far = (at_b, at_c) if h == 0 else (at_c, at_b)
            for k in range(phases):
                late = P1[k + 2] if k + 2 <= phases else P2[phases]
                value = jnp.where(near, P1[k], jnp.where(far, late, P2[k + 1]))
                parts.append(jnp.where(at_a, S[h * phases + k], value))
        held = jnp.stack(parts, 0)
        other = swap(held, 1)
        flow = jnp.where(core == 0, held, other)
        ghost = jnp.where(core == 0, other, held)
        for h in range(2):
            for k, q in enumerate(streams[u]):
                pieces[h, q] = flow[h * phases + k]
                pieces[2 + h, q] = ghost[h * phases + k]
    return jnp.stack(
        [jnp.concatenate([pieces[f, q] for q in range(4)], 1) for f in range(4)], 1
    )


def per_device(pert_field, base_store, section_owner, pert_ids, member_visc):
    _, comps, slab, planes, width = pert_field.shape
    length = slab * lax.axis_size("gx")
    member_pick = pert_ids[0] == jnp.arange(member_visc.shape[0], dtype=jnp.int32)
    viscosity = jnp.sum(jnp.where(member_pick, member_visc, 0.0))[None]
    levels_here = base_store.shape[0]
    owner_slot = section_owner[0] % levels_here
    owner_root = section_owner[0] // levels_here
    tiles = base_store.reshape(levels_here, comps, slab * planes, width)
    tile = tiles[0] if levels_here == 1 else lax.dynamic_index_in_dim(tiles, owner_slot, 0, False)
    coded = pack(tile, planes, 32)
    field = pert_field.reshape(comps, slab * planes, width)
    inner, depth, partial = unpack(field, viscosity, planes, 32)
    before, after = rims(inner, 2)
    along, across, sums = along_across(inner, before, after, partial, viscosity, length)
    arrived = spread(coded, owner_root)
    base, ghost = arrived[:, :2], arrived[:, 2:]
    base_before, base_after = rims(base, 2)
    return final(
        base, ghost, base_before, base_after, inner, along, across, depth, sums, length
    )


def solution(mesh):
    placed = (
        P("pert", None, "gx", None, None),
        P("pert", None, "gx", None, None),
        P(),
        P("pert"),
        P(),
    )
    return jax.shard_map(
        per_device,
        mesh=mesh,
        in_specs=placed,
        out_specs=P("pert", None, "gx", None, None),
        check_vma=False,
    )
```

time: 424 us -> 225 us (0.53)
  other arithmetic: 139 us -> 26.2 us
  local copies, waits for them, and re-layouts: 110 us -> 13.5 us
  Pallas kernels: 0 us -> 95.8 us
  waiting for transfers between devices: 105 us -> 61.8 us
  matrix products: 40 us -> 0 us
  starting transfers between devices: 7.74 us -> 24 us
  between operations: 16.9 us -> 1.85 us
    psum x1 -> x0, waiting for transfers between devices: 101 us -> none  [broadcast(): return lax.psum(kept, axis)]
    pallas_call x0 -> x4, Pallas kernels: none -> 95.8 us  [the longest x1 28 us: along_across(): pl.pallas_call(along_kernel, out_shape=(shape,) * 3, grid=(comps, pair),...]
    broadcast_in_dim x1 -> x0, other arithmetic: 73.8 us -> none  [per_device(): return updated[None]]
    slice x17 -> x1, local copies, waits for them, and re-layouts: 71.3 us -> 1.17 us  [rims(): first = lax.slice_in_dim(array, 0, reach, axis=axis_number)]
    ppermute x4 -> x20, waiting for transfers between devices: 3.39 us -> 61.8 us  [the longest x16 40.2 us: swap(): lax.ppermute(array, 'pert', [(i, i ^ bit) for i in range(lax.axis_size('p...]
    dot_general x2 -> x0, matrix products: 40 us -> none  [the longest x1 37.4 us: along_terms(): jnp.einsum('ij,cjzy->cizy', inverse, compact_rhs, precision=lax.Precision...]
    unnamed x20 -> x72, local copies, waits for them, and re-layouts: 22.1 us -> 3.76 us
    ppermute x4 -> x20, starting transfers between devices: 7.74 us -> 24 us  [the longest x16 18.7 us: swap(): lax.ppermute(array, 'pert', [(i, i ^ bit) for i in range(lax.axis_size('p...]
  transfers between devices with their start and end apart: 5 -> 20, of which waited for: 2 -> 14; matrix products, arithmetic and copies ran while one was open for 26% -> 13% of each run, Pallas kernels for 0% -> 25%
where the time goes in v1:
time: 225 us; the launch traced here: 223 us
  Pallas kernels  95.8 us (43%)
  waiting for transfers between devices  61.8 us (27%)
  other arithmetic  26.2 us (12%)
  starting transfers between devices  24 us (11%)
  local copies, waits for them, and re-layouts  13.5 us (6%)
    ppermute x16, waiting for transfers between devices, swap(): lax.ppermute(array, 'pert', [(i, i ^ bit) for i in range(lax.axis_size('p...  40.2 us
    pallas_call x1, Pallas kernels, along_across(): pl.pallas_call(along_kernel, out_shape=(shape,) * 3, grid=(comps, pair),...  28 us
    pallas_call x1, Pallas kernels, unpack(): pl.pallas_call(unpack_kernel, out_shape=(shape,) * 3, grid=(comps, slab /...  27.9 us
    ppermute x4, waiting for transfers between devices, rims(): return (lax.ppermute(last, 'gx', up), lax.ppermute(first, 'gx', down))  21.7 us
    pallas_call x1, Pallas kernels, final(): pl.pallas_call(final_kernel, out_shape=jax.ShapeDtypeStruct((1, comps, sl...  21.6 us
    ppermute x16, starting transfers between devices, swap(): lax.ppermute(array, 'pert', [(i, i ^ bit) for i in range(lax.axis_size('p...  18.7 us
    pallas_call x1, Pallas kernels, pack(): pl.pallas_call(pack_kernel, out_shape=jax.ShapeDtypeStruct((comps, 4, sla...  18.3 us
    another operation x6, other arithmetic, spread(): held = jnp.stack(parts, 0)  6.8 us
  transfers between devices with their start and end apart: 20, of which 14 were waited for; matrix products, arithmetic and copies ran while one was open for 13% of the time, Pallas kernels for 25%

profile of v1, /device:TPU:0, one launch (start us, length us, event | category | flops | bytes accessed | tf_op | source)
XLA Modules:
  0.0 223.2 jit_solution(13038284039264906068)
XLA Ops:
  0.0 18.3 %shard_map.100 = s16[3,4,256,1024]{3,2,1,0:T(8,128)(2,1)} custom-call(bf16[128,256]{1,0:T(8,128)(2,1)} %constant.59.clone.weights, bf16[3,2048,1024]{2,1,0:T(8,128)(2,1)} %bitcast.182), custom_call_target="tpu_custom_call" | custom-call | bytes 25165824 | tf_op jit(solution)/shard_map/pallas_call | solution.py:97
  18.3 3.6 %slice_bitcast_fusion.26 = (s16[1,3,64,1024]{3,2,1,0:T(8,128)(2,1)S(1)}, s16[1,3,64,1024]{3,2,1,0:T(8,128)(2,1)S(1)}, s16[1,3,64,1024]{3,2,1,0:T(8,128)(2,1)S(1)...) fusion(s16[3,4,256,1024]{3,2,1,0:T(8,128)(2,1)} %shard_map.100), kind=kLoop, calls=%fused_computation.50 | loop fusion | bytes 12582912 | tf_op jit(solution)/shard_map/stack;squeeze | solution.py:334
  24.0 1.5 broadcast_select_fusion.3
  26.7 2.4 %select_select_fusion.1 = s16[4,3,64,1024]{3,2,1,0:T(8,128)(2,1)S(1)} fusion(s16[4,3,64,1024]{3,2,1,0:T(8,128)(2,1)} %collective-permute-done, pred[]{:T(512)S(6)} %eq.32, pred[]{:T(512)S(6)} %eq.30, s16[1,3,64,1024]{3,2,1,0:T(8,128)(2,1)S(1)} %get-tuple-element.26, s16[1,3,64,1024]{3,2,1,0:T(8,128)(2,1)S(1)} %get-tuple-element.27, ...), kind=kLoop, calls=%fused_computation.17 | loop fusion | flops 6291456 | bytes 6291458 | tf_op jit(solution)/shard_map/jit(_where)/select_n | solution.py:339
  30.1 2.9 %collective-permute-start.1 = (s16[3,64,1024]{2,1,0:T(8,128)(2,1)}, s16[3,64,1024]{2,1,0:T(8,128)(2,1)}, u32[]{:S(2)}, u32[]{:S(2)}) collective-permute-start(s16[3,64,1024]{2,1,0:T(8,128)(2,1)} %get-tuple-element.70), channel_id=1, source_target_pairs={{0,8},{4,12},{8,0},{12,4},{16,24},{20,28},{24,16},{28,20},{1,9},{5... | collective-permute-start | bytes 1179656 | tf_op jit(solution)/shard_map/ppermute | solution.py:317
  33.0 2.1 select_select_fusion
  36.6 6.6 %collective-permute-done.1 = s16[3,64,1024]{2,1,0:T(8,128)(2,1)} collective-permute-done((s16[3,64,1024]{2,1,0:T(8,128)(2,1)}, s16[3,64,1024]{2,1,0:T(8,128)(2,1)}, u32[]{:S(2)}, u32[]{:S(2)}) %collective-permute-start.1) | collective-permute-done | bytes 393248 | tf_op jit(solution)/shard_map/ppermute | solution.py:317
  44.3 2.2 collective-permute-start.2
  46.5 4.5 %collective-permute-done.9 = s16[3,64,1024]{2,1,0:T(8,128)(2,1)S(1)} collective-permute-done((s16[3,64,1024]{2,1,0:T(8,128)(2,1)}, s16[3,64,1024]{2,1,0:T(8,128)(2,1)S(1)}, u32[]{:S(2)}, u32[]{:S(2)}) %collective-permute-start.9) | collective-permute-done | bytes 393248 | tf_op jit(solution)/shard_map/ppermute | solution.py:317
  51.9 1.8 collective-permute-start.10
  58.7 5.6 %collective-permute-done.10 = s16[3,64,1024]{2,1,0:T(8,128)(2,1)} collective-permute-done((s16[3,64,1024]{2,1,0:T(8,128)(2,1)}, s16[3,64,1024]{2,1,0:T(8,128)(2,1)}, u32[]{:S(2)}, u32[]{:S(2)}) %collective-permute-start.10) | collective-permute-done | bytes 393248 | tf_op jit(solution)/shard_map/ppermute | solution.py:317
  65.4 1.8 collective-permute-start.11
  67.2 5.5 %collective-permute-done.4 = s16[3,64,1024]{2,1,0:T(8,128)(2,1)} collective-permute-done((s16[3,64,1024]{2,1,0:T(8,128)(2,1)}, s16[3,64,1024]{2,1,0:T(8,128)(2,1)}, u32[]{:S(2)}, u32[]{:S(2)}) %collective-permute-start.4) | collective-permute-done | bytes 393248 | tf_op jit(solution)/shard_map/ppermute | solution.py:317
  72.7 1.8 select_bitcast_fusion.7
  74.5 1.8 collective-permute-start.5
  76.3 3.5 %collective-permute-done.12 = s16[3,64,1024]{2,1,0:T(8,128)(2,1)S(1)} collective-permute-done((s16[3,64,1024]{2,1,0:T(8,128)(2,1)}, s16[3,64,1024]{2,1,0:T(8,128)(2,1)S(1)}, u32[]{:S(2)}, u32[]{:S(2)}) %collective-permute-start.12) | collective-permute-done | bytes 393248 | tf_op jit(solution)/shard_map/ppermute | solution.py:317
  79.8 1.6 select_bitcast_fusion.3
  81.4 1.5 collective-permute-start.13
  85.2 6.6 %collective-permute-done.13 = s16[3,64,1024]{2,1,0:T(8,128)(2,1)S(1)} collective-permute-done((s16[3,64,1024]{2,1,0:T(8,128)(2,1)S(1)}, s16[3,64,1024]{2,1,0:T(8,128)(2,1)S(1)}, u32[]{:S(2)}, u32[]{:S(2)}) %collective-permute-start.13) | collective-permute-done | bytes 393248 | tf_op jit(solution)/shard_map/ppermute | solution.py:317
  95.0 6.3 %collective-permute-done.14 = s16[3,64,1024]{2,1,0:T(8,128)(2,1)S(1)} collective-permute-done((s16[3,64,1024]{2,1,0:T(8,128)(2,1)S(1)}, s16[3,64,1024]{2,1,0:T(8,128)(2,1)S(1)}, u32[]{:S(2)}, u32[]{:S(2)}) %collective-permute-start.14) | collective-permute-done | bytes 393248 | tf_op jit(solution)/shard_map/ppermute | solution.py:317
  104.4 27.9 %shard_map.101 = (f32[3,2,256,1024]{3,2,1,0:T(8,128)}, f32[3,2,256,1024]{3,2,1,0:T(8,128)}, f32[3,2,256,1024]{3,2,1,0:T(8,128)}) custom-call(f32[1]{0:T(128)} %bitcast.56.viscosity, bf16[192,256]{1,0:T(8,128)(2,1)} %constant.60.clone.weights, f32[3,2048,1024]{2,1,0:T(8,128)} %bitcast.181), custom_call_target="tpu_custom_call" | custom-call | bytes 44040192 | tf_op jit(solution)/shard_map/pallas_call | solution.py:131
  133.4 3.2 %collective-permute-start.19 = (f32[3,2,16,1024]{3,2,1,0:T(8,128)S(1)}, f32[3,2,16,1024]{3,2,1,0:T(8,128)S(1)}, u32[]{:S(2)}, u32[]{:S(2)}) collective-permute-start(f32[3,2,16,1024]{3,2,1,0:T(8,128)S(1)} %get-tuple-element.17), channel_id=1, source_target_pairs={{1,0},{2,1},{3,2},{0,3},{5,4},{6,5},{7,6},{4,7},{9,8},{10,9},{11,1... | collective-permute-start | bytes 1179656 | tf_op jit(solution)/shard_map/ppermute | solution.py:313
  136.6 9.5 %collective-permute-done.19.after = f32[3,2,16,1024]{3,2,1,0:T(8,128)S(1)} collective-permute-done((f32[3,2,16,1024]{3,2,1,0:T(8,128)S(1)}, f32[3,2,16,1024]{3,2,1,0:T(8,128)S(1)}, u32[]{:S(2)}, u32[]{:S(2)}) %collective-permute-start.19) | collective-permute-done | bytes 393248 | tf_op jit(solution)/shard_map/ppermute | solution.py:313
  146.1 8.9 %collective-permute-done.18.before = f32[3,2,16,1024]{3,2,1,0:T(8,128)S(1)} collective-permute-done((f32[3,2,16,1024]{3,2,1,0:T(8,128)S(1)}, f32[3,2,16,1024]{3,2,1,0:T(8,128)S(1)}, u32[]{:S(2)}, u32[]{:S(2)}) %collective-permute-start.18) | collective-permute-done | bytes 393248 | tf_op jit(solution)/shard_map/ppermute | solution.py:313
  155.7 28.0 %shard_map.102 = (f32[3,2,256,1024]{3,2,1,0:T(8,128)}, f32[3,2,256,1024]{3,2,1,0:T(8,128)}, f32[3,2,256,1024]{3,2,1,0:T(8,128)}) custom-call(f32[1]{0:T(128)} %bitcast.56.viscosity, bf16[256,160]{1,0:T(8,128)(2,1)} %constant.61.clone.m_top, bf16[128,160]{1,0:T(8,128)(2,1)} %constant.62.clone.m_low, f32[3,2,256,1024]{3,2,1,0:T(8,128)} %get-tuple-element.11.inner, ...), custom_call_target="tpu_custom_call" | custom-call | bytes 31457280 | tf_op jit(solution)/shard_map/pallas_call | solution.py:199
  183.8 2.3 %broadcast_select_fusion.1 = (s16[4,3,64,1024]{3,2,1,0:T(8,128)(2,1)S(1)}, s16[4,3,64,1024]{3,2,1,0:T(8,128)(2,1)S(1)}) fusion(s16[4,3,64,1024]{3,2,1,0:T(8,128)(2,1)} %collective-permute-done.7, pred[]{:T(512)S(6)} %eq.30, s16[1,3,64,1024]{3,2,1,0:T(8,128)(2,1)S(1)} %copy-done.5, s16[1,3,64,1024]{3,2,1,0:T(8,128)(2,1)S(1)} %copy-done.27, ...), kind=kLoop, calls=%fused_computation.19 | loop fusion | flops 3932160 | bytes 6291457 | tf_op jit(solution)/shard_map/jit(_where)/select_n | solution.py:367
  187.1 2.3 %broadcast_select_fusion = (s16[4,3,64,1024]{3,2,1,0:T(8,128)(2,1)S(1)}, s16[4,3,64,1024]{3,2,1,0:T(8,128)(2,1)S(1)}) fusion(s16[4,3,64,1024]{3,2,1,0:T(8,128)(2,1)} %collective-permute-done.15, pred[]{:T(512)S(6)} %eq.30, s16[1,3,64,1024]{3,2,1,0:T(8,128)(2,1)S(1)} %copy-done.1, s16[1,3,64,1024]{3,2,1,0:T(8,128)(2,1)S(1)} %get-tuple-element.44, ...), kind=kLoop, calls=%fused_computation.18 | loop fusion | flops 3932160 | bytes 6291457 | tf_op jit(solution)/shard_map/jit(_where)/select_n | solution.py:367
  190.1 1.8 collective-permute-start.17
  193.0 2.3 %copy.28.ghost = s16[3,2,256,1024]{3,2,1,0:T(8,128)(2,1)} copy(s16[3,2,256,1024]{3,2,0,1:T(8,128)(2,1)S(1)} %pad_add_fusion.1) | data formatting | bytes 6291456 | tf_op jit(solution)/shard_map/stack | solution.py:372
  195.3 2.2 pad_add_fusion.base
  198.1 2.8 %collective-permute-done.16.before = s16[3,2,16,1024]{3,2,1,0:T(8,128)(2,1)S(1)} collective-permute-done((s16[3,2,16,1024]{3,2,1,0:T(8,128)(2,1)S(1)}, s16[3,2,16,1024]{3,2,1,0:T(8,128)(2,1)S(1)}, u32[]{:S(2)}, u32[]{:S(2)}) %collective-permute-start.16) | collective-permute-done | bytes 196640 | tf_op jit(solution)/shard_map/ppermute | solution.py:313
  201.5 21.6 %shard_map.103 = f32[1,3,256,2,1024]{4,3,2,1,0:T(2,128)} custom-call(bf16[64,64]{1,0:T(8,128)(2,1)} %constant.63.clone.m_both, s16[3,2,256,1024]{3,2,1,0:T(8,128)(2,1)} %pad_add_fusion.base, s16[3,2,256,1024]{3,2,1,0:T(8,128)(2,1)} %copy.28.ghost, s16[3,2,16,1024]{3,2,1,0:T(8,128)(2,1)} %copy-done.34, s16[3,2,16,1024]{3,2,1,0:T(8,128)(2,1)} %copy-done.33, ...), custom_call_target="tpu_custom_call" | custom-call | bytes 44040192 | tf_op jit(solution)/shard_map/pallas_call | solution.py:290
  (117 shorter events, 26.9 us)
Async XLA Ops:
  23.1 3.6 %collective-permute-start = (s16[4,3,64,1024]{3,2,1,0:T(8,128)(2,1)S(1)}, s16[4,3,64,1024]{3,2,1,0:T(8,128)(2,1)}, u32[]{:S(2)}, u32[]{:S(2)}) collective-permute-start(s16[4,3,64,1024]{3,2,1,0:T(8,128)(2,1)S(1)} %broadcast_select_fusion.5), channel_id=1, source_target_pairs={{0,4},{4,0},{8,12},{12,8},{16,20},{20,16},{24,28},{28,24},{1,5},{5... | collective-permute-start | bytes 4718600 | tf_op jit(solution)/shard_map/ppermute | solution.py:317
  25.5 7.5 %collective-permute-start.8 = (s16[4,3,64,1024]{3,2,1,0:T(8,128)(2,1)}, s16[4,3,64,1024]{3,2,1,0:T(8,128)(2,1)}, u32[]{:S(2)}, u32[]{:S(2)}) collective-permute-start(s16[4,3,64,1024]{3,2,1,0:T(8,128)(2,1)} %broadcast_select_fusion.3), channel_id=1, source_target_pairs={{0,4},{4,0},{8,12},{12,8},{16,20},{20,16},{24,28},{28,24},{1,5},{5... | collective-permute-start | bytes 4718600 | tf_op jit(solution)/shard_map/ppermute | solution.py:317
  26.7 6.3 %copy-start.17 = (s16[1,3,64,1024]{3,2,1,0:T(8,128)(2,1)S(1)}, s16[1,3,64,1024]{3,2,1,0:T(8,128)(2,1)}, u32[]{:S(2)}) copy-start(s16[1,3,64,1024]{3,2,1,0:T(8,128)(2,1)} %copy-done.16) | copy-start | bytes 1179652
  26.7 6.3 %copy-start.19 = (s16[1,3,64,1024]{3,2,1,0:T(8,128)(2,1)S(1)}, s16[1,3,64,1024]{3,2,1,0:T(8,128)(2,1)}, u32[]{:S(2)}) copy-start(s16[1,3,64,1024]{3,2,1,0:T(8,128)(2,1)} %copy-done.18) | copy-start | bytes 1179652
  30.1 13.1 %collective-permute-start.1 = (s16[3,64,1024]{2,1,0:T(8,128)(2,1)}, s16[3,64,1024]{2,1,0:T(8,128)(2,1)}, u32[]{:S(2)}, u32[]{:S(2)}) collective-permute-start(s16[3,64,1024]{2,1,0:T(8,128)(2,1)} %get-tuple-element.70), channel_id=1, source_target_pairs={{0,8},{4,12},{8,0},{12,4},{16,24},{20,28},{24,16},{28,20},{1,9},{5... | collective-permute-start | bytes 1179656 | tf_op jit(solution)/shard_map/ppermute | solution.py:317
  36.0 15.0 %collective-permute-start.9 = (s16[3,64,1024]{2,1,0:T(8,128)(2,1)}, s16[3,64,1024]{2,1,0:T(8,128)(2,1)S(1)}, u32[]{:S(2)}, u32[]{:S(2)}) collective-permute-start(s16[3,64,1024]{2,1,0:T(8,128)(2,1)} %get-tuple-element.67), channel_id=1, source_target_pairs={{0,8},{4,12},{8,0},{12,4},{16,24},{20,28},{24,16},{28,20},{1,9},{5... | collective-permute-start | bytes 1179656 | tf_op jit(solution)/shard_map/ppermute | solution.py:317
  44.3 10.4 %collective-permute-start.2 = (s16[3,64,1024]{2,1,0:T(8,128)(2,1)S(1)}, s16[3,64,1024]{2,1,0:T(8,128)(2,1)S(1)}, u32[]{:S(2)}, u32[]{:S(2)}) collective-permute-start(s16[3,64,1024]{2,1,0:T(8,128)(2,1)S(1)} %broadcast_select_fusion.13), channel_id=1, source_target_pairs={{0,16},{4,20},{8,24},{12,28},{16,0},{20,4},{24,8},{28,12},{1,17},{... | collective-permute-start | bytes 1179656 | tf_op jit(solution)/shard_map/ppermute | solution.py:317
  51.0 14.4 %copy-start.28 = (s16[3,64,1024]{2,1,0:T(8,128)(2,1)}, s16[3,64,1024]{2,1,0:T(8,128)(2,1)S(1)}, u32[]{:S(2)}) copy-start(s16[3,64,1024]{2,1,0:T(8,128)(2,1)S(1)} %collective-permute-done.9) | copy-start | bytes 1179652
  51.9 12.3 %collective-permute-start.10 = (s16[3,64,1024]{2,1,0:T(8,128)(2,1)}, s16[3,64,1024]{2,1,0:T(8,128)(2,1)}, u32[]{:S(2)}, u32[]{:S(2)}) collective-permute-start(s16[3,64,1024]{2,1,0:T(8,128)(2,1)} %broadcast_select_fusion.9), channel_id=1, source_target_pairs={{0,16},{4,20},{8,24},{12,28},{16,0},{20,4},{24,8},{28,12},{1,17},{... | collective-permute-start | bytes 1179656 | tf_op jit(solution)/shard_map/ppermute | solution.py:317
  53.7 19.0 %collective-permute-start.4 = (s16[3,64,1024]{2,1,0:T(8,128)(2,1)}, s16[3,64,1024]{2,1,0:T(8,128)(2,1)}, u32[]{:S(2)}, u32[]{:S(2)}) collective-permute-start(s16[3,64,1024]{2,1,0:T(8,128)(2,1)} %get-tuple-element.69), channel_id=1, source_target_pairs={{0,16},{4,20},{8,24},{12,28},{16,0},{20,4},{24,8},{28,12},{1,17},{... | collective-permute-start | bytes 1179656 | tf_op jit(solution)/shard_map/ppermute | solution.py:317
  56.3 16.4 %collective-permute-start.3 = (s16[3,64,1024]{2,1,0:T(8,128)(2,1)}, s16[3,64,1024]{2,1,0:T(8,128)(2,1)}, u32[]{:S(2)}, u32[]{:S(2)}) collective-permute-start(s16[3,64,1024]{2,1,0:T(8,128)(2,1)} %broadcast_select_fusion.12), channel_id=1, source_target_pairs={{0,8},{4,12},{8,0},{12,4},{16,24},{20,28},{24,16},{28,20},{1,9},{5... | collective-permute-start | bytes 1179656 | tf_op jit(solution)/shard_map/ppermute | solution.py:317
  57.7 22.1 %collective-permute-start.12 = (s16[3,64,1024]{2,1,0:T(8,128)(2,1)}, s16[3,64,1024]{2,1,0:T(8,128)(2,1)S(1)}, u32[]{:S(2)}, u32[]{:S(2)}) collective-permute-start(s16[3,64,1024]{2,1,0:T(8,128)(2,1)} %get-tuple-element.66), channel_id=1, source_target_pairs={{0,16},{4,20},{8,24},{12,28},{16,0},{20,4},{24,8},{28,12},{1,17},{... | collective-permute-start | bytes 1179656 | tf_op jit(solution)/shard_map/ppermute | solution.py:317
  65.4 14.4 %collective-permute-start.11 = (s16[3,64,1024]{2,1,0:T(8,128)(2,1)S(1)}, s16[3,64,1024]{2,1,0:T(8,128)(2,1)S(1)}, u32[]{:S(2)}, u32[]{:S(2)}) collective-permute-start(s16[3,64,1024]{2,1,0:T(8,128)(2,1)S(1)} %broadcast_select_fusion.8), channel_id=1, source_target_pairs={{0,8},{4,12},{8,0},{12,4},{16,24},{20,28},{24,16},{28,20},{1,9},{5... | collective-permute-start | bytes 1179656 | tf_op jit(solution)/shard_map/ppermute | solution.py:317
  67.2 12.6 %copy-start.29 = (s16[3,64,1024]{2,1,0:T(8,128)(2,1)S(1)}, s16[3,64,1024]{2,1,0:T(8,128)(2,1)}, u32[]{:S(2)}) copy-start(s16[3,64,1024]{2,1,0:T(8,128)(2,1)} %copy-done.28) | copy-start | bytes 1179652
  74.5 19.1 %copy-start.2 = (s16[1,3,64,1024]{3,2,1,0:T(8,128)(2,1)}, s16[1,3,64,1024]{3,2,1,0:T(8,128)(2,1)S(1)}, u32[]{:S(2)}) copy-start(s16[1,3,64,1024]{3,2,1,0:T(8,128)(2,1)S(1)} %get-tuple-element.45) | copy-start | bytes 1179652
  74.5 19.1 %copy-start.4 = (s16[1,3,64,1024]{3,2,1,0:T(8,128)(2,1)}, s16[1,3,64,1024]{3,2,1,0:T(8,128)(2,1)S(1)}, u32[]{:S(2)}) copy-start(s16[1,3,64,1024]{3,2,1,0:T(8,128)(2,1)S(1)} %get-tuple-element.46) | copy-start | bytes 1179652
  74.5 9.1 %collective-permute-start.5 = (s16[3,64,1024]{2,1,0:T(8,128)(2,1)S(1)}, s16[3,64,1024]{2,1,0:T(8,128)(2,1)S(1)}, u32[]{:S(2)}, u32[]{:S(2)}) collective-permute-start(s16[3,64,1024]{2,1,0:T(8,128)(2,1)S(1)} %get-tuple-element.68), channel_id=1, source_target_pairs={{0,8},{4,12},{8,0},{12,4},{16,24},{20,28},{24,16},{28,20},{1,9},{5... | collective-permute-start | bytes 1179656 | tf_op jit(solution)/shard_map/ppermute | solution.py:317
  81.4 20.3 %copy-start = (s16[1,3,64,1024]{3,2,1,0:T(8,128)(2,1)}, s16[1,3,64,1024]{3,2,1,0:T(8,128)(2,1)S(1)}, u32[]{:S(2)}) copy-start(s16[1,3,64,1024]{3,2,1,0:T(8,128)(2,1)S(1)} %get-tuple-element.42) | copy-start | bytes 1179652
  81.4 10.4 %collective-permute-start.13 = (s16[3,64,1024]{2,1,0:T(8,128)(2,1)S(1)}, s16[3,64,1024]{2,1,0:T(8,128)(2,1)S(1)}, u32[]{:S(2)}, u32[]{:S(2)}) collective-permute-start(s16[3,64,1024]{2,1,0:T(8,128)(2,1)S(1)} %get-tuple-element.65), channel_id=1, source_target_pairs={{0,8},{4,12},{8,0},{12,4},{16,24},{20,28},{24,16},{28,20},{1,9},{5... | collective-permute-start | bytes 1179656 | tf_op jit(solution)/shard_map/ppermute | solution.py:317
  83.8 9.4 %collective-permute-start.6 = (s16[3,64,1024]{2,1,0:T(8,128)(2,1)S(1)}, s16[3,64,1024]{2,1,0:T(8,128)(2,1)S(1)}, u32[]{:S(2)}, u32[]{:S(2)}) collective-permute-start(s16[3,64,1024]{2,1,0:T(8,128)(2,1)S(1)} %broadcast_select_fusion.10), channel_id=1, source_target_pairs={{0,16},{4,20},{8,24},{12,28},{16,0},{20,4},{24,8},{28,12},{1,17},{... | collective-permute-start | bytes 1179656 | tf_op jit(solution)/shard_map/ppermute | solution.py:317
  91.9 9.4 %collective-permute-start.14 = (s16[3,64,1024]{2,1,0:T(8,128)(2,1)S(1)}, s16[3,64,1024]{2,1,0:T(8,128)(2,1)S(1)}, u32[]{:S(2)}, u32[]{:S(2)}) collective-permute-start(s16[3,64,1024]{2,1,0:T(8,128)(2,1)S(1)} %broadcast_select_fusion.6), channel_id=1, source_target_pairs={{0,16},{4,20},{8,24},{12,28},{16,0},{20,4},{24,8},{28,12},{1,17},{... | collective-permute-start | bytes 1179656 | tf_op jit(solution)/shard_map/ppermute | solution.py:317
  95.0 88.7 %collective-permute-start.7 = (s16[4,3,64,1024]{3,2,1,0:T(8,128)(2,1)}, s16[4,3,64,1024]{3,2,1,0:T(8,128)(2,1)}, u32[]{:S(2)}, u32[]{:S(2)}) collective-permute-start(s16[4,3,64,1024]{3,2,1,0:T(8,128)(2,1)} %pad_add_fusion.4), channel_id=1, source_target_pairs={{0,4},{4,0},{8,12},{12,8},{16,20},{20,16},{24,28},{28,24},{1,5},{5... | collective-permute-start | bytes 4718600 | tf_op jit(solution)/shard_map/ppermute | solution.py:317
  103.1 83.4 %collective-permute-start.15 = (s16[4,3,64,1024]{3,2,1,0:T(8,128)(2,1)}, s16[4,3,64,1024]{3,2,1,0:T(8,128)(2,1)}, u32[]{:S(2)}, u32[]{:S(2)}) collective-permute-start(s16[4,3,64,1024]{3,2,1,0:T(8,128)(2,1)} %pad_add_fusion.7), channel_id=1, source_target_pairs={{0,4},{4,0},{8,12},{12,8},{16,20},{20,16},{24,28},{28,24},{1,5},{5... | collective-permute-start | bytes 4718600 | tf_op jit(solution)/shard_map/ppermute | solution.py:317
  133.4 12.6 %collective-permute-start.19 = (f32[3,2,16,1024]{3,2,1,0:T(8,128)S(1)}, f32[3,2,16,1024]{3,2,1,0:T(8,128)S(1)}, u32[]{:S(2)}, u32[]{:S(2)}) collective-permute-start(f32[3,2,16,1024]{3,2,1,0:T(8,128)S(1)} %get-tuple-element.17), channel_id=1, source_target_pairs={{1,0},{2,1},{3,2},{0,3},{5,4},{6,5},{7,6},{4,7},{9,8},{10,9},{11,1... | collective-permute-start | bytes 1179656 | tf_op jit(solution)/shard_map/ppermute | solution.py:313
  136.6 18.4 %collective-permute-start.18 = (f32[3,2,16,1024]{3,2,1,0:T(8,128)S(1)}, f32[3,2,16,1024]{3,2,1,0:T(8,128)S(1)}, u32[]{:S(2)}, u32[]{:S(2)}) collective-permute-start(f32[3,2,16,1024]{3,2,1,0:T(8,128)S(1)} %get-tuple-element.18), channel_id=1, source_target_pairs={{0,1},{1,2},{2,3},{3,0},{4,5},{5,6},{6,7},{7,4},{8,9},{9,10},{10,1... | collective-permute-start | bytes 1179656 | tf_op jit(solution)/shard_map/ppermute | solution.py:313
  146.1 8.9 %copy-start.31 = (f32[3,2,16,1024]{3,2,1,0:T(8,128)}, f32[3,2,16,1024]{3,2,1,0:T(8,128)S(1)}, u32[]{:S(2)}) copy-start(f32[3,2,16,1024]{3,2,1,0:T(8,128)S(1)} %collective-permute-done.19.after) | copy-start | bytes 1179652
  155.7 28.0 %copy-start.3 = (s16[1,3,64,1024]{3,2,1,0:T(8,128)(2,1)S(1)}, s16[1,3,64,1024]{3,2,1,0:T(8,128)(2,1)}, u32[]{:S(2)}) copy-start(s16[1,3,64,1024]{3,2,1,0:T(8,128)(2,1)} %copy-done.2) | copy-start | bytes 1179652
  155.7 28.0 %copy-start.5 = (s16[1,3,64,1024]{3,2,1,0:T(8,128)(2,1)S(1)}, s16[1,3,64,1024]{3,2,1,0:T(8,128)(2,1)}, u32[]{:S(2)}) copy-start(s16[1,3,64,1024]{3,2,1,0:T(8,128)(2,1)} %copy-done.4) | copy-start | bytes 1179652
  155.7 28.0 %copy-start.25 = (s16[1,3,64,1024]{3,2,1,0:T(8,128)(2,1)S(1)}, s16[1,3,64,1024]{3,2,1,0:T(8,128)(2,1)}, u32[]{:S(2)}) copy-start(s16[1,3,64,1024]{3,2,1,0:T(8,128)(2,1)} %copy-done.24) | copy-start | bytes 1179652
  155.7 28.0 %copy-start.27 = (s16[1,3,64,1024]{3,2,1,0:T(8,128)(2,1)S(1)}, s16[1,3,64,1024]{3,2,1,0:T(8,128)(2,1)}, u32[]{:S(2)}) copy-start(s16[1,3,64,1024]{3,2,1,0:T(8,128)(2,1)} %copy-done.26) | copy-start | bytes 1179652
  190.1 8.0 %collective-permute-start.17 = (s16[3,2,16,1024]{3,2,1,0:T(8,128)(2,1)S(1)}, s16[3,2,16,1024]{3,2,1,0:T(8,128)(2,1)S(1)}, u32[]{:S(2)}, u32[]{:S(2)}) collective-permute-start(s16[3,2,16,1024]{3,2,1,0:T(8,128)(2,1)S(1)} %get-tuple-element.35), channel_id=1, source_target_pairs={{1,0},{2,1},{3,2},{0,3},{5,4},{6,5},{7,6},{4,7},{9,8},{10,9},{11,1... | collective-permute-start | bytes 589832 | tf_op jit(solution)/shard_map/ppermute | solution.py:313
  191.9 9.0 %collective-permute-start.16 = (s16[3,2,16,1024]{3,2,1,0:T(8,128)(2,1)S(1)}, s16[3,2,16,1024]{3,2,1,0:T(8,128)(2,1)S(1)}, u32[]{:S(2)}, u32[]{:S(2)}) collective-permute-start(s16[3,2,16,1024]{3,2,1,0:T(8,128)(2,1)S(1)} %get-tuple-element.36), channel_id=1, source_target_pairs={{0,1},{1,2},{2,3},{3,0},{4,5},{5,6},{6,7},{7,4},{8,9},{9,10},{10,1... | collective-permute-start | bytes 589832 | tf_op jit(solution)/shard_map/ppermute | solution.py:313
  (24 other events, 48.6 us)

commit v2 on v1

v2 whole, which is shorter than its diff:
```python
import functools

import jax
import jax.numpy as jnp
import numpy as np
from jax import lax
from jax.experimental import pallas as pl
from jax.experimental.pallas import tpu as pltpu
from jax.sharding import PartitionSpec as P

section_step = 0.25
reach = 16
code_scale = 4096.0
phases = 2
streams = ((0, 3), (1, 2))


def compact_kernel(length):
    wave = 2.0 * np.pi * np.arange(length) / length
    symbol = 14.0 / 9.0 * np.sin(wave) + 1.0 / 18.0 * np.sin(2.0 * wave)
    symbol = 1j * symbol / (1.0 + 2.0 / 3.0 * np.cos(wave))
    return np.real(np.fft.ifft(symbol))


def along_matrices(rows, length):
    kernel = compact_kernel(length)
    first = np.zeros((rows, rows + 2 * reach))
    second = np.zeros((rows, rows + 2 * reach))
    for i in range(rows):
        for k in range(-reach, reach + 1):
            first[i, i + reach + k] = kernel[-k % length]
        for k, weight in ((0, -980.0), (1, 270.0), (2, -27.0), (3, 2.0)):
            second[i, i + reach + k] = weight
            second[i, i + reach - k] = weight
    high = first.astype(jnp.bfloat16)
    low = (first - high.astype(np.float64)).astype(jnp.bfloat16)
    return high, low, second.astype(jnp.bfloat16)


first_taps = ((1, 45.0), (2, -9.0), (3, 1.0))
second_taps = ((0, -490.0), (1, 270.0), (2, -27.0), (3, 2.0))


def depth_matrix(rows, planes, fields):
    matrix = np.zeros((len(fields) * rows, rows * planes))
    for f, taps in enumerate(fields):
        for i in range(rows):
            for z, weight in taps:
                matrix[f * rows + i, i * planes + z] += weight
    return matrix.astype(jnp.bfloat16)


def first_at(z):
    return [(z + k, w) for k, w in first_taps] + [(z - k, -w) for k, w in first_taps]


def second_at(z):
    taps = [(z + k, w) for k, w in second_taps]
    return taps + [(z - k, w) for k, w in second_taps if k > 0]


def product(a, b):
    return jnp.dot(a, b, preferred_element_type=jnp.float32)


def split(values):
    high = values.astype(jnp.bfloat16)
    return high, (values - high.astype(jnp.float32)).astype(jnp.bfloat16)


def shifted_pairs(values):
    width = values.shape[-1]
    return [
        (pltpu.roll(values, width - k, 1), pltpu.roll(values, k, 1)) for k in (1, 2, 3)
    ]


def first_across(pairs):
    (u1, d1), (u2, d2), (u3, d3) = pairs
    return 0.75 * (u1 - d1) - 0.15 * (u2 - d2) + (1.0 / 60.0) * (u3 - d3)


def pack_kernel(core, weights, tile, mine, theirs):
    rows = weights.shape[0] // 4
    blocks = mine.shape[3] // rows

    def store(kept, sent):
        for b in range(blocks):
            depth = weights.shape[1]
            mixed = product(weights[...], tile[0, b * depth : (b + 1) * depth])
            for f in range(4):
                scale = code_scale if f < 2 else code_scale / 60.0
                part = jnp.round(mixed[f * rows : (f + 1) * rows] * scale)
                target = kept if f < 2 else sent
                code = part.astype(jnp.int32).astype(jnp.int16)
                target[f % 2, 0, 0, b * rows : (b + 1) * rows] = code

    @pl.when(core[0] == 0)
    def _():
        store(mine, theirs)

    @pl.when(core[0] != 0)
    def _():
        store(theirs, mine)


def pack(tile, planes, core, which):
    comps, deep, width = tile.shape
    quarter = deep // planes // 4
    x_rows = min(quarter, 32)
    ghost = [[t for t in first_at(z) if t[0] not in (3, 4)] for z in (3, 4)]
    weights = depth_matrix(x_rows, planes, [[(3, 1.0)], [(4, 1.0)]] + ghost)
    first, second = streams[which]
    shape = jax.ShapeDtypeStruct((2, 2, comps, quarter, width), jnp.int16)
    spec = pl.BlockSpec((2, 1, 1, quarter, width), lambda k, c: (0, k, c, 0, 0))
    return pl.pallas_call(
        pack_kernel,
        out_shape=(shape,) * 2,
        grid=(2, comps),
        in_specs=[
            pl.BlockSpec(memory_space=pltpu.SMEM),
            pl.BlockSpec(weights.shape, lambda k, c: (0, 0)),
            pl.BlockSpec(
                (1, quarter * planes, width), lambda k, c: (c, first + k * (second - first), 0)
            ),
        ],
        out_specs=(spec,) * 2,
        cost_estimate=pl.CostEstimate(
            flops=0, bytes_accessed=2 * comps * deep * width, transcendentals=0
        ),
    )(core, jnp.asarray(weights), tile)


def field_kernel(
    viscosity, m_top, m_low, field, before, after, inner, depth, along, across, sums, high_s, low_s, curve_s
):
    slab, width = inner.shape[2:]
    rows = m_low.shape[0]
    planes = field.shape[1] // slab
    lanes = field.shape[2]
    column = pl.program_id(1)
    gain = viscosity[0] * section_step
    side = pl.ds(pl.multiple_of(column * lanes, lanes), lanes)

    def unpack(i, carry):
        start = pl.multiple_of(i * 8, 8)
        plane = [field[0, pl.ds(start * planes + z, 8, planes), :] for z in range(planes)]
        at = (pl.ds(start, 8), side)
        for p in range(2):
            z = 3 + p
            centre = plane[z]
            u1, u2, u3 = plane[z + 1], plane[z + 2], plane[z + 3]
            d1, d2, d3 = plane[z - 1], plane[z - 2], plane[z - 3]
            slope = 0.75 * (u1 - d1) - 0.15 * (u2 - d2) + (1.0 / 60.0) * (u3 - d3)
            curve = 1.5 * (u1 + d1) - 0.15 * (u2 + d2) + (1.0 / 90.0) * (u3 + d3)
            inner[(0, p) + at] = centre
            depth[(0, p) + at] = slope
            sums[(0, p) + at] = centre + gain * (curve - (49.0 / 18.0) * centre)
        return carry

    lax.fori_loop(0, slab // 8, unpack, 0, unroll=4)

    @pl.when(column == pl.num_programs(1) - 1)
    def _():
        field_rest(
            gain, m_top, m_low, before, after, inner, along, across, sums, high_s, low_s, curve_s
        )


def field_rest(
    gain, m_top, m_low, before, after, inner, along, across, sums, high_s, low_s, curve_s
):
    slab = inner.shape[2]
    rows = m_low.shape[0]
    for p in range(2):
        for start, rim in ((0, before), (reach + slab, after)):
            high, low = split(rim[0, :, p])
            high_s[start : start + reach, :] = high
            low_s[start : start + reach, :] = low

        def fill(i, carry):
            start = pl.multiple_of(i * 16, 16)
            high, low = split(inner[0, p, pl.ds(start, 16), :])
            at = pl.ds(pl.multiple_of(start + reach, 16), 16)
            high_s[at, :] = high
            low_s[at, :] = low
            return carry

        lax.fori_loop(0, slab // 16, fill, 0)
        for b in range(slab // rows):
            window = pl.ds(b * rows, rows + 2 * reach)
            high, low = high_s[window, :], low_s[window, :]
            both = product(m_top[...], high) + product(m_top[...], low)
            along[0, p, b * rows : (b + 1) * rows] = both[:rows] + product(m_low[...], high)
            curve_s[b * rows : (b + 1) * rows] = both[rows:]

        def body(i, carry):
            at = pl.ds(pl.multiple_of(i * 8, 8), 8)
            pairs = shifted_pairs(inner[0, p, at, :])
            across[0, p, at, :] = first_across(pairs)
            (u1, d1), (u2, d2), (u3, d3) = pairs
            curve = 1.5 * (u1 + d1) - 0.15 * (u2 + d2) + (1.0 / 90.0) * (u3 + d3)
            curve = curve + (1.0 / 180.0) * curve_s[at, :]
            sums[0, p, at, :] = sums[0, p, at, :] + gain * curve
            return carry

        lax.fori_loop(0, slab // 8, body, 0)


def field_terms(field, before, after, viscosity, length):
    comps, slab, planes, width = field.shape
    lanes = 128
    flat = field.reshape(comps, slab * planes, width)
    rows = min(slab, 128)
    high, low, second = along_matrices(rows, length)
    top = np.concatenate([high, second], 0)
    shape = jax.ShapeDtypeStruct((comps, 2, slab, width), jnp.float32)
    spec = pl.BlockSpec((1, 2, slab, width), lambda c, t: (c, 0, 0, 0))
    rim = pl.BlockSpec((1, reach, 2, width), lambda c, t: (c, 0, 0, 0))
    return pl.pallas_call(
        field_kernel,
        out_shape=(shape,) * 5,
        grid=(comps, width // lanes),
        in_specs=[
            pl.BlockSpec(memory_space=pltpu.SMEM),
            pl.BlockSpec(top.shape, lambda c, t: (0, 0)),
            pl.BlockSpec(low.shape, lambda c, t: (0, 0)),
            pl.BlockSpec((1, slab * planes, lanes), lambda c, t: (c, 0, t)),
            rim,
            rim,
        ],
        out_specs=(spec,) * 5,
        scratch_shapes=[
            pltpu.VMEM((slab + 2 * reach, width), jnp.bfloat16),
            pltpu.VMEM((slab + 2 * reach, width), jnp.bfloat16),
            pltpu.VMEM((slab, width), jnp.float32),
        ],
        cost_estimate=pl.CostEstimate(
            flops=0, bytes_accessed=9 * 4 * comps * slab * planes * width // 4, transcendentals=0
        ),
    )(viscosity, jnp.asarray(top), jnp.asarray(low), flat, before, after)


def final_kernel(
    core, m_both, held0, other0, held1, other1, before, after,
    inner, depth, along, across, sums, out, base_s, ghost_s, slope_s,
):
    step = pl.program_id(0)
    rows = inner.shape[2]
    quarter = held0.shape[3]
    slab = 4 * quarter
    inverse = 1.0 / code_scale

    def decoded(values):
        return values.astype(jnp.int32).astype(jnp.float32) * inverse

    def load(flow, ghost):
        for u in range(2):
            for k in range(2):
                first = streams[u][k] * quarter
                for c in range(3):
                    for p in range(2):

                        def fill(i, carry):
                            start = pl.multiple_of(i * 16, 16)
                            here = pl.ds(start, 16)
                            to = pl.ds(pl.multiple_of(start + first + reach, 16), 16)
                            values = decoded(flow[u][p, k, c, here, :])
                            base_s[c, p, to, :] = values.astype(jnp.bfloat16)
                            to = pl.ds(pl.multiple_of(start + first, 16), 16)
                            ghost_s[c, p, to, :] = ghost[u][p, k, c, here, :]
                            return carry

                        lax.fori_loop(0, quarter // 16, fill, 0)

    @pl.when(step == 0)
    def _():
        for c in range(3):
            for p in range(2):
                base_s[c, p, 0:reach] = decoded(before[p, c]).astype(jnp.bfloat16)
                base_s[c, p, reach + slab :] = decoded(after[p, c]).astype(jnp.bfloat16)

        @pl.when(core[0] == 0)
        def _():
            load((held0, held1), (other0, other1))

        @pl.when(core[0] != 0)
        def _():
            load((other0, other1), (held0, held1))

    origin = pl.multiple_of(step * rows, 32)
    for c in range(3):
        for p in range(2):
            both = product(m_both[...], base_s[c, p, pl.ds(origin, rows + 2 * reach), :])
            slope_s[c, p] = both[:rows] + both[rows:]

    def body(i, carry):
        start = pl.multiple_of(i * 16, 16)
        at = pl.ds(start, 16)
        there = pl.ds(pl.multiple_of(origin + start, 16), 16)
        inside = pl.ds(pl.multiple_of(origin + reach + start, 16), 16)
        flow = [
            [base_s[c, p, inside, :].astype(jnp.float32) for p in range(2)] for c in range(3)
        ]
        for p in range(2):
            move = [inner[c, p, at, :] for c in range(3)]
            for c in range(3):
                dz = decoded(ghost_s[c, p, there, :])
                if p == 0:
                    dz = dz + 0.75 * flow[c][1]
                else:
                    dz = dz - 0.75 * flow[c][0]
                dy = first_across(shifted_pairs(flow[c][p]))
                total = flow[0][p] * along[c, p, at, :] + flow[1][p] * across[c, p, at, :]
                total = total + flow[2][p] * depth[c, p, at, :]
                total = total + move[0] * slope_s[c, p, at, :] + move[1] * dy + move[2] * dz
                out[0, c, at, p, :] = sums[c, p, at, :] - section_step * total
        return carry

    lax.fori_loop(0, rows // 16, body, 0)


def final(core, pieces, before, after, terms, length):
    inner = terms[0]
    comps, pair, slab, width = inner.shape
    rows = 32
    high, low, _ = along_matrices(rows, length)
    both = np.concatenate([high, low], 0)
    whole = pl.BlockSpec(pieces[0].shape, lambda i: (0, 0, 0, 0, 0))
    rim = pl.BlockSpec(before.shape, lambda i: (0, 0, 0, 0))
    spec = pl.BlockSpec((comps, pair, rows, width), lambda i: (0, 0, i, 0))
    return pl.pallas_call(
        final_kernel,
        out_shape=jax.ShapeDtypeStruct((1, comps, slab, pair, width), jnp.float32),
        grid=(slab // rows,),
        in_specs=[
            pl.BlockSpec(memory_space=pltpu.SMEM),
            pl.BlockSpec(both.shape, lambda i: (0, 0)),
        ]
        + [whole] * 4
        + [rim] * 2
        + [spec] * 5,
        out_specs=pl.BlockSpec((1, comps, rows, pair, width), lambda i: (0, 0, i, 0, 0)),
        scratch_shapes=[
            pltpu.VMEM((comps, pair, slab + 2 * reach, width), jnp.bfloat16),
            pltpu.VMEM((comps, pair, slab, width), jnp.int16),
            pltpu.VMEM((comps, pair, rows, width), jnp.float32),
        ],
        cost_estimate=pl.CostEstimate(
            flops=0, bytes_accessed=7 * 4 * inner.size, transcendentals=0
        ),
    )(core, jnp.asarray(both), *pieces, before, after, *terms)


def ring(last, first):
    size = lax.axis_size("gx")
    up = [(i, (i + 1) % size) for i in range(size)]
    down = [(j, i) for i, j in up]
    return lax.ppermute(last, "gx", up), lax.ppermute(first, "gx", down)


def swap(array, bit):
    return lax.ppermute(array, "pert", [(i, i ^ bit) for i in range(lax.axis_size("pert"))])


def exchange(mine, theirs, root, fill_first, fill_second):
    me = lax.axis_index("pert")
    is_root = me == root
    place = (me // 2) ^ (root // 2)
    at_a, at_b, at_c = place == 0, place == 1, place == 2
    source = []
    for u in range(2):
        source.append(jnp.where(is_root, mine[u], swap(theirs[u], 1)))
    source = list(fill_first(*source))
    X = [[], []]
    Y = [[], []]
    terms = None
    for s in range(phases + 1):
        for u in range(2):
            k = min(s, phases - 1)
            one, two = source[u][0, k], source[u][1, k]
            if s == phases:
                one, two = two, one
            if s > 0:
                one = jnp.where(at_a, one, Y[u][s - 1])
                two = jnp.where(at_a, two, X[u][s - 1])
            X[u].append(swap(one, 2))
            Y[u].append(swap(two, 4))
        if s == 0:
            X[0][0], Y[0][0], terms = fill_second(X[0][0], Y[0][0])
    held = []
    for u in range(2):
        parts = []
        for h in range(2):
            P1, P2 = (X[u], Y[u]) if h == 0 else (Y[u], X[u])
            near, far = (at_b, at_c) if h == 0 else (at_c, at_b)
            row = []
            for k in range(phases):
                late = P1[k + 2] if k + 2 <= phases else P2[phases]
                value = jnp.where(near, P1[k], jnp.where(far, late, P2[k + 1]))
                row.append(jnp.where(at_a, source[u][h, k], value))
            parts.append(jnp.stack(row, 0))
        held.append(jnp.stack(parts, 0))
    other = [swap(h, 1) for h in held]
    return held[0], other[0], held[1], other[1], terms


def per_device(pert_field, base_store, section_owner, pert_ids, member_visc):
    _, comps, slab, planes, width = pert_field.shape
    length = slab * lax.axis_size("gx")
    member_pick = pert_ids[0] == jnp.arange(member_visc.shape[0], dtype=jnp.int32)
    viscosity = jnp.sum(jnp.where(member_pick, member_visc, 0.0))[None]
    levels_here = base_store.shape[0]
    owner_slot = section_owner[0] % levels_here
    owner_root = section_owner[0] // levels_here
    tiles = base_store.reshape(levels_here, comps, slab * planes, width)
    tile = tiles[0] if levels_here == 1 else lax.dynamic_index_in_dim(tiles, owner_slot, 0, False)
    field = pert_field[0]
    me = lax.axis_index("pert")
    in_pairs = lax.axis_size("pert") == 8
    core = (me % 2 if in_pairs else jnp.zeros_like(me)).astype(jnp.int32)[None]
    halves = [pack(tile, planes, core, u) for u in range(2)]
    before, after = ring(
        field[:, slab - reach :, 3:5],
        field[:, :reach, 3:5],
    )
    if in_pairs:
        held_field = []

        def fill_first(*source):
            kept = lax.optimization_barrier((field,) + source)
            held_field.append(kept[0])
            return kept[1:]

        def fill_second(x, y):
            terms = field_terms(held_field[0], before, after, viscosity, length)
            x, y, *terms = lax.optimization_barrier((x, y) + tuple(terms))
            return x, y, terms

        *pieces, terms = exchange(
            [h[0] for h in halves], [h[1] for h in halves], owner_root, fill_first, fill_second
        )
    else:
        terms = field_terms(field, before, after, viscosity, length)
        pieces = [
            lax.psum(jnp.where(me == owner_root, a, 0).astype(jnp.float32), "pert").astype(a.dtype)
            for h in halves
            for a in h
        ]
    rim = jnp.where(core[0] == 0, pieces[0], pieces[1])
    quarter = slab // 4
    base_before, base_after = ring(rim[:, 1, :, quarter - reach :], rim[:, 0, :, :reach])
    return final(core, pieces, base_before, base_after, terms, length)


def solution(mesh):
    placed = (
        P("pert", None, "gx", None, None),
        P("pert", None, "gx", None, None),
        P(),
        P("pert"),
        P(),
    )
    return jax.shard_map(
        per_device,
        mesh=mesh,
        in_specs=placed,
        out_specs=P("pert", None, "gx", None, None),
        check_vma=False,
    )
```

time: 225 us -> 201 us (0.89)
  waiting for transfers between devices: 61.8 us -> 44.6 us
  other arithmetic: 26.2 us -> 10.8 us
  starting transfers between devices: 24 us -> 28.8 us
  Pallas kernels: 95.8 us -> 98.7 us
    ppermute x4, waiting for transfers between devices: 21.7 us -> 9.79 us  [ring(): return (lax.ppermute(last, 'gx', up), lax.ppermute(first, 'gx', down))]
    select_n x12 -> x9, other arithmetic: 15.4 us -> 4.38 us  [the longest x2 1.36 us: exchange(): source.append(jnp.where(is_root, mine[u], swap(theirs[u], 1)))]
    ppermute x16, waiting for transfers between devices: 40.2 us -> 34.8 us  [swap(): lax.ppermute(array, 'pert', [(i, i ^ bit) for i in range(lax.axis_size('p...]
    another operation x13 -> x8, other arithmetic: 10.2 us -> 5.74 us  [the longest x4 3.99 us: exchange(): parts.append(jnp.stack(row, 0))]
    another operation x2 -> x1, local copies, waits for them, and re-layouts: 5.89 us -> 2.67 us  [exchange(): held.append(jnp.stack(parts, 0))]
    ppermute x16, starting transfers between devices: 18.7 us -> 21.8 us  [swap(): lax.ppermute(array, 'pert', [(i, i ^ bit) for i in range(lax.axis_size('p...]
    ppermute x0 -> x1, local copies, waits for them, and re-layouts: none -> 2.67 us  [swap(): lax.ppermute(array, 'pert', [(i, i ^ bit) for i in range(lax.axis_size('p...]
    pallas_call x3, Pallas kernels: 74.2 us -> 76.6 us  [the longest x1 63 us: field_terms(): pl.pallas_call(field_kernel, out_shape=(shape,) * 5, grid=(comps, width /...]
  transfers between devices with their start and end apart: 20 -> 20, of which waited for: 14 -> 11; matrix products, arithmetic and copies ran while one was open for 13% -> 11% of each run, Pallas kernels for 25% -> 35%
where the time goes in v2:
time: 201 us; the launch traced here: 199 us
  Pallas kernels  98.7 us (49%)
  waiting for transfers between devices  44.6 us (22%)
  starting transfers between devices  28.8 us (14%)
  local copies, waits for them, and re-layouts  14.3 us (7%)
  other arithmetic  10.8 us (5%)
    pallas_call x1, Pallas kernels, field_terms(): pl.pallas_call(field_kernel, out_shape=(shape,) * 5, grid=(comps, width /...  63 us
    ppermute x16, waiting for transfers between devices, swap(): lax.ppermute(array, 'pert', [(i, i ^ bit) for i in range(lax.axis_size('p...  34.8 us
    pallas_call x1, Pallas kernels, final(): pl.pallas_call(final_kernel, out_shape=jax.ShapeDtypeStruct((1, comps, sl...  22.1 us
    ppermute x16, starting transfers between devices, swap(): lax.ppermute(array, 'pert', [(i, i ^ bit) for i in range(lax.axis_size('p...  21.8 us
    pallas_call x2, Pallas kernels, pack(): pl.pallas_call(pack_kernel, out_shape=(shape,) * 2, grid=(2, comps), in_s...  13.5 us
    ppermute x4, waiting for transfers between devices, ring(): return (lax.ppermute(last, 'gx', up), lax.ppermute(first, 'gx', down))  9.79 us
    ppermute x4, starting transfers between devices, ring(): return (lax.ppermute(last, 'gx', up), lax.ppermute(first, 'gx', down))  7.05 us
  transfers between devices with their start and end apart: 20, of which 11 were waited for; matrix products, arithmetic and copies ran while one was open for 11% of the time, Pallas kernels for 35%

profile of v2, /device:TPU:0, one launch (start us, length us, event | category | flops | bytes accessed | tf_op | source)
XLA Modules:
  0.0 198.6 jit_solution(12490570388014650649)
XLA Ops:
  0.0 6.8 %shard_map.101 = (s16[2,2,3,64,1024]{4,3,2,1,0:T(8,128)(2,1)}, s16[2,2,3,64,1024]{4,3,2,1,0:T(8,128)(2,1)}) custom-call(s32[1]{0:T(128)} %bitcast.core, bf16[128,256]{1,0:T(8,128)(2,1)} %constant.57.clone.weights, bf16[3,2048,1024]{2,1,0:T(8,128)(2,1)} %bitcast.83), custom_call_target="tpu_custom_call" | custom-call | bytes 12582912 | tf_op jit(solution)/shard_map/pallas_call | solution.py:116
  7.2 6.8 %shard_map.100 = (s16[2,2,3,64,1024]{4,3,2,1,0:T(8,128)(2,1)}, s16[2,2,3,64,1024]{4,3,2,1,0:T(8,128)(2,1)}) custom-call(s32[1]{0:T(128)} %bitcast.core, bf16[128,256]{1,0:T(8,128)(2,1)} %constant.57.clone.weights, bf16[3,2048,1024]{2,1,0:T(8,128)(2,1)} %bitcast.84), custom_call_target="tpu_custom_call" | custom-call | bytes 12582912 | tf_op jit(solution)/shard_map/pallas_call | solution.py:116
  14.0 3.3 %fusion.5 = (f32[3,16,2,1024]{3,2,1,0:T(2,128)}, f32[3,16,2,1024]{3,2,1,0:T(2,128)}) fusion(f32[3,256,8,1024]{3,2,1,0:T(8,128)} %bitcast.85), kind=kLoop, calls=%fused_computation.37 | loop fusion | bytes 1572864 | tf_op jit(solution)/shard_map/slice | solution.py:425
  17.3 5.0 %collective-permute-start.5 = (f32[3,16,2,1024]{3,2,1,0:T(2,128)}, f32[3,16,2,1024]{3,2,1,0:T(2,128)}, u32[]{:S(2)}, u32[]{:S(2)}) collective-permute-start(f32[3,16,2,1024]{3,2,1,0:T(2,128)} %get-tuple-element.43), channel_id=1, source_target_pairs={{1,0},{2,1},{3,2},{0,3},{5,4},{6,5},{7,6},{4,7},{9,8},{10,9},{11,1... | collective-permute-start | bytes 1179656 | tf_op jit(solution)/shard_map/ppermute | solution.py:359
  27.2 3.7 %collective-permute-start.3 = (s16[3,64,1024]{2,1,0:T(8,128)(2,1)}, s16[3,64,1024]{2,1,0:T(8,128)(2,1)}, u32[]{:S(2)}, u32[]{:S(2)}) collective-permute-start(s16[3,64,1024]{2,1,0:T(8,128)(2,1)} %get-tuple-element.59), channel_id=1, source_target_pairs={{0,16},{4,20},{8,24},{12,28},{16,0},{20,4},{24,8},{28,12},{1,17},{... | collective-permute-start | bytes 1179656 | tf_op jit(solution)/shard_map/ppermute | solution.py:363
  31.0 1.5 collective-permute-start.2
  35.3 5.3 %collective-permute-done.4.before = f32[3,16,2,1024]{3,2,1,0:T(2,128)} collective-permute-done((f32[3,16,2,1024]{3,2,1,0:T(2,128)}, f32[3,16,2,1024]{3,2,1,0:T(2,128)}, u32[]{:S(2)}, u32[]{:S(2)}) %collective-permute-start.4) | collective-permute-done | bytes 393248 | tf_op jit(solution)/shard_map/ppermute | solution.py:359
  40.6 63.0 %shard_map.102 = (f32[3,2,256,1024]{3,2,1,0:T(8,128)}, f32[3,2,256,1024]{3,2,1,0:T(8,128)}, f32[3,2,256,1024]{3,2,1,0:T(8,128)}, f32[3,2,256,1024]{3,2,1,0:T(8,128)}, f32[3,2,256,1024]{3,2,1,0:T(8,128)}) custom-call(f32[1]{0:T(128)} %bitcast.7.viscosity, bf16[256,160]{1,0:T(8,128)(2,1)} %constant.58.clone.m_top, bf16[128,160]{1,0:T(8,128)(2,1)} %constant.59.clone.m_low, ...), custom_call_target="tpu_custom_call" | custom-call | bytes 56623104 | tf_op jit(solution)/shard_map/pallas_call | solution.py:220
  103.8 1.6 collective-permute-start.6
  106.3 1.5 collective-permute-start.12
  107.8 8.1 %collective-permute-done.6 = s16[3,64,1024]{2,1,0:T(8,128)(2,1)S(1)} collective-permute-done((s16[3,64,1024]{2,1,0:T(8,128)(2,1)S(1)}, s16[3,64,1024]{2,1,0:T(8,128)(2,1)S(1)}, u32[]{:S(2)}, u32[]{:S(2)}) %collective-permute-start.6) | collective-permute-done | bytes 393248 | tf_op jit(solution)/shard_map/ppermute | solution.py:363
  117.5 1.5 collective-permute-start.7
  119.1 1.5 collective-permute-start.14
  120.6 3.9 %collective-permute-done.12 = s16[3,64,1024]{2,1,0:T(8,128)(2,1)} collective-permute-done((s16[3,64,1024]{2,1,0:T(8,128)(2,1)}, s16[3,64,1024]{2,1,0:T(8,128)(2,1)}, u32[]{:S(2)}, u32[]{:S(2)}) %collective-permute-start.12) | collective-permute-done | bytes 393248 | tf_op jit(solution)/shard_map/ppermute | solution.py:363
  124.6 2.6 %collective-permute-start.13 = (s16[3,64,1024]{2,1,0:T(8,128)(2,1)S(1)}, s16[3,64,1024]{2,1,0:T(8,128)(2,1)S(1)}, u32[]{:S(2)}, u32[]{:S(2)}) collective-permute-start(s16[3,64,1024]{2,1,0:T(8,128)(2,1)S(1)} %bitcast_select_fusion.4), channel_id=1, source_target_pairs={{0,8},{4,12},{8,0},{12,4},{16,24},{20,28},{24,16},{28,20},{1,9},{5... | collective-permute-start | bytes 1179656 | tf_op jit(solution)/shard_map/ppermute | solution.py:363
  127.1 1.7 select_bitcast_fusion.3
  129.7 1.3 collective-permute-done.14
  131.0 6.2 %collective-permute-done.13 = s16[3,64,1024]{2,1,0:T(8,128)(2,1)S(1)} collective-permute-done((s16[3,64,1024]{2,1,0:T(8,128)(2,1)S(1)}, s16[3,64,1024]{2,1,0:T(8,128)(2,1)S(1)}, u32[]{:S(2)}, u32[]{:S(2)}) %collective-permute-start.13) | collective-permute-done | bytes 393248 | tf_op jit(solution)/shard_map/ppermute | solution.py:363
  137.2 1.6 select_bitcast_fusion.1
  138.7 2.2 %collective-permute-start.15 = (s16[3,64,1024]{2,1,0:T(8,128)(2,1)S(1)}, s16[3,64,1024]{2,1,0:T(8,128)(2,1)S(1)}, u32[]{:S(2)}, u32[]{:S(2)}) collective-permute-start(s16[3,64,1024]{2,1,0:T(8,128)(2,1)S(1)} %get-tuple-element.55), channel_id=1, source_target_pairs={{0,8},{4,12},{8,0},{12,4},{16,24},{20,28},{24,16},{28,20},{1,9},{5... | collective-permute-start | bytes 1179656 | tf_op jit(solution)/shard_map/ppermute | solution.py:363
  140.9 4.6 %collective-permute-done.8 = s16[3,64,1024]{2,1,0:T(8,128)(2,1)S(1)} collective-permute-done((s16[3,64,1024]{2,1,0:T(8,128)(2,1)S(1)}, s16[3,64,1024]{2,1,0:T(8,128)(2,1)S(1)}, u32[]{:S(2)}, u32[]{:S(2)}) %collective-permute-start.8) | collective-permute-done | bytes 393248 | tf_op jit(solution)/shard_map/ppermute | solution.py:363
  145.7 2.1 %collective-permute-start.9 = (s16[3,64,1024]{2,1,0:T(8,128)(2,1)S(1)}, s16[3,64,1024]{2,1,0:T(8,128)(2,1)S(1)}, u32[]{:S(2)}, u32[]{:S(2)}) collective-permute-start(s16[3,64,1024]{2,1,0:T(8,128)(2,1)S(1)} %bitcast_select_fusion.7), channel_id=1, source_target_pairs={{0,16},{4,20},{8,24},{12,28},{16,0},{20,4},{24,8},{28,12},{1,17},{... | collective-permute-start | bytes 1179656 | tf_op jit(solution)/shard_map/ppermute | solution.py:363
  147.8 3.0 %collective-permute-done.15 = s16[3,64,1024]{2,1,0:T(8,128)(2,1)S(1)} collective-permute-done((s16[3,64,1024]{2,1,0:T(8,128)(2,1)S(1)}, s16[3,64,1024]{2,1,0:T(8,128)(2,1)S(1)}, u32[]{:S(2)}, u32[]{:S(2)}) %collective-permute-start.15) | collective-permute-done | bytes 393248 | tf_op jit(solution)/shard_map/ppermute | solution.py:363
  151.0 1.6 collective-permute-start.16
  152.6 4.7 %collective-permute-done.9 = s16[3,64,1024]{2,1,0:T(8,128)(2,1)S(1)} collective-permute-done((s16[3,64,1024]{2,1,0:T(8,128)(2,1)S(1)}, s16[3,64,1024]{2,1,0:T(8,128)(2,1)S(1)}, u32[]{:S(2)}, u32[]{:S(2)}) %collective-permute-start.9) | collective-permute-done | bytes 393248 | tf_op jit(solution)/shard_map/ppermute | solution.py:363
  157.8 1.4 pad_add_fusion
  159.1 2.9 %collective-permute-done.16 = s16[3,64,1024]{2,1,0:T(8,128)(2,1)S(1)} collective-permute-done((s16[3,64,1024]{2,1,0:T(8,128)(2,1)S(1)}, s16[3,64,1024]{2,1,0:T(8,128)(2,1)S(1)}, u32[]{:S(2)}, u32[]{:S(2)}) %collective-permute-start.16) | collective-permute-done | bytes 393248 | tf_op jit(solution)/shard_map/ppermute | solution.py:363
  163.9 1.8 collective-permute-start.19
  166.0 2.7 %copy.12.held0 = s16[2,2,3,64,1024]{4,3,2,1,0:T(8,128)(2,1)} copy(s16[2,2,3,64,1024]{4,3,2,0,1:T(8,128)(2,1)} %pad_add_fusion) | data formatting | bytes 3145728 | tf_op jit(solution)/shard_map/stack | solution.py:403
  168.7 2.7 %copy.13.other0 = s16[2,2,3,64,1024]{4,3,2,1,0:T(8,128)(2,1)} copy(s16[2,2,3,64,1024]{4,3,2,0,1:T(8,128)(2,1)} %collective-permute-done.10) | data formatting | bytes 3145728 | tf_op jit(solution)/shard_map/ppermute | solution.py:363
  171.4 4.5 %collective-permute-done.18.before = s16[2,3,16,1024]{3,2,1,0:T(8,128)(2,1)S(1)} collective-permute-done((s16[2,3,16,1024]{3,2,1,0:T(8,128)(2,1)S(1)}, s16[2,3,16,1024]{3,2,1,0:T(8,128)(2,1)S(1)}, u32[]{:S(2)}, u32[]{:S(2)}) %collective-permute-start.18) | collective-permute-done | bytes 196640 | tf_op jit(solution)/shard_map/ppermute | solution.py:359
  176.5 22.1 %shard_map.103 = f32[1,3,256,2,1024]{4,3,2,1,0:T(2,128)} custom-call(s32[1]{0:T(128)} %bitcast.core, bf16[64,64]{1,0:T(8,128)(2,1)} %constant.60.clone.m_both, s16[2,2,3,64,1024]{4,3,2,1,0:T(8,128)(2,1)} %copy.12.held0, s16[2,2,3,64,1024]{4,3,2,1,0:T(8,128)(2,1)} %copy.13.other0, s16[2,2,3,64,1024]{4,3,2,1,0:T(8,128)(2,1)} %copy-done, ...), custom_call_target="tpu_custom_call" | custom-call | bytes 44040192 | tf_op jit(solution)/shard_map/pallas_call | solution.py:332
  (52 shorter events, 14.2 us)
Async XLA Ops:
  6.8 16.2 %collective-permute-start.1 = (s16[2,2,3,64,1024]{4,3,2,1,0:T(8,128)(2,1)}, s16[2,2,3,64,1024]{4,3,2,1,0:T(8,128)(2,1)S(1)}, u32[]{:S(2)}, u32[]{:S(2)}) collective-permute-start(s16[2,2,3,64,1024]{4,3,2,1,0:T(8,128)(2,1)} %get-tuple-element.27), channel_id=1, source_target_pairs={{0,4},{4,0},{8,12},{12,8},{16,20},{20,16},{24,28},{28,24},{1,5},{5... | collective-permute-start | bytes 4718600 | tf_op jit(solution)/shard_map/ppermute | solution.py:363
  14.0 10.2 %copy-start.2 = (s16[2,2,3,64,1024]{4,3,2,1,0:T(8,128)(2,1)S(1)}, s16[2,2,3,64,1024]{4,3,2,1,0:T(8,128)(2,1)}, u32[]{:S(2)}) copy-start(s16[2,2,3,64,1024]{4,3,2,1,0:T(8,128)(2,1)} %get-tuple-element.26) | copy-start | bytes 4718596
  14.0 10.9 %collective-permute-start = (s16[2,2,3,64,1024]{4,3,2,1,0:T(8,128)(2,1)}, s16[2,2,3,64,1024]{4,3,2,1,0:T(8,128)(2,1)}, u32[]{:S(2)}, u32[]{:S(2)}) collective-permute-start(s16[2,2,3,64,1024]{4,3,2,1,0:T(8,128)(2,1)} %get-tuple-element.25), channel_id=1, source_target_pairs={{0,4},{4,0},{8,12},{12,8},{16,20},{20,16},{24,28},{28,24},{1,5},{5... | collective-permute-start | bytes 4718600 | tf_op jit(solution)/shard_map/ppermute | solution.py:363
  17.3 18.0 %collective-permute-start.5 = (f32[3,16,2,1024]{3,2,1,0:T(2,128)}, f32[3,16,2,1024]{3,2,1,0:T(2,128)}, u32[]{:S(2)}, u32[]{:S(2)}) collective-permute-start(f32[3,16,2,1024]{3,2,1,0:T(2,128)} %get-tuple-element.43), channel_id=1, source_target_pairs={{1,0},{2,1},{3,2},{0,3},{5,4},{6,5},{7,6},{4,7},{9,8},{10,9},{11,1... | collective-permute-start | bytes 1179656 | tf_op jit(solution)/shard_map/ppermute | solution.py:359
  22.3 18.3 %collective-permute-start.4 = (f32[3,16,2,1024]{3,2,1,0:T(2,128)}, f32[3,16,2,1024]{3,2,1,0:T(2,128)}, u32[]{:S(2)}, u32[]{:S(2)}) collective-permute-start(f32[3,16,2,1024]{3,2,1,0:T(2,128)} %get-tuple-element.44), channel_id=1, source_target_pairs={{0,1},{1,2},{2,3},{3,0},{4,5},{5,6},{6,7},{7,4},{8,9},{9,10},{10,1... | collective-permute-start | bytes 1179656 | tf_op jit(solution)/shard_map/ppermute | solution.py:359
  23.0 1.2 copy-start.3
  24.2 1.4 copy-start.1
  26.3 6.9 %copy-start.7 = (f32[64]{0:T(128)S(1)}, f32[64]{0:T(128)}, u32[]{:S(2)}) copy-start(f32[64]{0:T(128)} %param.14) | copy-start | bytes 772
  27.2 76.4 %collective-permute-start.3 = (s16[3,64,1024]{2,1,0:T(8,128)(2,1)}, s16[3,64,1024]{2,1,0:T(8,128)(2,1)}, u32[]{:S(2)}, u32[]{:S(2)}) collective-permute-start(s16[3,64,1024]{2,1,0:T(8,128)(2,1)} %get-tuple-element.59), channel_id=1, source_target_pairs={{0,16},{4,20},{8,24},{12,28},{16,0},{20,4},{24,8},{28,12},{1,17},{... | collective-permute-start | bytes 1179656 | tf_op jit(solution)/shard_map/ppermute | solution.py:363
  31.0 72.7 %collective-permute-start.2 = (s16[3,64,1024]{2,1,0:T(8,128)(2,1)}, s16[3,64,1024]{2,1,0:T(8,128)(2,1)S(1)}, u32[]{:S(2)}, u32[]{:S(2)}) collective-permute-start(s16[3,64,1024]{2,1,0:T(8,128)(2,1)} %get-tuple-element.60), channel_id=1, source_target_pairs={{0,8},{4,12},{8,0},{12,4},{16,24},{20,28},{24,16},{28,20},{1,9},{5... | collective-permute-start | bytes 1179656 | tf_op jit(solution)/shard_map/ppermute | solution.py:363
  34.7 70.7 %collective-permute-start.11 = (s16[3,64,1024]{2,1,0:T(8,128)(2,1)}, s16[3,64,1024]{2,1,0:T(8,128)(2,1)}, u32[]{:S(2)}, u32[]{:S(2)}) collective-permute-start(s16[3,64,1024]{2,1,0:T(8,128)(2,1)} %get-tuple-element.57), channel_id=1, source_target_pairs={{0,8},{4,12},{8,0},{12,4},{16,24},{20,28},{24,16},{28,20},{1,9},{5... | collective-permute-start | bytes 1179656 | tf_op jit(solution)/shard_map/ppermute | solution.py:363
  103.8 12.1 %collective-permute-start.6 = (s16[3,64,1024]{2,1,0:T(8,128)(2,1)S(1)}, s16[3,64,1024]{2,1,0:T(8,128)(2,1)S(1)}, u32[]{:S(2)}, u32[]{:S(2)}) collective-permute-start(s16[3,64,1024]{2,1,0:T(8,128)(2,1)S(1)} %bitcast_select_fusion.11), channel_id=1, source_target_pairs={{0,16},{4,20},{8,24},{12,28},{16,0},{20,4},{24,8},{28,12},{1,17},{... | collective-permute-start | bytes 1179656 | tf_op jit(solution)/shard_map/ppermute | solution.py:363
  106.3 18.1 %collective-permute-start.12 = (s16[3,64,1024]{2,1,0:T(8,128)(2,1)}, s16[3,64,1024]{2,1,0:T(8,128)(2,1)}, u32[]{:S(2)}, u32[]{:S(2)}) collective-permute-start(s16[3,64,1024]{2,1,0:T(8,128)(2,1)} %bitcast_select_fusion.5), channel_id=1, source_target_pairs={{0,16},{4,20},{8,24},{12,28},{16,0},{20,4},{24,8},{28,12},{1,17},{... | collective-permute-start | bytes 1179656 | tf_op jit(solution)/shard_map/ppermute | solution.py:363
  115.9 0.8 copy-start.4
  117.5 9.6 %collective-permute-start.7 = (s16[3,64,1024]{2,1,0:T(8,128)(2,1)}, s16[3,64,1024]{2,1,0:T(8,128)(2,1)}, u32[]{:S(2)}, u32[]{:S(2)}) collective-permute-start(s16[3,64,1024]{2,1,0:T(8,128)(2,1)} %bitcast_select_fusion.10), channel_id=1, source_target_pairs={{0,8},{4,12},{8,0},{12,4},{16,24},{20,28},{24,16},{28,20},{1,9},{5... | collective-permute-start | bytes 1179656 | tf_op jit(solution)/shard_map/ppermute | solution.py:363
  119.1 12.0 %collective-permute-start.14 = (s16[3,64,1024]{2,1,0:T(8,128)(2,1)}, s16[3,64,1024]{2,1,0:T(8,128)(2,1)S(1)}, u32[]{:S(2)}, u32[]{:S(2)}) collective-permute-start(s16[3,64,1024]{2,1,0:T(8,128)(2,1)} %get-tuple-element.56), channel_id=1, source_target_pairs={{0,16},{4,20},{8,24},{12,28},{16,0},{20,4},{24,8},{28,12},{1,17},{... | collective-permute-start | bytes 1179656 | tf_op jit(solution)/shard_map/ppermute | solution.py:363
  124.6 12.6 %collective-permute-start.13 = (s16[3,64,1024]{2,1,0:T(8,128)(2,1)S(1)}, s16[3,64,1024]{2,1,0:T(8,128)(2,1)S(1)}, u32[]{:S(2)}, u32[]{:S(2)}) collective-permute-start(s16[3,64,1024]{2,1,0:T(8,128)(2,1)S(1)} %bitcast_select_fusion.4), channel_id=1, source_target_pairs={{0,8},{4,12},{8,0},{12,4},{16,24},{20,28},{24,16},{28,20},{1,9},{5... | collective-permute-start | bytes 1179656 | tf_op jit(solution)/shard_map/ppermute | solution.py:363
  128.8 16.8 %collective-permute-start.8 = (s16[3,64,1024]{2,1,0:T(8,128)(2,1)S(1)}, s16[3,64,1024]{2,1,0:T(8,128)(2,1)S(1)}, u32[]{:S(2)}, u32[]{:S(2)}) collective-permute-start(s16[3,64,1024]{2,1,0:T(8,128)(2,1)S(1)} %get-tuple-element.58), channel_id=1, source_target_pairs={{0,8},{4,12},{8,0},{12,4},{16,24},{20,28},{24,16},{28,20},{1,9},{5... | collective-permute-start | bytes 1179656 | tf_op jit(solution)/shard_map/ppermute | solution.py:363
  138.7 12.1 %collective-permute-start.15 = (s16[3,64,1024]{2,1,0:T(8,128)(2,1)S(1)}, s16[3,64,1024]{2,1,0:T(8,128)(2,1)S(1)}, u32[]{:S(2)}, u32[]{:S(2)}) collective-permute-start(s16[3,64,1024]{2,1,0:T(8,128)(2,1)S(1)} %get-tuple-element.55), channel_id=1, source_target_pairs={{0,8},{4,12},{8,0},{12,4},{16,24},{20,28},{24,16},{28,20},{1,9},{5... | collective-permute-start | bytes 1179656 | tf_op jit(solution)/shard_map/ppermute | solution.py:363
  145.7 11.5 %collective-permute-start.9 = (s16[3,64,1024]{2,1,0:T(8,128)(2,1)S(1)}, s16[3,64,1024]{2,1,0:T(8,128)(2,1)S(1)}, u32[]{:S(2)}, u32[]{:S(2)}) collective-permute-start(s16[3,64,1024]{2,1,0:T(8,128)(2,1)S(1)} %bitcast_select_fusion.7), channel_id=1, source_target_pairs={{0,16},{4,20},{8,24},{12,28},{16,0},{20,4},{24,8},{28,12},{1,17},{... | collective-permute-start | bytes 1179656 | tf_op jit(solution)/shard_map/ppermute | solution.py:363
  151.0 11.1 %collective-permute-start.16 = (s16[3,64,1024]{2,1,0:T(8,128)(2,1)S(1)}, s16[3,64,1024]{2,1,0:T(8,128)(2,1)S(1)}, u32[]{:S(2)}, u32[]{:S(2)}) collective-permute-start(s16[3,64,1024]{2,1,0:T(8,128)(2,1)S(1)} %bitcast_select_fusion.1), channel_id=1, source_target_pairs={{0,16},{4,20},{8,24},{12,28},{16,0},{20,4},{24,8},{28,12},{1,17},{... | collective-permute-start | bytes 1179656 | tf_op jit(solution)/shard_map/ppermute | solution.py:363
  159.1 3.8 %collective-permute-start.10 = (s16[2,2,3,64,1024]{4,3,2,0,1:T(8,128)(2,1)}, s16[2,2,3,64,1024]{4,3,2,0,1:T(8,128)(2,1)}, u32[]{:S(2)}, u32[]{:S(2)}) collective-permute-start(s16[2,2,3,64,1024]{4,3,2,0,1:T(8,128)(2,1)} %pad_add_fusion), channel_id=1, source_target_pairs={{0,4},{4,0},{8,12},{12,8},{16,20},{20,16},{24,28},{28,24},{1,5},{5... | collective-permute-start | bytes 4718600 | tf_op jit(solution)/shard_map/ppermute | solution.py:363
  162.7 1.2 copy-start
  162.7 8.7 %collective-permute-start.17 = (s16[2,2,3,64,1024]{4,3,2,1,0:T(8,128)(2,1)S(1)}, s16[2,2,3,64,1024]{4,3,2,1,0:T(8,128)(2,1)}, u32[]{:S(2)}, u32[]{:S(2)}) collective-permute-start(s16[2,2,3,64,1024]{4,3,2,1,0:T(8,128)(2,1)S(1)} %pad_add_fusion.1.held1), channel_id=1, source_target_pairs={{0,4},{4,0},{8,12},{12,8},{16,20},{20,16},{24,28},{28,24},{1,5},{5... | collective-permute-start | bytes 4718600 | tf_op jit(solution)/shard_map/ppermute | solution.py:363
  163.9 7.4 %collective-permute-start.19 = (s16[2,3,16,1024]{3,2,1,0:T(8,128)(2,1)S(1)}, s16[2,3,16,1024]{3,2,1,0:T(8,128)(2,1)S(1)}, u32[]{:S(2)}, u32[]{:S(2)}) collective-permute-start(s16[2,3,16,1024]{3,2,1,0:T(8,128)(2,1)S(1)} %get-tuple-element.53), channel_id=1, source_target_pairs={{1,0},{2,1},{3,2},{0,3},{5,4},{6,5},{7,6},{4,7},{9,8},{10,9},{11,1... | collective-permute-start | bytes 589832 | tf_op jit(solution)/shard_map/ppermute | solution.py:359
  165.7 10.1 %collective-permute-start.18 = (s16[2,3,16,1024]{3,2,1,0:T(8,128)(2,1)S(1)}, s16[2,3,16,1024]{3,2,1,0:T(8,128)(2,1)S(1)}, u32[]{:S(2)}, u32[]{:S(2)}) collective-permute-start(s16[2,3,16,1024]{3,2,1,0:T(8,128)(2,1)S(1)} %get-tuple-element.54), channel_id=1, source_target_pairs={{0,1},{1,2},{2,3},{3,0},{4,5},{5,6},{6,7},{7,4},{8,9},{9,10},{10,1... | collective-permute-start | bytes 589832 | tf_op jit(solution)/shard_map/ppermute | solution.py:359
  171.4 4.5 %copy-start.5 = (s16[2,3,16,1024]{3,2,1,0:T(8,128)(2,1)}, s16[2,3,16,1024]{3,2,1,0:T(8,128)(2,1)S(1)}, u32[]{:S(2)}) copy-start(s16[2,3,16,1024]{3,2,1,0:T(8,128)(2,1)S(1)} %collective-permute-done.19.after) | copy-start | bytes 589828
  175.8 0.7 copy-start.6

commit v3 on v2

--- a/solution.py
+++ b/solution.py
@@ -13,6 +13,10 @@
 code_scale = 4096.0
 phases = 2
 streams = ((0, 3), (1, 2))
+
+
+def grant(mib):
+    return pltpu.CompilerParams(vmem_limit_bytes=mib << 20)
 
 
 def compact_kernel(length):
@@ -125,6 +129,7 @@
             ),
         ],
         out_specs=(spec,) * 2,
+        compiler_params=grant(16),
         cost_estimate=pl.CostEstimate(
             flops=0, bytes_accessed=2 * comps * deep * width, transcendentals=0
         ),
@@ -139,6 +144,7 @@
     planes = field.shape[1] // slab
     lanes = field.shape[2]
     column = pl.program_id(1)
+    comp = pl.program_id(0)
     gain = viscosity[0] * section_step
     side = pl.ds(pl.multiple_of(column * lanes, lanes), lanes)
 
@@ -153,9 +159,9 @@
             d1, d2, d3 = plane[z - 1], plane[z - 2], plane[z - 3]
             slope = 0.75 * (u1 - d1) - 0.15 * (u2 - d2) + (1.0 / 60.0) * (u3 - d3)
             curve = 1.5 * (u1 + d1) - 0.15 * (u2 + d2) + (1.0 / 90.0) * (u3 + d3)
-            inner[(0, p) + at] = centre
-            depth[(0, p) + at] = slope
-            sums[(0, p) + at] = centre + gain * (curve - (49.0 / 18.0) * centre)
+            inner[(comp, p) + at] = centre
+            depth[(comp, p) + at] = slope
+            sums[(comp, p) + at] = centre + gain * (curve - (49.0 / 18.0) * centre)
         return carry
 
     lax.fori_loop(0, slab // 8, unpack, 0, unroll=4)
@@ -163,14 +169,15 @@
     @pl.when(column == pl.num_programs(1) - 1)
     def _():
         field_rest(
-            gain, m_top, m_low, before, after, inner, along, across, sums, high_s, low_s, curve_s
+            gain, m_top, m_low, before, after, inner.at[comp], along.at[comp], across.at[comp],
+            sums.at[comp], high_s, low_s, curve_s,
         )
 
 
 def field_rest(
     gain, m_top, m_low, before, after, inner, along, across, sums, high_s, low_s, curve_s
 ):
-    slab = inner.shape[2]
+    slab = inner.shape[1]
     rows = m_low.shape[0]
     for p in range(2):
         for start, rim in ((0, before), (reach + slab, after)):
@@ -180,42 +187,43 @@
 
         def fill(i, carry):
             start = pl.multiple_of(i * 16, 16)
-            high, low = split(inner[0, p, pl.ds(start, 16), :])
+            high, low = split(inner[p, pl.ds(start, 16), :])
             at = pl.ds(pl.multiple_of(start + reach, 16), 16)
             high_s[at, :] = high
             low_s[at, :] = low
             return carry
 
-        lax.fori_loop(0, slab // 16, fill, 0)
+        lax.fori_loop(0, slab // 16, fill, 0, unroll=2)
         for b in range(slab // rows):
             window = pl.ds(b * rows, rows + 2 * reach)
             high, low = high_s[window, :], low_s[window, :]
             both = product(m_top[...], high) + product(m_top[...], low)
-            along[0, p, b * rows : (b + 1) * rows] = both[:rows] + product(m_low[...], high)
+            along[p, b * rows : (b + 1) * rows] = both[:rows] + product(m_low[...], high)
             curve_s[b * rows : (b + 1) * rows] = both[rows:]
 
         def body(i, carry):
             at = pl.ds(pl.multiple_of(i * 8, 8), 8)
-            pairs = shifted_pairs(inner[0, p, at, :])
-            across[0, p, at, :] = first_across(pairs)
+            pairs = shifted_pairs(inner[p, at, :])
+            across[p, at, :] = first_across(pairs)
             (u1, d1), (u2, d2), (u3, d3) = pairs
             curve = 1.5 * (u1 + d1) - 0.15 * (u2 + d2) + (1.0 / 90.0) * (u3 + d3)
             curve = curve + (1.0 / 180.0) * curve_s[at, :]
-            sums[0, p, at, :] = sums[0, p, at, :] + gain * curve
+            sums[p, at, :] = sums[p, at, :] + gain * curve
             return carry
 
-        lax.fori_loop(0, slab // 8, body, 0)
-
-
-def field_terms(field, before, after, viscosity, length):
+        lax.fori_loop(0, slab // 8, body, 0, unroll=4)
+
+
+def field_terms(field, viscosity, length):
     comps, slab, planes, width = field.shape
+    before, after = ring(field[:, slab - reach :, 3:5], field[:, :reach, 3:5])
     lanes = 128
     flat = field.reshape(comps, slab * planes, width)
     rows = min(slab, 128)
     high, low, second = along_matrices(rows, length)
     top = np.concatenate([high, second], 0)
-    shape = jax.ShapeDtypeStruct((comps, 2, slab, width), jnp.float32)
-    spec = pl.BlockSpec((1, 2, slab, width), lambda c, t: (c, 0, 0, 0))
+    shape = pltpu.VMEM((comps, 2, slab, width), jnp.float32)
+    spec = pl.BlockSpec(memory_space=pltpu.VMEM)
     rim = pl.BlockSpec((1, reach, 2, width), lambda c, t: (c, 0, 0, 0))
     return pl.pallas_call(
         field_kernel,
@@ -230,6 +238,7 @@
             rim,
         ],
         out_specs=(spec,) * 5,
+        compiler_params=grant(14),
         scratch_shapes=[
             pltpu.VMEM((slab + 2 * reach, width), jnp.bfloat16),
             pltpu.VMEM((slab + 2 * reach, width), jnp.bfloat16),
@@ -246,7 +255,7 @@
     inner, depth, along, across, sums, out, base_s, ghost_s, slope_s,
 ):
     step = pl.program_id(0)
-    rows = inner.shape[2]
+    rows = slope_s.shape[2]
     quarter = held0.shape[3]
     slab = 4 * quarter
     inverse = 1.0 / code_scale
@@ -303,7 +312,7 @@
             [base_s[c, p, inside, :].astype(jnp.float32) for p in range(2)] for c in range(3)
         ]
         for p in range(2):
-            move = [inner[c, p, at, :] for c in range(3)]
+            move = [inner[c, p, there, :] for c in range(3)]
             for c in range(3):
                 dz = decoded(ghost_s[c, p, there, :])
                 if p == 0:
@@ -311,24 +320,25 @@
                 else:
                     dz = dz - 0.75 * flow[c][0]
                 dy = first_across(shifted_pairs(flow[c][p]))
-                total = flow[0][p] * along[c, p, at, :] + flow[1][p] * across[c, p, at, :]
-                total = total + flow[2][p] * depth[c, p, at, :]
+                total = flow[0][p] * along[c, p, there, :] + flow[1][p] * across[c, p, there, :]
+                total = total + flow[2][p] * depth[c, p, there, :]
                 total = total + move[0] * slope_s[c, p, at, :] + move[1] * dy + move[2] * dz
-                out[0, c, at, p, :] = sums[c, p, at, :] - section_step * total
+                out[0, c, at, p, :] = sums[c, p, there, :] - section_step * total
         return carry
 
     lax.fori_loop(0, rows // 16, body, 0)
 
 
 def final(core, pieces, before, after, terms, length):
-    inner = terms[0]
-    comps, pair, slab, width = inner.shape
+    comps, pair, slab, width = terms[0].shape
     rows = 32
     high, low, _ = along_matrices(rows, length)
     both = np.concatenate([high, low], 0)
-    whole = pl.BlockSpec(pieces[0].shape, lambda i: (0, 0, 0, 0, 0))
+    whole = pl.BlockSpec(
+        pieces[0].shape, lambda i: (0, 0, 0, 0, 0), pipeline_mode=pl.Buffered(1)
+    )
     rim = pl.BlockSpec(before.shape, lambda i: (0, 0, 0, 0))
-    spec = pl.BlockSpec((comps, pair, rows, width), lambda i: (0, 0, i, 0))
+    spec = pl.BlockSpec(memory_space=pltpu.VMEM)
     return pl.pallas_call(
         final_kernel,
         out_shape=jax.ShapeDtypeStruct((1, comps, slab, pair, width), jnp.float32),
@@ -341,13 +351,14 @@
         + [rim] * 2
         + [spec] * 5,
         out_specs=pl.BlockSpec((1, comps, rows, pair, width), lambda i: (0, 0, i, 0, 0)),
+        compiler_params=grant(24),
         scratch_shapes=[
             pltpu.VMEM((comps, pair, slab + 2 * reach, width), jnp.bfloat16),
             pltpu.VMEM((comps, pair, slab, width), jnp.int16),
             pltpu.VMEM((comps, pair, rows, width), jnp.float32),
         ],
         cost_estimate=pl.CostEstimate(
-            flops=0, bytes_accessed=7 * 4 * inner.size, transcendentals=0
+            flops=0, bytes_accessed=8 * comps * pair * slab * width, transcendentals=0
         ),
     )(core, jnp.asarray(both), *pieces, before, after, *terms)
 
@@ -384,6 +395,7 @@
             if s > 0:
                 one = jnp.where(at_a, one, Y[u][s - 1])
                 two = jnp.where(at_a, two, X[u][s - 1])
+                one, two = lax.optimization_barrier((one, two))
             X[u].append(swap(one, 2))
             Y[u].append(swap(two, 4))
         if s == 0:
@@ -420,10 +432,6 @@
     in_pairs = lax.axis_size("pert") == 8
     core = (me % 2 if in_pairs else jnp.zeros_like(me)).astype(jnp.int32)[None]
     halves = [pack(tile, planes, core, u) for u in range(2)]
-    before, after = ring(
-        field[:, slab - reach :, 3:5],
-        field[:, :reach, 3:5],
-    )
     if in_pairs:
         held_field = []
 
@@ -433,7 +441,7 @@
             return kept[1:]
 
         def fill_second(x, y):
-            terms = field_terms(held_field[0], before, after, viscosity, length)
+            terms = field_terms(held_field[0], viscosity, length)
             x, y, *terms = lax.optimization_barrier((x, y) + tuple(terms))
             return x, y, terms
 
@@ -441,7 +449,7 @@
             [h[0] for h in halves], [h[1] for h in halves], owner_root, fill_first, fill_second
         )
     else:
-        terms = field_terms(field, before, after, viscosity, length)
+        terms = field_terms(field, viscosity, length)
         pieces = [
             lax.psum(jnp.where(me == owner_root, a, 0).astype(jnp.float32), "pert").astype(a.dtype)
             for h in halves

time: 201 us -> 185 us (0.920)
  Pallas kernels: 98.7 us -> 69.7 us
  local copies, waits for them, and re-layouts: 14.3 us -> 35.4 us
  starting transfers between devices: 28.8 us -> 19.9 us
  other arithmetic: 10.8 us -> 18.2 us
  waiting for transfers between devices: 44.6 us -> 39.4 us
    unnamed x16 -> x58, local copies, waits for them, and re-layouts: 3.72 us -> 27.5 us
    pallas_call x1, Pallas kernels: 63 us -> 42.2 us  [field_terms(): pl.pallas_call(field_kernel, out_shape=(shape,) * 5, grid=(comps, width /...]
    ppermute x16, waiting for transfers between devices: 34.8 us -> 21.7 us  [swap(): lax.ppermute(array, 'pert', [(i, i ^ bit) for i in range(lax.axis_size('p...]
    ppermute x16, starting transfers between devices: 21.8 us -> 12.8 us  [swap(): lax.ppermute(array, 'pert', [(i, i ^ bit) for i in range(lax.axis_size('p...]
    ppermute x4, waiting for transfers between devices: 9.79 us -> 17.7 us  [ring(): return (lax.ppermute(last, 'gx', up), lax.ppermute(first, 'gx', down))]
    pallas_call x2, Pallas kernels: 13.5 us -> 7.05 us  [pack(): pl.pallas_call(pack_kernel, out_shape=(shape,) * 2, grid=(2, comps), in_s...]
    select_n x2, other arithmetic: 1.36 us -> 5.35 us  [exchange(): source.append(jnp.where(is_root, mine[u], swap(theirs[u], 1)))]
    select_n x4, other arithmetic: 1.31 us -> 4.18 us  [exchange(): two = jnp.where(at_a, two, X[u][s - 1])]
  transfers between devices with their start and end apart: 20 -> 20, of which waited for: 11 -> 10; matrix products, arithmetic and copies ran while one was open for 11% -> 11% of each run, Pallas kernels for 35% -> 25%
where the time goes in v3:
time: 185 us; the launch traced here: 184 us
  Pallas kernels  69.7 us (38%)
  waiting for transfers between devices  39.4 us (21%)
  local copies, waits for them, and re-layouts  35.4 us (19%)
  starting transfers between devices  19.9 us (11%)
  other arithmetic  18.2 us (10%)
    pallas_call x1, Pallas kernels, field_terms(): pl.pallas_call(field_kernel, out_shape=(shape,) * 5, grid=(comps, width /...  42.2 us
    unnamed x58, local copies, waits for them, and re-layouts  27.5 us
    ppermute x16, waiting for transfers between devices, swap(): lax.ppermute(array, 'pert', [(i, i ^ bit) for i in range(lax.axis_size('p...  21.7 us
    pallas_call x1, Pallas kernels, final(): pl.pallas_call(final_kernel, out_shape=jax.ShapeDtypeStruct((1, comps, sl...  20.5 us
    ppermute x4, waiting for transfers between devices, ring(): return (lax.ppermute(last, 'gx', up), lax.ppermute(first, 'gx', down))  17.7 us
    ppermute x16, starting transfers between devices, swap(): lax.ppermute(array, 'pert', [(i, i ^ bit) for i in range(lax.axis_size('p...  12.8 us
    ppermute x4, starting transfers between devices, ring(): return (lax.ppermute(last, 'gx', up), lax.ppermute(first, 'gx', down))  7.13 us
    pallas_call x2, Pallas kernels, pack(): pl.pallas_call(pack_kernel, out_shape=(shape,) * 2, grid=(2, comps), in_s...  7.05 us
  transfers between devices with their start and end apart: 20, of which 10 were waited for; matrix products, arithmetic and copies ran while one was open for 11% of the time, Pallas kernels for 25%

profile of v3, /device:TPU:0, one launch (start us, length us, event | category | flops | bytes accessed | tf_op | source)
XLA Modules:
  0.0 184.2 jit_solution(17584634289501537090)
XLA Ops:
  0.0 4.6 %copy-done = bf16[1,3,256,8,1024]{4,3,2,1,0:T(8,128)(2,1)S(1)} copy-done((bf16[1,3,256,8,1024]{4,3,2,1,0:T(8,128)(2,1)S(1)}, bf16[1,3,256,8,1024]{4,3,2,1,0:T(8,128)(2,1)}, u32[]{:S(2)}) %copy-start) | copy-done | bytes 12582936
  5.4 3.5 %shard_map.101 = (s16[2,2,3,64,1024]{4,3,2,1,0:T(8,128)(2,1)S(1)}, s16[2,2,3,64,1024]{4,3,2,1,0:T(8,128)(2,1)}) custom-call(s32[1]{0:T(128)} %bitcast.core, bf16[128,256]{1,0:T(8,128)(2,1)S(1)} %copy-done.9, bf16[3,2048,1024]{2,1,0:T(8,128)(2,1)S(1)} %bitcast.83), custom_call_target="tpu_custom_call" | custom-call | bytes 12582912 | tf_op jit(solution)/shard_map/pallas_call | solution.py:120
  9.4 3.5 %shard_map.100 = (s16[2,2,3,64,1024]{4,3,2,1,0:T(8,128)(2,1)S(1)}, s16[2,2,3,64,1024]{4,3,2,1,0:T(8,128)(2,1)}) custom-call(s32[1]{0:T(128)} %bitcast.core, bf16[128,256]{1,0:T(8,128)(2,1)S(1)} %copy-done.9, bf16[3,2048,1024]{2,1,0:T(8,128)(2,1)S(1)} %bitcast.84), custom_call_target="tpu_custom_call" | custom-call | bytes 12582912 | tf_op jit(solution)/shard_map/pallas_call | solution.py:120
  13.6 3.3 %broadcast_select_fusion.1 = s16[2,2,3,64,1024]{4,3,2,1,0:T(8,128)(2,1)} fusion(s16[2,2,3,64,1024]{4,3,2,1,0:T(8,128)(2,1)S(1)} %get-tuple-element.34, s16[2,2,3,64,1024]{4,3,2,1,0:T(8,128)(2,1)} %collective-permute-done.1, pred[]{:T(512)S(6)} %eq.24), kind=kLoop, calls=%fused_computation.3 | loop fusion | flops 786432 | bytes 4718593 | tf_op jit(solution)/shard_map/jit(_where)/select_n | solution.py:384
  16.9 2.1 %broadcast_select_fusion.2 = s16[2,2,3,64,1024]{4,3,2,1,0:T(8,128)(2,1)S(1)} fusion(s16[2,2,3,64,1024]{4,3,2,1,0:T(8,128)(2,1)S(1)} %get-tuple-element.32, s16[2,2,3,64,1024]{4,3,2,1,0:T(8,128)(2,1)} %collective-permute-done, pred[]{:T(512)S(6)} %eq.24), kind=kLoop, calls=%fused_computation.4 | loop fusion | flops 786432 | bytes 4718593 | tf_op jit(solution)/shard_map/jit(_where)/select_n | solution.py:384
  19.0 3.8 %fusion.5 = (f32[3,16,2,1024]{3,2,1,0:T(2,128)}, f32[3,16,2,1024]{3,2,1,0:T(2,128)}) fusion(f32[3,256,8,1024]{3,2,1,0:T(8,128)} %bitcast.85), kind=kLoop, calls=%fused_computation.37 | loop fusion | bytes 1572864 | tf_op jit(solution)/shard_map/slice | solution.py:219
  22.8 5.1 %collective-permute-start.5 = (f32[3,16,2,1024]{3,2,1,0:T(2,128)}, f32[3,16,2,1024]{3,2,1,0:T(2,128)S(1)}, u32[]{:S(2)}, u32[]{:S(2)}) collective-permute-start(f32[3,16,2,1024]{3,2,1,0:T(2,128)} %get-tuple-element.59), channel_id=1, source_target_pairs={{1,0},{2,1},{3,2},{0,3},{5,4},{6,5},{7,6},{4,7},{9,8},{10,9},{11,1... | collective-permute-start | bytes 1179656 | tf_op jit(solution)/shard_map/ppermute | solution.py:370
  31.7 2.1 %collective-permute-start.11 = (s16[3,64,1024]{2,1,0:T(8,128)(2,1)S(1)}, s16[3,64,1024]{2,1,0:T(8,128)(2,1)S(1)}, u32[]{:S(2)}, u32[]{:S(2)}) collective-permute-start(s16[3,64,1024]{2,1,0:T(8,128)(2,1)S(1)} %get-tuple-element.77), channel_id=1, source_target_pairs={{0,8},{4,12},{8,0},{12,4},{16,24},{20,28},{24,16},{28,20},{1,9},{5... | collective-permute-start | bytes 1179656 | tf_op jit(solution)/shard_map/ppermute | solution.py:374
  33.8 3.9 %collective-permute-done.5.after = f32[3,16,2,1024]{3,2,1,0:T(2,128)S(1)} collective-permute-done((f32[3,16,2,1024]{3,2,1,0:T(2,128)}, f32[3,16,2,1024]{3,2,1,0:T(2,128)S(1)}, u32[]{:S(2)}, u32[]{:S(2)}) %collective-permute-start.5) | collective-permute-done | bytes 393248 | tf_op jit(solution)/shard_map/ppermute | solution.py:370
  39.2 6.7 %collective-permute-done.4.before = f32[3,16,2,1024]{3,2,1,0:T(2,128)S(1)} collective-permute-done((f32[3,16,2,1024]{3,2,1,0:T(2,128)}, f32[3,16,2,1024]{3,2,1,0:T(2,128)S(1)}, u32[]{:S(2)}, u32[]{:S(2)}) %collective-permute-start.4) | collective-permute-done | bytes 393248 | tf_op jit(solution)/shard_map/ppermute | solution.py:370
  46.0 42.2 %shard_map.102 = (f32[3,2,256,1024]{3,2,1,0:T(8,128)S(1)}, f32[3,2,256,1024]{3,2,1,0:T(8,128)S(1)}, f32[3,2,256,1024]{3,2,1,0:T(8,128)S(1)}, f32[3,2,256,1024]{3,2,1,0:T(8,128)S(1)}, f32[3,2,256,1024]{3,2,1,0:T(8,128)S(1)}) custom-call(f32[1]{0:T(128)} %bitcast.7.viscosity, bf16[256,160]{1,0:T(8,128)(2,1)S(1)} %copy-done.10, ...), custom_call_target="tpu_custom_call" | custom-call | bytes 56623104 | tf_op jit(solution)/shard_map/pallas_call | solution.py:228
  88.1 2.7 %copy-done.1 = f32[3,2,256,1024]{3,2,1,0:T(8,128)} copy-done((f32[3,2,256,1024]{3,2,1,0:T(8,128)}, f32[3,2,256,1024]{3,2,1,0:T(8,128)S(1)}, u32[]{:S(2)}) %copy-start.1) | copy-done | bytes 6291480
  90.8 2.6 %copy-done.3 = f32[3,2,256,1024]{3,2,1,0:T(8,128)} copy-done((f32[3,2,256,1024]{3,2,1,0:T(8,128)}, f32[3,2,256,1024]{3,2,1,0:T(8,128)S(1)}, u32[]{:S(2)}) %copy-start.3) | copy-done | bytes 6291480
  93.4 2.7 %copy-done.5 = f32[3,2,256,1024]{3,2,1,0:T(8,128)} copy-done((f32[3,2,256,1024]{3,2,1,0:T(8,128)}, f32[3,2,256,1024]{3,2,1,0:T(8,128)S(1)}, u32[]{:S(2)}) %copy-start.5) | copy-done | bytes 6291480
  96.1 2.7 %copy-done.7 = f32[3,2,256,1024]{3,2,1,0:T(8,128)} copy-done((f32[3,2,256,1024]{3,2,1,0:T(8,128)}, f32[3,2,256,1024]{3,2,1,0:T(8,128)S(1)}, u32[]{:S(2)}) %copy-start.7) | copy-done | bytes 6291480
  98.8 2.7 %copy-done.8 = f32[3,2,256,1024]{3,2,1,0:T(8,128)} copy-done((f32[3,2,256,1024]{3,2,1,0:T(8,128)}, f32[3,2,256,1024]{3,2,1,0:T(8,128)S(1)}, u32[]{:S(2)}) %copy-start.8) | copy-done | bytes 6291480
  104.7 1.9 %collective-permute-start.13 = (s16[3,64,1024]{2,1,0:T(8,128)(2,1)}, s16[3,64,1024]{2,1,0:T(8,128)(2,1)}, u32[]{:S(2)}, u32[]{:S(2)}) collective-permute-start(s16[3,64,1024]{2,1,0:T(8,128)(2,1)} %get-tuple-element.50), channel_id=1, source_target_pairs={{0,16},{4,20},{8,24},{12,28},{16,0},{20,4},{24,8},{28,12},{1,17},{... | collective-permute-start | bytes 1179656 | tf_op jit(solution)/shard_map/ppermute | solution.py:374
  107.2 6.7 %collective-permute-done.6 = s16[3,64,1024]{2,1,0:T(8,128)(2,1)S(1)} collective-permute-done((s16[3,64,1024]{2,1,0:T(8,128)(2,1)S(1)}, s16[3,64,1024]{2,1,0:T(8,128)(2,1)S(1)}, u32[]{:S(2)}, u32[]{:S(2)}) %collective-permute-start.6) | collective-permute-done | bytes 393248 | tf_op jit(solution)/shard_map/ppermute | solution.py:374
  116.8 2.0 %collective-permute-start.9 = (s16[3,64,1024]{2,1,0:T(8,128)(2,1)}, s16[3,64,1024]{2,1,0:T(8,128)(2,1)}, u32[]{:S(2)}, u32[]{:S(2)}) collective-permute-start(s16[3,64,1024]{2,1,0:T(8,128)(2,1)} %get-tuple-element.48), channel_id=1, source_target_pairs={{0,16},{4,20},{8,24},{12,28},{16,0},{20,4},{24,8},{28,12},{1,17},{... | collective-permute-start | bytes 1179656 | tf_op jit(solution)/shard_map/ppermute | solution.py:374
  118.7 3.7 %collective-permute-done.13 = s16[3,64,1024]{2,1,0:T(8,128)(2,1)} collective-permute-done((s16[3,64,1024]{2,1,0:T(8,128)(2,1)}, s16[3,64,1024]{2,1,0:T(8,128)(2,1)}, u32[]{:S(2)}, u32[]{:S(2)}) %collective-permute-start.13) | collective-permute-done | bytes 393248 | tf_op jit(solution)/shard_map/ppermute | solution.py:374
  126.4 6.0 %collective-permute-done.8 = s16[3,64,1024]{2,1,0:T(8,128)(2,1)} collective-permute-done((s16[3,64,1024]{2,1,0:T(8,128)(2,1)}, s16[3,64,1024]{2,1,0:T(8,128)(2,1)}, u32[]{:S(2)}, u32[]{:S(2)}) %collective-permute-start.8) | collective-permute-done | bytes 393248 | tf_op jit(solution)/shard_map/ppermute | solution.py:374
  132.4 2.1 %select_bitcast_fusion.3 = (s16[1,3,64,1024]{3,2,1,0:T(8,128)(2,1)S(1)}, s16[1,3,64,1024]{3,2,1,0:T(8,128)(2,1)S(1)}, s16[1,3,64,1024]{3,2,1,0:T(8,128)(2,1)S(1)}, s16[1,3,64,1024]{3,2,1,0:T(8,128)(2,1)S(1)}) fusion(s16[3,64,1024]{2,1,0:T(8,128)(2,1)S(1)} %copy-done.20, s16[3,64,1024]{2,1,0:T(8,128)(2,1)} %collective-permute-done.8, ...), kind=kLoop, calls=%fused_computation.30 | loop fusion | flops 1966080 | bytes 5505027 | tf_op jit(solution)/shard_map/stack | solution.py:414
  136.5 2.2 %collective-permute-done.15 = s16[3,64,1024]{2,1,0:T(8,128)(2,1)S(1)} collective-permute-done((s16[3,64,1024]{2,1,0:T(8,128)(2,1)S(1)}, s16[3,64,1024]{2,1,0:T(8,128)(2,1)S(1)}, u32[]{:S(2)}, u32[]{:S(2)}) %collective-permute-start.15) | collective-permute-done | bytes 393248 | tf_op jit(solution)/shard_map/ppermute | solution.py:374
  138.6 2.0 %select_bitcast_fusion.1 = (s16[1,3,64,1024]{3,2,1,0:T(8,128)(2,1)S(1)}, s16[1,3,64,1024]{3,2,1,0:T(8,128)(2,1)S(1)}, s16[1,3,64,1024]{3,2,1,0:T(8,128)(2,1)S(1)}, s16[1,3,64,1024]{3,2,1,0:T(8,128)(2,1)S(1)}) fusion(s16[3,64,1024]{2,1,0:T(8,128)(2,1)S(1)} %copy-done.22, s16[3,64,1024]{2,1,0:T(8,128)(2,1)S(1)} %collective-permute-done.15, ...), kind=kLoop, calls=%fused_computation.26 | loop fusion | flops 1966080 | bytes 5505027 | tf_op jit(solution)/shard_map/stack | solution.py:414
  141.1 2.1 %broadcast_select_fusion = s16[2,2,3,64,1024]{4,3,2,0,1:T(8,128)(2,1)S(1)} fusion(s16[2,2,3,64,1024]{4,3,2,0,1:T(8,128)(2,1)} %collective-permute-done.10, pred[]{:T(512)S(6)} %eq.29, s16[1,2,3,64,1024]{4,3,2,0,1:T(8,128)(2,1)} %copy-done.18, s16[1,2,3,64,1024]{4,3,2,0,1:T(8,128)(2,1)} %copy-done.17), kind=kLoop, calls=%fused_computation.2 | loop fusion | flops 1572864 | bytes 4718593 | tf_op jit(solution)/shard_map/jit(_where)/select_n | solution.py:458
  143.2 1.7 collective-permute-start.19
  148.3 2.6 %collective-permute-done.19.after = s16[2,3,16,1024]{3,2,1,0:T(8,128)(2,1)S(1)} collective-permute-done((s16[2,3,16,1024]{3,2,1,0:T(8,128)(2,1)S(1)}, s16[2,3,16,1024]{3,2,1,0:T(8,128)(2,1)S(1)}, u32[]{:S(2)}, u32[]{:S(2)}) %collective-permute-start.19) | collective-permute-done | bytes 196640 | tf_op jit(solution)/shard_map/ppermute | solution.py:370
  151.0 4.4 %collective-permute-done.18.before = s16[2,3,16,1024]{3,2,1,0:T(8,128)(2,1)S(1)} collective-permute-done((s16[2,3,16,1024]{3,2,1,0:T(8,128)(2,1)S(1)}, s16[2,3,16,1024]{3,2,1,0:T(8,128)(2,1)S(1)}, u32[]{:S(2)}, u32[]{:S(2)}) %collective-permute-start.18) | collective-permute-done | bytes 196640 | tf_op jit(solution)/shard_map/ppermute | solution.py:370
  155.4 2.8 %copy-done.2 = f32[3,2,256,1024]{3,2,1,0:T(8,128)S(1)} copy-done((f32[3,2,256,1024]{3,2,1,0:T(8,128)S(1)}, f32[3,2,256,1024]{3,2,1,0:T(8,128)}, u32[]{:S(2)}) %copy-start.2) | copy-done | bytes 6291480
  158.2 2.8 %copy-done.4 = f32[3,2,256,1024]{3,2,1,0:T(8,128)S(1)} copy-done((f32[3,2,256,1024]{3,2,1,0:T(8,128)S(1)}, f32[3,2,256,1024]{3,2,1,0:T(8,128)}, u32[]{:S(2)}) %copy-start.4) | copy-done | bytes 6291480
  161.0 2.8 %copy-done.6 = f32[3,2,256,1024]{3,2,1,0:T(8,128)S(1)} copy-done((f32[3,2,256,1024]{3,2,1,0:T(8,128)S(1)}, f32[3,2,256,1024]{3,2,1,0:T(8,128)}, u32[]{:S(2)}) %copy-start.6) | copy-done | bytes 6291480
  163.8 20.5 %shard_map.103 = f32[1,3,256,2,1024]{4,3,2,1,0:T(2,128)} custom-call(s32[1]{0:T(128)} %bitcast.core, bf16[64,64]{1,0:T(8,128)(2,1)S(1)} %copy-done.12, s16[2,2,3,64,1024]{4,3,2,1,0:T(8,128)(2,1)S(1)} %copy.12.held0, s16[2,2,3,64,1024]{4,3,2,1,0:T(8,128)(2,1)S(1)} %copy.13.other0, s16[2,2,3,64,1024]{4,3,2,1,0:T(8,128)(2,1)S(1)} %pad_add_fusion.1.held1, ...), custom_call_target="tpu_custom_call" | custom-call | bytes 12582912 | tf_op jit(solution)/shard_map/pallas_call | solution.py:342
  (90 shorter events, 22.2 us)
Async XLA Ops:
  9.0 4.7 %collective-permute-start.1 = (s16[2,2,3,64,1024]{4,3,2,1,0:T(8,128)(2,1)}, s16[2,2,3,64,1024]{4,3,2,1,0:T(8,128)(2,1)}, u32[]{:S(2)}, u32[]{:S(2)}) collective-permute-start(s16[2,2,3,64,1024]{4,3,2,1,0:T(8,128)(2,1)} %get-tuple-element.35), channel_id=1, source_target_pairs={{0,4},{4,0},{8,12},{12,8},{16,20},{20,16},{24,28},{28,24},{1,5},{5... | collective-permute-start | bytes 4718600 | tf_op jit(solution)/shard_map/ppermute | solution.py:374
  12.9 4.0 %collective-permute-start = (s16[2,2,3,64,1024]{4,3,2,1,0:T(8,128)(2,1)}, s16[2,2,3,64,1024]{4,3,2,1,0:T(8,128)(2,1)}, u32[]{:S(2)}, u32[]{:S(2)}) collective-permute-start(s16[2,2,3,64,1024]{4,3,2,1,0:T(8,128)(2,1)} %get-tuple-element.33), channel_id=1, source_target_pairs={{0,4},{4,0},{8,12},{12,8},{16,20},{20,16},{24,28},{28,24},{1,5},{5... | collective-permute-start | bytes 4718600 | tf_op jit(solution)/shard_map/ppermute | solution.py:374
  19.0 9.8 %copy-start.14 = (s16[2,2,3,64,1024]{4,3,2,1,0:T(8,128)(2,1)}, s16[2,2,3,64,1024]{4,3,2,1,0:T(8,128)(2,1)S(1)}, u32[]{:S(2)}) copy-start(s16[2,2,3,64,1024]{4,3,2,1,0:T(8,128)(2,1)S(1)} %broadcast_select_fusion.2) | copy-start | bytes 4718596
  19.0 12.0 %copy-start.28 = (f32[64]{0:T(128)S(1)}, f32[64]{0:T(128)}, u32[]{:S(2)}) copy-start(f32[64]{0:T(128)} %param.14) | copy-start | bytes 772
  19.0 12.7 %copy-start.13 = (s16[2,2,3,64,1024]{4,3,2,1,0:T(8,128)(2,1)S(1)}, s16[2,2,3,64,1024]{4,3,2,1,0:T(8,128)(2,1)}, u32[]{:S(2)}) copy-start(s16[2,2,3,64,1024]{4,3,2,1,0:T(8,128)(2,1)} %broadcast_select_fusion.1) | copy-start | bytes 4718596
  22.8 14.9 %collective-permute-start.5 = (f32[3,16,2,1024]{3,2,1,0:T(2,128)}, f32[3,16,2,1024]{3,2,1,0:T(2,128)S(1)}, u32[]{:S(2)}, u32[]{:S(2)}) collective-permute-start(f32[3,16,2,1024]{3,2,1,0:T(2,128)} %get-tuple-element.59), channel_id=1, source_target_pairs={{1,0},{2,1},{3,2},{0,3},{5,4},{6,5},{7,6},{4,7},{9,8},{10,9},{11,1... | collective-permute-start | bytes 1179656 | tf_op jit(solution)/shard_map/ppermute | solution.py:370
  27.8 18.1 %copy-start.10 = (bf16[256,160]{1,0:T(8,128)(2,1)S(1)}, bf16[256,160]{1,0:T(8,128)(2,1)}, u32[]{:S(2)}) copy-start(bf16[256,160]{1,0:T(8,128)(2,1)} %constant.58.clone.m_top) | copy-start | bytes 245764
  27.8 18.1 %copy-start.11 = (bf16[128,160]{1,0:T(8,128)(2,1)S(1)}, bf16[128,160]{1,0:T(8,128)(2,1)}, u32[]{:S(2)}) copy-start(bf16[128,160]{1,0:T(8,128)(2,1)} %constant.59.clone.m_low) | copy-start | bytes 122884
  27.8 18.1 %collective-permute-start.4 = (f32[3,16,2,1024]{3,2,1,0:T(2,128)}, f32[3,16,2,1024]{3,2,1,0:T(2,128)S(1)}, u32[]{:S(2)}, u32[]{:S(2)}) collective-permute-start(f32[3,16,2,1024]{3,2,1,0:T(2,128)} %get-tuple-element.60), channel_id=1, source_target_pairs={{0,1},{1,2},{2,3},{3,0},{4,5},{5,6},{6,7},{7,4},{8,9},{9,10},{10,1... | collective-permute-start | bytes 1179656 | tf_op jit(solution)/shard_map/ppermute | solution.py:370
  28.8 72.7 %collective-permute-start.3 = (s16[3,64,1024]{2,1,0:T(8,128)(2,1)}, s16[3,64,1024]{2,1,0:T(8,128)(2,1)S(1)}, u32[]{:S(2)}, u32[]{:S(2)}) collective-permute-start(s16[3,64,1024]{2,1,0:T(8,128)(2,1)} %get-tuple-element.85), channel_id=1, source_target_pairs={{0,16},{4,20},{8,24},{12,28},{16,0},{20,4},{24,8},{28,12},{1,17},{... | collective-permute-start | bytes 1179656 | tf_op jit(solution)/shard_map/ppermute | solution.py:374
  30.3 71.2 %collective-permute-start.2 = (s16[3,64,1024]{2,1,0:T(8,128)(2,1)}, s16[3,64,1024]{2,1,0:T(8,128)(2,1)S(1)}, u32[]{:S(2)}, u32[]{:S(2)}) collective-permute-start(s16[3,64,1024]{2,1,0:T(8,128)(2,1)} %get-tuple-element.86), channel_id=1, source_target_pairs={{0,8},{4,12},{8,0},{12,4},{16,24},{20,28},{24,16},{28,20},{1,9},{5... | collective-permute-start | bytes 1179656 | tf_op jit(solution)/shard_map/ppermute | solution.py:374
  31.7 71.7 %collective-permute-start.11 = (s16[3,64,1024]{2,1,0:T(8,128)(2,1)S(1)}, s16[3,64,1024]{2,1,0:T(8,128)(2,1)S(1)}, u32[]{:S(2)}, u32[]{:S(2)}) collective-permute-start(s16[3,64,1024]{2,1,0:T(8,128)(2,1)S(1)} %get-tuple-element.77), channel_id=1, source_target_pairs={{0,8},{4,12},{8,0},{12,4},{16,24},{20,28},{24,16},{28,20},{1,9},{5... | collective-permute-start | bytes 1179656 | tf_op jit(solution)/shard_map/ppermute | solution.py:374
  37.7 65.8 %collective-permute-start.12 = (s16[3,64,1024]{2,1,0:T(8,128)(2,1)S(1)}, s16[3,64,1024]{2,1,0:T(8,128)(2,1)S(1)}, u32[]{:S(2)}, u32[]{:S(2)}) collective-permute-start(s16[3,64,1024]{2,1,0:T(8,128)(2,1)S(1)} %get-tuple-element.78), channel_id=1, source_target_pairs={{0,16},{4,20},{8,24},{12,28},{16,0},{20,4},{24,8},{28,12},{1,17},{... | collective-permute-start | bytes 1179656 | tf_op jit(solution)/shard_map/ppermute | solution.py:374
  46.0 55.5 %copy-start.15 = (s16[2,2,3,64,1024]{4,3,2,1,0:T(8,128)(2,1)S(1)}, s16[2,2,3,64,1024]{4,3,2,1,0:T(8,128)(2,1)}, u32[]{:S(2)}) copy-start(s16[2,2,3,64,1024]{4,3,2,1,0:T(8,128)(2,1)} %copy-done.14) | copy-start | bytes 4718596
  101.8 12.1 %collective-permute-start.6 = (s16[3,64,1024]{2,1,0:T(8,128)(2,1)S(1)}, s16[3,64,1024]{2,1,0:T(8,128)(2,1)S(1)}, u32[]{:S(2)}, u32[]{:S(2)}) collective-permute-start(s16[3,64,1024]{2,1,0:T(8,128)(2,1)S(1)} %get-tuple-element.45), channel_id=1, source_target_pairs={{0,16},{4,20},{8,24},{12,28},{16,0},{20,4},{24,8},{28,12},{1,17},{... | collective-permute-start | bytes 1179656 | tf_op jit(solution)/shard_map/ppermute | solution.py:374
  103.4 12.1 %collective-permute-start.7 = (s16[3,64,1024]{2,1,0:T(8,128)(2,1)S(1)}, s16[3,64,1024]{2,1,0:T(8,128)(2,1)S(1)}, u32[]{:S(2)}, u32[]{:S(2)}) collective-permute-start(s16[3,64,1024]{2,1,0:T(8,128)(2,1)S(1)} %get-tuple-element.46), channel_id=1, source_target_pairs={{0,8},{4,12},{8,0},{12,4},{16,24},{20,28},{24,16},{28,20},{1,9},{5... | collective-permute-start | bytes 1179656 | tf_op jit(solution)/shard_map/ppermute | solution.py:374
  103.5 13.2 %copy-start.21 = (s16[3,64,1024]{2,1,0:T(8,128)(2,1)}, s16[3,64,1024]{2,1,0:T(8,128)(2,1)S(1)}, u32[]{:S(2)}) copy-start(s16[3,64,1024]{2,1,0:T(8,128)(2,1)S(1)} %collective-permute-done.11) | copy-start | bytes 1179652
  103.5 13.2 %copy-start.23 = (s16[3,64,1024]{2,1,0:T(8,128)(2,1)}, s16[3,64,1024]{2,1,0:T(8,128)(2,1)S(1)}, u32[]{:S(2)}) copy-start(s16[3,64,1024]{2,1,0:T(8,128)(2,1)S(1)} %collective-permute-done.12) | copy-start | bytes 1179652
  104.7 17.7 %collective-permute-start.13 = (s16[3,64,1024]{2,1,0:T(8,128)(2,1)}, s16[3,64,1024]{2,1,0:T(8,128)(2,1)}, u32[]{:S(2)}, u32[]{:S(2)}) collective-permute-start(s16[3,64,1024]{2,1,0:T(8,128)(2,1)} %get-tuple-element.50), channel_id=1, source_target_pairs={{0,16},{4,20},{8,24},{12,28},{16,0},{20,4},{24,8},{28,12},{1,17},{... | collective-permute-start | bytes 1179656 | tf_op jit(solution)/shard_map/ppermute | solution.py:374
  106.7 17.3 %collective-permute-start.14 = (s16[3,64,1024]{2,1,0:T(8,128)(2,1)}, s16[3,64,1024]{2,1,0:T(8,128)(2,1)}, u32[]{:S(2)}, u32[]{:S(2)}) collective-permute-start(s16[3,64,1024]{2,1,0:T(8,128)(2,1)} %get-tuple-element.51), channel_id=1, source_target_pairs={{0,8},{4,12},{8,0},{12,4},{16,24},{20,28},{24,16},{28,20},{1,9},{5... | collective-permute-start | bytes 1179656 | tf_op jit(solution)/shard_map/ppermute | solution.py:374
  116.7 15.8 %copy-start.16 = (s16[2,2,3,64,1024]{4,3,2,1,0:T(8,128)(2,1)S(1)}, s16[2,2,3,64,1024]{4,3,2,1,0:T(8,128)(2,1)}, u32[]{:S(2)}) copy-start(s16[2,2,3,64,1024]{4,3,2,1,0:T(8,128)(2,1)} %copy-done.14) | copy-start | bytes 4718596
  116.7 15.7 %collective-permute-start.8 = (s16[3,64,1024]{2,1,0:T(8,128)(2,1)}, s16[3,64,1024]{2,1,0:T(8,128)(2,1)}, u32[]{:S(2)}, u32[]{:S(2)}) collective-permute-start(s16[3,64,1024]{2,1,0:T(8,128)(2,1)} %get-tuple-element.47), channel_id=1, source_target_pairs={{0,8},{4,12},{8,0},{12,4},{16,24},{20,28},{24,16},{28,20},{1,9},{5... | collective-permute-start | bytes 1179656 | tf_op jit(solution)/shard_map/ppermute | solution.py:374
  116.8 15.7 %collective-permute-start.9 = (s16[3,64,1024]{2,1,0:T(8,128)(2,1)}, s16[3,64,1024]{2,1,0:T(8,128)(2,1)}, u32[]{:S(2)}, u32[]{:S(2)}) collective-permute-start(s16[3,64,1024]{2,1,0:T(8,128)(2,1)} %get-tuple-element.48), channel_id=1, source_target_pairs={{0,16},{4,20},{8,24},{12,28},{16,0},{20,4},{24,8},{28,12},{1,17},{... | collective-permute-start | bytes 1179656 | tf_op jit(solution)/shard_map/ppermute | solution.py:374
  118.7 13.7 %copy-start.20 = (s16[3,64,1024]{2,1,0:T(8,128)(2,1)S(1)}, s16[3,64,1024]{2,1,0:T(8,128)(2,1)}, u32[]{:S(2)}) copy-start(s16[3,64,1024]{2,1,0:T(8,128)(2,1)} %copy-done.19) | copy-start | bytes 1179652
  118.7 13.7 %copy-start.26 = (s16[3,64,1024]{2,1,0:T(8,128)(2,1)S(1)}, s16[3,64,1024]{2,1,0:T(8,128)(2,1)}, u32[]{:S(2)}) copy-start(s16[3,64,1024]{2,1,0:T(8,128)(2,1)} %copy-done.25) | copy-start | bytes 1179652
  125.4 13.2 %collective-permute-start.15 = (s16[3,64,1024]{2,1,0:T(8,128)(2,1)S(1)}, s16[3,64,1024]{2,1,0:T(8,128)(2,1)S(1)}, u32[]{:S(2)}, u32[]{:S(2)}) collective-permute-start(s16[3,64,1024]{2,1,0:T(8,128)(2,1)S(1)} %get-tuple-element.52), channel_id=1, source_target_pairs={{0,8},{4,12},{8,0},{12,4},{16,24},{20,28},{24,16},{28,20},{1,9},{5... | collective-permute-start | bytes 1179656 | tf_op jit(solution)/shard_map/ppermute | solution.py:374
  125.5 13.1 %collective-permute-start.16 = (s16[3,64,1024]{2,1,0:T(8,128)(2,1)S(1)}, s16[3,64,1024]{2,1,0:T(8,128)(2,1)S(1)}, u32[]{:S(2)}, u32[]{:S(2)}) collective-permute-start(s16[3,64,1024]{2,1,0:T(8,128)(2,1)S(1)} %get-tuple-element.53), channel_id=1, source_target_pairs={{0,16},{4,20},{8,24},{12,28},{16,0},{20,4},{24,8},{28,12},{1,17},{... | collective-permute-start | bytes 1179656 | tf_op jit(solution)/shard_map/ppermute | solution.py:374
  136.4 4.6 %collective-permute-start.10 = (s16[2,2,3,64,1024]{4,3,2,0,1:T(8,128)(2,1)}, s16[2,2,3,64,1024]{4,3,2,0,1:T(8,128)(2,1)}, u32[]{:S(2)}, u32[]{:S(2)}) collective-permute-start(s16[2,2,3,64,1024]{4,3,2,0,1:T(8,128)(2,1)} %pad_add_fusion), channel_id=1, source_target_pairs={{0,4},{4,0},{8,12},{12,8},{16,20},{20,16},{24,28},{28,24},{1,5},{5... | collective-permute-start | bytes 4718600 | tf_op jit(solution)/shard_map/ppermute | solution.py:374
  141.0 7.4 %collective-permute-start.17 = (s16[2,2,3,64,1024]{4,3,2,1,0:T(8,128)(2,1)S(1)}, s16[2,2,3,64,1024]{4,3,2,1,0:T(8,128)(2,1)S(1)}, u32[]{:S(2)}, u32[]{:S(2)}) collective-permute-start(s16[2,2,3,64,1024]{4,3,2,1,0:T(8,128)(2,1)S(1)} %pad_add_fusion.1.held1), channel_id=1, source_target_pairs={{0,4},{4,0},{8,12},{12,8},{16,20},{20,16},{24,28},{28,24},{1,5},{5... | collective-permute-start | bytes 4718600 | tf_op jit(solution)/shard_map/ppermute | solution.py:374
  143.2 7.8 %collective-permute-start.19 = (s16[2,3,16,1024]{3,2,1,0:T(8,128)(2,1)S(1)}, s16[2,3,16,1024]{3,2,1,0:T(8,128)(2,1)S(1)}, u32[]{:S(2)}, u32[]{:S(2)}) collective-permute-start(s16[2,3,16,1024]{3,2,1,0:T(8,128)(2,1)S(1)} %get-tuple-element.69), channel_id=1, source_target_pairs={{1,0},{2,1},{3,2},{0,3},{5,4},{6,5},{7,6},{4,7},{9,8},{10,9},{11,1... | collective-permute-start | bytes 589832 | tf_op jit(solution)/shard_map/ppermute | solution.py:370
  144.9 10.5 %collective-permute-start.18 = (s16[2,3,16,1024]{3,2,1,0:T(8,128)(2,1)S(1)}, s16[2,3,16,1024]{3,2,1,0:T(8,128)(2,1)S(1)}, u32[]{:S(2)}, u32[]{:S(2)}) collective-permute-start(s16[2,3,16,1024]{3,2,1,0:T(8,128)(2,1)S(1)} %get-tuple-element.70), channel_id=1, source_target_pairs={{0,1},{1,2},{2,3},{3,0},{4,5},{5,6},{6,7},{7,4},{8,9},{9,10},{10,1... | collective-permute-start | bytes 589832 | tf_op jit(solution)/shard_map/ppermute | solution.py:370
  146.8 8.6 %copy-start.12 = (bf16[64,64]{1,0:T(8,128)(2,1)S(1)}, bf16[64,64]{1,0:T(8,128)(2,1)}, u32[]{:S(2)}) copy-start(bf16[64,64]{1,0:T(8,128)(2,1)} %constant.60.clone.m_both) | copy-start | bytes 24580
  (17 other events, 45.1 us)

commit v4 on v3

v4 whole, which is shorter than its diff:
```python
import functools

import jax
import jax.numpy as jnp
import numpy as np
from jax import lax
from jax.experimental import pallas as pl
from jax.experimental.pallas import tpu as pltpu
from jax.sharding import PartitionSpec as P

section_step = 0.25
reach = 16
lanes = 128
code_scale = 4096.0
phases = 2
streams = ((0, 3), (1, 2))


def grant(mib):
    return pltpu.CompilerParams(vmem_limit_bytes=mib << 20)


def compact_kernel(length):
    wave = 2.0 * np.pi * np.arange(length) / length
    symbol = 14.0 / 9.0 * np.sin(wave) + 1.0 / 18.0 * np.sin(2.0 * wave)
    symbol = 1j * symbol / (1.0 + 2.0 / 3.0 * np.cos(wave))
    return np.real(np.fft.ifft(symbol))


def along_matrices(rows, length):
    kernel = compact_kernel(length)
    first = np.zeros((rows, rows + 2 * reach))
    second = np.zeros((rows, rows + 2 * reach))
    for i in range(rows):
        for k in range(-reach, reach + 1):
            first[i, i + reach + k] = kernel[-k % length]
        for k, weight in ((0, -980.0), (1, 270.0), (2, -27.0), (3, 2.0)):
            second[i, i + reach + k] = weight
            second[i, i + reach - k] = weight
    high = first.astype(jnp.bfloat16)
    low = (first - high.astype(np.float64)).astype(jnp.bfloat16)
    return high, low, second.astype(jnp.bfloat16)


first_taps = ((1, 45.0), (2, -9.0), (3, 1.0))
second_taps = ((0, -490.0), (1, 270.0), (2, -27.0), (3, 2.0))


def depth_matrix(rows, planes, fields):
    matrix = np.zeros((len(fields) * rows, rows * planes))
    for f, taps in enumerate(fields):
        for i in range(rows):
            for z, weight in taps:
                matrix[f * rows + i, i * planes + z] += weight
    return matrix.astype(jnp.bfloat16)


def first_at(z):
    return [(z + k, w) for k, w in first_taps] + [(z - k, -w) for k, w in first_taps]


def second_at(z):
    taps = [(z + k, w) for k, w in second_taps]
    return taps + [(z - k, w) for k, w in second_taps if k > 0]


def across_matrix(orders):
    matrix = np.zeros((2 * lanes, lanes * len(orders)))
    for o, taps in enumerate(orders):
        for i in range(lanes):
            for k, weight in taps:
                matrix[lanes // 2 + i + k, o * lanes + i] += weight
    return matrix.astype(jnp.bfloat16)


def half_turned(values):
    half = lanes // 2
    return jnp.concatenate([values[:, -half:], values, values[:, :half]], 1)


def product(a, b):
    return jnp.dot(a, b, preferred_element_type=jnp.float32)


def split(values):
    high = values.astype(jnp.bfloat16)
    return high, (values - high.astype(jnp.float32)).astype(jnp.bfloat16)


def pack_kernel(core, weights, tile, mine, theirs):
    rows = weights.shape[0] // 4
    blocks = mine.shape[3] // rows

    def store(kept, sent):
        for b in range(blocks):
            depth = weights.shape[1]
            mixed = product(weights[...], tile[0, b * depth : (b + 1) * depth])
            for f in range(4):
                scale = code_scale if f < 2 else code_scale / 60.0
                part = jnp.round(mixed[f * rows : (f + 1) * rows] * scale)
                target = kept if f < 2 else sent
                code = part.astype(jnp.int32).astype(jnp.int16)
                target[f % 2, 0, 0, b * rows : (b + 1) * rows] = code

    @pl.when(core[0] == 0)
    def _():
        store(mine, theirs)

    @pl.when(core[0] != 0)
    def _():
        store(theirs, mine)


def pack(tile, planes, core, which):
    comps, deep, width = tile.shape
    quarter = deep // planes // 4
    x_rows = min(quarter, 32)
    ghost = [[t for t in first_at(z) if t[0] not in (3, 4)] for z in (3, 4)]
    weights = depth_matrix(x_rows, planes, [[(3, 1.0)], [(4, 1.0)]] + ghost)
    first, second = streams[which]
    shape = jax.ShapeDtypeStruct((2, 2, comps, quarter, width), jnp.int16)
    spec = pl.BlockSpec((2, 1, 1, quarter, width), lambda k, c: (0, k, c, 0, 0))
    return pl.pallas_call(
        pack_kernel,
        out_shape=(shape,) * 2,
        grid=(2, comps),
        in_specs=[
            pl.BlockSpec(memory_space=pltpu.SMEM),
            pl.BlockSpec(weights.shape, lambda k, c: (0, 0)),
            pl.BlockSpec(
                (1, quarter * planes, width), lambda k, c: (c, first + k * (second - first), 0)
            ),
        ],
        out_specs=(spec,) * 2,
        compiler_params=grant(16),
        cost_estimate=pl.CostEstimate(
            flops=0, bytes_accessed=2 * comps * deep * width, transcendentals=0
        ),
    )(core, jnp.asarray(weights), tile)


def depth_across_kernel(
    viscosity, turn, field, inner, depth, across, sums, token, columns, high_s, low_s, arrived
):
    slab, width = inner.shape[2:]
    planes = field.shape[1] // slab
    tiles = width // lanes
    gain = viscosity[0] * section_step

    def fetch(c, t):
        source = field.at[c, :, pl.ds(t * lanes, lanes)]
        return pltpu.make_async_copy(source, columns.at[t], arrived.at[t])

    c = pl.program_id(0)

    @pl.when(c == 0)
    def _():
        for t in range(tiles):
            fetch(0, t).start()

    for t in range(tiles):
        fetch(c, t).wait()

        def unpack(i, carry):
            start = pl.multiple_of(i * 8, 8)
            plane = [columns[t, pl.ds(start * planes + z, 8, planes), :] for z in range(planes)]
            at = (pl.ds(start, 8), pl.ds(t * lanes, lanes))
            for p in range(2):
                z = 3 + p
                centre = plane[z]
                u1, u2, u3 = plane[z + 1], plane[z + 2], plane[z + 3]
                d1, d2, d3 = plane[z - 1], plane[z - 2], plane[z - 3]
                slope = 0.75 * (u1 - d1) - 0.15 * (u2 - d2) + (1.0 / 60.0) * (u3 - d3)
                curve = 1.5 * (u1 + d1) - 0.15 * (u2 + d2) + (1.0 / 90.0) * (u3 + d3)
                inner[(0, p) + at] = centre
                depth[(0, p) + at] = slope
                sums[(0, p) + at] = centre + gain * (curve - (49.0 / 18.0) * centre)
            return carry

        lax.fori_loop(0, slab // 8, unpack, 0, unroll=4)

        @pl.when(c < pl.num_programs(0) - 1)
        def _():
            fetch(c + 1, t).start()

    for p in range(2):

        def fill(i, carry):
            at = pl.ds(pl.multiple_of(i * 16, 16), 16)
            high, low = split(inner[0, p, at, :])
            high_s[at, :] = half_turned(high)
            low_s[at, :] = half_turned(low)
            return carry

        lax.fori_loop(0, slab // 16, fill, 0, unroll=2)
        for t in range(tiles):
            side = pl.ds(t * lanes, lanes)
            window = pl.ds(t * lanes, 2 * lanes)
            both = product(high_s[:, window], turn[...]) + product(low_s[:, window], turn[...])
            across[0, p, :, side] = both[:, :lanes] * (1.0 / 60.0)
            curve = both[:, lanes:] * (gain / 180.0)
            sums[0, p, :, side] = sums[0, p, :, side] + curve
    token[...] = jnp.zeros_like(token)


def depth_across(field, viscosity):
    comps, slab, planes, width = field.shape
    flat = field.reshape(comps, slab * planes, width)
    turn = across_matrix([first_at(0), [t for t in second_at(0) if t[0] != 0]])
    shape = jax.ShapeDtypeStruct((comps, 2, slab, width), jnp.float32)
    spec = pl.BlockSpec((1, 2, slab, width), lambda c: (c, 0, 0, 0))
    mark = pl.BlockSpec((8, lanes), lambda c: (0, 0))
    return pl.pallas_call(
        depth_across_kernel,
        out_shape=(shape,) * 4 + (jax.ShapeDtypeStruct((8, lanes), jnp.int32),),
        grid=(comps,),
        in_specs=[
            pl.BlockSpec(memory_space=pltpu.SMEM),
            pl.BlockSpec(turn.shape, lambda c: (0, 0)),
            pl.BlockSpec(memory_space=pl.ANY),
        ],
        out_specs=(spec,) * 4 + (mark,),
        compiler_params=grant(56),
        scratch_shapes=[
            pltpu.VMEM((width // lanes, slab * planes, lanes), jnp.float32),
            pltpu.VMEM((slab, width + lanes), jnp.bfloat16),
            pltpu.VMEM((slab, width + lanes), jnp.bfloat16),
            pltpu.SemaphoreType.DMA((width // lanes,)),
        ],
        cost_estimate=pl.CostEstimate(
            flops=0, bytes_accessed=4 * comps * slab * planes * width * 2, transcendentals=0
        ),
    )(viscosity, jnp.asarray(turn), flat)


def along_kernel(
    viscosity, m_all, m_top, before, after, inner, partial, along, sums, token, high_s, low_s
):
    slab = inner.shape[2]
    rows = m_top.shape[0] // 2
    gain = viscosity[0] * (section_step / 180.0)

    for start, rim in ((0, before), (reach + slab, after)):
        high, low = split(rim[0, 0])
        high_s[start : start + reach, :] = high
        low_s[start : start + reach, :] = low

    def fill(i, carry):
        start = pl.multiple_of(i * 16, 16)
        high, low = split(inner[0, 0, pl.ds(start, 16), :])
        at = pl.ds(pl.multiple_of(start + reach, 16), 16)
        high_s[at, :] = high
        low_s[at, :] = low
        return carry

    lax.fori_loop(0, slab // 16, fill, 0, unroll=2)
    for b in range(slab // rows):
        window = pl.ds(b * rows, rows + 2 * reach)
        at = pl.ds(b * rows, rows)
        one = product(m_all[...], high_s[window, :])
        two = product(m_top[...], low_s[window, :])
        along[0, 0, at, :] = one[:rows] + one[2 * rows :] + two[:rows]
        curve = one[rows : 2 * rows] + two[rows:]
        sums[0, 0, at, :] = partial[0, 0, at, :] + gain * curve
    token[...] = jnp.zeros_like(token)


def along_terms(inner, partial, before, after, viscosity, length):
    comps, pair, slab, width = inner.shape
    rows = min(slab, 128)
    high, low, second = along_matrices(rows, length)
    top = np.concatenate([high, second], 0)
    everything = np.concatenate([high, second, low], 0)
    shape = jax.ShapeDtypeStruct(inner.shape, jnp.float32)
    spec = pl.BlockSpec((1, 1, slab, width), lambda c, p: (c, p, 0, 0))
    rim = pl.BlockSpec((1, 1, reach, width), lambda c, p: (c, p, 0, 0))
    mark = pl.BlockSpec((8, lanes), lambda c, p: (0, 0))
    return pl.pallas_call(
        along_kernel,
        out_shape=(shape, shape, jax.ShapeDtypeStruct((8, lanes), jnp.int32)),
        grid=(comps, pair),
        in_specs=[
            pl.BlockSpec(memory_space=pltpu.SMEM),
            pl.BlockSpec(everything.shape, lambda c, p: (0, 0)),
            pl.BlockSpec(top.shape, lambda c, p: (0, 0)),
            rim,
            rim,
            spec,
            spec,
        ],
        out_specs=(spec, spec, mark),
        compiler_params=grant(50),
        scratch_shapes=[
            pltpu.VMEM((slab + 2 * reach, width), jnp.bfloat16),
            pltpu.VMEM((slab + 2 * reach, width), jnp.bfloat16),
        ],
        cost_estimate=pl.CostEstimate(
            flops=0, bytes_accessed=4 * inner.size * 5, transcendentals=0
        ),
    )(viscosity, jnp.asarray(everything), jnp.asarray(top), before, after, inner, partial)


def final_kernel(
    core, m_both, turn, held0, other0, held1, other1, before, after,
    inner, depth, along, across, sums, out, base_s, turned_s, flow_s, ghost_s, slope_s, side_s, arrived,
):
    step = pl.program_id(0)
    rows = slope_s.shape[2]
    quarter = held0.shape[3]
    slab = 4 * quarter
    inverse = 1.0 / code_scale

    def decoded(values):
        return values.astype(jnp.int32).astype(jnp.float32) * inverse

    def load(flow, ghost):
        copies = []
        for u in range(2):
            for k in range(2):
                at = pl.ds(streams[u][k] * quarter, quarter)
                for n, (source, target) in enumerate(((flow, flow_s), (ghost, ghost_s))):
                    copies.append(
                        pltpu.make_async_copy(
                            source[u].at[k], target.at[:, :, at], arrived.at[4 * n + 2 * u + k]
                        )
                    )
        for copy in copies:
            copy.start()
        for copy in copies:
            copy.wait()

    @pl.when(step == 0)
    def _():
        for c in range(3):
            for p in range(2):
                base_s[c, p, 0:reach] = decoded(before[p, c]).astype(jnp.bfloat16)
                base_s[c, p, reach + slab :] = decoded(after[p, c]).astype(jnp.bfloat16)

        @pl.when(core[0] == 0)
        def _():
            load((held0, held1), (other0, other1))

        @pl.when(core[0] != 0)
        def _():
            load((other0, other1), (held0, held1))

        def fill(i, carry):
            start = pl.multiple_of(i * 16, 16)
            to = pl.ds(pl.multiple_of(start + reach, 16), 16)
            for c in range(3):
                for p in range(2):
                    values = decoded(flow_s[p, c, pl.ds(start, 16), :])
                    base_s[c, p, to, :] = values.astype(jnp.bfloat16)
            return carry

        lax.fori_loop(0, slab // 16, fill, 0)

    origin = pl.multiple_of(step * rows, 32)
    def derive(c, carry):
        for p in range(2):
            both = product(m_both[...], base_s[c, p, pl.ds(origin, rows + 2 * reach), :])
            slope_s[c, p] = both[:rows] + both[rows:]
            for r in range(0, rows, 16):
                here = pl.ds(pl.multiple_of(origin + reach + r, 16), 16)
                turned_s[r : r + 16, :] = half_turned(base_s[c, p, here, :])
            for t in range(side_s.shape[3] // lanes):
                window = turned_s[:, pl.ds(t * lanes, 2 * lanes)]
                side_s[c, p, :, pl.ds(t * lanes, lanes)] = product(window, turn[...])
        return carry

    lax.fori_loop(0, 3, derive, 0)

    def body(i, carry):
        start = pl.multiple_of(i * 16, 16)
        at = pl.ds(start, 16)
        there = pl.ds(pl.multiple_of(origin + start, 16), 16)
        inside = pl.ds(pl.multiple_of(origin + reach + start, 16), 16)
        flow = [
            [base_s[c, p, inside, :].astype(jnp.float32) for p in range(2)] for c in range(3)
        ]
        for p in range(2):
            move = [inner[c, p, at, :] for c in range(3)]
            for c in range(3):
                dz = decoded(ghost_s[p, c, there, :])
                if p == 0:
                    dz = dz + 0.75 * flow[c][1]
                else:
                    dz = dz - 0.75 * flow[c][0]
                dy = side_s[c, p, at, :] * (1.0 / 60.0)
                total = flow[0][p] * along[c, p, at, :] + flow[1][p] * across[c, p, at, :]
                total = total + flow[2][p] * depth[c, p, at, :]
                total = total + move[0] * slope_s[c, p, at, :] + move[1] * dy + move[2] * dz
                out[0, c, at, p, :] = sums[c, p, at, :] - section_step * total
        return carry

    lax.fori_loop(0, rows // 16, body, 0)


def final(core, pieces, before, after, terms, length):
    comps, pair, slab, width = terms[0].shape
    rows = min(slab, 32)
    turn = across_matrix([first_at(0)])
    high, low, _ = along_matrices(rows, length)
    both = np.concatenate([high, low], 0)
    whole = pl.BlockSpec(memory_space=pl.ANY)
    rim = pl.BlockSpec(before.shape, lambda i: (0, 0, 0, 0))
    spec = pl.BlockSpec((comps, pair, rows, width), lambda i: (0, 0, i, 0))
    return pl.pallas_call(
        final_kernel,
        out_shape=jax.ShapeDtypeStruct((1, comps, slab, pair, width), jnp.float32),
        grid=(slab // rows,),
        in_specs=[
            pl.BlockSpec(memory_space=pltpu.SMEM),
            pl.BlockSpec(both.shape, lambda i: (0, 0)),
            pl.BlockSpec(turn.shape, lambda i: (0, 0)),
        ]
        + [whole] * 4
        + [rim] * 2
        + [spec] * 5,
        out_specs=pl.BlockSpec((1, comps, rows, pair, width), lambda i: (0, 0, i, 0, 0)),
        compiler_params=grant(58),
        scratch_shapes=[
            pltpu.VMEM((comps, pair, slab + 2 * reach, width), jnp.bfloat16),
            pltpu.VMEM((rows, width + lanes), jnp.bfloat16),
            pltpu.VMEM((pair, comps, slab, width), jnp.int16),
            pltpu.VMEM((pair, comps, slab, width), jnp.int16),
            pltpu.VMEM((comps, pair, rows, width), jnp.float32),
            pltpu.VMEM((comps, pair, rows, width), jnp.float32),
            pltpu.SemaphoreType.DMA((8,)),
        ],
        cost_estimate=pl.CostEstimate(
            flops=0, bytes_accessed=8 * comps * pair * slab * width, transcendentals=0
        ),
    )(core, jnp.asarray(both), jnp.asarray(turn), *pieces, before, after, *terms)


def ring(last, first):
    size = lax.axis_size("gx")
    up = [(i, (i + 1) % size) for i in range(size)]
    down = [(j, i) for i, j in up]
    return lax.ppermute(last, "gx", up), lax.ppermute(first, "gx", down)


def swap(array, bit):
    return lax.ppermute(array, "pert", [(i, i ^ bit) for i in range(lax.axis_size("pert"))])


def exchange(mine, theirs, root, gate, work):
    me = lax.axis_index("pert")
    is_root = me == root
    place = (me // 2) ^ (root // 2)
    at_a, at_b, at_c = place == 0, place == 1, place == 2
    handed = [swap(t, 1) for t in theirs]

    def owned(u, h, k):
        return jnp.where(is_root, mine[u][h, k], handed[u][h, k])

    opening = [owned(u, h, 0) for u in range(2) for h in range(2)]
    opening = gate(opening)
    source = [
        [[opening[2 * u + h]] + [owned(u, h, k) for k in range(1, phases)] for h in range(2)]
        for u in range(2)
    ]
    X = [[], []]
    Y = [[], []]
    for s in range(phases + 1):
        for u in range(2):
            k = min(s, phases - 1)
            one, two = source[u][0][k], source[u][1][k]
            if s == phases:
                one, two = two, one
            if s > 0:
                one = jnp.where(at_a, one, Y[u][s - 1])
                two = jnp.where(at_a, two, X[u][s - 1])
                one, two = lax.optimization_barrier((one, two))
            X[u].append(swap(one, 2))
            Y[u].append(swap(two, 4))
        if s < phases:
            place = place + work[s]()
            at_a, at_b, at_c = place == 0, place == 1, place == 2
    held = []
    for u in range(2):
        parts = []
        for k in range(phases):
            row = []
            for h in range(2):
                P1, P2 = (X[u], Y[u]) if h == 0 else (Y[u], X[u])
                near, far = (at_b, at_c) if h == 0 else (at_c, at_b)
                late = P1[k + 2] if k + 2 <= phases else P2[phases]
                value = jnp.where(near, P1[k], jnp.where(far, late, P2[k + 1]))
                row.append(jnp.where(at_a, source[u][h][k], value))
            parts.append(jnp.stack(row, 0))
        held.append(jnp.stack(parts, 0))
    other = [swap(h, 1) for h in held]
    return held[0], other[0], held[1], other[1]


def per_device(pert_field, base_store, section_owner, pert_ids, member_visc):
    _, comps, slab, planes, width = pert_field.shape
    length = slab * lax.axis_size("gx")
    member_pick = pert_ids[0] == jnp.arange(member_visc.shape[0], dtype=jnp.int32)
    viscosity = jnp.sum(jnp.where(member_pick, member_visc, 0.0))[None]
    levels_here = base_store.shape[0]
    owner_slot = section_owner[0] % levels_here
    owner_root = section_owner[0] // levels_here
    tiles = base_store.reshape(levels_here, comps, slab * planes, width)
    tile = tiles[0] if levels_here == 1 else lax.dynamic_index_in_dim(tiles, owner_slot, 0, False)
    me = lax.axis_index("pert")
    in_pairs = lax.axis_size("pert") == 8
    core = (me % 2 if in_pairs else jnp.zeros_like(me)).astype(jnp.int32)[None]
    halves = [pack(tile, planes, core, u) for u in range(2)]
    done = {"field": pert_field[0], "viscosity": viscosity}

    def gate(opening):
        field, *opening = lax.optimization_barrier((done["field"], *opening))
        done["field"] = field
        return opening

    def early():
        *done["early"], token = depth_across(done["field"], viscosity)
        inner = done["early"][0]
        done["rims"] = ring(inner[:, :, slab - reach :], inner[:, :, :reach])
        return token[0, 0]

    def late():
        inner, depth, across, partial = done["early"]
        along, sums, token = along_terms(inner, partial, *done["rims"], viscosity, length)
        done["terms"] = (inner, depth, along, across, sums)
        return token[0, 0]

    if in_pairs:
        pieces = exchange(
            [h[0] for h in halves], [h[1] for h in halves], owner_root, gate, (early, late)
        )
    else:
        early()
        late()
        pieces = [
            lax.psum(jnp.where(me == owner_root, a, 0).astype(jnp.float32), "pert").astype(a.dtype)
            for h in halves
            for a in h
        ]
        pieces = [a.transpose(1, 0, 2, 3, 4) for a in pieces]
    quarter = slab // 4
    edges = [(1, slice(quarter - reach, quarter)), (0, slice(0, reach))]
    edges = [
        jnp.where(core[0] == 0, pieces[0][k][:, :, at], pieces[1][k][:, :, at]) for k, at in edges
    ]
    base_before, base_after = ring(*edges)
    return final(core, pieces, base_before, base_after, done["terms"], length)


def solution(mesh):
    placed = (
        P("pert", None, "gx", None, None),
        P("pert", None, "gx", None, None),
        P(),
        P("pert"),
        P(),
    )
    return jax.shard_map(
        per_device,
        mesh=mesh,
        in_specs=placed,
        out_specs=P("pert", None, "gx", None, None),
        check_vma=False,
    )
```

time: 185 us -> 157 us (0.85)
  local copies, waits for them, and re-layouts: 35.4 us -> 12.4 us
  waiting for transfers between devices: 39.4 us -> 34.7 us
  Pallas kernels: 69.7 us -> 67.2 us
    unnamed x58 -> x50, local copies, waits for them, and re-layouts: 27.5 us -> 8.49 us
    pallas_call x1 -> x2, Pallas kernels: 42.2 us -> 36.3 us  [the longest x1 22.5 us: depth_across(): pl.pallas_call(depth_across_kernel, out_shape=(shape,) * 4 + (jax.ShapeDt...]
    ppermute x16, waiting for transfers between devices: 21.7 us -> 16.3 us  [swap(): lax.ppermute(array, 'pert', [(i, i ^ bit) for i in range(lax.axis_size('p...]
    select_n x3 -> x8, other arithmetic: 7.41 us -> 11.5 us  [the longest x4 6.85 us: exchange(): one = jnp.where(at_a, one, Y[u][s - 1])]
    select_n x4 -> x2, other arithmetic: 4.18 us -> 0.26 us  [exchange(): two = jnp.where(at_a, two, X[u][s - 1])]
    pallas_call x1, Pallas kernels: 20.5 us -> 23.9 us  [final(): pl.pallas_call(final_kernel, out_shape=jax.ShapeDtypeStruct((1, comps, sl...]
    another operation x2 -> x4, other arithmetic: 4.16 us -> 4.76 us  [exchange(): parts.append(jnp.stack(row, 0))]
    slice x1 -> x3, local copies, waits for them, and re-layouts: 3.78 us -> 3.77 us  [the longest x1 2.09 us: early(): done['rims'] = ring(inner[:, :, slab - reach:], inner[:, :, :reach])]
  transfers between devices with their start and end apart: 20 -> 20, of which waited for: 10 -> 9; matrix products, arithmetic and copies ran while one was open for 11% -> 13% of each run, Pallas kernels for 25% -> 25%
where the time goes in v4:
time: 157 us
  Pallas kernels  67.2 us (43%)
  waiting for transfers between devices  34.7 us (22%)
  starting transfers between devices  20.8 us (13%)
  other arithmetic  19 us (12%)
  local copies, waits for them, and re-layouts  12.4 us (8%)
  between operations  2.87 us (2%)
    pallas_call x1, Pallas kernels, final(): pl.pallas_call(final_kernel, out_shape=jax.ShapeDtypeStruct((1, comps, sl...  23.9 us
    pallas_call x1, Pallas kernels, depth_across(): pl.pallas_call(depth_across_kernel, out_shape=(shape,) * 4 + (jax.ShapeDt...  22.5 us
    ppermute x4, waiting for transfers between devices, ring(): return (lax.ppermute(last, 'gx', up), lax.ppermute(first, 'gx', down))  18.4 us
    ppermute x16, waiting for transfers between devices, swap(): lax.ppermute(array, 'pert', [(i, i ^ bit) for i in range(lax.axis_size('p...  16.3 us
    ppermute x16, starting transfers between devices, swap(): lax.ppermute(array, 'pert', [(i, i ^ bit) for i in range(lax.axis_size('p...  14.5 us
    pallas_call x1, Pallas kernels, along_terms(): pl.pallas_call(along_kernel, out_shape=(shape, shape, jax.ShapeDtypeStruc...  13.8 us
    unnamed x50, local copies, waits for them, and re-layouts  8.49 us
    pallas_call x2, Pallas kernels, pack(): pl.pallas_call(pack_kernel, out_shape=(shape,) * 2, grid=(2, comps), in_s...  7.1 us
  transfers between devices with their start and end apart: 20, of which 9 were waited for; matrix products, arithmetic and copies ran while one was open for 13% of the time, Pallas kernels for 25%

profile of v4, /device:TPU:0, one launch (start us, length us, event | category | flops | bytes accessed | tf_op | source)
XLA Modules:
  0.0 156.9 jit_solution(8928031075208440469)
XLA Ops:
  0.0 4.6 %copy-done = bf16[1,3,256,8,1024]{4,3,2,1,0:T(8,128)(2,1)S(1)} copy-done((bf16[1,3,256,8,1024]{4,3,2,1,0:T(8,128)(2,1)S(1)}, bf16[1,3,256,8,1024]{4,3,2,1,0:T(8,128)(2,1)}, u32[]{:S(2)}) %copy-start) | copy-done | bytes 12582936
  5.4 3.6 %shard_map.119 = (s16[2,2,3,64,1024]{4,3,2,1,0:T(8,128)(2,1)S(1)}, s16[2,2,3,64,1024]{4,3,2,1,0:T(8,128)(2,1)}) custom-call(s32[1]{0:T(128)} %bitcast.core, bf16[128,256]{1,0:T(8,128)(2,1)S(1)} %copy-done.1, bf16[3,2048,1024]{2,1,0:T(8,128)(2,1)S(1)} %bitcast.63), custom_call_target="tpu_custom_call" | custom-call | bytes 12582912 | tf_op jit(solution)/shard_map/pallas_call | solution.py:123
  9.4 3.5 %shard_map.118 = (s16[2,2,3,64,1024]{4,3,2,1,0:T(8,128)(2,1)S(1)}, s16[2,2,3,64,1024]{4,3,2,1,0:T(8,128)(2,1)}) custom-call(s32[1]{0:T(128)} %bitcast.core, bf16[128,256]{1,0:T(8,128)(2,1)S(1)} %copy-done.1, bf16[3,2048,1024]{2,1,0:T(8,128)(2,1)S(1)} %bitcast.64), custom_call_target="tpu_custom_call" | custom-call | bytes 12582912 | tf_op jit(solution)/shard_map/pallas_call | solution.py:123
  13.7 2.2 %fusion.6 = (s16[3,64,1024]{2,1,0:T(8,128)(2,1)S(1)}, s16[3,64,1024]{2,1,0:T(8,128)(2,1)}) fusion(s16[2,2,3,64,1024]{4,3,2,1,0:T(8,128)(2,1)} %collective-permute-done.1, s16[2,2,3,64,1024]{4,3,2,1,0:T(8,128)(2,1)S(1)} %get-tuple-element.32, pred[]{:T(512)S(6)} %eq.29), kind=kLoop, calls=%fused_computation.23 | loop fusion | flops 393216 | bytes 2359297 | tf_op jit(solution)/shard_map/jit(_where)/select_n | solution.py:456
  16.7 2.3 %fusion.8 = (s16[3,64,1024]{2,1,0:T(8,128)(2,1)}, s16[3,64,1024]{2,1,0:T(8,128)(2,1)}) fusion(s16[2,2,3,64,1024]{4,3,2,1,0:T(8,128)(2,1)} %collective-permute-done, s16[2,2,3,64,1024]{4,3,2,1,0:T(8,128)(2,1)S(1)} %get-tuple-element.30, pred[]{:T(512)S(6)} %eq.29), kind=kLoop, calls=%fused_computation.27 | loop fusion | flops 393216 | bytes 2359297 | tf_op jit(solution)/shard_map/jit(_where)/select_n | solution.py:456
  19.0 2.6 %collective-permute-start.4 = (s16[3,64,1024]{2,1,0:T(8,128)(2,1)}, s16[3,64,1024]{2,1,0:T(8,128)(2,1)}, u32[]{:S(2)}, u32[]{:S(2)}) collective-permute-start(s16[3,64,1024]{2,1,0:T(8,128)(2,1)} %get-tuple-element.39), channel_id=1, source_target_pairs={{0,8},{4,12},{8,0},{12,4},{16,24},{20,28},{24,16},{28,20},{1,9},{5... | collective-permute-start | bytes 1179656 | tf_op jit(solution)/shard_map/ppermute | solution.py:445
  21.7 1.5 collective-permute-start.5
  25.1 22.5 %shard_map.120 = (f32[3,2,256,1024]{3,2,1,0:T(8,128)}, f32[3,2,256,1024]{3,2,1,0:T(8,128)}, f32[3,2,256,1024]{3,2,1,0:T(8,128)}, f32[3,2,256,1024]{3,2,1,0:T(8,128)}, s32[8,128]{1,0:T(8,128)}) custom-call(f32[1]{0:T(128)} %bitcast.3.viscosity, bf16[256,256]{1,0:T(8,128)(2,1)} %constant.62.clone.turn, f32[3,2048,1024]{2,1,0:T(8,128)} %bitcast.65), custom_call_target="tpu_custom_call" | custom-call | bytes 50331648 | tf_op jit(solution)/shard_map/pallas_call | solution.py:213
  47.6 2.1 %fusion.19 = (f32[3,2,16,1024]{3,2,1,0:T(8,128)}, f32[3,2,16,1024]{3,2,1,0:T(8,128)}) fusion(f32[3,2,256,1024]{3,2,1,0:T(8,128)} %get-tuple-element.36.inner), kind=kLoop, calls=%fused_computation.52 | loop fusion | bytes 1572864 | tf_op jit(solution)/shard_map/slice | solution.py:522
  51.4 4.1 %collective-permute-start.3 = (f32[3,2,16,1024]{3,2,1,0:T(8,128)}, f32[3,2,16,1024]{3,2,1,0:T(8,128)S(1)}, u32[]{:S(2)}, u32[]{:S(2)}) collective-permute-start(f32[3,2,16,1024]{3,2,1,0:T(8,128)} %get-tuple-element.63), channel_id=1, source_target_pairs={{1,0},{2,1},{3,2},{0,3},{5,4},{6,5},{7,6},{4,7},{9,8},{10,9},{11,1... | collective-permute-start | bytes 1179656 | tf_op jit(solution)/shard_map/ppermute | solution.py:441
  55.5 2.9 %broadcast_select_fusion.3 = (s16[3,64,1024]{2,1,0:T(8,128)(2,1)}, s16[3,64,1024]{2,1,0:T(8,128)(2,1)}, s16[3,64,1024]{2,1,0:T(8,128)(2,1)}, s16[3,64,1024]{2,1,0:T(8,128)(2,1)}) fusion(s16[3,64,1024]{2,1,0:T(8,128)(2,1)} %collective-permute-done.5, pred[]{:T(512)S(6)} %eq.33, s16[2,2,3,64,1024]{4,3,2,1,0:T(8,128)(2,1)} %collective-permute-done, ...), kind=kLoop, calls=%fused_computation.41 | loop fusion | flops 786432 | bytes 3932162 | tf_op jit(solution)/shard_map/jit(_where)/select_n | solution.py:473
  58.5 1.5 collective-permute-start.7
  60.0 1.5 collective-permute-start.6
  61.5 2.6 %broadcast_select_fusion.1 = (s16[3,64,1024]{2,1,0:T(8,128)(2,1)S(1)}, s16[3,64,1024]{2,1,0:T(8,128)(2,1)S(1)}, s16[3,64,1024]{2,1,0:T(8,128)(2,1)}, s16[3,64,1024]{2,1,0:T(8,128)(2,1)S(1)}) fusion(s16[3,64,1024]{2,1,0:T(8,128)(2,1)} %collective-permute-done.12, pred[]{:T(512)S(6)} %eq.33, s16[2,2,3,64,1024]{4,3,2,1,0:T(8,128)(2,1)} %collective-permute-done.1, ...), kind=kLoop, calls=%fused_computation.39 | loop fusion | flops 786432 | bytes 3932162 | tf_op jit(solution)/shard_map/jit(_where)/select_n | solution.py:473
  64.2 1.3 collective-permute-done.3.after
  65.4 7.4 %collective-permute-done.2.before = f32[3,2,16,1024]{3,2,1,0:T(8,128)S(1)} collective-permute-done((f32[3,2,16,1024]{3,2,1,0:T(8,128)}, f32[3,2,16,1024]{3,2,1,0:T(8,128)S(1)}, u32[]{:S(2)}, u32[]{:S(2)}) %collective-permute-start.2) | collective-permute-done | bytes 393248 | tf_op jit(solution)/shard_map/ppermute | solution.py:441
  72.9 13.8 %shard_map.121 = (f32[3,2,256,1024]{3,2,1,0:T(8,128)}, f32[3,2,256,1024]{3,2,1,0:T(8,128)}, s32[8,128]{1,0:T(8,128)S(1)}) custom-call(f32[1]{0:T(128)} %bitcast.3.viscosity, bf16[384,160]{1,0:T(8,128)(2,1)S(1)} %copy-done.2, bf16[256,160]{1,0:T(8,128)(2,1)S(1)} %copy-done.3, f32[3,2,16,1024]{3,2,1,0:T(8,128)S(1)} %collective-permute-done.2.before, ...), custom_call_target="tpu_custom_call" | custom-call | bytes 31457280 | tf_op jit(solution)/shard_map/pallas_call | solution.py:278
  87.9 1.6 %collective-permute-start.13 = (s16[3,64,1024]{2,1,0:T(8,128)(2,1)S(1)}, s16[3,64,1024]{2,1,0:T(8,128)(2,1)S(1)}, u32[]{:S(2)}, u32[]{:S(2)}) collective-permute-start(s16[3,64,1024]{2,1,0:T(8,128)(2,1)S(1)} %copy-done.21), channel_id=1, source_target_pairs={{0,16},{4,20},{8,24},{12,28},{16,0},{20,4},{24,8},{28,12},{1,17},{... | collective-permute-start | bytes 1179656 | tf_op jit(solution)/shard_map/ppermute | solution.py:445
  89.4 1.5 collective-permute-start.14
  93.3 6.6 %collective-permute-done.13 = s16[3,64,1024]{2,1,0:T(8,128)(2,1)S(1)} collective-permute-done((s16[3,64,1024]{2,1,0:T(8,128)(2,1)S(1)}, s16[3,64,1024]{2,1,0:T(8,128)(2,1)S(1)}, u32[]{:S(2)}, u32[]{:S(2)}) %collective-permute-start.13) | collective-permute-done | bytes 393248 | tf_op jit(solution)/shard_map/ppermute | solution.py:445
  100.1 1.4 collective-permute-done.14
  101.6 1.6 %collective-permute-start.15 = (s16[3,64,1024]{2,1,0:T(8,128)(2,1)S(1)}, s16[3,64,1024]{2,1,0:T(8,128)(2,1)S(1)}, u32[]{:S(2)}, u32[]{:S(2)}) collective-permute-start(s16[3,64,1024]{2,1,0:T(8,128)(2,1)S(1)} %broadcast_select_fusion.5), channel_id=1, source_target_pairs={{0,8},{4,12},{8,0},{12,4},{16,24},{20,28},{24,16},{28,20},{1,9},{5... | collective-permute-start | bytes 1179656 | tf_op jit(solution)/shard_map/ppermute | solution.py:445
  103.7 6.2 %collective-permute-done.8 = s16[3,64,1024]{2,1,0:T(8,128)(2,1)S(1)} collective-permute-done((s16[3,64,1024]{2,1,0:T(8,128)(2,1)S(1)}, s16[3,64,1024]{2,1,0:T(8,128)(2,1)S(1)}, u32[]{:S(2)}, u32[]{:S(2)}) %collective-permute-start.8) | collective-permute-done | bytes 393248 | tf_op jit(solution)/shard_map/ppermute | solution.py:445
  109.9 1.4 select_bitcast_fusion.7
  111.3 1.6 %select_bitcast_fusion.6 = (s16[1,3,64,1024]{3,2,1,0:T(8,128)(2,1)S(1)}, s16[1,3,64,1024]{3,2,1,0:T(8,128)(2,1)S(1)}) fusion(s16[3,64,1024]{2,1,0:T(8,128)(2,1)} %get-tuple-element.40, s16[3,64,1024]{2,1,0:T(8,128)(2,1)} %collective-permute-done.5, s16[3,64,1024]{2,1,0:T(8,128)(2,1)S(1)} %collective-permute-done.9, ...), kind=kLoop, calls=%fused_computation.36 | loop fusion | flops 983040 | bytes 2752515 | tf_op jit(solution)/shard_map/stack | solution.py:492
  114.1 1.2 collective-permute-done.15
  115.8 1.4 select_bitcast_fusion.2
  117.4 1.3 pad_add_fusion.1.held1
  120.6 1.9 %collective-permute-start.19 = (s16[2,3,16,1024]{3,2,1,0:T(8,128)(2,1)S(1)}, s16[2,3,16,1024]{3,2,1,0:T(8,128)(2,1)S(1)}, u32[]{:S(2)}, u32[]{:S(2)}) collective-permute-start(s16[2,3,16,1024]{3,2,1,0:T(8,128)(2,1)S(1)} %fusion.13), channel_id=1, source_target_pairs={{1,0},{2,1},{3,2},{0,3},{5,4},{6,5},{7,6},{4,7},{9,8},{10,9},{11,1... | collective-permute-start | bytes 589832 | tf_op jit(solution)/shard_map/ppermute | solution.py:441
  122.7 5.5 %collective-permute-done.19.after = s16[2,3,16,1024]{3,2,1,0:T(8,128)(2,1)S(1)} collective-permute-done((s16[2,3,16,1024]{3,2,1,0:T(8,128)(2,1)S(1)}, s16[2,3,16,1024]{3,2,1,0:T(8,128)(2,1)S(1)}, u32[]{:S(2)}, u32[]{:S(2)}) %collective-permute-start.19) | collective-permute-done | bytes 196640 | tf_op jit(solution)/shard_map/ppermute | solution.py:441
  128.3 4.1 %collective-permute-done.18.before = s16[2,3,16,1024]{3,2,1,0:T(8,128)(2,1)S(1)} collective-permute-done((s16[2,3,16,1024]{3,2,1,0:T(8,128)(2,1)S(1)}, s16[2,3,16,1024]{3,2,1,0:T(8,128)(2,1)S(1)}, u32[]{:S(2)}, u32[]{:S(2)}) %collective-permute-start.18) | collective-permute-done | bytes 196640 | tf_op jit(solution)/shard_map/ppermute | solution.py:441
  133.1 23.9 %shard_map.122 = f32[1,3,256,2,1024]{4,3,2,1,0:T(2,128)} custom-call(s32[1]{0:T(128)} %bitcast.core, bf16[64,64]{1,0:T(8,128)(2,1)} %constant.65.clone.m_both, bf16[256,128]{1,0:T(8,128)(2,1)} %constant.66.clone.turn, s16[2,2,3,64,1024]{4,3,2,1,0:T(8,128)(2,1)} %copy-done.4, s16[2,2,3,64,1024]{4,3,2,1,0:T(8,128)(2,1)} %copy-done.5, ...), custom_call_target="tpu_custom_call" | custom-call | bytes 12582912 | tf_op jit(solution)/shard_map/pallas_call | solution.py:408
  (86 shorter events, 12.7 us)
Async XLA Ops:
  0.0 4.6 %copy-start = (bf16[1,3,256,8,1024]{4,3,2,1,0:T(8,128)(2,1)S(1)}, bf16[1,3,256,8,1024]{4,3,2,1,0:T(8,128)(2,1)}, u32[]{:S(2)}) copy-start(bf16[1,3,256,8,1024]{4,3,2,1,0:T(8,128)(2,1)} %param.13) | copy-start | bytes 37748740
  9.0 4.7 %collective-permute-start.1 = (s16[2,2,3,64,1024]{4,3,2,1,0:T(8,128)(2,1)}, s16[2,2,3,64,1024]{4,3,2,1,0:T(8,128)(2,1)}, u32[]{:S(2)}, u32[]{:S(2)}) collective-permute-start(s16[2,2,3,64,1024]{4,3,2,1,0:T(8,128)(2,1)} %get-tuple-element.33), channel_id=1, source_target_pairs={{0,4},{4,0},{8,12},{12,8},{16,20},{20,16},{24,28},{28,24},{1,5},{5... | collective-permute-start | bytes 4718600 | tf_op jit(solution)/shard_map/ppermute | solution.py:445
  12.9 3.8 %collective-permute-start = (s16[2,2,3,64,1024]{4,3,2,1,0:T(8,128)(2,1)}, s16[2,2,3,64,1024]{4,3,2,1,0:T(8,128)(2,1)}, u32[]{:S(2)}, u32[]{:S(2)}) collective-permute-start(s16[2,2,3,64,1024]{4,3,2,1,0:T(8,128)(2,1)} %get-tuple-element.31), channel_id=1, source_target_pairs={{0,4},{4,0},{8,12},{12,8},{16,20},{20,16},{24,28},{28,24},{1,5},{5... | collective-permute-start | bytes 4718600 | tf_op jit(solution)/shard_map/ppermute | solution.py:445
  15.9 31.7 %copy-start.18 = (s16[3,64,1024]{2,1,0:T(8,128)(2,1)}, s16[3,64,1024]{2,1,0:T(8,128)(2,1)S(1)}, u32[]{:S(2)}) copy-start(s16[3,64,1024]{2,1,0:T(8,128)(2,1)S(1)} %get-tuple-element.46) | copy-start | bytes 1179652
  15.9 8.0 %copy-start.24 = (f32[64]{0:T(128)S(1)}, f32[64]{0:T(128)}, u32[]{:S(2)}) copy-start(f32[64]{0:T(128)} %param.16) | copy-start | bytes 772
  19.0 36.5 %collective-permute-start.4 = (s16[3,64,1024]{2,1,0:T(8,128)(2,1)}, s16[3,64,1024]{2,1,0:T(8,128)(2,1)}, u32[]{:S(2)}, u32[]{:S(2)}) collective-permute-start(s16[3,64,1024]{2,1,0:T(8,128)(2,1)} %get-tuple-element.39), channel_id=1, source_target_pairs={{0,8},{4,12},{8,0},{12,4},{16,24},{20,28},{24,16},{28,20},{1,9},{5... | collective-permute-start | bytes 1179656 | tf_op jit(solution)/shard_map/ppermute | solution.py:445
  21.7 33.9 %collective-permute-start.5 = (s16[3,64,1024]{2,1,0:T(8,128)(2,1)}, s16[3,64,1024]{2,1,0:T(8,128)(2,1)}, u32[]{:S(2)}, u32[]{:S(2)}) collective-permute-start(s16[3,64,1024]{2,1,0:T(8,128)(2,1)} %get-tuple-element.40), channel_id=1, source_target_pairs={{0,16},{4,20},{8,24},{12,28},{16,0},{20,4},{24,8},{28,12},{1,17},{... | collective-permute-start | bytes 1179656 | tf_op jit(solution)/shard_map/ppermute | solution.py:445
  24.5 35.5 %collective-permute-start.11 = (s16[3,64,1024]{2,1,0:T(8,128)(2,1)}, s16[3,64,1024]{2,1,0:T(8,128)(2,1)}, u32[]{:S(2)}, u32[]{:S(2)}) collective-permute-start(s16[3,64,1024]{2,1,0:T(8,128)(2,1)} %get-tuple-element.45), channel_id=1, source_target_pairs={{0,8},{4,12},{8,0},{12,4},{16,24},{20,28},{24,16},{28,20},{1,9},{5... | collective-permute-start | bytes 1179656 | tf_op jit(solution)/shard_map/ppermute | solution.py:445
  25.0 36.5 %collective-permute-start.12 = (s16[3,64,1024]{2,1,0:T(8,128)(2,1)S(1)}, s16[3,64,1024]{2,1,0:T(8,128)(2,1)}, u32[]{:S(2)}, u32[]{:S(2)}) collective-permute-start(s16[3,64,1024]{2,1,0:T(8,128)(2,1)S(1)} %get-tuple-element.46), channel_id=1, source_target_pairs={{0,16},{4,20},{8,24},{12,28},{16,0},{20,4},{24,8},{28,12},{1,17},{... | collective-permute-start | bytes 1179656 | tf_op jit(solution)/shard_map/ppermute | solution.py:445
  51.4 14.0 %collective-permute-start.3 = (f32[3,2,16,1024]{3,2,1,0:T(8,128)}, f32[3,2,16,1024]{3,2,1,0:T(8,128)S(1)}, u32[]{:S(2)}, u32[]{:S(2)}) collective-permute-start(f32[3,2,16,1024]{3,2,1,0:T(8,128)} %get-tuple-element.63), channel_id=1, source_target_pairs={{1,0},{2,1},{3,2},{0,3},{5,4},{6,5},{7,6},{4,7},{9,8},{10,9},{11,1... | collective-permute-start | bytes 1179656 | tf_op jit(solution)/shard_map/ppermute | solution.py:441
  55.5 17.3 %collective-permute-start.2 = (f32[3,2,16,1024]{3,2,1,0:T(8,128)}, f32[3,2,16,1024]{3,2,1,0:T(8,128)S(1)}, u32[]{:S(2)}, u32[]{:S(2)}) collective-permute-start(f32[3,2,16,1024]{3,2,1,0:T(8,128)} %get-tuple-element.64), channel_id=1, source_target_pairs={{0,1},{1,2},{2,3},{3,0},{4,5},{5,6},{6,7},{7,4},{8,9},{9,10},{10,1... | collective-permute-start | bytes 1179656 | tf_op jit(solution)/shard_map/ppermute | solution.py:441
  58.5 14.4 %copy-start.2 = (bf16[384,160]{1,0:T(8,128)(2,1)S(1)}, bf16[384,160]{1,0:T(8,128)(2,1)}, u32[]{:S(2)}) copy-start(bf16[384,160]{1,0:T(8,128)(2,1)} %constant.63.clone.m_all) | copy-start | bytes 368644
  58.5 14.4 %copy-start.3 = (bf16[256,160]{1,0:T(8,128)(2,1)S(1)}, bf16[256,160]{1,0:T(8,128)(2,1)}, u32[]{:S(2)}) copy-start(bf16[256,160]{1,0:T(8,128)(2,1)} %constant.64.clone.m_top) | copy-start | bytes 245764
  58.5 32.5 %collective-permute-start.7 = (s16[3,64,1024]{2,1,0:T(8,128)(2,1)}, s16[3,64,1024]{2,1,0:T(8,128)(2,1)S(1)}, u32[]{:S(2)}, u32[]{:S(2)}) collective-permute-start(s16[3,64,1024]{2,1,0:T(8,128)(2,1)} %get-tuple-element.42), channel_id=1, source_target_pairs={{0,8},{4,12},{8,0},{12,4},{16,24},{20,28},{24,16},{28,20},{1,9},{5... | collective-permute-start | bytes 1179656 | tf_op jit(solution)/shard_map/ppermute | solution.py:445
  60.0 31.1 %collective-permute-start.6 = (s16[3,64,1024]{2,1,0:T(8,128)(2,1)}, s16[3,64,1024]{2,1,0:T(8,128)(2,1)}, u32[]{:S(2)}, u32[]{:S(2)}) collective-permute-start(s16[3,64,1024]{2,1,0:T(8,128)(2,1)} %get-tuple-element.41), channel_id=1, source_target_pairs={{0,16},{4,20},{8,24},{12,28},{16,0},{20,4},{24,8},{28,12},{1,17},{... | collective-permute-start | bytes 1179656 | tf_op jit(solution)/shard_map/ppermute | solution.py:445
  64.2 35.8 %copy-start.6 = (s16[3,64,1024]{2,1,0:T(8,128)(2,1)}, s16[3,64,1024]{2,1,0:T(8,128)(2,1)S(1)}, u32[]{:S(2)}) copy-start(s16[3,64,1024]{2,1,0:T(8,128)(2,1)S(1)} %get-tuple-element.66) | copy-start | bytes 1179652
  72.9 15.0 %copy-start.21 = (s16[3,64,1024]{2,1,0:T(8,128)(2,1)S(1)}, s16[3,64,1024]{2,1,0:T(8,128)(2,1)}, u32[]{:S(2)}) copy-start(s16[3,64,1024]{2,1,0:T(8,128)(2,1)} %get-tuple-element.47) | copy-start | bytes 1179652
  72.9 18.1 %copy-start.8 = (s16[3,64,1024]{2,1,0:T(8,128)(2,1)S(1)}, s16[3,64,1024]{2,1,0:T(8,128)(2,1)}, u32[]{:S(2)}) copy-start(s16[3,64,1024]{2,1,0:T(8,128)(2,1)} %get-tuple-element.62) | copy-start | bytes 1179652
  72.9 18.2 %copy-start.9 = (s16[3,64,1024]{2,1,0:T(8,128)(2,1)S(1)}, s16[3,64,1024]{2,1,0:T(8,128)(2,1)}, u32[]{:S(2)}) copy-start(s16[3,64,1024]{2,1,0:T(8,128)(2,1)} %get-tuple-element.68) | copy-start | bytes 1179652
  87.9 12.1 %collective-permute-start.13 = (s16[3,64,1024]{2,1,0:T(8,128)(2,1)S(1)}, s16[3,64,1024]{2,1,0:T(8,128)(2,1)S(1)}, u32[]{:S(2)}, u32[]{:S(2)}) collective-permute-start(s16[3,64,1024]{2,1,0:T(8,128)(2,1)S(1)} %copy-done.21), channel_id=1, source_target_pairs={{0,16},{4,20},{8,24},{12,28},{16,0},{20,4},{24,8},{28,12},{1,17},{... | collective-permute-start | bytes 1179656 | tf_op jit(solution)/shard_map/ppermute | solution.py:445
  89.4 12.1 %collective-permute-start.14 = (s16[3,64,1024]{2,1,0:T(8,128)(2,1)S(1)}, s16[3,64,1024]{2,1,0:T(8,128)(2,1)S(1)}, u32[]{:S(2)}, u32[]{:S(2)}) collective-permute-start(s16[3,64,1024]{2,1,0:T(8,128)(2,1)S(1)} %get-tuple-element.48), channel_id=1, source_target_pairs={{0,8},{4,12},{8,0},{12,4},{16,24},{20,28},{24,16},{28,20},{1,9},{5... | collective-permute-start | bytes 1179656 | tf_op jit(solution)/shard_map/ppermute | solution.py:445
  92.3 17.7 %collective-permute-start.8 = (s16[3,64,1024]{2,1,0:T(8,128)(2,1)S(1)}, s16[3,64,1024]{2,1,0:T(8,128)(2,1)S(1)}, u32[]{:S(2)}, u32[]{:S(2)}) collective-permute-start(s16[3,64,1024]{2,1,0:T(8,128)(2,1)S(1)} %broadcast_select_fusion.7), channel_id=1, source_target_pairs={{0,8},{4,12},{8,0},{12,4},{16,24},{20,28},{24,16},{28,20},{1,9},{5... | collective-permute-start | bytes 1179656 | tf_op jit(solution)/shard_map/ppermute | solution.py:445
  92.8 18.5 %collective-permute-start.9 = (s16[3,64,1024]{2,1,0:T(8,128)(2,1)S(1)}, s16[3,64,1024]{2,1,0:T(8,128)(2,1)S(1)}, u32[]{:S(2)}, u32[]{:S(2)}) collective-permute-start(s16[3,64,1024]{2,1,0:T(8,128)(2,1)S(1)} %broadcast_select_fusion.6), channel_id=1, source_target_pairs={{0,16},{4,20},{8,24},{12,28},{16,0},{20,4},{24,8},{28,12},{1,17},{... | collective-permute-start | bytes 1179656 | tf_op jit(solution)/shard_map/ppermute | solution.py:445
  101.6 13.7 %collective-permute-start.15 = (s16[3,64,1024]{2,1,0:T(8,128)(2,1)S(1)}, s16[3,64,1024]{2,1,0:T(8,128)(2,1)S(1)}, u32[]{:S(2)}, u32[]{:S(2)}) collective-permute-start(s16[3,64,1024]{2,1,0:T(8,128)(2,1)S(1)} %broadcast_select_fusion.5), channel_id=1, source_target_pairs={{0,8},{4,12},{8,0},{12,4},{16,24},{20,28},{24,16},{28,20},{1,9},{5... | collective-permute-start | bytes 1179656 | tf_op jit(solution)/shard_map/ppermute | solution.py:445
  103.2 12.5 %collective-permute-start.16 = (s16[3,64,1024]{2,1,0:T(8,128)(2,1)S(1)}, s16[3,64,1024]{2,1,0:T(8,128)(2,1)S(1)}, u32[]{:S(2)}, u32[]{:S(2)}) collective-permute-start(s16[3,64,1024]{2,1,0:T(8,128)(2,1)S(1)} %broadcast_select_fusion.4), channel_id=1, source_target_pairs={{0,16},{4,20},{8,24},{12,28},{16,0},{20,4},{24,8},{28,12},{1,17},{... | collective-permute-start | bytes 1179656 | tf_op jit(solution)/shard_map/ppermute | solution.py:445
  114.0 3.1 %copy-start.4 = (s16[2,2,3,64,1024]{4,3,2,1,0:T(8,128)(2,1)}, s16[2,2,3,64,1024]{4,3,2,1,0:T(8,128)(2,1)S(1)}, u32[]{:S(2)}) copy-start(s16[2,2,3,64,1024]{4,3,2,1,0:T(8,128)(2,1)S(1)} %pad_add_fusion.held0) | copy-start | bytes 4718596
  114.0 4.6 %collective-permute-start.10 = (s16[2,2,3,64,1024]{4,3,2,1,0:T(8,128)(2,1)S(1)}, s16[2,2,3,64,1024]{4,3,2,1,0:T(8,128)(2,1)S(1)}, u32[]{:S(2)}, u32[]{:S(2)}) collective-permute-start(s16[2,2,3,64,1024]{4,3,2,1,0:T(8,128)(2,1)S(1)} %pad_add_fusion.held0), channel_id=1, source_target_pairs={{0,4},{4,0},{8,12},{12,8},{16,20},{20,16},{24,28},{28,24},{1,5},{5... | collective-permute-start | bytes 4718600 | tf_op jit(solution)/shard_map/ppermute | solution.py:445
  118.6 4.1 %collective-permute-start.17 = (s16[2,2,3,64,1024]{4,3,2,1,0:T(8,128)(2,1)}, s16[2,2,3,64,1024]{4,3,2,1,0:T(8,128)(2,1)}, u32[]{:S(2)}, u32[]{:S(2)}) collective-permute-start(s16[2,2,3,64,1024]{4,3,2,1,0:T(8,128)(2,1)} %pad_add_fusion.1.held1), channel_id=1, source_target_pairs={{0,4},{4,0},{8,12},{12,8},{16,20},{20,16},{24,28},{28,24},{1,5},{5... | collective-permute-start | bytes 4718600 | tf_op jit(solution)/shard_map/ppermute | solution.py:445
  118.7 1.9 %copy-start.15 = (s16[1,3,64,1024]{3,2,1,0:T(8,128)(2,1)S(1)}, s16[1,3,64,1024]{3,2,1,0:T(8,128)(2,1)}, u32[]{:S(2)}) copy-start(s16[1,3,64,1024]{3,2,1,0:T(8,128)(2,1)} %copy-done.14) | copy-start | bytes 1179652
  120.6 7.6 %collective-permute-start.19 = (s16[2,3,16,1024]{3,2,1,0:T(8,128)(2,1)S(1)}, s16[2,3,16,1024]{3,2,1,0:T(8,128)(2,1)S(1)}, u32[]{:S(2)}, u32[]{:S(2)}) collective-permute-start(s16[2,3,16,1024]{3,2,1,0:T(8,128)(2,1)S(1)} %fusion.13), channel_id=1, source_target_pairs={{1,0},{2,1},{3,2},{0,3},{5,4},{6,5},{7,6},{4,7},{9,8},{10,9},{11,1... | collective-permute-start | bytes 589832 | tf_op jit(solution)/shard_map/ppermute | solution.py:441
  122.5 9.9 %collective-permute-start.18 = (s16[2,3,16,1024]{3,2,1,0:T(8,128)(2,1)S(1)}, s16[2,3,16,1024]{3,2,1,0:T(8,128)(2,1)S(1)}, u32[]{:S(2)}, u32[]{:S(2)}) collective-permute-start(s16[2,3,16,1024]{3,2,1,0:T(8,128)(2,1)S(1)} %fusion.11), channel_id=1, source_target_pairs={{0,1},{1,2},{2,3},{3,0},{4,5},{5,6},{6,7},{7,4},{8,9},{9,10},{10,1... | collective-permute-start | bytes 589832 | tf_op jit(solution)/shard_map/ppermute | solution.py:441
  128.3 4.1 %copy-start.22 = (s16[2,3,16,1024]{3,2,1,0:T(8,128)(2,1)}, s16[2,3,16,1024]{3,2,1,0:T(8,128)(2,1)S(1)}, u32[]{:S(2)}) copy-start(s16[2,3,16,1024]{3,2,1,0:T(8,128)(2,1)S(1)} %collective-permute-done.19.after) | copy-start | bytes 589828
  (13 other events, 17.3 us)

commit v5 on v4

--- a/solution.py
+++ b/solution.py
@@ -139,8 +139,9 @@
     )(core, jnp.asarray(weights), tile)
 
 
-def depth_across_kernel(
-    viscosity, turn, field, inner, depth, across, sums, token, columns, high_s, low_s, arrived
+def field_kernel(
+    viscosity, turn, m_all, m_top, before, after, field, inner, depth, along, across, sums, token,
+    columns, high_s, low_s, high_x, low_x, arrived,
 ):
     slab, width = inner.shape[2:]
     planes = field.shape[1] // slab
@@ -183,16 +184,33 @@
         def _():
             fetch(c + 1, t).start()
 
+    rows = m_top.shape[0] // 2
     for p in range(2):
+        for start, rim in ((0, before), (reach + slab, after)):
+            high, low = split(rim[0, :, p])
+            high_x[start : start + reach, :] = high
+            low_x[start : start + reach, :] = low
 
         def fill(i, carry):
-            at = pl.ds(pl.multiple_of(i * 16, 16), 16)
+            start = pl.multiple_of(i * 16, 16)
+            at = pl.ds(start, 16)
+            to = pl.ds(pl.multiple_of(start + reach, 16), 16)
             high, low = split(inner[0, p, at, :])
+            high_x[to, :] = high
+            low_x[to, :] = low
             high_s[at, :] = half_turned(high)
             low_s[at, :] = half_turned(low)
             return carry
 
         lax.fori_loop(0, slab // 16, fill, 0, unroll=2)
+        for b in range(slab // rows):
+            window = pl.ds(b * rows, rows + 2 * reach)
+            at = pl.ds(b * rows, rows)
+            one = product(m_all[...], high_x[window, :])
+            two = product(m_top[...], low_x[window, :])
+            along[0, p, at, :] = one[:rows] + one[2 * rows :] + two[:rows]
+            curve = (gain / 180.0) * (one[rows : 2 * rows] + two[rows:])
+            sums[0, p, at, :] = sums[0, p, at, :] + curve
         for t in range(tiles):
             side = pl.ds(t * lanes, lanes)
             window = pl.ds(t * lanes, 2 * lanes)
@@ -203,101 +221,47 @@
     token[...] = jnp.zeros_like(token)
 
 
-def depth_across(field, viscosity):
+def field_terms(field, before, after, viscosity, length):
     comps, slab, planes, width = field.shape
     flat = field.reshape(comps, slab * planes, width)
+    rows = min(slab, 128)
+    high, low, second = along_matrices(rows, length)
+    top = np.concatenate([high, second], 0)
+    everything = np.concatenate([high, second, low], 0)
+    rim = pl.BlockSpec((1, reach, 2, width), lambda c: (c, 0, 0, 0))
     turn = across_matrix([first_at(0), [t for t in second_at(0) if t[0] != 0]])
     shape = jax.ShapeDtypeStruct((comps, 2, slab, width), jnp.float32)
     spec = pl.BlockSpec((1, 2, slab, width), lambda c: (c, 0, 0, 0))
     mark = pl.BlockSpec((8, lanes), lambda c: (0, 0))
     return pl.pallas_call(
-        depth_across_kernel,
-        out_shape=(shape,) * 4 + (jax.ShapeDtypeStruct((8, lanes), jnp.int32),),
+        field_kernel,
+        out_shape=(shape,) * 5 + (jax.ShapeDtypeStruct((8, lanes), jnp.int32),),
         grid=(comps,),
         in_specs=[
             pl.BlockSpec(memory_space=pltpu.SMEM),
             pl.BlockSpec(turn.shape, lambda c: (0, 0)),
+            pl.BlockSpec(everything.shape, lambda c: (0, 0)),
+            pl.BlockSpec(top.shape, lambda c: (0, 0)),
+            rim,
+            rim,
             pl.BlockSpec(memory_space=pl.ANY),
         ],
-        out_specs=(spec,) * 4 + (mark,),
-        compiler_params=grant(56),
+        out_specs=(spec,) * 5 + (mark,),
+        compiler_params=grant(42),
         scratch_shapes=[
             pltpu.VMEM((width // lanes, slab * planes, lanes), jnp.float32),
             pltpu.VMEM((slab, width + lanes), jnp.bfloat16),
             pltpu.VMEM((slab, width + lanes), jnp.bfloat16),
+            pltpu.VMEM((slab + 2 * reach, width), jnp.bfloat16),
+            pltpu.VMEM((slab + 2 * reach, width), jnp.bfloat16),
             pltpu.SemaphoreType.DMA((width // lanes,)),
         ],
         cost_estimate=pl.CostEstimate(
             flops=0, bytes_accessed=4 * comps * slab * planes * width * 2, transcendentals=0
         ),
-    )(viscosity, jnp.asarray(turn), flat)
-
-
-def along_kernel(
-    viscosity, m_all, m_top, before, after, inner, partial, along, sums, token, high_s, low_s
-):
-    slab = inner.shape[2]
-    rows = m_top.shape[0] // 2
-    gain = viscosity[0] * (section_step / 180.0)
-
-    for start, rim in ((0, before), (reach + slab, after)):
-        high, low = split(rim[0, 0])
-        high_s[start : start + reach, :] = high
-        low_s[start : start + reach, :] = low
-
-    def fill(i, carry):
-        start = pl.multiple_of(i * 16, 16)
-        high, low = split(inner[0, 0, pl.ds(start, 16), :])
-        at = pl.ds(pl.multiple_of(start + reach, 16), 16)
-        high_s[at, :] = high
-        low_s[at, :] = low
-        return carry
-
-    lax.fori_loop(0, slab // 16, fill, 0, unroll=2)
-    for b in range(slab // rows):
-        window = pl.ds(b * rows, rows + 2 * reach)
-        at = pl.ds(b * rows, rows)
-        one = product(m_all[...], high_s[window, :])
-        two = product(m_top[...], low_s[window, :])
-        along[0, 0, at, :] = one[:rows] + one[2 * rows :] + two[:rows]
-        curve = one[rows : 2 * rows] + two[rows:]
-        sums[0, 0, at, :] = partial[0, 0, at, :] + gain * curve
-    token[...] = jnp.zeros_like(token)
-
-
-def along_terms(inner, partial, before, after, viscosity, length):
-    comps, pair, slab, width = inner.shape
-    rows = min(slab, 128)
-    high, low, second = along_matrices(rows, length)
-    top = np.concatenate([high, second], 0)
-    everything = np.concatenate([high, second, low], 0)
-    shape = jax.ShapeDtypeStruct(inner.shape, jnp.float32)
-    spec = pl.BlockSpec((1, 1, slab, width), lambda c, p: (c, p, 0, 0))
-    rim = pl.BlockSpec((1, 1, reach, width), lambda c, p: (c, p, 0, 0))
-    mark = pl.BlockSpec((8, lanes), lambda c, p: (0, 0))
-    return pl.pallas_call(
-        along_kernel,
-        out_shape=(shape, shape, jax.ShapeDtypeStruct((8, lanes), jnp.int32)),
-        grid=(comps, pair),
-        in_specs=[
-            pl.BlockSpec(memory_space=pltpu.SMEM),
-            pl.BlockSpec(everything.shape, lambda c, p: (0, 0)),
-            pl.BlockSpec(top.shape, lambda c, p: (0, 0)),
-            rim,
-            rim,
-            spec,
-            spec,
-        ],
-        out_specs=(spec, spec, mark),
-        compiler_params=grant(50),
-        scratch_shapes=[
-            pltpu.VMEM((slab + 2 * reach, width), jnp.bfloat16),
-            pltpu.VMEM((slab + 2 * reach, width), jnp.bfloat16),
-        ],
-        cost_estimate=pl.CostEstimate(
-            flops=0, bytes_accessed=4 * inner.size * 5, transcendentals=0
-        ),
-    )(viscosity, jnp.asarray(everything), jnp.asarray(top), before, after, inner, partial)
+    )(
+        viscosity, jnp.asarray(turn), jnp.asarray(everything), jnp.asarray(top), before, after, flat
+    )
 
 
 def final_kernel(
@@ -445,7 +409,7 @@
     return lax.ppermute(array, "pert", [(i, i ^ bit) for i in range(lax.axis_size("pert"))])
 
 
-def exchange(mine, theirs, root, gate, work):
+def exchange(mine, theirs, root, core, gate, work):
     me = lax.axis_index("pert")
     is_root = me == root
     place = (me // 2) ^ (root // 2)
@@ -472,11 +436,12 @@
             if s > 0:
                 one = jnp.where(at_a, one, Y[u][s - 1])
                 two = jnp.where(at_a, two, X[u][s - 1])
-                one, two = lax.optimization_barrier((one, two))
+                one, two, place = lax.optimization_barrier((one, two, place))
+                at_a, at_b, at_c = place == 0, place == 1, place == 2
             X[u].append(swap(one, 2))
             Y[u].append(swap(two, 4))
-        if s < phases:
-            place = place + work[s]()
+        if s == 0:
+            place = place + work()
             at_a, at_b, at_c = place == 0, place == 1, place == 2
     held = []
     for u in range(2):
@@ -491,8 +456,20 @@
                 row.append(jnp.where(at_a, source[u][h][k], value))
             parts.append(jnp.stack(row, 0))
         held.append(jnp.stack(parts, 0))
+    quarter = held[0].shape[3]
+    size = lax.axis_size("gx")
+    pairs = [
+        (c * size + i, c * size + (i + 1) % size)
+        for c in range(0, lax.axis_size("pert"), 2)
+        for i in range(size)
+    ]
+    both = ("pert", "gx")
+    before = lax.ppermute(held[0][1][:, :, quarter - reach :], both, pairs)
+    after = lax.ppermute(held[0][0][:, :, :reach], both, [(j, i) for i, j in pairs])
+    rims = jnp.stack([before, after], 0)
     other = [swap(h, 1) for h in held]
-    return held[0], other[0], held[1], other[1]
+    rims = jnp.where(core == 0, rims, swap(rims, 1))
+    return (held[0], other[0], held[1], other[1]), rims[0], rims[1]
 
 
 def per_device(pert_field, base_store, section_owner, pert_ids, member_visc):
@@ -508,45 +485,37 @@
     me = lax.axis_index("pert")
     in_pairs = lax.axis_size("pert") == 8
     core = (me % 2 if in_pairs else jnp.zeros_like(me)).astype(jnp.int32)[None]
+    field = pert_field[0]
+    last, first, tile = lax.optimization_barrier(
+        (field[:, slab - reach :, 3:5], field[:, :reach, 3:5], tile)
+    )
+    before, after = ring(last, first)
     halves = [pack(tile, planes, core, u) for u in range(2)]
-    done = {"field": pert_field[0], "viscosity": viscosity}
+    done = {"field": field}
 
     def gate(opening):
-        field, *opening = lax.optimization_barrier((done["field"], *opening))
-        done["field"] = field
+        done["field"], *opening = lax.optimization_barrier((done["field"], *opening))
         return opening
 
-    def early():
-        *done["early"], token = depth_across(done["field"], viscosity)
-        inner = done["early"][0]
-        done["rims"] = ring(inner[:, :, slab - reach :], inner[:, :, :reach])
+    def work():
+        *done["terms"], token = field_terms(done["field"], before, after, viscosity, length)
         return token[0, 0]
 
-    def late():
-        inner, depth, across, partial = done["early"]
-        along, sums, token = along_terms(inner, partial, *done["rims"], viscosity, length)
-        done["terms"] = (inner, depth, along, across, sums)
-        return token[0, 0]
-
     if in_pairs:
-        pieces = exchange(
-            [h[0] for h in halves], [h[1] for h in halves], owner_root, gate, (early, late)
-        )
+        mine, theirs = [h[0] for h in halves], [h[1] for h in halves]
+        pieces, base_before, base_after = exchange(mine, theirs, owner_root, core[0], gate, work)
     else:
-        early()
-        late()
+        work()
         pieces = [
             lax.psum(jnp.where(me == owner_root, a, 0).astype(jnp.float32), "pert").astype(a.dtype)
             for h in halves
             for a in h
         ]
         pieces = [a.transpose(1, 0, 2, 3, 4) for a in pieces]
-    quarter = slab // 4
-    edges = [(1, slice(quarter - reach, quarter)), (0, slice(0, reach))]
-    edges = [
-        jnp.where(core[0] == 0, pieces[0][k][:, :, at], pieces[1][k][:, :, at]) for k, at in edges
-    ]
-    base_before, base_after = ring(*edges)
+        quarter = slab // 4
+        base_before, base_after = ring(
+            pieces[0][1][:, :, quarter - reach :], pieces[0][0][:, :, :reach]
+        )
     return final(core, pieces, base_before, base_after, done["terms"], length)
 
 

time: 157 us -> 154 us (0.981)
  Pallas kernels: 67.2 us -> 58.4 us
  starting transfers between devices: 20.8 us -> 27.9 us
  waiting for transfers between devices: 34.7 us -> 29 us
  local copies, waits for them, and re-layouts: 12.4 us -> 14.6 us
  other arithmetic: 19 us -> 21 us
    ppermute x4 -> x2, waiting for transfers between devices: 18.4 us -> 5.57 us  [ring(): return (lax.ppermute(last, 'gx', up), lax.ppermute(first, 'gx', down))]
    pallas_call x2 -> x1, Pallas kernels: 36.3 us -> 27.4 us  [field_terms(): pl.pallas_call(field_kernel, out_shape=(shape,) * 5 + (jax.ShapeDtypeStru...]
    ppermute x0 -> x2, starting transfers between devices: none -> 7.64 us  [the longest x1 4.03 us: exchange(): lax.ppermute(held[0][0][:, :, :reach], both, [(j, i) for i, j in pairs])]
    select_n x2 -> x3, other arithmetic: 0.26 us -> 4.76 us  [exchange(): two = jnp.where(at_a, two, X[u][s - 1])]
    ppermute x0 -> x2, waiting for transfers between devices: none -> 3.86 us  [the longest x1 2 us: exchange(): lax.ppermute(held[0][0][:, :, :reach], both, [(j, i) for i, j in pairs])]
    ppermute x16 -> x17, waiting for transfers between devices: 16.3 us -> 19.6 us  [swap(): lax.ppermute(array, 'pert', [(i, i ^ bit) for i in range(lax.axis_size('p...]
    select_n x4 -> x3, other arithmetic: 6.85 us -> 4.69 us  [exchange(): one = jnp.where(at_a, one, Y[u][s - 1])]
    unnamed x50 -> x28, local copies, waits for them, and re-layouts: 8.49 us -> 10 us
  transfers between devices with their start and end apart: 20 -> 21, of which waited for: 9 -> 9; matrix products, arithmetic and copies ran while one was open for 13% -> 15% of each run, Pallas kernels for 25% -> 20%
where the time goes in v5:
time: 154 us; the launch traced here: 153 us
  Pallas kernels  58.4 us (38%)
  waiting for transfers between devices  29 us (19%)
  starting transfers between devices  27.9 us (18%)
  other arithmetic  21 us (14%)
  local copies, waits for them, and re-layouts  14.6 us (9%)
  between operations  2.19 us (1%)
    pallas_call x1, Pallas kernels, field_terms(): pl.pallas_call(field_kernel, out_shape=(shape,) * 5 + (jax.ShapeDtypeStru...  27.4 us
    pallas_call x1, Pallas kernels, final(): pl.pallas_call(final_kernel, out_shape=jax.ShapeDtypeStruct((1, comps, sl...  23.9 us
    ppermute x17, waiting for transfers between devices, swap(): lax.ppermute(array, 'pert', [(i, i ^ bit) for i in range(lax.axis_size('p...  19.6 us
    ppermute x17, starting transfers between devices, swap(): lax.ppermute(array, 'pert', [(i, i ^ bit) for i in range(lax.axis_size('p...  15.2 us
    unnamed x28, local copies, waits for them, and re-layouts  10 us
    pallas_call x2, Pallas kernels, pack(): pl.pallas_call(pack_kernel, out_shape=(shape,) * 2, grid=(2, comps), in_s...  7.06 us
    ppermute x2, waiting for transfers between devices, ring(): return (lax.ppermute(last, 'gx', up), lax.ppermute(first, 'gx', down))  5.57 us
    ppermute x2, starting transfers between devices, ring(): return (lax.ppermute(last, 'gx', up), lax.ppermute(first, 'gx', down))  5.06 us
  transfers between devices with their start and end apart: 21, of which 9 were waited for; matrix products, arithmetic and copies ran while one was open for 15% of the time, Pallas kernels for 20%

profile of v5, /device:TPU:0, one launch (start us, length us, event | category | flops | bytes accessed | tf_op | source)
XLA Modules:
  0.0 153.1 jit_solution(10318303461250914892)
XLA Ops:
  0.0 3.2 %fusion.17 = (f32[3,16,2,1024]{3,2,1,0:T(2,128)}, f32[3,16,2,1024]{3,2,1,0:T(2,128)}) fusion(f32[3,256,8,1024]{3,2,1,0:T(8,128)} %bitcast.66), kind=kLoop, calls=%fused_computation.52 | loop fusion | bytes 1572864 | tf_op jit(solution)/shard_map/slice | solution.py:490
  3.3 4.6 %copy-done = bf16[1,3,256,8,1024]{4,3,2,1,0:T(8,128)(2,1)S(1)} copy-done((bf16[1,3,256,8,1024]{4,3,2,1,0:T(8,128)(2,1)S(1)}, bf16[1,3,256,8,1024]{4,3,2,1,0:T(8,128)(2,1)}, u32[]{:S(2)}) %copy-start) | copy-done | bytes 12582936
  7.8 3.6 %shard_map.119 = (s16[2,2,3,64,1024]{4,3,2,1,0:T(8,128)(2,1)S(1)}, s16[2,2,3,64,1024]{4,3,2,1,0:T(8,128)(2,1)}) custom-call(s32[1]{0:T(128)} %bitcast.core, bf16[128,256]{1,0:T(8,128)(2,1)S(1)} %copy-done.2, bf16[3,2048,1024]{2,1,0:T(8,128)(2,1)S(1)} %bitcast.64), custom_call_target="tpu_custom_call" | custom-call | bytes 12582912 | tf_op jit(solution)/shard_map/pallas_call | solution.py:123
  11.8 3.5 %shard_map.118 = (s16[2,2,3,64,1024]{4,3,2,1,0:T(8,128)(2,1)S(1)}, s16[2,2,3,64,1024]{4,3,2,1,0:T(8,128)(2,1)}) custom-call(s32[1]{0:T(128)} %bitcast.core, bf16[128,256]{1,0:T(8,128)(2,1)S(1)} %copy-done.2, bf16[3,2048,1024]{2,1,0:T(8,128)(2,1)S(1)} %bitcast.65), custom_call_target="tpu_custom_call" | custom-call | bytes 12582912 | tf_op jit(solution)/shard_map/pallas_call | solution.py:123
  15.4 3.0 %collective-permute-start = (f32[3,16,2,1024]{3,2,1,0:T(2,128)}, f32[3,16,2,1024]{3,2,1,0:T(2,128)S(1)}, u32[]{:S(2)}, u32[]{:S(2)}) collective-permute-start(f32[3,16,2,1024]{3,2,1,0:T(2,128)} %get-tuple-element.35), channel_id=1, source_target_pairs={{0,1},{1,2},{2,3},{3,0},{4,5},{5,6},{6,7},{7,4},{8,9},{9,10},{10,1... | collective-permute-start | bytes 1179656 | tf_op jit(solution)/shard_map/ppermute | solution.py:405
  18.4 2.0 %collective-permute-start.1 = (f32[3,16,2,1024]{3,2,1,0:T(2,128)}, f32[3,16,2,1024]{3,2,1,0:T(2,128)}, u32[]{:S(2)}, u32[]{:S(2)}) collective-permute-start(f32[3,16,2,1024]{3,2,1,0:T(2,128)} %get-tuple-element.36), channel_id=1, source_target_pairs={{1,0},{2,1},{3,2},{0,3},{5,4},{6,5},{7,6},{4,7},{9,8},{10,9},{11,1... | collective-permute-start | bytes 1179656 | tf_op jit(solution)/shard_map/ppermute | solution.py:405
  21.1 2.3 %fusion.6 = (s16[3,64,1024]{2,1,0:T(8,128)(2,1)}, s16[3,64,1024]{2,1,0:T(8,128)(2,1)}) fusion(s16[2,2,3,64,1024]{4,3,2,1,0:T(8,128)(2,1)} %collective-permute-done.3, s16[2,2,3,64,1024]{4,3,2,1,0:T(8,128)(2,1)S(1)} %get-tuple-element.40, pred[]{:T(512)S(6)} %eq.37), kind=kLoop, calls=%fused_computation.21 | loop fusion | flops 393216 | bytes 2359297 | tf_op jit(solution)/shard_map/jit(_where)/select_n | solution.py:420
  23.4 2.3 %fusion.8 = (s16[3,64,1024]{2,1,0:T(8,128)(2,1)}, s16[3,64,1024]{2,1,0:T(8,128)(2,1)}) fusion(s16[2,2,3,64,1024]{4,3,2,1,0:T(8,128)(2,1)} %collective-permute-done.2, s16[2,2,3,64,1024]{4,3,2,1,0:T(8,128)(2,1)S(1)} %get-tuple-element.38, pred[]{:T(512)S(6)} %eq.37), kind=kLoop, calls=%fused_computation.25 | loop fusion | flops 393216 | bytes 2359297 | tf_op jit(solution)/shard_map/jit(_where)/select_n | solution.py:420
  25.7 1.7 %collective-permute-start.4 = (s16[3,64,1024]{2,1,0:T(8,128)(2,1)}, s16[3,64,1024]{2,1,0:T(8,128)(2,1)}, u32[]{:S(2)}, u32[]{:S(2)}) collective-permute-start(s16[3,64,1024]{2,1,0:T(8,128)(2,1)} %get-tuple-element.44), channel_id=1, source_target_pairs={{0,16},{4,20},{8,24},{12,28},{16,0},{20,4},{24,8},{28,12},{1,17},{... | collective-permute-start | bytes 1179656 | tf_op jit(solution)/shard_map/ppermute | solution.py:409
  27.5 1.5 collective-permute-start.5
  30.8 1.6 %collective-permute-start.7 = (s16[3,64,1024]{2,1,0:T(8,128)(2,1)}, s16[3,64,1024]{2,1,0:T(8,128)(2,1)}, u32[]{:S(2)}, u32[]{:S(2)}) collective-permute-start(s16[3,64,1024]{2,1,0:T(8,128)(2,1)} %get-tuple-element.48), channel_id=1, source_target_pairs={{0,8},{4,12},{8,0},{12,4},{16,24},{20,28},{24,16},{28,20},{1,9},{5... | collective-permute-start | bytes 1179656 | tf_op jit(solution)/shard_map/ppermute | solution.py:409
  32.3 5.6 %collective-permute-done.1.after = f32[3,16,2,1024]{3,2,1,0:T(2,128)} collective-permute-done((f32[3,16,2,1024]{3,2,1,0:T(2,128)}, f32[3,16,2,1024]{3,2,1,0:T(2,128)}, u32[]{:S(2)}, u32[]{:S(2)}) %collective-permute-start.1) | collective-permute-done | bytes 393248 | tf_op jit(solution)/shard_map/ppermute | solution.py:405
  40.7 27.4 %shard_map.120 = (f32[3,2,256,1024]{3,2,1,0:T(8,128)S(1)}, f32[3,2,256,1024]{3,2,1,0:T(8,128)}, f32[3,2,256,1024]{3,2,1,0:T(8,128)}, f32[3,2,256,1024]{3,2,1,0:T...) custom-call(f32[1]{0:T(128)} %bitcast.3.viscosity, bf16[256,256]{1,0:T(8,128)(2,1)S(1)} %copy-done.5, ...), custom_call_target="tpu_custom_call" | custom-call | bytes 50331648 | tf_op jit(solution)/shard_map/pallas_call | solution.py:236
  68.1 2.7 %copy-done.1 = f32[3,2,256,1024]{3,2,1,0:T(8,128)} copy-done((f32[3,2,256,1024]{3,2,1,0:T(8,128)}, f32[3,2,256,1024]{3,2,1,0:T(8,128)S(1)}, u32[]{:S(2)}) %copy-start.1) | copy-done | bytes 6291480
  71.9 2.7 %broadcast_select_fusion.8 = (s16[3,64,1024]{2,1,0:T(8,128)(2,1)}, s16[3,64,1024]{2,1,0:T(8,128)(2,1)S(1)}, s16[3,64,1024]{2,1,0:T(8,128)(2,1)}, s16[3,64,1024]{2,1,0:T(8,128)(2,1)}) fusion(s16[3,64,1024]{2,1,0:T(8,128)(2,1)} %collective-permute-done.4, pred[]{:T(512)S(6)} %eq.38, s16[2,2,3,64,1024]{4,3,2,1,0:T(8,128)(2,1)} %collective-permute-done.2, ...), kind=kLoop, calls=%fused_computation.45 | loop fusion | flops 786432 | bytes 3932162 | tf_op jit(solution)/shard_map/jit(_where)/select_n | solution.py:437
  75.8 1.7 %collective-permute-start.9 = (s16[3,64,1024]{2,1,0:T(8,128)(2,1)}, s16[3,64,1024]{2,1,0:T(8,128)(2,1)}, u32[]{:S(2)}, u32[]{:S(2)}) collective-permute-start(s16[3,64,1024]{2,1,0:T(8,128)(2,1)} %get-tuple-element.51), channel_id=1, source_target_pairs={{0,8},{4,12},{8,0},{12,4},{16,24},{20,28},{24,16},{28,20},{1,9},{5... | collective-permute-start | bytes 1179656 | tf_op jit(solution)/shard_map/ppermute | solution.py:409
  77.6 2.7 %broadcast_select_fusion.5 = (s16[3,64,1024]{2,1,0:T(8,128)(2,1)}, s16[3,64,1024]{2,1,0:T(8,128)(2,1)S(1)}, s16[3,64,1024]{2,1,0:T(8,128)(2,1)}, s16[3,64,1024]{2,1,0:T(8,128)(2,1)S(1)}) fusion(s16[3,64,1024]{2,1,0:T(8,128)(2,1)} %collective-permute-done.7, pred[]{:T(512)S(6)} %eq.39, s16[2,2,3,64,1024]{4,3,2,1,0:T(8,128)(2,1)} %collective-permute-done.3, ...), kind=kLoop, calls=%fused_computation.42 | loop fusion | flops 786432 | bytes 3932162 | tf_op jit(solution)/shard_map/jit(_where)/select_n | solution.py:438
  81.4 5.6 %collective-permute-done.8 = s16[3,64,1024]{2,1,0:T(8,128)(2,1)} collective-permute-done((s16[3,64,1024]{2,1,0:T(8,128)(2,1)}, s16[3,64,1024]{2,1,0:T(8,128)(2,1)}, u32[]{:S(2)}, u32[]{:S(2)}) %collective-permute-start.8) | collective-permute-done | bytes 393248 | tf_op jit(solution)/shard_map/ppermute | solution.py:409
  89.4 1.8 %collective-permute-start.12 = (s16[3,64,1024]{2,1,0:T(8,128)(2,1)S(1)}, s16[3,64,1024]{2,1,0:T(8,128)(2,1)}, u32[]{:S(2)}, u32[]{:S(2)}) collective-permute-start(s16[3,64,1024]{2,1,0:T(8,128)(2,1)S(1)} %broadcast_select_fusion.4), channel_id=1, source_target_pairs={{0,8},{4,12},{8,0},{12,4},{16,24},{20,28},{24,16},{28,20},{1,9},{5... | collective-permute-start | bytes 1179656 | tf_op jit(solution)/shard_map/ppermute | solution.py:409
  92.3 4.2 %collective-permute-done.11 = s16[3,64,1024]{2,1,0:T(8,128)(2,1)S(1)} collective-permute-done((s16[3,64,1024]{2,1,0:T(8,128)(2,1)}, s16[3,64,1024]{2,1,0:T(8,128)(2,1)S(1)}, u32[]{:S(2)}, u32[]{:S(2)}) %collective-permute-start.11) | collective-permute-done | bytes 393248 | tf_op jit(solution)/shard_map/ppermute | solution.py:409
  98.3 1.7 %collective-permute-start.15 = (s16[3,64,1024]{2,1,0:T(8,128)(2,1)}, s16[3,64,1024]{2,1,0:T(8,128)(2,1)S(1)}, u32[]{:S(2)}, u32[]{:S(2)}) collective-permute-start(s16[3,64,1024]{2,1,0:T(8,128)(2,1)} %broadcast_select_fusion.2), channel_id=1, source_target_pairs={{0,8},{4,12},{8,0},{12,4},{16,24},{20,28},{24,16},{28,20},{1,9},{5... | collective-permute-start | bytes 1179656 | tf_op jit(solution)/shard_map/ppermute | solution.py:409
  100.6 4.5 %collective-permute-done.12 = s16[3,64,1024]{2,1,0:T(8,128)(2,1)} collective-permute-done((s16[3,64,1024]{2,1,0:T(8,128)(2,1)S(1)}, s16[3,64,1024]{2,1,0:T(8,128)(2,1)}, u32[]{:S(2)}, u32[]{:S(2)}) %collective-permute-start.12) | collective-permute-done | bytes 393248 | tf_op jit(solution)/shard_map/ppermute | solution.py:409
  105.1 1.5 select_bitcast_fusion.7
  106.6 1.5 select_bitcast_fusion.6
  108.5 3.0 %collective-permute-done.15 = s16[3,64,1024]{2,1,0:T(8,128)(2,1)S(1)} collective-permute-done((s16[3,64,1024]{2,1,0:T(8,128)(2,1)}, s16[3,64,1024]{2,1,0:T(8,128)(2,1)S(1)}, u32[]{:S(2)}, u32[]{:S(2)}) %collective-permute-start.15) | collective-permute-done | bytes 393248 | tf_op jit(solution)/shard_map/ppermute | solution.py:409
  111.9 1.4 select_bitcast_fusion.2
  113.8 3.6 %collective-permute-start.18 = (s16[2,3,16,1024]{3,2,1,0:T(8,128)(2,1)S(1)}, s16[2,3,16,1024]{3,2,1,0:T(8,128)(2,1)S(1)}, u32[]{:S(2)}, u32[]{:S(2)}) collective-permute-start(s16[2,3,16,1024]{3,2,1,0:T(8,128)(2,1)S(1)} %fusion.10), channel_id=1, source_target_pairs={{0,1},{1,2},{2,3},{3,0},{8,9},{9,10},{10,11},{11,8},{16,17},{17,18... | collective-permute-start | bytes 589832 | tf_op jit(solution)/shard_map/ppermute | solution.py:467
  117.5 4.0 %collective-permute-start.19 = (s16[2,3,16,1024]{3,2,1,0:T(8,128)(2,1)S(1)}, s16[2,3,16,1024]{3,2,1,0:T(8,128)(2,1)S(1)}, u32[]{:S(2)}, u32[]{:S(2)}) collective-permute-start(s16[2,3,16,1024]{3,2,1,0:T(8,128)(2,1)S(1)} %fusion.11), channel_id=1, source_target_pairs={{1,0},{2,1},{3,2},{0,3},{9,8},{10,9},{11,10},{8,11},{17,16},{18,17... | collective-permute-start | bytes 589832 | tf_op jit(solution)/shard_map/ppermute | solution.py:468
  121.5 1.9 %collective-permute-done.18 = s16[2,3,16,1024]{3,2,1,0:T(8,128)(2,1)S(1)} collective-permute-done((s16[2,3,16,1024]{3,2,1,0:T(8,128)(2,1)S(1)}, s16[2,3,16,1024]{3,2,1,0:T(8,128)(2,1)S(1)}, u32[]{:S(2)}, u32[]{:S(2)}) %collective-permute-start.18) | collective-permute-done | bytes 196640 | tf_op jit(solution)/shard_map/ppermute | solution.py:467
  123.4 2.0 %collective-permute-done.19 = s16[2,3,16,1024]{3,2,1,0:T(8,128)(2,1)S(1)} collective-permute-done((s16[2,3,16,1024]{3,2,1,0:T(8,128)(2,1)S(1)}, s16[2,3,16,1024]{3,2,1,0:T(8,128)(2,1)S(1)}, u32[]{:S(2)}, u32[]{:S(2)}) %collective-permute-start.19) | collective-permute-done | bytes 196640 | tf_op jit(solution)/shard_map/ppermute | solution.py:468
  126.1 2.1 %collective-permute-done.20 = s16[2,2,3,16,1024]{4,3,2,1,0:T(8,128)(2,1)} collective-permute-done((s16[2,2,3,16,1024]{4,3,2,1,0:T(8,128)(2,1)}, s16[2,2,3,16,1024]{4,3,2,1,0:T(8,128)(2,1)}, u32[]{:S(2)}, u32[]{:S(2)}) %collective-permute-start.20) | collective-permute-done | bytes 393248 | tf_op jit(solution)/shard_map/ppermute | solution.py:409
  129.2 23.9 %shard_map.121 = f32[1,3,256,2,1024]{4,3,2,1,0:T(2,128)} custom-call(s32[1]{0:T(128)} %bitcast.core, bf16[64,64]{1,0:T(8,128)(2,1)} %constant.65.clone.m_both, bf16[256,128]{1,0:T(8,128)(2,1)} %constant.66.clone.turn, s16[2,2,3,64,1024]{4,3,2,1,0:T(8,128)(2,1)} %copy-done.6, s16[2,2,3,64,1024]{4,3,2,1,0:T(8,128)(2,1)} %collective-permute-done.14.other0, ...), custom_call_target="tpu_custom_call" | custom-call | bytes 12582912 | tf_op jit(solution)/shard_map/pallas_call | solution.py:372
  (66 shorter events, 16.0 us)
Async XLA Ops:
  0.0 3.2 %copy-start.2 = (bf16[128,256]{1,0:T(8,128)(2,1)S(1)}, bf16[128,256]{1,0:T(8,128)(2,1)}, u32[]{:S(2)}) copy-start(bf16[128,256]{1,0:T(8,128)(2,1)} %constant.61.clone.weights) | copy-start | bytes 196612
  3.3 4.6 %copy-start = (bf16[1,3,256,8,1024]{4,3,2,1,0:T(8,128)(2,1)S(1)}, bf16[1,3,256,8,1024]{4,3,2,1,0:T(8,128)(2,1)}, u32[]{:S(2)}) copy-start(bf16[1,3,256,8,1024]{4,3,2,1,0:T(8,128)(2,1)} %param.13) | copy-start | bytes 37748740
  11.4 9.7 %collective-permute-start.3 = (s16[2,2,3,64,1024]{4,3,2,1,0:T(8,128)(2,1)}, s16[2,2,3,64,1024]{4,3,2,1,0:T(8,128)(2,1)}, u32[]{:S(2)}, u32[]{:S(2)}) collective-permute-start(s16[2,2,3,64,1024]{4,3,2,1,0:T(8,128)(2,1)} %get-tuple-element.41), channel_id=1, source_target_pairs={{0,4},{4,0},{8,12},{12,8},{16,20},{20,16},{24,28},{28,24},{1,5},{5... | collective-permute-start | bytes 4718600 | tf_op jit(solution)/shard_map/ppermute | solution.py:409
  15.3 8.1 %collective-permute-start.2 = (s16[2,2,3,64,1024]{4,3,2,1,0:T(8,128)(2,1)}, s16[2,2,3,64,1024]{4,3,2,1,0:T(8,128)(2,1)}, u32[]{:S(2)}, u32[]{:S(2)}) collective-permute-start(s16[2,2,3,64,1024]{4,3,2,1,0:T(8,128)(2,1)} %get-tuple-element.39), channel_id=1, source_target_pairs={{0,4},{4,0},{8,12},{12,8},{16,20},{20,16},{24,28},{28,24},{1,5},{5... | collective-permute-start | bytes 4718600 | tf_op jit(solution)/shard_map/ppermute | solution.py:409
  15.4 15.4 %collective-permute-start = (f32[3,16,2,1024]{3,2,1,0:T(2,128)}, f32[3,16,2,1024]{3,2,1,0:T(2,128)S(1)}, u32[]{:S(2)}, u32[]{:S(2)}) collective-permute-start(f32[3,16,2,1024]{3,2,1,0:T(2,128)} %get-tuple-element.35), channel_id=1, source_target_pairs={{0,1},{1,2},{2,3},{3,0},{4,5},{5,6},{6,7},{7,4},{8,9},{9,10},{10,1... | collective-permute-start | bytes 1179656 | tf_op jit(solution)/shard_map/ppermute | solution.py:405
  18.4 19.5 %collective-permute-start.1 = (f32[3,16,2,1024]{3,2,1,0:T(2,128)}, f32[3,16,2,1024]{3,2,1,0:T(2,128)}, u32[]{:S(2)}, u32[]{:S(2)}) collective-permute-start(f32[3,16,2,1024]{3,2,1,0:T(2,128)} %get-tuple-element.36), channel_id=1, source_target_pairs={{1,0},{2,1},{3,2},{0,3},{5,4},{6,5},{7,6},{4,7},{9,8},{10,9},{11,1... | collective-permute-start | bytes 1179656 | tf_op jit(solution)/shard_map/ppermute | solution.py:405
  23.4 6.2 %copy-start.13 = (f32[64]{0:T(128)S(1)}, f32[64]{0:T(128)}, u32[]{:S(2)}) copy-start(f32[64]{0:T(128)} %param.16) | copy-start | bytes 772
  25.7 46.1 %collective-permute-start.4 = (s16[3,64,1024]{2,1,0:T(8,128)(2,1)}, s16[3,64,1024]{2,1,0:T(8,128)(2,1)}, u32[]{:S(2)}, u32[]{:S(2)}) collective-permute-start(s16[3,64,1024]{2,1,0:T(8,128)(2,1)} %get-tuple-element.44), channel_id=1, source_target_pairs={{0,16},{4,20},{8,24},{12,28},{16,0},{20,4},{24,8},{28,12},{1,17},{... | collective-permute-start | bytes 1179656 | tf_op jit(solution)/shard_map/ppermute | solution.py:409
  27.5 44.4 %collective-permute-start.5 = (s16[3,64,1024]{2,1,0:T(8,128)(2,1)}, s16[3,64,1024]{2,1,0:T(8,128)(2,1)}, u32[]{:S(2)}, u32[]{:S(2)}) collective-permute-start(s16[3,64,1024]{2,1,0:T(8,128)(2,1)} %get-tuple-element.45), channel_id=1, source_target_pairs={{0,8},{4,12},{8,0},{12,4},{16,24},{20,28},{24,16},{28,20},{1,9},{5... | collective-permute-start | bytes 1179656 | tf_op jit(solution)/shard_map/ppermute | solution.py:409
  30.2 47.3 %collective-permute-start.6 = (s16[3,64,1024]{2,1,0:T(8,128)(2,1)}, s16[3,64,1024]{2,1,0:T(8,128)(2,1)}, u32[]{:S(2)}, u32[]{:S(2)}) collective-permute-start(s16[3,64,1024]{2,1,0:T(8,128)(2,1)} %get-tuple-element.47), channel_id=1, source_target_pairs={{0,16},{4,20},{8,24},{12,28},{16,0},{20,4},{24,8},{28,12},{1,17},{... | collective-permute-start | bytes 1179656 | tf_op jit(solution)/shard_map/ppermute | solution.py:409
  30.8 46.8 %collective-permute-start.7 = (s16[3,64,1024]{2,1,0:T(8,128)(2,1)}, s16[3,64,1024]{2,1,0:T(8,128)(2,1)}, u32[]{:S(2)}, u32[]{:S(2)}) collective-permute-start(s16[3,64,1024]{2,1,0:T(8,128)(2,1)} %get-tuple-element.48), channel_id=1, source_target_pairs={{0,8},{4,12},{8,0},{12,4},{16,24},{20,28},{24,16},{28,20},{1,9},{5... | collective-permute-start | bytes 1179656 | tf_op jit(solution)/shard_map/ppermute | solution.py:409
  68.1 2.7 %copy-start.1 = (f32[3,2,256,1024]{3,2,1,0:T(8,128)}, f32[3,2,256,1024]{3,2,1,0:T(8,128)S(1)}, u32[]{:S(2)}) copy-start(f32[3,2,256,1024]{3,2,1,0:T(8,128)S(1)} %get-tuple-element.60.inner) | copy-start | bytes 18874372
  74.6 12.4 %collective-permute-start.8 = (s16[3,64,1024]{2,1,0:T(8,128)(2,1)}, s16[3,64,1024]{2,1,0:T(8,128)(2,1)}, u32[]{:S(2)}, u32[]{:S(2)}) collective-permute-start(s16[3,64,1024]{2,1,0:T(8,128)(2,1)} %get-tuple-element.50), channel_id=1, source_target_pairs={{0,16},{4,20},{8,24},{12,28},{16,0},{20,4},{24,8},{28,12},{1,17},{... | collective-permute-start | bytes 1179656 | tf_op jit(solution)/shard_map/ppermute | solution.py:409
  75.8 11.1 %copy-start.8 = (s16[3,64,1024]{2,1,0:T(8,128)(2,1)S(1)}, s16[3,64,1024]{2,1,0:T(8,128)(2,1)}, u32[]{:S(2)}) copy-start(s16[3,64,1024]{2,1,0:T(8,128)(2,1)} %get-tuple-element.78) | copy-start | bytes 1179652
  75.8 12.4 %collective-permute-start.9 = (s16[3,64,1024]{2,1,0:T(8,128)(2,1)}, s16[3,64,1024]{2,1,0:T(8,128)(2,1)}, u32[]{:S(2)}, u32[]{:S(2)}) collective-permute-start(s16[3,64,1024]{2,1,0:T(8,128)(2,1)} %get-tuple-element.51), channel_id=1, source_target_pairs={{0,8},{4,12},{8,0},{12,4},{16,24},{20,28},{24,16},{28,20},{1,9},{5... | collective-permute-start | bytes 1179656 | tf_op jit(solution)/shard_map/ppermute | solution.py:409
  80.3 17.1 %collective-permute-start.10 = (s16[3,64,1024]{2,1,0:T(8,128)(2,1)}, s16[3,64,1024]{2,1,0:T(8,128)(2,1)S(1)}, u32[]{:S(2)}, u32[]{:S(2)}) collective-permute-start(s16[3,64,1024]{2,1,0:T(8,128)(2,1)} %get-tuple-element.53), channel_id=1, source_target_pairs={{0,16},{4,20},{8,24},{12,28},{16,0},{20,4},{24,8},{28,12},{1,17},{... | collective-permute-start | bytes 1179656 | tf_op jit(solution)/shard_map/ppermute | solution.py:409
  80.6 15.9 %collective-permute-start.11 = (s16[3,64,1024]{2,1,0:T(8,128)(2,1)}, s16[3,64,1024]{2,1,0:T(8,128)(2,1)S(1)}, u32[]{:S(2)}, u32[]{:S(2)}) collective-permute-start(s16[3,64,1024]{2,1,0:T(8,128)(2,1)} %get-tuple-element.54), channel_id=1, source_target_pairs={{0,8},{4,12},{8,0},{12,4},{16,24},{20,28},{24,16},{28,20},{1,9},{5... | collective-permute-start | bytes 1179656 | tf_op jit(solution)/shard_map/ppermute | solution.py:409
  89.4 15.7 %collective-permute-start.12 = (s16[3,64,1024]{2,1,0:T(8,128)(2,1)S(1)}, s16[3,64,1024]{2,1,0:T(8,128)(2,1)}, u32[]{:S(2)}, u32[]{:S(2)}) collective-permute-start(s16[3,64,1024]{2,1,0:T(8,128)(2,1)S(1)} %broadcast_select_fusion.4), channel_id=1, source_target_pairs={{0,8},{4,12},{8,0},{12,4},{16,24},{20,28},{24,16},{28,20},{1,9},{5... | collective-permute-start | bytes 1179656 | tf_op jit(solution)/shard_map/ppermute | solution.py:409
  91.1 15.4 %collective-permute-start.13 = (s16[3,64,1024]{2,1,0:T(8,128)(2,1)S(1)}, s16[3,64,1024]{2,1,0:T(8,128)(2,1)S(1)}, u32[]{:S(2)}, u32[]{:S(2)}) collective-permute-start(s16[3,64,1024]{2,1,0:T(8,128)(2,1)S(1)} %broadcast_select_fusion.3), channel_id=1, source_target_pairs={{0,16},{4,20},{8,24},{12,28},{16,0},{20,4},{24,8},{28,12},{1,17},{... | collective-permute-start | bytes 1179656 | tf_op jit(solution)/shard_map/ppermute | solution.py:409
  97.4 9.1 %copy-start.11 = (s16[3,64,1024]{2,1,0:T(8,128)(2,1)}, s16[3,64,1024]{2,1,0:T(8,128)(2,1)S(1)}, u32[]{:S(2)}) copy-start(s16[3,64,1024]{2,1,0:T(8,128)(2,1)S(1)} %collective-permute-done.10) | copy-start | bytes 1179652
  98.3 13.2 %collective-permute-start.15 = (s16[3,64,1024]{2,1,0:T(8,128)(2,1)}, s16[3,64,1024]{2,1,0:T(8,128)(2,1)S(1)}, u32[]{:S(2)}, u32[]{:S(2)}) collective-permute-start(s16[3,64,1024]{2,1,0:T(8,128)(2,1)} %broadcast_select_fusion.2), channel_id=1, source_target_pairs={{0,8},{4,12},{8,0},{12,4},{16,24},{20,28},{24,16},{28,20},{1,9},{5... | collective-permute-start | bytes 1179656 | tf_op jit(solution)/shard_map/ppermute | solution.py:409
  100.1 11.8 %collective-permute-start.16 = (s16[3,64,1024]{2,1,0:T(8,128)(2,1)}, s16[3,64,1024]{2,1,0:T(8,128)(2,1)S(1)}, u32[]{:S(2)}, u32[]{:S(2)}) collective-permute-start(s16[3,64,1024]{2,1,0:T(8,128)(2,1)} %broadcast_select_fusion.1), channel_id=1, source_target_pairs={{0,16},{4,20},{8,24},{12,28},{16,0},{20,4},{24,8},{28,12},{1,17},{... | collective-permute-start | bytes 1179656 | tf_op jit(solution)/shard_map/ppermute | solution.py:409
  108.2 3.3 %copy-start.10 = (s16[3,64,1024]{2,1,0:T(8,128)(2,1)S(1)}, s16[3,64,1024]{2,1,0:T(8,128)(2,1)}, u32[]{:S(2)}) copy-start(s16[3,64,1024]{2,1,0:T(8,128)(2,1)} %get-tuple-element.48) | copy-start | bytes 1179652
  108.2 3.3 %copy-start.12 = (s16[3,64,1024]{2,1,0:T(8,128)(2,1)S(1)}, s16[3,64,1024]{2,1,0:T(8,128)(2,1)}, u32[]{:S(2)}) copy-start(s16[3,64,1024]{2,1,0:T(8,128)(2,1)} %copy-done.11) | copy-start | bytes 1179652
  108.4 4.9 %copy-start.6 = (s16[2,2,3,64,1024]{4,3,2,1,0:T(8,128)(2,1)}, s16[2,2,3,64,1024]{4,3,2,1,0:T(8,128)(2,1)S(1)}, u32[]{:S(2)}) copy-start(s16[2,2,3,64,1024]{4,3,2,1,0:T(8,128)(2,1)S(1)} %pad_add_fusion.held0) | copy-start | bytes 4718596
  108.4 3.5 %copy-start.9 = (s16[3,64,1024]{2,1,0:T(8,128)(2,1)S(1)}, s16[3,64,1024]{2,1,0:T(8,128)(2,1)}, u32[]{:S(2)}) copy-start(s16[3,64,1024]{2,1,0:T(8,128)(2,1)} %get-tuple-element.47) | copy-start | bytes 1179652
  108.4 20.8 %collective-permute-start.14 = (s16[2,2,3,64,1024]{4,3,2,1,0:T(8,128)(2,1)S(1)}, s16[2,2,3,64,1024]{4,3,2,1,0:T(8,128)(2,1)}, u32[]{:S(2)}, u32[]{:S(2)}) collective-permute-start(s16[2,2,3,64,1024]{4,3,2,1,0:T(8,128)(2,1)S(1)} %pad_add_fusion.held0), channel_id=1, source_target_pairs={{0,4},{4,0},{8,12},{12,8},{16,20},{20,16},{24,28},{28,24},{1,5},{5... | collective-permute-start | bytes 4718600 | tf_op jit(solution)/shard_map/ppermute | solution.py:409
  113.7 14.7 %copy-start.7 = (s16[2,2,3,64,1024]{4,3,2,1,0:T(8,128)(2,1)}, s16[2,2,3,64,1024]{4,3,2,1,0:T(8,128)(2,1)S(1)}, u32[]{:S(2)}) copy-start(s16[2,2,3,64,1024]{4,3,2,1,0:T(8,128)(2,1)S(1)} %pad_add_fusion.1.held1) | copy-start | bytes 4718596
  113.7 15.5 %collective-permute-start.17 = (s16[2,2,3,64,1024]{4,3,2,1,0:T(8,128)(2,1)S(1)}, s16[2,2,3,64,1024]{4,3,2,1,0:T(8,128)(2,1)}, u32[]{:S(2)}, u32[]{:S(2)}) collective-permute-start(s16[2,2,3,64,1024]{4,3,2,1,0:T(8,128)(2,1)S(1)} %pad_add_fusion.1.held1), channel_id=1, source_target_pairs={{0,4},{4,0},{8,12},{12,8},{16,20},{20,16},{24,28},{28,24},{1,5},{5... | collective-permute-start | bytes 4718600 | tf_op jit(solution)/shard_map/ppermute | solution.py:409
  113.8 9.5 %collective-permute-start.18 = (s16[2,3,16,1024]{3,2,1,0:T(8,128)(2,1)S(1)}, s16[2,3,16,1024]{3,2,1,0:T(8,128)(2,1)S(1)}, u32[]{:S(2)}, u32[]{:S(2)}) collective-permute-start(s16[2,3,16,1024]{3,2,1,0:T(8,128)(2,1)S(1)} %fusion.10), channel_id=1, source_target_pairs={{0,1},{1,2},{2,3},{3,0},{8,9},{9,10},{10,11},{11,8},{16,17},{17,18... | collective-permute-start | bytes 589832 | tf_op jit(solution)/shard_map/ppermute | solution.py:467
  117.5 7.9 %collective-permute-start.19 = (s16[2,3,16,1024]{3,2,1,0:T(8,128)(2,1)S(1)}, s16[2,3,16,1024]{3,2,1,0:T(8,128)(2,1)S(1)}, u32[]{:S(2)}, u32[]{:S(2)}) collective-permute-start(s16[2,3,16,1024]{3,2,1,0:T(8,128)(2,1)S(1)} %fusion.11), channel_id=1, source_target_pairs={{1,0},{2,1},{3,2},{0,3},{9,8},{10,9},{11,10},{8,11},{17,16},{18,17... | collective-permute-start | bytes 589832 | tf_op jit(solution)/shard_map/ppermute | solution.py:468
  126.1 2.1 %collective-permute-start.20 = (s16[2,2,3,16,1024]{4,3,2,1,0:T(8,128)(2,1)}, s16[2,2,3,16,1024]{4,3,2,1,0:T(8,128)(2,1)}, u32[]{:S(2)}, u32[]{:S(2)}) collective-permute-start(s16[2,2,3,16,1024]{4,3,2,1,0:T(8,128)(2,1)} %pad_add_fusion.4), channel_id=1, source_target_pairs={{0,4},{4,0},{8,12},{12,8},{16,20},{20,16},{24,28},{28,24},{1,5},{5... | collective-permute-start | bytes 1179656 | tf_op jit(solution)/shard_map/ppermute | solution.py:409
  (3 other events, 2.7 us)

commit v6 on v5

--- a/solution.py
+++ b/solution.py
@@ -14,6 +14,7 @@
 code_scale = 4096.0
 phases = 2
 streams = ((0, 3), (1, 2))
+shares = {(0, 1): 0, (1, 1): 1, (2, 0): 2}
 
 
 def grant(mib):
@@ -140,7 +141,7 @@
 
 
 def field_kernel(
-    viscosity, turn, m_all, m_top, before, after, field, inner, depth, along, across, sums, token,
+    c, viscosity, turn, m_all, m_top, before, after, field, inner, depth, along, across, sums, token,
     columns, high_s, low_s, high_x, low_x, arrived,
 ):
     slab, width = inner.shape[2:]
@@ -148,19 +149,14 @@
     tiles = width // lanes
     gain = viscosity[0] * section_step
 
-    def fetch(c, t):
+    def fetch(t):
         source = field.at[c, :, pl.ds(t * lanes, lanes)]
         return pltpu.make_async_copy(source, columns.at[t], arrived.at[t])
 
-    c = pl.program_id(0)
-
-    @pl.when(c == 0)
-    def _():
-        for t in range(tiles):
-            fetch(0, t).start()
-
     for t in range(tiles):
-        fetch(c, t).wait()
+        fetch(t).start()
+    for t in range(tiles):
+        fetch(t).wait()
 
         def unpack(i, carry):
             start = pl.multiple_of(i * 8, 8)
@@ -179,10 +175,6 @@
             return carry
 
         lax.fori_loop(0, slab // 8, unpack, 0, unroll=4)
-
-        @pl.when(c < pl.num_programs(0) - 1)
-        def _():
-            fetch(c + 1, t).start()
 
     rows = m_top.shape[0] // 2
     for p in range(2):
@@ -221,33 +213,33 @@
     token[...] = jnp.zeros_like(token)
 
 
-def field_terms(field, before, after, viscosity, length):
+def field_terms(c, field, before, after, viscosity, length):
     comps, slab, planes, width = field.shape
     flat = field.reshape(comps, slab * planes, width)
     rows = min(slab, 128)
     high, low, second = along_matrices(rows, length)
     top = np.concatenate([high, second], 0)
     everything = np.concatenate([high, second, low], 0)
-    rim = pl.BlockSpec((1, reach, 2, width), lambda c: (c, 0, 0, 0))
+    rim = pl.BlockSpec((1, reach, 2, width), lambda i: (c, 0, 0, 0))
     turn = across_matrix([first_at(0), [t for t in second_at(0) if t[0] != 0]])
-    shape = jax.ShapeDtypeStruct((comps, 2, slab, width), jnp.float32)
-    spec = pl.BlockSpec((1, 2, slab, width), lambda c: (c, 0, 0, 0))
-    mark = pl.BlockSpec((8, lanes), lambda c: (0, 0))
+    shape = jax.ShapeDtypeStruct((1, 2, slab, width), jnp.float32)
+    spec = pl.BlockSpec((1, 2, slab, width), lambda i: (0, 0, 0, 0))
+    mark = pl.BlockSpec((8, lanes), lambda i: (0, 0))
     return pl.pallas_call(
-        field_kernel,
+        functools.partial(field_kernel, c),
         out_shape=(shape,) * 5 + (jax.ShapeDtypeStruct((8, lanes), jnp.int32),),
-        grid=(comps,),
+        grid=(1,),
         in_specs=[
             pl.BlockSpec(memory_space=pltpu.SMEM),
-            pl.BlockSpec(turn.shape, lambda c: (0, 0)),
-            pl.BlockSpec(everything.shape, lambda c: (0, 0)),
-            pl.BlockSpec(top.shape, lambda c: (0, 0)),
+            pl.BlockSpec(turn.shape, lambda i: (0, 0)),
+            pl.BlockSpec(everything.shape, lambda i: (0, 0)),
+            pl.BlockSpec(top.shape, lambda i: (0, 0)),
             rim,
             rim,
             pl.BlockSpec(memory_space=pl.ANY),
         ],
         out_specs=(spec,) * 5 + (mark,),
-        compiler_params=grant(42),
+        compiler_params=grant(57),
         scratch_shapes=[
             pltpu.VMEM((width // lanes, slab * planes, lanes), jnp.float32),
             pltpu.VMEM((slab, width + lanes), jnp.bfloat16),
@@ -257,17 +249,17 @@
             pltpu.SemaphoreType.DMA((width // lanes,)),
         ],
         cost_estimate=pl.CostEstimate(
-            flops=0, bytes_accessed=4 * comps * slab * planes * width * 2, transcendentals=0
+            flops=0, bytes_accessed=4 * slab * planes * width * 2, transcendentals=0
         ),
     )(
         viscosity, jnp.asarray(turn), jnp.asarray(everything), jnp.asarray(top), before, after, flat
     )
 
 
-def final_kernel(
-    core, m_both, turn, held0, other0, held1, other1, before, after,
-    inner, depth, along, across, sums, out, base_s, turned_s, flow_s, ghost_s, slope_s, side_s, arrived,
-):
+def final_kernel(core, m_both, turn, held0, other0, held1, other1, before, after, *refs):
+    terms, scratch = refs[:15], refs[15:]
+    inner, depth, along, across, sums = [terms[n::5] for n in range(5)]
+    out, base_s, turned_s, flow_s, ghost_s, slope_s, side_s, arrived = scratch
     step = pl.program_id(0)
     rows = slope_s.shape[2]
     quarter = held0.shape[3]
@@ -343,7 +335,7 @@
             [base_s[c, p, inside, :].astype(jnp.float32) for p in range(2)] for c in range(3)
         ]
         for p in range(2):
-            move = [inner[c, p, at, :] for c in range(3)]
+            move = [inner[c][0, p, at, :] for c in range(3)]
             for c in range(3):
                 dz = decoded(ghost_s[p, c, there, :])
                 if p == 0:
@@ -351,24 +343,25 @@
                 else:
                     dz = dz - 0.75 * flow[c][0]
                 dy = side_s[c, p, at, :] * (1.0 / 60.0)
-                total = flow[0][p] * along[c, p, at, :] + flow[1][p] * across[c, p, at, :]
-                total = total + flow[2][p] * depth[c, p, at, :]
+                total = flow[0][p] * along[c][0, p, at, :] + flow[1][p] * across[c][0, p, at, :]
+                total = total + flow[2][p] * depth[c][0, p, at, :]
                 total = total + move[0] * slope_s[c, p, at, :] + move[1] * dy + move[2] * dz
-                out[0, c, at, p, :] = sums[c, p, at, :] - section_step * total
+                out[0, c, at, p, :] = sums[c][0, p, at, :] - section_step * total
         return carry
 
     lax.fori_loop(0, rows // 16, body, 0)
 
 
 def final(core, pieces, before, after, terms, length):
-    comps, pair, slab, width = terms[0].shape
+    _, pair, slab, width = terms[0].shape
+    comps = len(terms) // 5
     rows = min(slab, 32)
     turn = across_matrix([first_at(0)])
     high, low, _ = along_matrices(rows, length)
     both = np.concatenate([high, low], 0)
     whole = pl.BlockSpec(memory_space=pl.ANY)
     rim = pl.BlockSpec(before.shape, lambda i: (0, 0, 0, 0))
-    spec = pl.BlockSpec((comps, pair, rows, width), lambda i: (0, 0, i, 0))
+    spec = pl.BlockSpec((1, pair, rows, width), lambda i: (0, 0, i, 0))
     return pl.pallas_call(
         final_kernel,
         out_shape=jax.ShapeDtypeStruct((1, comps, slab, pair, width), jnp.float32),
@@ -380,7 +373,7 @@
         ]
         + [whole] * 4
         + [rim] * 2
-        + [spec] * 5,
+        + [spec] * 15,
         out_specs=pl.BlockSpec((1, comps, rows, pair, width), lambda i: (0, 0, i, 0, 0)),
         compiler_params=grant(58),
         scratch_shapes=[
@@ -420,7 +413,7 @@
         return jnp.where(is_root, mine[u][h, k], handed[u][h, k])
 
     opening = [owned(u, h, 0) for u in range(2) for h in range(2)]
-    opening = gate(opening)
+    opening = gate(*opening)
     source = [
         [[opening[2 * u + h]] + [owned(u, h, k) for k in range(1, phases)] for h in range(2)]
         for u in range(2)
@@ -436,13 +429,13 @@
             if s > 0:
                 one = jnp.where(at_a, one, Y[u][s - 1])
                 two = jnp.where(at_a, two, X[u][s - 1])
-                one, two, place = lax.optimization_barrier((one, two, place))
+                one, two, place = gate(one, two, place)
                 at_a, at_b, at_c = place == 0, place == 1, place == 2
             X[u].append(swap(one, 2))
             Y[u].append(swap(two, 4))
-        if s == 0:
-            place = place + work()
-            at_a, at_b, at_c = place == 0, place == 1, place == 2
+            if (s, u) in shares:
+                place = place + work(shares[s, u])
+                at_a, at_b, at_c = place == 0, place == 1, place == 2
     held = []
     for u in range(2):
         parts = []
@@ -456,17 +449,20 @@
                 row.append(jnp.where(at_a, source[u][h][k], value))
             parts.append(jnp.stack(row, 0))
         held.append(jnp.stack(parts, 0))
-    quarter = held[0].shape[3]
-    size = lax.axis_size("gx")
-    pairs = [
-        (c * size + i, c * size + (i + 1) % size)
-        for c in range(0, lax.axis_size("pert"), 2)
-        for i in range(size)
-    ]
-    both = ("pert", "gx")
-    before = lax.ppermute(held[0][1][:, :, quarter - reach :], both, pairs)
-    after = lax.ppermute(held[0][0][:, :, :reach], both, [(j, i) for i, j in pairs])
-    rims = jnp.stack([before, after], 0)
+        if u == 0:
+            quarter = held[0].shape[3]
+            size = lax.axis_size("gx")
+            pairs = [
+                (c * size + i, c * size + (i + 1) % size)
+                for c in range(0, lax.axis_size("pert"), 2)
+                for i in range(size)
+            ]
+            both = ("pert", "gx")
+            before = lax.ppermute(held[0][1][:, :, quarter - reach :], both, pairs)
+            after = lax.ppermute(held[0][0][:, :, :reach], both, [(j, i) for i, j in pairs])
+            rims = jnp.stack([before, after], 0)
+            before, after, place = lax.optimization_barrier((before, after, place))
+            at_a, at_b, at_c = place == 0, place == 1, place == 2
     other = [swap(h, 1) for h in held]
     rims = jnp.where(core == 0, rims, swap(rims, 1))
     return (held[0], other[0], held[1], other[1]), rims[0], rims[1]
@@ -491,21 +487,23 @@
     )
     before, after = ring(last, first)
     halves = [pack(tile, planes, core, u) for u in range(2)]
-    done = {"field": field}
-
-    def gate(opening):
-        done["field"], *opening = lax.optimization_barrier((done["field"], *opening))
-        return opening
-
-    def work():
-        *done["terms"], token = field_terms(done["field"], before, after, viscosity, length)
+    done = {"field": field, "terms": []}
+
+    def gate(*values):
+        done["field"], *values = lax.optimization_barrier((done["field"], *values))
+        return values
+
+    def work(c):
+        *terms, token = field_terms(c, done["field"], before, after, viscosity, length)
+        done["terms"] += terms
         return token[0, 0]
 
     if in_pairs:
         mine, theirs = [h[0] for h in halves], [h[1] for h in halves]
         pieces, base_before, base_after = exchange(mine, theirs, owner_root, core[0], gate, work)
     else:
-        work()
+        for c in range(comps):
+            work(c)
         pieces = [
             lax.psum(jnp.where(me == owner_root, a, 0).astype(jnp.float32), "pert").astype(a.dtype)
             for h in halves

time: 154 us -> 149 us (0.968)
  waiting for transfers between devices: 29 us -> 11.5 us
  Pallas kernels: 58.4 us -> 69.9 us
  other arithmetic: 21 us -> 24.2 us
  local copies, waits for them, and re-layouts: 14.6 us -> 12.4 us
  between operations: 2.19 us -> 3.75 us
    ppermute x17, waiting for transfers between devices: 19.6 us -> 2.52 us  [swap(): lax.ppermute(array, 'pert', [(i, i ^ bit) for i in range(lax.axis_size('p...]
    pallas_call x1 -> x3, Pallas kernels: 27.4 us -> 39 us  [field_terms(): pl.pallas_call(functools.partial(field_kernel, c), out_shape=(shape,) * 5...]
    unnamed x28 -> x24, local copies, waits for them, and re-layouts: 10 us -> 4.62 us
    slice x1 -> x3, local copies, waits for them, and re-layouts: 0.5 us -> 3.7 us  [work(): return token[0, 0]]
  transfers between devices with their start and end apart: 21 -> 21, of which waited for: 9 -> 4; matrix products, arithmetic and copies ran while one was open for 15% -> 19% of each run, Pallas kernels for 20% -> 29%
where the time goes in v6:
time: 149 us
  Pallas kernels  69.9 us (47%)
  starting transfers between devices  26.9 us (18%)
  other arithmetic  24.2 us (16%)
  local copies, waits for them, and re-layouts  12.4 us (8%)
  waiting for transfers between devices  11.5 us (8%)
  between operations  3.75 us (3%)
    pallas_call x3, Pallas kernels, field_terms(): pl.pallas_call(functools.partial(field_kernel, c), out_shape=(shape,) * 5...  39 us
    pallas_call x1, Pallas kernels, final(): pl.pallas_call(final_kernel, out_shape=jax.ShapeDtypeStruct((1, comps, sl...  23.8 us
    ppermute x17, starting transfers between devices, swap(): lax.ppermute(array, 'pert', [(i, i ^ bit) for i in range(lax.axis_size('p...  14.2 us
    pallas_call x2, Pallas kernels, pack(): pl.pallas_call(pack_kernel, out_shape=(shape,) * 2, grid=(2, comps), in_s...  7.07 us
    another operation x6, other arithmetic, exchange(): parts.append(jnp.stack(row, 0))  5.97 us
    ppermute x2, waiting for transfers between devices, ring(): return (lax.ppermute(last, 'gx', up), lax.ppermute(first, 'gx', down))  5.58 us
    ppermute x2, starting transfers between devices, ring(): return (lax.ppermute(last, 'gx', up), lax.ppermute(first, 'gx', down))  5.06 us
    select_n x3, other arithmetic, exchange(): two = jnp.where(at_a, two, X[u][s - 1])  4.83 us
  transfers between devices with their start and end apart: 21, of which 4 were waited for; matrix products, arithmetic and copies ran while one was open for 19% of the time, Pallas kernels for 29%

profile of v6, /device:TPU:0, one launch (start us, length us, event | category | flops | bytes accessed | tf_op | source)
XLA Modules:
  0.0 148.6 jit_solution(593146449338421399)
XLA Ops:
  0.0 3.2 %fusion.17 = (f32[3,16,2,1024]{3,2,1,0:T(2,128)}, f32[3,16,2,1024]{3,2,1,0:T(2,128)}) fusion(f32[3,256,8,1024]{3,2,1,0:T(8,128)} %bitcast.70), kind=kLoop, calls=%fused_computation.52 | loop fusion | bytes 1572864 | tf_op jit(solution)/shard_map/slice | solution.py:486
  3.2 4.6 %copy-done = bf16[1,3,256,8,1024]{4,3,2,1,0:T(8,128)(2,1)S(1)} copy-done((bf16[1,3,256,8,1024]{4,3,2,1,0:T(8,128)(2,1)S(1)}, bf16[1,3,256,8,1024]{4,3,2,1,0:T(8,128)(2,1)}, u32[]{:S(2)}) %copy-start) | copy-done | bytes 12582936
  7.8 3.6 %shard_map.173 = (s16[2,2,3,64,1024]{4,3,2,1,0:T(8,128)(2,1)S(1)}, s16[2,2,3,64,1024]{4,3,2,1,0:T(8,128)(2,1)}) custom-call(s32[1]{0:T(128)} %bitcast.core, bf16[128,256]{1,0:T(8,128)(2,1)S(1)} %copy-done.1, bf16[3,2048,1024]{2,1,0:T(8,128)(2,1)S(1)} %bitcast.68), custom_call_target="tpu_custom_call" | custom-call | bytes 12582912 | tf_op jit(solution)/shard_map/pallas_call | solution.py:124
  11.8 3.5 %shard_map.172 = (s16[2,2,3,64,1024]{4,3,2,1,0:T(8,128)(2,1)S(1)}, s16[2,2,3,64,1024]{4,3,2,1,0:T(8,128)(2,1)}) custom-call(s32[1]{0:T(128)} %bitcast.core, bf16[128,256]{1,0:T(8,128)(2,1)S(1)} %copy-done.1, bf16[3,2048,1024]{2,1,0:T(8,128)(2,1)S(1)} %bitcast.69), custom_call_target="tpu_custom_call" | custom-call | bytes 12582912 | tf_op jit(solution)/shard_map/pallas_call | solution.py:124
  15.4 3.0 %collective-permute-start.2 = (f32[3,16,2,1024]{3,2,1,0:T(2,128)}, f32[3,16,2,1024]{3,2,1,0:T(2,128)S(1)}, u32[]{:S(2)}, u32[]{:S(2)}) collective-permute-start(f32[3,16,2,1024]{3,2,1,0:T(2,128)} %get-tuple-element.57), channel_id=1, source_target_pairs={{0,1},{1,2},{2,3},{3,0},{4,5},{5,6},{6,7},{7,4},{8,9},{9,10},{10,1... | collective-permute-start | bytes 1179656 | tf_op jit(solution)/shard_map/ppermute | solution.py:398
  18.4 2.0 %collective-permute-start.3 = (f32[3,16,2,1024]{3,2,1,0:T(2,128)}, f32[3,16,2,1024]{3,2,1,0:T(2,128)}, u32[]{:S(2)}, u32[]{:S(2)}) collective-permute-start(f32[3,16,2,1024]{3,2,1,0:T(2,128)} %get-tuple-element.58), channel_id=1, source_target_pairs={{1,0},{2,1},{3,2},{0,3},{5,4},{6,5},{7,6},{4,7},{9,8},{10,9},{11,1... | collective-permute-start | bytes 1179656 | tf_op jit(solution)/shard_map/ppermute | solution.py:398
  21.1 2.3 %fusion.6 = (s16[3,64,1024]{2,1,0:T(8,128)(2,1)}, s16[3,64,1024]{2,1,0:T(8,128)(2,1)}) fusion(s16[2,2,3,64,1024]{4,3,2,1,0:T(8,128)(2,1)} %collective-permute-done.1, s16[2,2,3,64,1024]{4,3,2,1,0:T(8,128)(2,1)S(1)} %get-tuple-element.54, pred[]{:T(512)S(6)} %eq.44), kind=kLoop, calls=%fused_computation.21 | loop fusion | flops 393216 | bytes 2359297 | tf_op jit(solution)/shard_map/jit(_where)/select_n | solution.py:413
  23.4 2.3 %fusion.8 = (s16[3,64,1024]{2,1,0:T(8,128)(2,1)}, s16[3,64,1024]{2,1,0:T(8,128)(2,1)}) fusion(s16[2,2,3,64,1024]{4,3,2,1,0:T(8,128)(2,1)} %collective-permute-done, s16[2,2,3,64,1024]{4,3,2,1,0:T(8,128)(2,1)S(1)} %get-tuple-element.52, pred[]{:T(512)S(6)} %eq.44), kind=kLoop, calls=%fused_computation.25 | loop fusion | flops 393216 | bytes 2359297 | tf_op jit(solution)/shard_map/jit(_where)/select_n | solution.py:413
  25.7 1.7 %collective-permute-start.4 = (s16[3,64,1024]{2,1,0:T(8,128)(2,1)}, s16[3,64,1024]{2,1,0:T(8,128)(2,1)}, u32[]{:S(2)}, u32[]{:S(2)}) collective-permute-start(s16[3,64,1024]{2,1,0:T(8,128)(2,1)} %get-tuple-element.60), channel_id=1, source_target_pairs={{0,16},{4,20},{8,24},{12,28},{16,0},{20,4},{24,8},{28,12},{1,17},{... | collective-permute-start | bytes 1179656 | tf_op jit(solution)/shard_map/ppermute | solution.py:402
  27.4 1.5 %collective-permute-start.5 = (s16[3,64,1024]{2,1,0:T(8,128)(2,1)}, s16[3,64,1024]{2,1,0:T(8,128)(2,1)}, u32[]{:S(2)}, u32[]{:S(2)}) collective-permute-start(s16[3,64,1024]{2,1,0:T(8,128)(2,1)} %get-tuple-element.61), channel_id=1, source_target_pairs={{0,8},{4,12},{8,0},{12,4},{16,24},{20,28},{24,16},{28,20},{1,9},{5... | collective-permute-start | bytes 1179656 | tf_op jit(solution)/shard_map/ppermute | solution.py:402
  30.7 1.6 %collective-permute-start.7 = (s16[3,64,1024]{2,1,0:T(8,128)(2,1)}, s16[3,64,1024]{2,1,0:T(8,128)(2,1)}, u32[]{:S(2)}, u32[]{:S(2)}) collective-permute-start(s16[3,64,1024]{2,1,0:T(8,128)(2,1)} %get-tuple-element.65), channel_id=1, source_target_pairs={{0,8},{4,12},{8,0},{12,4},{16,24},{20,28},{24,16},{28,20},{1,9},{5... | collective-permute-start | bytes 1179656 | tf_op jit(solution)/shard_map/ppermute | solution.py:402
  32.3 5.6 %collective-permute-done.3.after = f32[3,16,2,1024]{3,2,1,0:T(2,128)} collective-permute-done((f32[3,16,2,1024]{3,2,1,0:T(2,128)}, f32[3,16,2,1024]{3,2,1,0:T(2,128)}, u32[]{:S(2)}, u32[]{:S(2)}) %collective-permute-start.3) | collective-permute-done | bytes 393248 | tf_op jit(solution)/shard_map/ppermute | solution.py:398
  37.9 13.0 %shard_map.174 = (f32[1,2,256,1024]{3,2,1,0:T(8,128)}, f32[1,2,256,1024]{3,2,1,0:T(8,128)}, f32[1,2,256,1024]{3,2,1,0:T(8,128)}, f32[1,2,256,1024]{3,2,1,0:T(8,1...) custom-call(f32[1]{0:T(128)} %bitcast.9.viscosity, bf16[256,256]{1,0:T(8,128)(2,1)} %constant.62.clone.turn, ...), custom_call_target="tpu_custom_call" | custom-call | bytes 16777216 | tf_op jit(solution)/shard_map/pallas_call | solution.py:228
  52.8 2.8 %broadcast_select_fusion.8 = (s16[3,64,1024]{2,1,0:T(8,128)(2,1)}, s16[3,64,1024]{2,1,0:T(8,128)(2,1)}, s16[3,64,1024]{2,1,0:T(8,128)(2,1)}, s16[3,64,1024]{2,1,0:T(8,128)(2,1)S(1)}) fusion(s16[3,64,1024]{2,1,0:T(8,128)(2,1)} %collective-permute-done.4, pred[]{:T(512)S(6)} %eq.47, s16[2,2,3,64,1024]{4,3,2,1,0:T(8,128)(2,1)} %collective-permute-done, ...), kind=kLoop, calls=%fused_computation.45 | loop fusion | flops 786432 | bytes 3932162 | tf_op jit(solution)/shard_map/jit(_where)/select_n | solution.py:430
  55.6 1.3 collective-permute-start.9
  56.8 1.8 %collective-permute-start.8 = (s16[3,64,1024]{2,1,0:T(8,128)(2,1)}, s16[3,64,1024]{2,1,0:T(8,128)(2,1)}, u32[]{:S(2)}, u32[]{:S(2)}) collective-permute-start(s16[3,64,1024]{2,1,0:T(8,128)(2,1)} %get-tuple-element.69), channel_id=1, source_target_pairs={{0,16},{4,20},{8,24},{12,28},{16,0},{20,4},{24,8},{28,12},{1,17},{... | collective-permute-start | bytes 1179656 | tf_op jit(solution)/shard_map/ppermute | solution.py:402
  58.6 2.8 %broadcast_select_fusion.5 = (s16[3,64,1024]{2,1,0:T(8,128)(2,1)}, s16[3,64,1024]{2,1,0:T(8,128)(2,1)S(1)}, s16[3,64,1024]{2,1,0:T(8,128)(2,1)}, s16[3,64,1024]{2,1,0:T(8,128)(2,1)S(1)}) fusion(s16[3,64,1024]{2,1,0:T(8,128)(2,1)} %collective-permute-done.7, pred[]{:T(512)S(6)} %eq.48, s16[2,2,3,64,1024]{4,3,2,1,0:T(8,128)(2,1)} %collective-permute-done.1, ...), kind=kLoop, calls=%fused_computation.42 | loop fusion | flops 786432 | bytes 3932162 | tf_op jit(solution)/shard_map/jit(_where)/select_n | solution.py:431
  62.4 13.0 %shard_map.175 = (f32[1,2,256,1024]{3,2,1,0:T(8,128)}, f32[1,2,256,1024]{3,2,1,0:T(8,128)}, f32[1,2,256,1024]{3,2,1,0:T(8,128)}, f32[1,2,256,1024]{3,2,1,0:T(8,1...) custom-call(f32[1]{0:T(128)} %bitcast.9.viscosity, bf16[256,256]{1,0:T(8,128)(2,1)} %constant.62.clone.turn, ...), custom_call_target="tpu_custom_call" | custom-call | bytes 16777216 | tf_op jit(solution)/shard_map/pallas_call | solution.py:228
  75.4 1.2 slice.94
  79.7 3.0 %collective-permute-start.13 = (s16[3,64,1024]{2,1,0:T(8,128)(2,1)S(1)}, s16[3,64,1024]{2,1,0:T(8,128)(2,1)}, u32[]{:S(2)}, u32[]{:S(2)}) collective-permute-start(s16[3,64,1024]{2,1,0:T(8,128)(2,1)S(1)} %broadcast_select_fusion.3), channel_id=1, source_target_pairs={{0,16},{4,20},{8,24},{12,28},{16,0},{20,4},{24,8},{28,12},{1,17},{... | collective-permute-start | bytes 1179656 | tf_op jit(solution)/shard_map/ppermute | solution.py:402
  82.7 13.0 %shard_map.176 = (f32[1,2,256,1024]{3,2,1,0:T(8,128)}, f32[1,2,256,1024]{3,2,1,0:T(8,128)}, f32[1,2,256,1024]{3,2,1,0:T(8,128)}, f32[1,2,256,1024]{3,2,1,0:T(8,1...) custom-call(f32[1]{0:T(128)} %bitcast.9.viscosity, bf16[256,256]{1,0:T(8,128)(2,1)} %constant.62.clone.turn, ...), custom_call_target="tpu_custom_call" | custom-call | bytes 16777216 | tf_op jit(solution)/shard_map/pallas_call | solution.py:228
  100.5 1.5 select_bitcast_fusion.6
  102.0 1.5 %select_bitcast_fusion.7 = (s16[1,3,64,1024]{3,2,1,0:T(8,128)(2,1)S(1)}, s16[1,3,64,1024]{3,2,1,0:T(8,128)(2,1)S(1)}) fusion(s16[3,64,1024]{2,1,0:T(8,128)(2,1)} %get-tuple-element.61, s16[3,64,1024]{2,1,0:T(8,128)(2,1)} %collective-permute-done.5, s16[3,64,1024]{2,1,0:T(8,128)(2,1)S(1)} %collective-permute-done.12, ...), kind=kLoop, calls=%fused_computation.36 | loop fusion | flops 983040 | bytes 2752515 | tf_op jit(solution)/shard_map/stack | solution.py:450
  103.5 3.0 %collective-permute-start.15 = (s16[2,3,16,1024]{3,2,1,0:T(8,128)(2,1)S(1)}, s16[2,3,16,1024]{3,2,1,0:T(8,128)(2,1)}, u32[]{:S(2)}, u32[]{:S(2)}) collective-permute-start(s16[2,3,16,1024]{3,2,1,0:T(8,128)(2,1)S(1)} %fusion.10), channel_id=1, source_target_pairs={{0,1},{1,2},{2,3},{3,0},{8,9},{9,10},{10,11},{11,8},{16,17},{17,18... | collective-permute-start | bytes 589832 | tf_op jit(solution)/shard_map/ppermute | solution.py:461
  106.5 4.6 %collective-permute-start.16 = (s16[2,3,16,1024]{3,2,1,0:T(8,128)(2,1)S(1)}, s16[2,3,16,1024]{3,2,1,0:T(8,128)(2,1)}, u32[]{:S(2)}, u32[]{:S(2)}) collective-permute-start(s16[2,3,16,1024]{3,2,1,0:T(8,128)(2,1)S(1)} %fusion.11), channel_id=1, source_target_pairs={{1,0},{2,1},{3,2},{0,3},{9,8},{10,9},{11,10},{8,11},{17,16},{18,17... | collective-permute-start | bytes 589832 | tf_op jit(solution)/shard_map/ppermute | solution.py:462
  111.7 1.4 collective-permute-done.15
  113.0 2.0 %collective-permute-done.16 = s16[2,3,16,1024]{3,2,1,0:T(8,128)(2,1)} collective-permute-done((s16[2,3,16,1024]{3,2,1,0:T(8,128)(2,1)S(1)}, s16[2,3,16,1024]{3,2,1,0:T(8,128)(2,1)}, u32[]{:S(2)}, u32[]{:S(2)}) %collective-permute-start.16) | collective-permute-done | bytes 196640 | tf_op jit(solution)/shard_map/ppermute | solution.py:462
  115.1 1.6 %select_bitcast_fusion.3 = (s16[1,3,64,1024]{3,2,1,0:T(8,128)(2,1)S(1)}, s16[1,3,64,1024]{3,2,1,0:T(8,128)(2,1)S(1)}) fusion(s16[3,64,1024]{2,1,0:T(8,128)(2,1)S(1)} %copy-done.7, s16[3,64,1024]{2,1,0:T(8,128)(2,1)} %collective-permute-done.7, s16[3,64,1024]{2,1,0:T(8,128)(2,1)} %collective-permute-done.17, s16[3,64,1024]{2,1,0:T(8,128)(2,1)} %copy-done.10, ...), kind=kLoop, calls=%fused_computation.32 | loop fusion | flops 983040 | bytes 2752515 | tf_op jit(solution)/shard_map/stack | solution.py:450
  116.7 1.4 select_bitcast_fusion.2
  118.5 1.5 %pad_add_fusion.4 = s16[2,2,3,16,1024]{4,3,2,1,0:T(8,128)(2,1)S(1)} fusion(s16[1,2,3,16,1024]{4,3,2,1,0:T(8,128)(2,1)} %bitcast.33, s16[1,2,3,16,1024]{4,3,2,1,0:T(8,128)(2,1)} %bitcast.32), kind=kLoop, calls=%fused_computation.28 | loop fusion | flops 196608 | bytes 786432 | tf_op jit(solution)/shard_map/stack | solution.py:463
  120.2 2.5 %collective-permute-done.20 = s16[2,2,3,16,1024]{4,3,2,1,0:T(8,128)(2,1)} collective-permute-done((s16[2,2,3,16,1024]{4,3,2,1,0:T(8,128)(2,1)S(1)}, s16[2,2,3,16,1024]{4,3,2,1,0:T(8,128)(2,1)}, u32[]{:S(2)}, u32[]{:S(2)}) %collective-permute-start.20) | collective-permute-done | bytes 393248 | tf_op jit(solution)/shard_map/ppermute | solution.py:402
  124.6 23.8 %shard_map.177 = f32[1,3,256,2,1024]{4,3,2,1,0:T(2,128)} custom-call(s32[1]{0:T(128)} %bitcast.core, bf16[64,64]{1,0:T(8,128)(2,1)} %constant.65.clone.m_both, bf16[256,128]{1,0:T(8,128)(2,1)} %constant.66.clone.turn, s16[2,2,3,64,1024]{4,3,2,1,0:T(8,128)(2,1)} %copy-done.2, s16[2,2,3,64,1024]{4,3,2,1,0:T(8,128)(2,1)} %collective-permute-done.14.other0, ...), custom_call_target="tpu_custom_call" | custom-call | bytes 12582912 | tf_op jit(solution)/shard_map/pallas_call | solution.py:365
  (66 shorter events, 13.3 us)
Async XLA Ops:
  0.0 3.2 %copy-start.1 = (bf16[128,256]{1,0:T(8,128)(2,1)S(1)}, bf16[128,256]{1,0:T(8,128)(2,1)}, u32[]{:S(2)}) copy-start(bf16[128,256]{1,0:T(8,128)(2,1)} %constant.61.clone.weights) | copy-start | bytes 196612
  3.2 4.6 %copy-start = (bf16[1,3,256,8,1024]{4,3,2,1,0:T(8,128)(2,1)S(1)}, bf16[1,3,256,8,1024]{4,3,2,1,0:T(8,128)(2,1)}, u32[]{:S(2)}) copy-start(bf16[1,3,256,8,1024]{4,3,2,1,0:T(8,128)(2,1)} %param.19) | copy-start | bytes 37748740
  11.4 9.7 %collective-permute-start.1 = (s16[2,2,3,64,1024]{4,3,2,1,0:T(8,128)(2,1)}, s16[2,2,3,64,1024]{4,3,2,1,0:T(8,128)(2,1)}, u32[]{:S(2)}, u32[]{:S(2)}) collective-permute-start(s16[2,2,3,64,1024]{4,3,2,1,0:T(8,128)(2,1)} %get-tuple-element.55), channel_id=1, source_target_pairs={{0,4},{4,0},{8,12},{12,8},{16,20},{20,16},{24,28},{28,24},{1,5},{5... | collective-permute-start | bytes 4718600 | tf_op jit(solution)/shard_map/ppermute | solution.py:402
  15.3 8.1 %collective-permute-start = (s16[2,2,3,64,1024]{4,3,2,1,0:T(8,128)(2,1)}, s16[2,2,3,64,1024]{4,3,2,1,0:T(8,128)(2,1)}, u32[]{:S(2)}, u32[]{:S(2)}) collective-permute-start(s16[2,2,3,64,1024]{4,3,2,1,0:T(8,128)(2,1)} %get-tuple-element.53), channel_id=1, source_target_pairs={{0,4},{4,0},{8,12},{12,8},{16,20},{20,16},{24,28},{28,24},{1,5},{5... | collective-permute-start | bytes 4718600 | tf_op jit(solution)/shard_map/ppermute | solution.py:402
  15.4 15.4 %collective-permute-start.2 = (f32[3,16,2,1024]{3,2,1,0:T(2,128)}, f32[3,16,2,1024]{3,2,1,0:T(2,128)S(1)}, u32[]{:S(2)}, u32[]{:S(2)}) collective-permute-start(f32[3,16,2,1024]{3,2,1,0:T(2,128)} %get-tuple-element.57), channel_id=1, source_target_pairs={{0,1},{1,2},{2,3},{3,0},{4,5},{5,6},{6,7},{7,4},{8,9},{9,10},{10,1... | collective-permute-start | bytes 1179656 | tf_op jit(solution)/shard_map/ppermute | solution.py:398
  18.4 19.5 %collective-permute-start.3 = (f32[3,16,2,1024]{3,2,1,0:T(2,128)}, f32[3,16,2,1024]{3,2,1,0:T(2,128)}, u32[]{:S(2)}, u32[]{:S(2)}) collective-permute-start(f32[3,16,2,1024]{3,2,1,0:T(2,128)} %get-tuple-element.58), channel_id=1, source_target_pairs={{1,0},{2,1},{3,2},{0,3},{5,4},{6,5},{7,6},{4,7},{9,8},{10,9},{11,1... | collective-permute-start | bytes 1179656 | tf_op jit(solution)/shard_map/ppermute | solution.py:398
  23.4 6.2 %copy-start.11 = (f32[64]{0:T(128)S(1)}, f32[64]{0:T(128)}, u32[]{:S(2)}) copy-start(f32[64]{0:T(128)} %param.22) | copy-start | bytes 772
  25.7 27.1 %collective-permute-start.4 = (s16[3,64,1024]{2,1,0:T(8,128)(2,1)}, s16[3,64,1024]{2,1,0:T(8,128)(2,1)}, u32[]{:S(2)}, u32[]{:S(2)}) collective-permute-start(s16[3,64,1024]{2,1,0:T(8,128)(2,1)} %get-tuple-element.60), channel_id=1, source_target_pairs={{0,16},{4,20},{8,24},{12,28},{16,0},{20,4},{24,8},{28,12},{1,17},{... | collective-permute-start | bytes 1179656 | tf_op jit(solution)/shard_map/ppermute | solution.py:402
  27.4 25.3 %collective-permute-start.5 = (s16[3,64,1024]{2,1,0:T(8,128)(2,1)}, s16[3,64,1024]{2,1,0:T(8,128)(2,1)}, u32[]{:S(2)}, u32[]{:S(2)}) collective-permute-start(s16[3,64,1024]{2,1,0:T(8,128)(2,1)} %get-tuple-element.61), channel_id=1, source_target_pairs={{0,8},{4,12},{8,0},{12,4},{16,24},{20,28},{24,16},{28,20},{1,9},{5... | collective-permute-start | bytes 1179656 | tf_op jit(solution)/shard_map/ppermute | solution.py:402
  30.2 28.4 %collective-permute-start.6 = (s16[3,64,1024]{2,1,0:T(8,128)(2,1)}, s16[3,64,1024]{2,1,0:T(8,128)(2,1)}, u32[]{:S(2)}, u32[]{:S(2)}) collective-permute-start(s16[3,64,1024]{2,1,0:T(8,128)(2,1)} %get-tuple-element.64), channel_id=1, source_target_pairs={{0,16},{4,20},{8,24},{12,28},{16,0},{20,4},{24,8},{28,12},{1,17},{... | collective-permute-start | bytes 1179656 | tf_op jit(solution)/shard_map/ppermute | solution.py:402
  30.7 7.2 %copy-start.5 = (f32[3,16,2,1024]{3,2,1,0:T(2,128)}, f32[3,16,2,1024]{3,2,1,0:T(2,128)S(1)}, u32[]{:S(2)}) copy-start(f32[3,16,2,1024]{3,2,1,0:T(2,128)S(1)} %collective-permute-done.2.before) | copy-start | bytes 1179652
  30.7 27.9 %collective-permute-start.7 = (s16[3,64,1024]{2,1,0:T(8,128)(2,1)}, s16[3,64,1024]{2,1,0:T(8,128)(2,1)}, u32[]{:S(2)}, u32[]{:S(2)}) collective-permute-start(s16[3,64,1024]{2,1,0:T(8,128)(2,1)} %get-tuple-element.65), channel_id=1, source_target_pairs={{0,8},{4,12},{8,0},{12,4},{16,24},{20,28},{24,16},{28,20},{1,9},{5... | collective-permute-start | bytes 1179656 | tf_op jit(solution)/shard_map/ppermute | solution.py:402
  55.6 21.7 %collective-permute-start.9 = (s16[3,64,1024]{2,1,0:T(8,128)(2,1)}, s16[3,64,1024]{2,1,0:T(8,128)(2,1)}, u32[]{:S(2)}, u32[]{:S(2)}) collective-permute-start(s16[3,64,1024]{2,1,0:T(8,128)(2,1)} %get-tuple-element.70), channel_id=1, source_target_pairs={{0,8},{4,12},{8,0},{12,4},{16,24},{20,28},{24,16},{28,20},{1,9},{5... | collective-permute-start | bytes 1179656 | tf_op jit(solution)/shard_map/ppermute | solution.py:402
  56.8 21.6 %collective-permute-start.8 = (s16[3,64,1024]{2,1,0:T(8,128)(2,1)}, s16[3,64,1024]{2,1,0:T(8,128)(2,1)}, u32[]{:S(2)}, u32[]{:S(2)}) collective-permute-start(s16[3,64,1024]{2,1,0:T(8,128)(2,1)} %get-tuple-element.69), channel_id=1, source_target_pairs={{0,16},{4,20},{8,24},{12,28},{16,0},{20,4},{24,8},{28,12},{1,17},{... | collective-permute-start | bytes 1179656 | tf_op jit(solution)/shard_map/ppermute | solution.py:402
  61.4 37.1 %collective-permute-start.10 = (s16[3,64,1024]{2,1,0:T(8,128)(2,1)}, s16[3,64,1024]{2,1,0:T(8,128)(2,1)S(1)}, u32[]{:S(2)}, u32[]{:S(2)}) collective-permute-start(s16[3,64,1024]{2,1,0:T(8,128)(2,1)} %get-tuple-element.74), channel_id=1, source_target_pairs={{0,16},{4,20},{8,24},{12,28},{16,0},{20,4},{24,8},{28,12},{1,17},{... | collective-permute-start | bytes 1179656 | tf_op jit(solution)/shard_map/ppermute | solution.py:402
  61.6 35.9 %collective-permute-start.11 = (s16[3,64,1024]{2,1,0:T(8,128)(2,1)}, s16[3,64,1024]{2,1,0:T(8,128)(2,1)S(1)}, u32[]{:S(2)}, u32[]{:S(2)}) collective-permute-start(s16[3,64,1024]{2,1,0:T(8,128)(2,1)} %get-tuple-element.75), channel_id=1, source_target_pairs={{0,8},{4,12},{8,0},{12,4},{16,24},{20,28},{24,16},{28,20},{1,9},{5... | collective-permute-start | bytes 1179656 | tf_op jit(solution)/shard_map/ppermute | solution.py:402
  62.4 14.9 %copy-start.4 = (s16[3,64,1024]{2,1,0:T(8,128)(2,1)S(1)}, s16[3,64,1024]{2,1,0:T(8,128)(2,1)}, u32[]{:S(2)}) copy-start(s16[3,64,1024]{2,1,0:T(8,128)(2,1)} %get-tuple-element.104) | copy-start | bytes 1179652
  79.6 22.4 %collective-permute-start.12 = (s16[3,64,1024]{2,1,0:T(8,128)(2,1)S(1)}, s16[3,64,1024]{2,1,0:T(8,128)(2,1)S(1)}, u32[]{:S(2)}, u32[]{:S(2)}) collective-permute-start(s16[3,64,1024]{2,1,0:T(8,128)(2,1)S(1)} %broadcast_select_fusion.4), channel_id=1, source_target_pairs={{0,8},{4,12},{8,0},{12,4},{16,24},{20,28},{24,16},{28,20},{1,9},{5... | collective-permute-start | bytes 1179656 | tf_op jit(solution)/shard_map/ppermute | solution.py:402
  79.7 20.8 %collective-permute-start.13 = (s16[3,64,1024]{2,1,0:T(8,128)(2,1)S(1)}, s16[3,64,1024]{2,1,0:T(8,128)(2,1)}, u32[]{:S(2)}, u32[]{:S(2)}) collective-permute-start(s16[3,64,1024]{2,1,0:T(8,128)(2,1)S(1)} %broadcast_select_fusion.3), channel_id=1, source_target_pairs={{0,16},{4,20},{8,24},{12,28},{16,0},{20,4},{24,8},{28,12},{1,17},{... | collective-permute-start | bytes 1179656 | tf_op jit(solution)/shard_map/ppermute | solution.py:402
  98.5 12.8 %copy-start.10 = (s16[3,64,1024]{2,1,0:T(8,128)(2,1)}, s16[3,64,1024]{2,1,0:T(8,128)(2,1)S(1)}, u32[]{:S(2)}) copy-start(s16[3,64,1024]{2,1,0:T(8,128)(2,1)S(1)} %collective-permute-done.10) | copy-start | bytes 1179652
  99.4 15.6 %collective-permute-start.17 = (s16[3,64,1024]{2,1,0:T(8,128)(2,1)}, s16[3,64,1024]{2,1,0:T(8,128)(2,1)}, u32[]{:S(2)}, u32[]{:S(2)}) collective-permute-start(s16[3,64,1024]{2,1,0:T(8,128)(2,1)} %broadcast_select_fusion.2), channel_id=1, source_target_pairs={{0,8},{4,12},{8,0},{12,4},{16,24},{20,28},{24,16},{28,20},{1,9},{5... | collective-permute-start | bytes 1179656 | tf_op jit(solution)/shard_map/ppermute | solution.py:402
  99.7 16.9 %collective-permute-start.18 = (s16[3,64,1024]{2,1,0:T(8,128)(2,1)}, s16[3,64,1024]{2,1,0:T(8,128)(2,1)}, u32[]{:S(2)}, u32[]{:S(2)}) collective-permute-start(s16[3,64,1024]{2,1,0:T(8,128)(2,1)} %broadcast_select_fusion.1), channel_id=1, source_target_pairs={{0,16},{4,20},{8,24},{12,28},{16,0},{20,4},{24,8},{28,12},{1,17},{... | collective-permute-start | bytes 1179656 | tf_op jit(solution)/shard_map/ppermute | solution.py:402
  103.5 9.5 %collective-permute-start.15 = (s16[2,3,16,1024]{3,2,1,0:T(8,128)(2,1)S(1)}, s16[2,3,16,1024]{3,2,1,0:T(8,128)(2,1)}, u32[]{:S(2)}, u32[]{:S(2)}) collective-permute-start(s16[2,3,16,1024]{3,2,1,0:T(8,128)(2,1)S(1)} %fusion.10), channel_id=1, source_target_pairs={{0,1},{1,2},{2,3},{3,0},{8,9},{9,10},{10,11},{11,8},{16,17},{17,18... | collective-permute-start | bytes 589832 | tf_op jit(solution)/shard_map/ppermute | solution.py:461
  106.5 8.5 %collective-permute-start.16 = (s16[2,3,16,1024]{3,2,1,0:T(8,128)(2,1)S(1)}, s16[2,3,16,1024]{3,2,1,0:T(8,128)(2,1)}, u32[]{:S(2)}, u32[]{:S(2)}) collective-permute-start(s16[2,3,16,1024]{3,2,1,0:T(8,128)(2,1)S(1)} %fusion.11), channel_id=1, source_target_pairs={{1,0},{2,1},{3,2},{0,3},{9,8},{10,9},{11,10},{8,11},{17,16},{18,17... | collective-permute-start | bytes 589832 | tf_op jit(solution)/shard_map/ppermute | solution.py:462
  111.3 3.7 %copy-start.7 = (s16[3,64,1024]{2,1,0:T(8,128)(2,1)S(1)}, s16[3,64,1024]{2,1,0:T(8,128)(2,1)}, u32[]{:S(2)}) copy-start(s16[3,64,1024]{2,1,0:T(8,128)(2,1)} %get-tuple-element.65) | copy-start | bytes 1179652
  111.5 6.5 %copy-start.2 = (s16[2,2,3,64,1024]{4,3,2,1,0:T(8,128)(2,1)}, s16[2,2,3,64,1024]{4,3,2,1,0:T(8,128)(2,1)S(1)}, u32[]{:S(2)}) copy-start(s16[2,2,3,64,1024]{4,3,2,1,0:T(8,128)(2,1)S(1)} %pad_add_fusion.held0) | copy-start | bytes 4718596
  111.6 5.1 %copy-start.6 = (s16[3,64,1024]{2,1,0:T(8,128)(2,1)S(1)}, s16[3,64,1024]{2,1,0:T(8,128)(2,1)}, u32[]{:S(2)}) copy-start(s16[3,64,1024]{2,1,0:T(8,128)(2,1)} %get-tuple-element.64) | copy-start | bytes 1179652
  111.6 5.1 %copy-start.9 = (s16[3,64,1024]{2,1,0:T(8,128)(2,1)S(1)}, s16[3,64,1024]{2,1,0:T(8,128)(2,1)}, u32[]{:S(2)}) copy-start(s16[3,64,1024]{2,1,0:T(8,128)(2,1)} %copy-done.8) | copy-start | bytes 1179652
  111.6 13.1 %collective-permute-start.14 = (s16[2,2,3,64,1024]{4,3,2,1,0:T(8,128)(2,1)S(1)}, s16[2,2,3,64,1024]{4,3,2,1,0:T(8,128)(2,1)}, u32[]{:S(2)}, u32[]{:S(2)}) collective-permute-start(s16[2,2,3,64,1024]{4,3,2,1,0:T(8,128)(2,1)S(1)} %pad_add_fusion.held0), channel_id=1, source_target_pairs={{0,4},{4,0},{8,12},{12,8},{16,20},{20,16},{24,28},{28,24},{1,5},{5... | collective-permute-start | bytes 4718600 | tf_op jit(solution)/shard_map/ppermute | solution.py:402
  118.5 6.2 %copy-start.3 = (s16[2,2,3,64,1024]{4,3,2,1,0:T(8,128)(2,1)}, s16[2,2,3,64,1024]{4,3,2,1,0:T(8,128)(2,1)S(1)}, u32[]{:S(2)}) copy-start(s16[2,2,3,64,1024]{4,3,2,1,0:T(8,128)(2,1)S(1)} %pad_add_fusion.1.held1) | copy-start | bytes 4718596
  118.5 6.2 %collective-permute-start.19 = (s16[2,2,3,64,1024]{4,3,2,1,0:T(8,128)(2,1)S(1)}, s16[2,2,3,64,1024]{4,3,2,1,0:T(8,128)(2,1)}, u32[]{:S(2)}, u32[]{:S(2)}) collective-permute-start(s16[2,2,3,64,1024]{4,3,2,1,0:T(8,128)(2,1)S(1)} %pad_add_fusion.1.held1), channel_id=1, source_target_pairs={{0,4},{4,0},{8,12},{12,8},{16,20},{20,16},{24,28},{28,24},{1,5},{5... | collective-permute-start | bytes 4718600 | tf_op jit(solution)/shard_map/ppermute | solution.py:402
  120.1 2.6 %collective-permute-start.20 = (s16[2,2,3,16,1024]{4,3,2,1,0:T(8,128)(2,1)S(1)}, s16[2,2,3,16,1024]{4,3,2,1,0:T(8,128)(2,1)}, u32[]{:S(2)}, u32[]{:S(2)}) collective-permute-start(s16[2,2,3,16,1024]{4,3,2,1,0:T(8,128)(2,1)S(1)} %pad_add_fusion.4), channel_id=1, source_target_pairs={{0,4},{4,0},{8,12},{12,8},{16,20},{20,16},{24,28},{28,24},{1,5},{5... | collective-permute-start | bytes 1179656 | tf_op jit(solution)/shard_map/ppermute | solution.py:402
  (1 other events, 2.9 us)

commit v7 on v6

--- a/solution.py
+++ b/solution.py
@@ -141,9 +141,15 @@
 
 
 def field_kernel(
-    c, viscosity, turn, m_all, m_top, before, after, field, inner, depth, along, across, sums, token,
-    columns, high_s, low_s, high_x, low_x, arrived,
+    c, viscosity, turn, m_all, m_top, before, after, field, *refs
 ):
+    outs, token, terms = refs[:5], refs[5], refs[6:11]
+    columns, high_s, low_s, high_x, low_x, arrived, left = refs[11:]
+    inner, depth, along, across, sums = terms
+
+    def send(n, p):
+        return pltpu.make_async_copy(terms[n].at[0, p], outs[n].at[0, p], left.at[n, p])
+
     slab, width = inner.shape[2:]
     planes = field.shape[1] // slab
     tiles = width // lanes
@@ -176,10 +182,13 @@
 
         lax.fori_loop(0, slab // 8, unpack, 0, unroll=4)
 
+    for p in range(2):
+        send(0, p).start()
+        send(1, p).start()
     rows = m_top.shape[0] // 2
     for p in range(2):
         for start, rim in ((0, before), (reach + slab, after)):
-            high, low = split(rim[0, :, p])
+            high, low = split(rim[c, :, p])
             high_x[start : start + reach, :] = high
             low_x[start : start + reach, :] = low
 
@@ -203,6 +212,7 @@
             along[0, p, at, :] = one[:rows] + one[2 * rows :] + two[:rows]
             curve = (gain / 180.0) * (one[rows : 2 * rows] + two[rows:])
             sums[0, p, at, :] = sums[0, p, at, :] + curve
+        send(2, p).start()
         for t in range(tiles):
             side = pl.ds(t * lanes, lanes)
             window = pl.ds(t * lanes, 2 * lanes)
@@ -210,7 +220,12 @@
             across[0, p, :, side] = both[:, :lanes] * (1.0 / 60.0)
             curve = both[:, lanes:] * (gain / 180.0)
             sums[0, p, :, side] = sums[0, p, :, side] + curve
+        send(3, p).start()
+        send(4, p).start()
     token[...] = jnp.zeros_like(token)
+    for n in range(5):
+        for p in range(2):
+            send(n, p).wait()
 
 
 def field_terms(c, field, before, after, viscosity, length):
@@ -220,33 +235,27 @@
     high, low, second = along_matrices(rows, length)
     top = np.concatenate([high, second], 0)
     everything = np.concatenate([high, second, low], 0)
-    rim = pl.BlockSpec((1, reach, 2, width), lambda i: (c, 0, 0, 0))
     turn = across_matrix([first_at(0), [t for t in second_at(0) if t[0] != 0]])
     shape = jax.ShapeDtypeStruct((1, 2, slab, width), jnp.float32)
-    spec = pl.BlockSpec((1, 2, slab, width), lambda i: (0, 0, 0, 0))
-    mark = pl.BlockSpec((8, lanes), lambda i: (0, 0))
+    spec = pl.BlockSpec(memory_space=pltpu.HBM)
+    near = pl.BlockSpec(memory_space=pltpu.VMEM)
     return pl.pallas_call(
         functools.partial(field_kernel, c),
         out_shape=(shape,) * 5 + (jax.ShapeDtypeStruct((8, lanes), jnp.int32),),
-        grid=(1,),
-        in_specs=[
-            pl.BlockSpec(memory_space=pltpu.SMEM),
-            pl.BlockSpec(turn.shape, lambda i: (0, 0)),
-            pl.BlockSpec(everything.shape, lambda i: (0, 0)),
-            pl.BlockSpec(top.shape, lambda i: (0, 0)),
-            rim,
-            rim,
-            pl.BlockSpec(memory_space=pl.ANY),
-        ],
-        out_specs=(spec,) * 5 + (mark,),
+        in_specs=[pl.BlockSpec(memory_space=pltpu.SMEM)]
+        + [near] * 5
+        + [pl.BlockSpec(memory_space=pl.ANY)],
+        out_specs=(spec,) * 5 + (near,),
         compiler_params=grant(57),
-        scratch_shapes=[
+        scratch_shapes=[pltpu.VMEM((1, 2, slab, width), jnp.float32)] * 5
+        + [
             pltpu.VMEM((width // lanes, slab * planes, lanes), jnp.float32),
             pltpu.VMEM((slab, width + lanes), jnp.bfloat16),
             pltpu.VMEM((slab, width + lanes), jnp.bfloat16),
             pltpu.VMEM((slab + 2 * reach, width), jnp.bfloat16),
             pltpu.VMEM((slab + 2 * reach, width), jnp.bfloat16),
             pltpu.SemaphoreType.DMA((width // lanes,)),
+            pltpu.SemaphoreType.DMA((5, 2)),
         ],
         cost_estimate=pl.CostEstimate(
             flops=0, bytes_accessed=4 * slab * planes * width * 2, transcendentals=0

time: 149 us -> 148 us (level)
  transfers between devices with their start and end apart: 21 -> 21, of which waited for: 4 -> 4; matrix products, arithmetic and copies ran while one was open for 19% -> 19% of each run, Pallas kernels for 29% -> 28%
where the time goes in v7:
time: 148 us; the launch traced here: 147 us
  Pallas kernels  69.1 us (47%)
  starting transfers between devices  26.7 us (18%)
  other arithmetic  24 us (16%)
  local copies, waits for them, and re-layouts  12.4 us (8%)
  waiting for transfers between devices  11.5 us (8%)
  between operations  3.74 us (3%)
    pallas_call x3, Pallas kernels, field_terms(): pl.pallas_call(functools.partial(field_kernel, c), out_shape=(shape,) * 5...  38.2 us
    pallas_call x1, Pallas kernels, final(): pl.pallas_call(final_kernel, out_shape=jax.ShapeDtypeStruct((1, comps, sl...  23.8 us
    ppermute x17, starting transfers between devices, swap(): lax.ppermute(array, 'pert', [(i, i ^ bit) for i in range(lax.axis_size('p...  14 us
    pallas_call x2, Pallas kernels, pack(): pl.pallas_call(pack_kernel, out_shape=(shape,) * 2, grid=(2, comps), in_s...  7.07 us
    another operation x6, other arithmetic, exchange(): parts.append(jnp.stack(row, 0))  5.74 us
    ppermute x2, waiting for transfers between devices, ring(): return (lax.ppermute(last, 'gx', up), lax.ppermute(first, 'gx', down))  5.58 us
    ppermute x2, starting transfers between devices, ring(): return (lax.ppermute(last, 'gx', up), lax.ppermute(first, 'gx', down))  5.06 us
    select_n x3, other arithmetic, exchange(): two = jnp.where(at_a, two, X[u][s - 1])  4.83 us
  transfers between devices with their start and end apart: 21, of which 4 were waited for; matrix products, arithmetic and copies ran while one was open for 19% of the time, Pallas kernels for 28%

profile of v7, /device:TPU:0, one launch (start us, length us, event | category | flops | bytes accessed | tf_op | source)
XLA Modules:
  0.0 147.3 jit_solution(3034845843551572886)
XLA Ops:
  0.0 3.2 %fusion.17 = (f32[3,16,2,1024]{3,2,1,0:T(2,128)}, f32[3,16,2,1024]{3,2,1,0:T(2,128)}) fusion(f32[3,256,8,1024]{3,2,1,0:T(8,128)} %bitcast.70), kind=kLoop, calls=%fused_computation.52 | loop fusion | bytes 1572864 | tf_op jit(solution)/shard_map/slice | solution.py:495
  3.2 4.6 %copy-done = bf16[1,3,256,8,1024]{4,3,2,1,0:T(8,128)(2,1)S(1)} copy-done((bf16[1,3,256,8,1024]{4,3,2,1,0:T(8,128)(2,1)S(1)}, bf16[1,3,256,8,1024]{4,3,2,1,0:T(8,128)(2,1)}, u32[]{:S(2)}) %copy-start) | copy-done | bytes 12582936
  7.8 3.6 %shard_map.173 = (s16[2,2,3,64,1024]{4,3,2,1,0:T(8,128)(2,1)S(1)}, s16[2,2,3,64,1024]{4,3,2,1,0:T(8,128)(2,1)}) custom-call(s32[1]{0:T(128)} %bitcast.core, bf16[128,256]{1,0:T(8,128)(2,1)S(1)} %copy-done.1, bf16[3,2048,1024]{2,1,0:T(8,128)(2,1)S(1)} %bitcast.68), custom_call_target="tpu_custom_call" | custom-call | bytes 12582912 | tf_op jit(solution)/shard_map/pallas_call | solution.py:124
  11.8 3.5 %shard_map.172 = (s16[2,2,3,64,1024]{4,3,2,1,0:T(8,128)(2,1)S(1)}, s16[2,2,3,64,1024]{4,3,2,1,0:T(8,128)(2,1)}) custom-call(s32[1]{0:T(128)} %bitcast.core, bf16[128,256]{1,0:T(8,128)(2,1)S(1)} %copy-done.1, bf16[3,2048,1024]{2,1,0:T(8,128)(2,1)S(1)} %bitcast.69), custom_call_target="tpu_custom_call" | custom-call | bytes 12582912 | tf_op jit(solution)/shard_map/pallas_call | solution.py:124
  15.4 3.0 %collective-permute-start.2 = (f32[3,16,2,1024]{3,2,1,0:T(2,128)}, f32[3,16,2,1024]{3,2,1,0:T(2,128)S(1)}, u32[]{:S(2)}, u32[]{:S(2)}) collective-permute-start(f32[3,16,2,1024]{3,2,1,0:T(2,128)} %get-tuple-element.57), channel_id=1, source_target_pairs={{0,1},{1,2},{2,3},{3,0},{4,5},{5,6},{6,7},{7,4},{8,9},{9,10},{10,1... | collective-permute-start | bytes 1179656 | tf_op jit(solution)/shard_map/ppermute | solution.py:407
  18.4 2.0 %collective-permute-start.3 = (f32[3,16,2,1024]{3,2,1,0:T(2,128)}, f32[3,16,2,1024]{3,2,1,0:T(2,128)}, u32[]{:S(2)}, u32[]{:S(2)}) collective-permute-start(f32[3,16,2,1024]{3,2,1,0:T(2,128)} %get-tuple-element.58), channel_id=1, source_target_pairs={{1,0},{2,1},{3,2},{0,3},{5,4},{6,5},{7,6},{4,7},{9,8},{10,9},{11,1... | collective-permute-start | bytes 1179656 | tf_op jit(solution)/shard_map/ppermute | solution.py:407
  21.1 2.3 %fusion.6 = (s16[3,64,1024]{2,1,0:T(8,128)(2,1)}, s16[3,64,1024]{2,1,0:T(8,128)(2,1)}) fusion(s16[2,2,3,64,1024]{4,3,2,1,0:T(8,128)(2,1)} %collective-permute-done.1, s16[2,2,3,64,1024]{4,3,2,1,0:T(8,128)(2,1)S(1)} %get-tuple-element.54, pred[]{:T(512)S(6)} %eq.44), kind=kLoop, calls=%fused_computation.21 | loop fusion | flops 393216 | bytes 2359297 | tf_op jit(solution)/shard_map/jit(_where)/select_n | solution.py:422
  23.4 2.3 %fusion.8 = (s16[3,64,1024]{2,1,0:T(8,128)(2,1)}, s16[3,64,1024]{2,1,0:T(8,128)(2,1)}) fusion(s16[2,2,3,64,1024]{4,3,2,1,0:T(8,128)(2,1)} %collective-permute-done, s16[2,2,3,64,1024]{4,3,2,1,0:T(8,128)(2,1)S(1)} %get-tuple-element.52, pred[]{:T(512)S(6)} %eq.44), kind=kLoop, calls=%fused_computation.25 | loop fusion | flops 393216 | bytes 2359297 | tf_op jit(solution)/shard_map/jit(_where)/select_n | solution.py:422
  25.7 1.7 %collective-permute-start.4 = (s16[3,64,1024]{2,1,0:T(8,128)(2,1)}, s16[3,64,1024]{2,1,0:T(8,128)(2,1)}, u32[]{:S(2)}, u32[]{:S(2)}) collective-permute-start(s16[3,64,1024]{2,1,0:T(8,128)(2,1)} %get-tuple-element.60), channel_id=1, source_target_pairs={{0,16},{4,20},{8,24},{12,28},{16,0},{20,4},{24,8},{28,12},{1,17},{... | collective-permute-start | bytes 1179656 | tf_op jit(solution)/shard_map/ppermute | solution.py:411
  27.4 1.5 %collective-permute-start.5 = (s16[3,64,1024]{2,1,0:T(8,128)(2,1)}, s16[3,64,1024]{2,1,0:T(8,128)(2,1)}, u32[]{:S(2)}, u32[]{:S(2)}) collective-permute-start(s16[3,64,1024]{2,1,0:T(8,128)(2,1)} %get-tuple-element.61), channel_id=1, source_target_pairs={{0,8},{4,12},{8,0},{12,4},{16,24},{20,28},{24,16},{28,20},{1,9},{5... | collective-permute-start | bytes 1179656 | tf_op jit(solution)/shard_map/ppermute | solution.py:411
  30.7 1.6 %collective-permute-start.7 = (s16[3,64,1024]{2,1,0:T(8,128)(2,1)}, s16[3,64,1024]{2,1,0:T(8,128)(2,1)}, u32[]{:S(2)}, u32[]{:S(2)}) collective-permute-start(s16[3,64,1024]{2,1,0:T(8,128)(2,1)} %get-tuple-element.65), channel_id=1, source_target_pairs={{0,8},{4,12},{8,0},{12,4},{16,24},{20,28},{24,16},{28,20},{1,9},{5... | collective-permute-start | bytes 1179656 | tf_op jit(solution)/shard_map/ppermute | solution.py:411
  32.3 5.6 %collective-permute-done.3.after = f32[3,16,2,1024]{3,2,1,0:T(2,128)} collective-permute-done((f32[3,16,2,1024]{3,2,1,0:T(2,128)}, f32[3,16,2,1024]{3,2,1,0:T(2,128)}, u32[]{:S(2)}, u32[]{:S(2)}) %collective-permute-start.3) | collective-permute-done | bytes 393248 | tf_op jit(solution)/shard_map/ppermute | solution.py:407
  37.9 12.7 %shard_map.174 = (f32[1,2,256,1024]{3,2,1,0:T(8,128)}, f32[1,2,256,1024]{3,2,1,0:T(8,128)}, f32[1,2,256,1024]{3,2,1,0:T(8,128)}, f32[1,2,256,1024]{3,2,1,0:T(8,1...) custom-call(f32[1]{0:T(128)} %bitcast.9.viscosity, bf16[256,256]{1,0:T(8,128)(2,1)} %constant.62.clone.turn, ...), custom_call_target="tpu_custom_call" | custom-call | bytes 16777216 | tf_op jit(solution)/shard_map/pallas_call | solution.py:242
  52.5 2.8 %broadcast_select_fusion.8 = (s16[3,64,1024]{2,1,0:T(8,128)(2,1)}, s16[3,64,1024]{2,1,0:T(8,128)(2,1)}, s16[3,64,1024]{2,1,0:T(8,128)(2,1)}, s16[3,64,1024]{2,1,0:T(8,128)(2,1)S(1)}) fusion(s16[3,64,1024]{2,1,0:T(8,128)(2,1)} %collective-permute-done.4, pred[]{:T(512)S(6)} %eq.47, s16[2,2,3,64,1024]{4,3,2,1,0:T(8,128)(2,1)} %collective-permute-done, ...), kind=kLoop, calls=%fused_computation.45 | loop fusion | flops 786432 | bytes 3932162 | tf_op jit(solution)/shard_map/jit(_where)/select_n | solution.py:439
  55.2 1.5 %collective-permute-start.9 = (s16[3,64,1024]{2,1,0:T(8,128)(2,1)}, s16[3,64,1024]{2,1,0:T(8,128)(2,1)}, u32[]{:S(2)}, u32[]{:S(2)}) collective-permute-start(s16[3,64,1024]{2,1,0:T(8,128)(2,1)} %get-tuple-element.70), channel_id=1, source_target_pairs={{0,8},{4,12},{8,0},{12,4},{16,24},{20,28},{24,16},{28,20},{1,9},{5... | collective-permute-start | bytes 1179656 | tf_op jit(solution)/shard_map/ppermute | solution.py:411
  56.7 1.3 collective-permute-start.8
  58.0 2.8 %broadcast_select_fusion.5 = (s16[3,64,1024]{2,1,0:T(8,128)(2,1)}, s16[3,64,1024]{2,1,0:T(8,128)(2,1)S(1)}, s16[3,64,1024]{2,1,0:T(8,128)(2,1)}, s16[3,64,1024]{2,1,0:T(8,128)(2,1)S(1)}) fusion(s16[3,64,1024]{2,1,0:T(8,128)(2,1)} %collective-permute-done.7, pred[]{:T(512)S(6)} %eq.48, s16[2,2,3,64,1024]{4,3,2,1,0:T(8,128)(2,1)} %collective-permute-done.1, ...), kind=kLoop, calls=%fused_computation.42 | loop fusion | flops 786432 | bytes 3932162 | tf_op jit(solution)/shard_map/jit(_where)/select_n | solution.py:440
  61.9 12.7 %shard_map.175 = (f32[1,2,256,1024]{3,2,1,0:T(8,128)}, f32[1,2,256,1024]{3,2,1,0:T(8,128)}, f32[1,2,256,1024]{3,2,1,0:T(8,128)}, f32[1,2,256,1024]{3,2,1,0:T(8,1...) custom-call(f32[1]{0:T(128)} %bitcast.9.viscosity, bf16[256,256]{1,0:T(8,128)(2,1)} %constant.62.clone.turn, ...), custom_call_target="tpu_custom_call" | custom-call | bytes 16777216 | tf_op jit(solution)/shard_map/pallas_call | solution.py:242
  78.8 1.8 %collective-permute-start.12 = (s16[3,64,1024]{2,1,0:T(8,128)(2,1)S(1)}, s16[3,64,1024]{2,1,0:T(8,128)(2,1)S(1)}, u32[]{:S(2)}, u32[]{:S(2)}) collective-permute-start(s16[3,64,1024]{2,1,0:T(8,128)(2,1)S(1)} %broadcast_select_fusion.4), channel_id=1, source_target_pairs={{0,8},{4,12},{8,0},{12,4},{16,24},{20,28},{24,16},{28,20},{1,9},{5... | collective-permute-start | bytes 1179656 | tf_op jit(solution)/shard_map/ppermute | solution.py:411
  80.7 12.8 %shard_map.176 = (f32[1,2,256,1024]{3,2,1,0:T(8,128)}, f32[1,2,256,1024]{3,2,1,0:T(8,128)}, f32[1,2,256,1024]{3,2,1,0:T(8,128)}, f32[1,2,256,1024]{3,2,1,0:T(8,1...) custom-call(f32[1]{0:T(128)} %bitcast.9.viscosity, bf16[256,256]{1,0:T(8,128)(2,1)} %constant.62.clone.turn, ...), custom_call_target="tpu_custom_call" | custom-call | bytes 16777216 | tf_op jit(solution)/shard_map/pallas_call | solution.py:242
  97.2 1.9 %collective-permute-start.17 = (s16[3,64,1024]{2,1,0:T(8,128)(2,1)}, s16[3,64,1024]{2,1,0:T(8,128)(2,1)}, u32[]{:S(2)}, u32[]{:S(2)}) collective-permute-start(s16[3,64,1024]{2,1,0:T(8,128)(2,1)} %broadcast_select_fusion.2), channel_id=1, source_target_pairs={{0,8},{4,12},{8,0},{12,4},{16,24},{20,28},{24,16},{28,20},{1,9},{5... | collective-permute-start | bytes 1179656 | tf_op jit(solution)/shard_map/ppermute | solution.py:411
  99.4 1.5 %select_bitcast_fusion.6 = (s16[1,3,64,1024]{3,2,1,0:T(8,128)(2,1)S(1)}, s16[1,3,64,1024]{3,2,1,0:T(8,128)(2,1)S(1)}) fusion(s16[3,64,1024]{2,1,0:T(8,128)(2,1)} %get-tuple-element.60, s16[3,64,1024]{2,1,0:T(8,128)(2,1)} %collective-permute-done.4, s16[3,64,1024]{2,1,0:T(8,128)(2,1)} %collective-permute-done.13, ...), kind=kLoop, calls=%fused_computation.35 | loop fusion | flops 983040 | bytes 2752515 | tf_op jit(solution)/shard_map/stack | solution.py:459
  100.9 1.4 select_bitcast_fusion.7
  102.3 3.0 %collective-permute-start.15 = (s16[2,3,16,1024]{3,2,1,0:T(8,128)(2,1)S(1)}, s16[2,3,16,1024]{3,2,1,0:T(8,128)(2,1)}, u32[]{:S(2)}, u32[]{:S(2)}) collective-permute-start(s16[2,3,16,1024]{3,2,1,0:T(8,128)(2,1)S(1)} %fusion.10), channel_id=1, source_target_pairs={{0,1},{1,2},{2,3},{3,0},{8,9},{9,10},{10,11},{11,8},{16,17},{17,18... | collective-permute-start | bytes 589832 | tf_op jit(solution)/shard_map/ppermute | solution.py:470
  105.4 4.6 %collective-permute-start.16 = (s16[2,3,16,1024]{3,2,1,0:T(8,128)(2,1)S(1)}, s16[2,3,16,1024]{3,2,1,0:T(8,128)(2,1)}, u32[]{:S(2)}, u32[]{:S(2)}) collective-permute-start(s16[2,3,16,1024]{3,2,1,0:T(8,128)(2,1)S(1)} %fusion.11), channel_id=1, source_target_pairs={{1,0},{2,1},{3,2},{0,3},{9,8},{10,9},{11,10},{8,11},{17,16},{18,17... | collective-permute-start | bytes 589832 | tf_op jit(solution)/shard_map/ppermute | solution.py:471
  110.5 1.4 collective-permute-done.15
  111.9 2.0 %collective-permute-done.16 = s16[2,3,16,1024]{3,2,1,0:T(8,128)(2,1)} collective-permute-done((s16[2,3,16,1024]{3,2,1,0:T(8,128)(2,1)S(1)}, s16[2,3,16,1024]{3,2,1,0:T(8,128)(2,1)}, u32[]{:S(2)}, u32[]{:S(2)}) %collective-permute-start.16) | collective-permute-done | bytes 196640 | tf_op jit(solution)/shard_map/ppermute | solution.py:471
  113.9 1.5 %select_bitcast_fusion.3 = (s16[1,3,64,1024]{3,2,1,0:T(8,128)(2,1)S(1)}, s16[1,3,64,1024]{3,2,1,0:T(8,128)(2,1)S(1)}) fusion(s16[3,64,1024]{2,1,0:T(8,128)(2,1)S(1)} %copy-done.7, s16[3,64,1024]{2,1,0:T(8,128)(2,1)} %collective-permute-done.7, s16[3,64,1024]{2,1,0:T(8,128)(2,1)} %collective-permute-done.17, s16[3,64,1024]{2,1,0:T(8,128)(2,1)} %copy-done.10, ...), kind=kLoop, calls=%fused_computation.32 | loop fusion | flops 983040 | bytes 2752515 | tf_op jit(solution)/shard_map/stack | solution.py:459
  115.4 1.4 select_bitcast_fusion.2
  117.3 1.5 %pad_add_fusion.4 = s16[2,2,3,16,1024]{4,3,2,1,0:T(8,128)(2,1)S(1)} fusion(s16[1,2,3,16,1024]{4,3,2,1,0:T(8,128)(2,1)} %bitcast.33, s16[1,2,3,16,1024]{4,3,2,1,0:T(8,128)(2,1)} %bitcast.32), kind=kLoop, calls=%fused_computation.28 | loop fusion | flops 196608 | bytes 786432 | tf_op jit(solution)/shard_map/stack | solution.py:472
  118.9 2.5 %collective-permute-done.20 = s16[2,2,3,16,1024]{4,3,2,1,0:T(8,128)(2,1)} collective-permute-done((s16[2,2,3,16,1024]{4,3,2,1,0:T(8,128)(2,1)S(1)}, s16[2,2,3,16,1024]{4,3,2,1,0:T(8,128)(2,1)}, u32[]{:S(2)}, u32[]{:S(2)}) %collective-permute-start.20) | collective-permute-done | bytes 393248 | tf_op jit(solution)/shard_map/ppermute | solution.py:411
  123.3 23.8 %shard_map.177 = f32[1,3,256,2,1024]{4,3,2,1,0:T(2,128)} custom-call(s32[1]{0:T(128)} %bitcast.core, bf16[64,64]{1,0:T(8,128)(2,1)} %constant.65.clone.m_both, bf16[256,128]{1,0:T(8,128)(2,1)} %constant.66.clone.turn, s16[2,2,3,64,1024]{4,3,2,1,0:T(8,128)(2,1)} %copy-done.2, s16[2,2,3,64,1024]{4,3,2,1,0:T(8,128)(2,1)} %collective-permute-done.14.other0, ...), custom_call_target="tpu_custom_call" | custom-call | bytes 12582912 | tf_op jit(solution)/shard_map/pallas_call | solution.py:374
  (66 shorter events, 13.8 us)
Async XLA Ops:
  3.2 4.6 %copy-start = (bf16[1,3,256,8,1024]{4,3,2,1,0:T(8,128)(2,1)S(1)}, bf16[1,3,256,8,1024]{4,3,2,1,0:T(8,128)(2,1)}, u32[]{:S(2)}) copy-start(bf16[1,3,256,8,1024]{4,3,2,1,0:T(8,128)(2,1)} %param.19) | copy-start | bytes 37748740
  11.4 9.7 %collective-permute-start.1 = (s16[2,2,3,64,1024]{4,3,2,1,0:T(8,128)(2,1)}, s16[2,2,3,64,1024]{4,3,2,1,0:T(8,128)(2,1)}, u32[]{:S(2)}, u32[]{:S(2)}) collective-permute-start(s16[2,2,3,64,1024]{4,3,2,1,0:T(8,128)(2,1)} %get-tuple-element.55), channel_id=1, source_target_pairs={{0,4},{4,0},{8,12},{12,8},{16,20},{20,16},{24,28},{28,24},{1,5},{5... | collective-permute-start | bytes 4718600 | tf_op jit(solution)/shard_map/ppermute | solution.py:411
  15.3 8.1 %collective-permute-start = (s16[2,2,3,64,1024]{4,3,2,1,0:T(8,128)(2,1)}, s16[2,2,3,64,1024]{4,3,2,1,0:T(8,128)(2,1)}, u32[]{:S(2)}, u32[]{:S(2)}) collective-permute-start(s16[2,2,3,64,1024]{4,3,2,1,0:T(8,128)(2,1)} %get-tuple-element.53), channel_id=1, source_target_pairs={{0,4},{4,0},{8,12},{12,8},{16,20},{20,16},{24,28},{28,24},{1,5},{5... | collective-permute-start | bytes 4718600 | tf_op jit(solution)/shard_map/ppermute | solution.py:411
  15.4 15.4 %collective-permute-start.2 = (f32[3,16,2,1024]{3,2,1,0:T(2,128)}, f32[3,16,2,1024]{3,2,1,0:T(2,128)S(1)}, u32[]{:S(2)}, u32[]{:S(2)}) collective-permute-start(f32[3,16,2,1024]{3,2,1,0:T(2,128)} %get-tuple-element.57), channel_id=1, source_target_pairs={{0,1},{1,2},{2,3},{3,0},{4,5},{5,6},{6,7},{7,4},{8,9},{9,10},{10,1... | collective-permute-start | bytes 1179656 | tf_op jit(solution)/shard_map/ppermute | solution.py:407
  18.4 19.5 %collective-permute-start.3 = (f32[3,16,2,1024]{3,2,1,0:T(2,128)}, f32[3,16,2,1024]{3,2,1,0:T(2,128)}, u32[]{:S(2)}, u32[]{:S(2)}) collective-permute-start(f32[3,16,2,1024]{3,2,1,0:T(2,128)} %get-tuple-element.58), channel_id=1, source_target_pairs={{1,0},{2,1},{3,2},{0,3},{5,4},{6,5},{7,6},{4,7},{9,8},{10,9},{11,1... | collective-permute-start | bytes 1179656 | tf_op jit(solution)/shard_map/ppermute | solution.py:407
  23.4 6.2 %copy-start.11 = (f32[64]{0:T(128)S(1)}, f32[64]{0:T(128)}, u32[]{:S(2)}) copy-start(f32[64]{0:T(128)} %param.22) | copy-start | bytes 772
  25.7 26.7 %collective-permute-start.4 = (s16[3,64,1024]{2,1,0:T(8,128)(2,1)}, s16[3,64,1024]{2,1,0:T(8,128)(2,1)}, u32[]{:S(2)}, u32[]{:S(2)}) collective-permute-start(s16[3,64,1024]{2,1,0:T(8,128)(2,1)} %get-tuple-element.60), channel_id=1, source_target_pairs={{0,16},{4,20},{8,24},{12,28},{16,0},{20,4},{24,8},{28,12},{1,17},{... | collective-permute-start | bytes 1179656 | tf_op jit(solution)/shard_map/ppermute | solution.py:411
  27.4 25.0 %collective-permute-start.5 = (s16[3,64,1024]{2,1,0:T(8,128)(2,1)}, s16[3,64,1024]{2,1,0:T(8,128)(2,1)}, u32[]{:S(2)}, u32[]{:S(2)}) collective-permute-start(s16[3,64,1024]{2,1,0:T(8,128)(2,1)} %get-tuple-element.61), channel_id=1, source_target_pairs={{0,8},{4,12},{8,0},{12,4},{16,24},{20,28},{24,16},{28,20},{1,9},{5... | collective-permute-start | bytes 1179656 | tf_op jit(solution)/shard_map/ppermute | solution.py:411
  30.2 27.8 %collective-permute-start.6 = (s16[3,64,1024]{2,1,0:T(8,128)(2,1)}, s16[3,64,1024]{2,1,0:T(8,128)(2,1)}, u32[]{:S(2)}, u32[]{:S(2)}) collective-permute-start(s16[3,64,1024]{2,1,0:T(8,128)(2,1)} %get-tuple-element.64), channel_id=1, source_target_pairs={{0,16},{4,20},{8,24},{12,28},{16,0},{20,4},{24,8},{28,12},{1,17},{... | collective-permute-start | bytes 1179656 | tf_op jit(solution)/shard_map/ppermute | solution.py:411
  30.7 7.2 %copy-start.5 = (f32[3,16,2,1024]{3,2,1,0:T(2,128)}, f32[3,16,2,1024]{3,2,1,0:T(2,128)S(1)}, u32[]{:S(2)}) copy-start(f32[3,16,2,1024]{3,2,1,0:T(2,128)S(1)} %collective-permute-done.2.before) | copy-start | bytes 1179652
  30.7 27.3 %collective-permute-start.7 = (s16[3,64,1024]{2,1,0:T(8,128)(2,1)}, s16[3,64,1024]{2,1,0:T(8,128)(2,1)}, u32[]{:S(2)}, u32[]{:S(2)}) collective-permute-start(s16[3,64,1024]{2,1,0:T(8,128)(2,1)} %get-tuple-element.65), channel_id=1, source_target_pairs={{0,8},{4,12},{8,0},{12,4},{16,24},{20,28},{24,16},{28,20},{1,9},{5... | collective-permute-start | bytes 1179656 | tf_op jit(solution)/shard_map/ppermute | solution.py:411
  55.2 21.2 %collective-permute-start.9 = (s16[3,64,1024]{2,1,0:T(8,128)(2,1)}, s16[3,64,1024]{2,1,0:T(8,128)(2,1)}, u32[]{:S(2)}, u32[]{:S(2)}) collective-permute-start(s16[3,64,1024]{2,1,0:T(8,128)(2,1)} %get-tuple-element.70), channel_id=1, source_target_pairs={{0,8},{4,12},{8,0},{12,4},{16,24},{20,28},{24,16},{28,20},{1,9},{5... | collective-permute-start | bytes 1179656 | tf_op jit(solution)/shard_map/ppermute | solution.py:411
  56.7 20.9 %collective-permute-start.8 = (s16[3,64,1024]{2,1,0:T(8,128)(2,1)}, s16[3,64,1024]{2,1,0:T(8,128)(2,1)}, u32[]{:S(2)}, u32[]{:S(2)}) collective-permute-start(s16[3,64,1024]{2,1,0:T(8,128)(2,1)} %get-tuple-element.69), channel_id=1, source_target_pairs={{0,16},{4,20},{8,24},{12,28},{16,0},{20,4},{24,8},{28,12},{1,17},{... | collective-permute-start | bytes 1179656 | tf_op jit(solution)/shard_map/ppermute | solution.py:411
  60.8 35.5 %collective-permute-start.10 = (s16[3,64,1024]{2,1,0:T(8,128)(2,1)}, s16[3,64,1024]{2,1,0:T(8,128)(2,1)S(1)}, u32[]{:S(2)}, u32[]{:S(2)}) collective-permute-start(s16[3,64,1024]{2,1,0:T(8,128)(2,1)} %get-tuple-element.74), channel_id=1, source_target_pairs={{0,16},{4,20},{8,24},{12,28},{16,0},{20,4},{24,8},{28,12},{1,17},{... | collective-permute-start | bytes 1179656 | tf_op jit(solution)/shard_map/ppermute | solution.py:411
  61.5 33.8 %collective-permute-start.11 = (s16[3,64,1024]{2,1,0:T(8,128)(2,1)}, s16[3,64,1024]{2,1,0:T(8,128)(2,1)S(1)}, u32[]{:S(2)}, u32[]{:S(2)}) collective-permute-start(s16[3,64,1024]{2,1,0:T(8,128)(2,1)} %get-tuple-element.75), channel_id=1, source_target_pairs={{0,8},{4,12},{8,0},{12,4},{16,24},{20,28},{24,16},{28,20},{1,9},{5... | collective-permute-start | bytes 1179656 | tf_op jit(solution)/shard_map/ppermute | solution.py:411
  61.8 14.6 %copy-start.4 = (s16[3,64,1024]{2,1,0:T(8,128)(2,1)S(1)}, s16[3,64,1024]{2,1,0:T(8,128)(2,1)}, u32[]{:S(2)}) copy-start(s16[3,64,1024]{2,1,0:T(8,128)(2,1)} %get-tuple-element.104) | copy-start | bytes 1179652
  78.8 22.1 %collective-permute-start.12 = (s16[3,64,1024]{2,1,0:T(8,128)(2,1)S(1)}, s16[3,64,1024]{2,1,0:T(8,128)(2,1)S(1)}, u32[]{:S(2)}, u32[]{:S(2)}) collective-permute-start(s16[3,64,1024]{2,1,0:T(8,128)(2,1)S(1)} %broadcast_select_fusion.4), channel_id=1, source_target_pairs={{0,8},{4,12},{8,0},{12,4},{16,24},{20,28},{24,16},{28,20},{1,9},{5... | collective-permute-start | bytes 1179656 | tf_op jit(solution)/shard_map/ppermute | solution.py:411
  80.6 18.9 %collective-permute-start.13 = (s16[3,64,1024]{2,1,0:T(8,128)(2,1)S(1)}, s16[3,64,1024]{2,1,0:T(8,128)(2,1)}, u32[]{:S(2)}, u32[]{:S(2)}) collective-permute-start(s16[3,64,1024]{2,1,0:T(8,128)(2,1)S(1)} %broadcast_select_fusion.3), channel_id=1, source_target_pairs={{0,16},{4,20},{8,24},{12,28},{16,0},{20,4},{24,8},{28,12},{1,17},{... | collective-permute-start | bytes 1179656 | tf_op jit(solution)/shard_map/ppermute | solution.py:411
  95.4 4.0 %copy-start.8 = (s16[3,64,1024]{2,1,0:T(8,128)(2,1)}, s16[3,64,1024]{2,1,0:T(8,128)(2,1)S(1)}, u32[]{:S(2)}) copy-start(s16[3,64,1024]{2,1,0:T(8,128)(2,1)S(1)} %collective-permute-done.11) | copy-start | bytes 1179652
  96.3 13.9 %copy-start.10 = (s16[3,64,1024]{2,1,0:T(8,128)(2,1)}, s16[3,64,1024]{2,1,0:T(8,128)(2,1)S(1)}, u32[]{:S(2)}) copy-start(s16[3,64,1024]{2,1,0:T(8,128)(2,1)S(1)} %collective-permute-done.10) | copy-start | bytes 1179652
  97.2 16.7 %collective-permute-start.17 = (s16[3,64,1024]{2,1,0:T(8,128)(2,1)}, s16[3,64,1024]{2,1,0:T(8,128)(2,1)}, u32[]{:S(2)}, u32[]{:S(2)}) collective-permute-start(s16[3,64,1024]{2,1,0:T(8,128)(2,1)} %broadcast_select_fusion.2), channel_id=1, source_target_pairs={{0,8},{4,12},{8,0},{12,4},{16,24},{20,28},{24,16},{28,20},{1,9},{5... | collective-permute-start | bytes 1179656 | tf_op jit(solution)/shard_map/ppermute | solution.py:411
  99.1 16.2 %collective-permute-start.18 = (s16[3,64,1024]{2,1,0:T(8,128)(2,1)}, s16[3,64,1024]{2,1,0:T(8,128)(2,1)}, u32[]{:S(2)}, u32[]{:S(2)}) collective-permute-start(s16[3,64,1024]{2,1,0:T(8,128)(2,1)} %broadcast_select_fusion.1), channel_id=1, source_target_pairs={{0,16},{4,20},{8,24},{12,28},{16,0},{20,4},{24,8},{28,12},{1,17},{... | collective-permute-start | bytes 1179656 | tf_op jit(solution)/shard_map/ppermute | solution.py:411
  102.3 9.5 %collective-permute-start.15 = (s16[2,3,16,1024]{3,2,1,0:T(8,128)(2,1)S(1)}, s16[2,3,16,1024]{3,2,1,0:T(8,128)(2,1)}, u32[]{:S(2)}, u32[]{:S(2)}) collective-permute-start(s16[2,3,16,1024]{3,2,1,0:T(8,128)(2,1)S(1)} %fusion.10), channel_id=1, source_target_pairs={{0,1},{1,2},{2,3},{3,0},{8,9},{9,10},{10,11},{11,8},{16,17},{17,18... | collective-permute-start | bytes 589832 | tf_op jit(solution)/shard_map/ppermute | solution.py:470
  105.4 8.5 %collective-permute-start.16 = (s16[2,3,16,1024]{3,2,1,0:T(8,128)(2,1)S(1)}, s16[2,3,16,1024]{3,2,1,0:T(8,128)(2,1)}, u32[]{:S(2)}, u32[]{:S(2)}) collective-permute-start(s16[2,3,16,1024]{3,2,1,0:T(8,128)(2,1)S(1)} %fusion.11), channel_id=1, source_target_pairs={{1,0},{2,1},{3,2},{0,3},{9,8},{10,9},{11,10},{8,11},{17,16},{18,17... | collective-permute-start | bytes 589832 | tf_op jit(solution)/shard_map/ppermute | solution.py:471
  110.2 3.7 %copy-start.7 = (s16[3,64,1024]{2,1,0:T(8,128)(2,1)S(1)}, s16[3,64,1024]{2,1,0:T(8,128)(2,1)}, u32[]{:S(2)}) copy-start(s16[3,64,1024]{2,1,0:T(8,128)(2,1)} %get-tuple-element.65) | copy-start | bytes 1179652
  110.4 6.4 %copy-start.2 = (s16[2,2,3,64,1024]{4,3,2,1,0:T(8,128)(2,1)}, s16[2,2,3,64,1024]{4,3,2,1,0:T(8,128)(2,1)S(1)}, u32[]{:S(2)}) copy-start(s16[2,2,3,64,1024]{4,3,2,1,0:T(8,128)(2,1)S(1)} %pad_add_fusion.held0) | copy-start | bytes 4718596
  110.4 5.0 %copy-start.6 = (s16[3,64,1024]{2,1,0:T(8,128)(2,1)S(1)}, s16[3,64,1024]{2,1,0:T(8,128)(2,1)}, u32[]{:S(2)}) copy-start(s16[3,64,1024]{2,1,0:T(8,128)(2,1)} %get-tuple-element.64) | copy-start | bytes 1179652
  110.4 5.0 %copy-start.9 = (s16[3,64,1024]{2,1,0:T(8,128)(2,1)S(1)}, s16[3,64,1024]{2,1,0:T(8,128)(2,1)}, u32[]{:S(2)}) copy-start(s16[3,64,1024]{2,1,0:T(8,128)(2,1)} %copy-done.8) | copy-start | bytes 1179652
  110.4 12.9 %collective-permute-start.14 = (s16[2,2,3,64,1024]{4,3,2,1,0:T(8,128)(2,1)S(1)}, s16[2,2,3,64,1024]{4,3,2,1,0:T(8,128)(2,1)}, u32[]{:S(2)}, u32[]{:S(2)}) collective-permute-start(s16[2,2,3,64,1024]{4,3,2,1,0:T(8,128)(2,1)S(1)} %pad_add_fusion.held0), channel_id=1, source_target_pairs={{0,4},{4,0},{8,12},{12,8},{16,20},{20,16},{24,28},{28,24},{1,5},{5... | collective-permute-start | bytes 4718600 | tf_op jit(solution)/shard_map/ppermute | solution.py:411
  117.2 6.2 %copy-start.3 = (s16[2,2,3,64,1024]{4,3,2,1,0:T(8,128)(2,1)}, s16[2,2,3,64,1024]{4,3,2,1,0:T(8,128)(2,1)S(1)}, u32[]{:S(2)}) copy-start(s16[2,2,3,64,1024]{4,3,2,1,0:T(8,128)(2,1)S(1)} %pad_add_fusion.1.held1) | copy-start | bytes 4718596
  117.2 6.2 %collective-permute-start.19 = (s16[2,2,3,64,1024]{4,3,2,1,0:T(8,128)(2,1)S(1)}, s16[2,2,3,64,1024]{4,3,2,1,0:T(8,128)(2,1)}, u32[]{:S(2)}, u32[]{:S(2)}) collective-permute-start(s16[2,2,3,64,1024]{4,3,2,1,0:T(8,128)(2,1)S(1)} %pad_add_fusion.1.held1), channel_id=1, source_target_pairs={{0,4},{4,0},{8,12},{12,8},{16,20},{20,16},{24,28},{28,24},{1,5},{5... | collective-permute-start | bytes 4718600 | tf_op jit(solution)/shard_map/ppermute | solution.py:411
  118.8 2.6 %collective-permute-start.20 = (s16[2,2,3,16,1024]{4,3,2,1,0:T(8,128)(2,1)S(1)}, s16[2,2,3,16,1024]{4,3,2,1,0:T(8,128)(2,1)}, u32[]{:S(2)}, u32[]{:S(2)}) collective-permute-start(s16[2,2,3,16,1024]{4,3,2,1,0:T(8,128)(2,1)S(1)} %pad_add_fusion.4), channel_id=1, source_target_pairs={{0,4},{4,0},{8,12},{12,8},{16,20},{20,16},{24,28},{28,24},{1,5},{5... | collective-permute-start | bytes 1179656 | tf_op jit(solution)/shard_map/ppermute | solution.py:411
  (1 other events, 3.2 us)

commit v8 on v7

--- a/solution.py
+++ b/solution.py
@@ -14,7 +14,7 @@
 code_scale = 4096.0
 phases = 2
 streams = ((0, 3), (1, 2))
-shares = {(0, 1): 0, (1, 1): 1, (2, 0): 2}
+shares = {(0, 1): ((0, 1), 44), (1, 1): ((2,), 52)}
 
 
 def grant(mib):
@@ -140,113 +140,114 @@
     )(core, jnp.asarray(weights), tile)
 
 
-def field_kernel(
-    c, viscosity, turn, m_all, m_top, before, after, field, *refs
-):
-    outs, token, terms = refs[:5], refs[5], refs[6:11]
-    columns, high_s, low_s, high_x, low_x, arrived, left = refs[11:]
+def field_kernel(comps, viscosity, turn, m_all, m_top, before, after, field, out, token, *scratch):
+    terms = scratch[:5]
+    columns, high_s, low_s, high_x, low_x, arrived, left = scratch[5:]
     inner, depth, along, across, sums = terms
 
-    def send(n, p):
-        return pltpu.make_async_copy(terms[n].at[0, p], outs[n].at[0, p], left.at[n, p])
+    def send(i, n, p):
+        return pltpu.make_async_copy(terms[n].at[0, p], out.at[i, n, p], left.at[n, p])
 
     slab, width = inner.shape[2:]
     planes = field.shape[1] // slab
     tiles = width // lanes
     gain = viscosity[0] * section_step
 
-    def fetch(t):
+    def fetch(c, t):
         source = field.at[c, :, pl.ds(t * lanes, lanes)]
         return pltpu.make_async_copy(source, columns.at[t], arrived.at[t])
 
     for t in range(tiles):
-        fetch(t).start()
-    for t in range(tiles):
-        fetch(t).wait()
-
-        def unpack(i, carry):
-            start = pl.multiple_of(i * 8, 8)
-            plane = [columns[t, pl.ds(start * planes + z, 8, planes), :] for z in range(planes)]
-            at = (pl.ds(start, 8), pl.ds(t * lanes, lanes))
+        fetch(comps[0], t).start()
+    for i, c in enumerate(comps):
+        for t in range(tiles):
+            fetch(c, t).wait()
+
+            def unpack(r, carry):
+                start = pl.multiple_of(r * 8, 8)
+                plane = [columns[t, pl.ds(start * planes + z, 8, planes), :] for z in range(planes)]
+                at = (pl.ds(start, 8), pl.ds(t * lanes, lanes))
+                for p in range(2):
+                    z = 3 + p
+                    centre = plane[z]
+                    u1, u2, u3 = plane[z + 1], plane[z + 2], plane[z + 3]
+                    d1, d2, d3 = plane[z - 1], plane[z - 2], plane[z - 3]
+                    slope = 0.75 * (u1 - d1) - 0.15 * (u2 - d2) + (1.0 / 60.0) * (u3 - d3)
+                    curve = 1.5 * (u1 + d1) - 0.15 * (u2 + d2) + (1.0 / 90.0) * (u3 + d3)
+                    inner[(0, p) + at] = centre
+                    depth[(0, p) + at] = slope
+                    sums[(0, p) + at] = centre + gain * (curve - (49.0 / 18.0) * centre)
+                return carry
+
+            lax.fori_loop(0, slab // 8, unpack, 0, unroll=4)
+            if i + 1 < len(comps):
+                fetch(comps[i + 1], t).start()
+
+        for p in range(2):
+            send(i, 0, p).start()
+            send(i, 1, p).start()
+        rows = m_top.shape[0] // 2
+        for p in range(2):
+            for start, rim in ((0, before), (reach + slab, after)):
+                high, low = split(rim[c, :, p])
+                high_x[start : start + reach, :] = high
+                low_x[start : start + reach, :] = low
+
+            def fill(r, carry):
+                start = pl.multiple_of(r * 16, 16)
+                at = pl.ds(start, 16)
+                to = pl.ds(pl.multiple_of(start + reach, 16), 16)
+                high, low = split(inner[0, p, at, :])
+                high_x[to, :] = high
+                low_x[to, :] = low
+                high_s[at, :] = half_turned(high)
+                low_s[at, :] = half_turned(low)
+                return carry
+
+            lax.fori_loop(0, slab // 16, fill, 0, unroll=8)
+            for b in range(slab // rows):
+                window = pl.ds(b * rows, rows + 2 * reach)
+                at = pl.ds(b * rows, rows)
+                one = product(m_all[...], high_x[window, :])
+                two = product(m_top[...], low_x[window, :])
+                along[0, p, at, :] = one[:rows] + one[2 * rows :] + two[:rows]
+                curve = (gain / 180.0) * (one[rows : 2 * rows] + two[rows:])
+                sums[0, p, at, :] = sums[0, p, at, :] + curve
+            send(i, 2, p).start()
+            for t in range(tiles):
+                side = pl.ds(t * lanes, lanes)
+                window = pl.ds(t * lanes, 2 * lanes)
+                both = product(high_s[:, window], turn[...]) + product(low_s[:, window], turn[...])
+                across[0, p, :, side] = both[:, :lanes] * (1.0 / 60.0)
+                curve = both[:, lanes:] * (gain / 180.0)
+                sums[0, p, :, side] = sums[0, p, :, side] + curve
+            send(i, 3, p).start()
+            send(i, 4, p).start()
+        for n in range(5):
             for p in range(2):
-                z = 3 + p
-                centre = plane[z]
-                u1, u2, u3 = plane[z + 1], plane[z + 2], plane[z + 3]
-                d1, d2, d3 = plane[z - 1], plane[z - 2], plane[z - 3]
-                slope = 0.75 * (u1 - d1) - 0.15 * (u2 - d2) + (1.0 / 60.0) * (u3 - d3)
-                curve = 1.5 * (u1 + d1) - 0.15 * (u2 + d2) + (1.0 / 90.0) * (u3 + d3)
-                inner[(0, p) + at] = centre
-                depth[(0, p) + at] = slope
-                sums[(0, p) + at] = centre + gain * (curve - (49.0 / 18.0) * centre)
-            return carry
-
-        lax.fori_loop(0, slab // 8, unpack, 0, unroll=4)
-
-    for p in range(2):
-        send(0, p).start()
-        send(1, p).start()
-    rows = m_top.shape[0] // 2
-    for p in range(2):
-        for start, rim in ((0, before), (reach + slab, after)):
-            high, low = split(rim[c, :, p])
-            high_x[start : start + reach, :] = high
-            low_x[start : start + reach, :] = low
-
-        def fill(i, carry):
-            start = pl.multiple_of(i * 16, 16)
-            at = pl.ds(start, 16)
-            to = pl.ds(pl.multiple_of(start + reach, 16), 16)
-            high, low = split(inner[0, p, at, :])
-            high_x[to, :] = high
-            low_x[to, :] = low
-            high_s[at, :] = half_turned(high)
-            low_s[at, :] = half_turned(low)
-            return carry
-
-        lax.fori_loop(0, slab // 16, fill, 0, unroll=2)
-        for b in range(slab // rows):
-            window = pl.ds(b * rows, rows + 2 * reach)
-            at = pl.ds(b * rows, rows)
-            one = product(m_all[...], high_x[window, :])
-            two = product(m_top[...], low_x[window, :])
-            along[0, p, at, :] = one[:rows] + one[2 * rows :] + two[:rows]
-            curve = (gain / 180.0) * (one[rows : 2 * rows] + two[rows:])
-            sums[0, p, at, :] = sums[0, p, at, :] + curve
-        send(2, p).start()
-        for t in range(tiles):
-            side = pl.ds(t * lanes, lanes)
-            window = pl.ds(t * lanes, 2 * lanes)
-            both = product(high_s[:, window], turn[...]) + product(low_s[:, window], turn[...])
-            across[0, p, :, side] = both[:, :lanes] * (1.0 / 60.0)
-            curve = both[:, lanes:] * (gain / 180.0)
-            sums[0, p, :, side] = sums[0, p, :, side] + curve
-        send(3, p).start()
-        send(4, p).start()
-    token[...] = jnp.zeros_like(token)
-    for n in range(5):
-        for p in range(2):
-            send(n, p).wait()
-
-
-def field_terms(c, field, before, after, viscosity, length):
-    comps, slab, planes, width = field.shape
-    flat = field.reshape(comps, slab * planes, width)
+                send(i, n, p).wait()
+    token[0] = 0
+
+
+def field_terms(comps, room, field, before, after, viscosity, length):
+    _, slab, planes, width = field.shape
+    flat = field.reshape(-1, slab * planes, width)
     rows = min(slab, 128)
     high, low, second = along_matrices(rows, length)
     top = np.concatenate([high, second], 0)
     everything = np.concatenate([high, second, low], 0)
     turn = across_matrix([first_at(0), [t for t in second_at(0) if t[0] != 0]])
-    shape = jax.ShapeDtypeStruct((1, 2, slab, width), jnp.float32)
+    shape = jax.ShapeDtypeStruct((len(comps), 5, 2, slab, width), jnp.float32)
     spec = pl.BlockSpec(memory_space=pltpu.HBM)
     near = pl.BlockSpec(memory_space=pltpu.VMEM)
     return pl.pallas_call(
-        functools.partial(field_kernel, c),
-        out_shape=(shape,) * 5 + (jax.ShapeDtypeStruct((8, lanes), jnp.int32),),
+        functools.partial(field_kernel, comps),
+        out_shape=(shape, jax.ShapeDtypeStruct((1,), jnp.int32)),
         in_specs=[pl.BlockSpec(memory_space=pltpu.SMEM)]
         + [near] * 5
         + [pl.BlockSpec(memory_space=pl.ANY)],
-        out_specs=(spec,) * 5 + (near,),
-        compiler_params=grant(57),
+        out_specs=(spec, pl.BlockSpec(memory_space=pltpu.SMEM)),
+        compiler_params=grant(room),
         scratch_shapes=[pltpu.VMEM((1, 2, slab, width), jnp.float32)] * 5
         + [
             pltpu.VMEM((width // lanes, slab * planes, lanes), jnp.float32),
@@ -258,16 +259,21 @@
             pltpu.SemaphoreType.DMA((5, 2)),
         ],
         cost_estimate=pl.CostEstimate(
-            flops=0, bytes_accessed=4 * slab * planes * width * 2, transcendentals=0
+            flops=0, bytes_accessed=4 * len(comps) * slab * planes * width * 2, transcendentals=0
         ),
     )(
         viscosity, jnp.asarray(turn), jnp.asarray(everything), jnp.asarray(top), before, after, flat
     )
 
 
-def final_kernel(core, m_both, turn, held0, other0, held1, other1, before, after, *refs):
-    terms, scratch = refs[:15], refs[15:]
-    inner, depth, along, across, sums = [terms[n::5] for n in range(5)]
+def final_kernel(
+    groups, core, m_both, turn, held0, other0, held1, other1, before, after, before2, after2, *refs
+):
+    terms, scratch = refs[: len(groups)], refs[len(groups) :]
+    kept = {c: (g, i) for g, comps in enumerate(groups) for i, c in enumerate(comps)}
+    inner, depth, along, across, sums = [
+        [terms[kept[c][0]].at[kept[c][1], n] for c in range(3)] for n in range(5)
+    ]
     out, base_s, turned_s, flow_s, ghost_s, slope_s, side_s, arrived = scratch
     step = pl.program_id(0)
     rows = slope_s.shape[2]
@@ -278,7 +284,11 @@
     def decoded(values):
         return values.astype(jnp.int32).astype(jnp.float32) * inverse
 
-    def load(flow, ghost):
+    def load(flow, ghost, before, after):
+        for c in range(3):
+            for p in range(2):
+                base_s[c, p, 0:reach] = decoded(before[p, c]).astype(jnp.bfloat16)
+                base_s[c, p, reach + slab :] = decoded(after[p, c]).astype(jnp.bfloat16)
         copies = []
         for u in range(2):
             for k in range(2):
@@ -296,18 +306,13 @@
 
     @pl.when(step == 0)
     def _():
-        for c in range(3):
-            for p in range(2):
-                base_s[c, p, 0:reach] = decoded(before[p, c]).astype(jnp.bfloat16)
-                base_s[c, p, reach + slab :] = decoded(after[p, c]).astype(jnp.bfloat16)
-
         @pl.when(core[0] == 0)
         def _():
-            load((held0, held1), (other0, other1))
+            load((held0, held1), (other0, other1), before, after)
 
         @pl.when(core[0] != 0)
         def _():
-            load((other0, other1), (held0, held1))
+            load((other0, other1), (held0, held1), before2, after2)
 
         def fill(i, carry):
             start = pl.multiple_of(i * 16, 16)
@@ -344,7 +349,7 @@
             [base_s[c, p, inside, :].astype(jnp.float32) for p in range(2)] for c in range(3)
         ]
         for p in range(2):
-            move = [inner[c][0, p, at, :] for c in range(3)]
+            move = [inner[c][p, at, :] for c in range(3)]
             for c in range(3):
                 dz = decoded(ghost_s[p, c, there, :])
                 if p == 0:
@@ -352,27 +357,30 @@
                 else:
                     dz = dz - 0.75 * flow[c][0]
                 dy = side_s[c, p, at, :] * (1.0 / 60.0)
-                total = flow[0][p] * along[c][0, p, at, :] + flow[1][p] * across[c][0, p, at, :]
-                total = total + flow[2][p] * depth[c][0, p, at, :]
+                total = flow[0][p] * along[c][p, at, :] + flow[1][p] * across[c][p, at, :]
+                total = total + flow[2][p] * depth[c][p, at, :]
                 total = total + move[0] * slope_s[c, p, at, :] + move[1] * dy + move[2] * dz
-                out[0, c, at, p, :] = sums[c][0, p, at, :] - section_step * total
+                out[0, c, at, p, :] = sums[c][p, at, :] - section_step * total
         return carry
 
     lax.fori_loop(0, rows // 16, body, 0)
 
 
-def final(core, pieces, before, after, terms, length):
-    _, pair, slab, width = terms[0].shape
-    comps = len(terms) // 5
+def final(core, pieces, rims, terms, length):
+    _, _, pair, slab, width = terms[0].shape
+    comps = sum(t.shape[0] for t in terms)
+    groups = tuple(comps_of for comps_of, _ in shares.values())
     rows = min(slab, 32)
     turn = across_matrix([first_at(0)])
     high, low, _ = along_matrices(rows, length)
     both = np.concatenate([high, low], 0)
     whole = pl.BlockSpec(memory_space=pl.ANY)
-    rim = pl.BlockSpec(before.shape, lambda i: (0, 0, 0, 0))
-    spec = pl.BlockSpec((1, pair, rows, width), lambda i: (0, 0, i, 0))
+    rim = pl.BlockSpec(rims[0].shape, lambda i: (0, 0, 0, 0))
+    specs = [
+        pl.BlockSpec((t.shape[0], 5, pair, rows, width), lambda i: (0, 0, 0, i, 0)) for t in terms
+    ]
     return pl.pallas_call(
-        final_kernel,
+        functools.partial(final_kernel, groups),
         out_shape=jax.ShapeDtypeStruct((1, comps, slab, pair, width), jnp.float32),
         grid=(slab // rows,),
         in_specs=[
@@ -381,8 +389,8 @@
             pl.BlockSpec(turn.shape, lambda i: (0, 0)),
         ]
         + [whole] * 4
-        + [rim] * 2
-        + [spec] * 15,
+        + [rim] * 4
+        + specs,
         out_specs=pl.BlockSpec((1, comps, rows, pair, width), lambda i: (0, 0, i, 0, 0)),
         compiler_params=grant(58),
         scratch_shapes=[
@@ -397,7 +405,7 @@
         cost_estimate=pl.CostEstimate(
             flops=0, bytes_accessed=8 * comps * pair * slab * width, transcendentals=0
         ),
-    )(core, jnp.asarray(both), jnp.asarray(turn), *pieces, before, after, *terms)
+    )(core, jnp.asarray(both), jnp.asarray(turn), *pieces, *rims, *terms)
 
 
 def ring(last, first):
@@ -411,7 +419,7 @@
     return lax.ppermute(array, "pert", [(i, i ^ bit) for i in range(lax.axis_size("pert"))])
 
 
-def exchange(mine, theirs, root, core, gate, work):
+def exchange(mine, theirs, root, gate, work):
     me = lax.axis_index("pert")
     is_root = me == root
     place = (me // 2) ^ (root // 2)
@@ -469,12 +477,11 @@
             both = ("pert", "gx")
             before = lax.ppermute(held[0][1][:, :, quarter - reach :], both, pairs)
             after = lax.ppermute(held[0][0][:, :, :reach], both, [(j, i) for i, j in pairs])
-            rims = jnp.stack([before, after], 0)
             before, after, place = lax.optimization_barrier((before, after, place))
+            second = [swap(before, 1), swap(after, 1)]
             at_a, at_b, at_c = place == 0, place == 1, place == 2
     other = [swap(h, 1) for h in held]
-    rims = jnp.where(core == 0, rims, swap(rims, 1))
-    return (held[0], other[0], held[1], other[1]), rims[0], rims[1]
+    return (held[0], other[0], held[1], other[1]), (before, after, *second)
 
 
 def per_device(pert_field, base_store, section_owner, pert_ids, member_visc):
@@ -502,17 +509,17 @@
         done["field"], *values = lax.optimization_barrier((done["field"], *values))
         return values
 
-    def work(c):
-        *terms, token = field_terms(c, done["field"], before, after, viscosity, length)
-        done["terms"] += terms
-        return token[0, 0]
+    def work(share):
+        terms, token = field_terms(*share, done["field"], before, after, viscosity, length)
+        done["terms"].append(terms)
+        return token[0]
 
     if in_pairs:
         mine, theirs = [h[0] for h in halves], [h[1] for h in halves]
-        pieces, base_before, base_after = exchange(mine, theirs, owner_root, core[0], gate, work)
+        pieces, rims = exchange(mine, theirs, owner_root, gate, work)
     else:
-        for c in range(comps):
-            work(c)
+        for share in shares.values():
+            work(share)
         pieces = [
             lax.psum(jnp.where(me == owner_root, a, 0).astype(jnp.float32), "pert").astype(a.dtype)
             for h in halves
@@ -520,10 +527,8 @@
         ]
         pieces = [a.transpose(1, 0, 2, 3, 4) for a in pieces]
         quarter = slab // 4
-        base_before, base_after = ring(
-            pieces[0][1][:, :, quarter - reach :], pieces[0][0][:, :, :reach]
-        )
-    return final(core, pieces, base_before, base_after, done["terms"], length)
+        rims = ring(pieces[0][1][:, :, quarter - reach :], pieces[0][0][:, :, :reach]) * 2
+    return final(core, pieces, rims, done["terms"], length)
 
 
 def solution(mesh):

time: 148 us -> 145 us (0.980)
  waiting for transfers between devices: 11.5 us -> 19.1 us
  Pallas kernels: 69.1 us -> 62.4 us
  other arithmetic: 24 us -> 21.2 us
    ppermute x17 -> x18, waiting for transfers between devices: 2.52 us -> 10.1 us  [swap(): lax.ppermute(array, 'pert', [(i, i ^ bit) for i in range(lax.axis_size('p...]
    pallas_call x4 -> x3, Pallas kernels: 62 us -> 55.3 us  [the longest x2 31.4 us: field_terms(): pl.pallas_call(functools.partial(field_kernel, comps), out_shape=(shape,...]
    unnamed x24 -> x38, local copies, waits for them, and re-layouts: 4.62 us -> 8.56 us
    slice x3 -> x0, local copies, waits for them, and re-layouts: 3.7 us -> none  [work(): return token[0, 0]]
    another operation x1 -> x0, other arithmetic: 1.52 us -> none  [exchange(): rims = jnp.stack([before, after], 0)]
    ppermute x17 -> x18, starting transfers between devices: 14 us -> 14.4 us  [swap(): lax.ppermute(array, 'pert', [(i, i ^ bit) for i in range(lax.axis_size('p...]
  transfers between devices with their start and end apart: 21 -> 22, of which waited for: 4 -> 8; matrix products, arithmetic and copies ran while one was open for 19% -> 15% of each run, Pallas kernels for 28% -> 24%
where the time goes in v8:
time: 145 us
  Pallas kernels  62.4 us (43%)
  starting transfers between devices  27.1 us (19%)
  other arithmetic  21.2 us (15%)
  waiting for transfers between devices  19.1 us (13%)
  local copies, waits for them, and re-layouts  11.8 us (8%)
  between operations  3.03 us (2%)
    pallas_call x2, Pallas kernels, field_terms(): pl.pallas_call(functools.partial(field_kernel, comps), out_shape=(shape,...  31.4 us
    pallas_call x1, Pallas kernels, final(): pl.pallas_call(functools.partial(final_kernel, groups), out_shape=jax.Sha...  24 us
    ppermute x18, starting transfers between devices, swap(): lax.ppermute(array, 'pert', [(i, i ^ bit) for i in range(lax.axis_size('p...  14.4 us
    ppermute x18, waiting for transfers between devices, swap(): lax.ppermute(array, 'pert', [(i, i ^ bit) for i in range(lax.axis_size('p...  10.1 us
    unnamed x38, local copies, waits for them, and re-layouts  8.56 us
    pallas_call x2, Pallas kernels, pack(): pl.pallas_call(pack_kernel, out_shape=(shape,) * 2, grid=(2, comps), in_s...  7.03 us
    another operation x6, other arithmetic, exchange(): parts.append(jnp.stack(row, 0))  5.74 us
    ppermute x2, waiting for transfers between devices, ring(): return (lax.ppermute(last, 'gx', up), lax.ppermute(first, 'gx', down))  5.58 us
  transfers between devices with their start and end apart: 22, of which 8 were waited for; matrix products, arithmetic and copies ran while one was open for 15% of the time, Pallas kernels for 24%

profile of v8, /device:TPU:0, one launch (start us, length us, event | category | flops | bytes accessed | tf_op | source)
XLA Modules:
  0.0 144.7 jit_solution(14692212318461682314)
XLA Ops:
  0.0 3.2 %fusion.17 = (f32[3,16,2,1024]{3,2,1,0:T(2,128)}, f32[3,16,2,1024]{3,2,1,0:T(2,128)}) fusion(f32[3,256,8,1024]{3,2,1,0:T(8,128)} %bitcast.62), kind=kLoop, calls=%fused_computation.48 | loop fusion | bytes 1572864 | tf_op jit(solution)/shard_map/slice | solution.py:502
  3.2 4.6 %copy-done = bf16[1,3,256,8,1024]{4,3,2,1,0:T(8,128)(2,1)S(1)} copy-done((bf16[1,3,256,8,1024]{4,3,2,1,0:T(8,128)(2,1)S(1)}, bf16[1,3,256,8,1024]{4,3,2,1,0:T(8,128)(2,1)}, u32[]{:S(2)}) %copy-start) | copy-done | bytes 12582936
  7.8 3.5 %shard_map.146 = (s16[2,2,3,64,1024]{4,3,2,1,0:T(8,128)(2,1)S(1)}, s16[2,2,3,64,1024]{4,3,2,1,0:T(8,128)(2,1)}) custom-call(s32[1]{0:T(128)} %bitcast.core, bf16[128,256]{1,0:T(8,128)(2,1)S(1)} %copy-done.7, bf16[3,2048,1024]{2,1,0:T(8,128)(2,1)S(1)} %bitcast.60), custom_call_target="tpu_custom_call" | custom-call | bytes 12582912 | tf_op jit(solution)/shard_map/pallas_call | solution.py:124
  11.7 3.5 %shard_map.145 = (s16[2,2,3,64,1024]{4,3,2,1,0:T(8,128)(2,1)S(1)}, s16[2,2,3,64,1024]{4,3,2,1,0:T(8,128)(2,1)}) custom-call(s32[1]{0:T(128)} %bitcast.core, bf16[128,256]{1,0:T(8,128)(2,1)S(1)} %copy-done.7, bf16[3,2048,1024]{2,1,0:T(8,128)(2,1)S(1)} %bitcast.61), custom_call_target="tpu_custom_call" | custom-call | bytes 12582912 | tf_op jit(solution)/shard_map/pallas_call | solution.py:124
  15.3 3.0 %collective-permute-start.2 = (f32[3,16,2,1024]{3,2,1,0:T(2,128)}, f32[3,16,2,1024]{3,2,1,0:T(2,128)S(1)}, u32[]{:S(2)}, u32[]{:S(2)}) collective-permute-start(f32[3,16,2,1024]{3,2,1,0:T(2,128)} %get-tuple-element.44), channel_id=1, source_target_pairs={{0,1},{1,2},{2,3},{3,0},{4,5},{5,6},{6,7},{7,4},{8,9},{9,10},{10,1... | collective-permute-start | bytes 1179656 | tf_op jit(solution)/shard_map/ppermute | solution.py:415
  18.3 2.0 %collective-permute-start.3 = (f32[3,16,2,1024]{3,2,1,0:T(2,128)}, f32[3,16,2,1024]{3,2,1,0:T(2,128)}, u32[]{:S(2)}, u32[]{:S(2)}) collective-permute-start(f32[3,16,2,1024]{3,2,1,0:T(2,128)} %get-tuple-element.45), channel_id=1, source_target_pairs={{1,0},{2,1},{3,2},{0,3},{5,4},{6,5},{7,6},{4,7},{9,8},{10,9},{11,1... | collective-permute-start | bytes 1179656 | tf_op jit(solution)/shard_map/ppermute | solution.py:415
  21.0 2.3 %fusion.6 = (s16[3,64,1024]{2,1,0:T(8,128)(2,1)}, s16[3,64,1024]{2,1,0:T(8,128)(2,1)}) fusion(s16[2,2,3,64,1024]{4,3,2,1,0:T(8,128)(2,1)} %collective-permute-done.1, s16[2,2,3,64,1024]{4,3,2,1,0:T(8,128)(2,1)S(1)} %get-tuple-element.41, pred[]{:T(512)S(6)} %eq.41), kind=kLoop, calls=%fused_computation.21 | loop fusion | flops 393216 | bytes 2359297 | tf_op jit(solution)/shard_map/jit(_where)/select_n | solution.py:430
  23.4 2.3 %fusion.8 = (s16[3,64,1024]{2,1,0:T(8,128)(2,1)}, s16[3,64,1024]{2,1,0:T(8,128)(2,1)}) fusion(s16[2,2,3,64,1024]{4,3,2,1,0:T(8,128)(2,1)} %collective-permute-done, s16[2,2,3,64,1024]{4,3,2,1,0:T(8,128)(2,1)S(1)} %get-tuple-element.39, pred[]{:T(512)S(6)} %eq.41), kind=kLoop, calls=%fused_computation.25 | loop fusion | flops 393216 | bytes 2359297 | tf_op jit(solution)/shard_map/jit(_where)/select_n | solution.py:430
  25.7 1.7 %collective-permute-start.4 = (s16[3,64,1024]{2,1,0:T(8,128)(2,1)}, s16[3,64,1024]{2,1,0:T(8,128)(2,1)}, u32[]{:S(2)}, u32[]{:S(2)}) collective-permute-start(s16[3,64,1024]{2,1,0:T(8,128)(2,1)} %get-tuple-element.47), channel_id=1, source_target_pairs={{0,16},{4,20},{8,24},{12,28},{16,0},{20,4},{24,8},{28,12},{1,17},{... | collective-permute-start | bytes 1179656 | tf_op jit(solution)/shard_map/ppermute | solution.py:419
  27.4 1.5 %collective-permute-start.5 = (s16[3,64,1024]{2,1,0:T(8,128)(2,1)}, s16[3,64,1024]{2,1,0:T(8,128)(2,1)}, u32[]{:S(2)}, u32[]{:S(2)}) collective-permute-start(s16[3,64,1024]{2,1,0:T(8,128)(2,1)} %get-tuple-element.48), channel_id=1, source_target_pairs={{0,8},{4,12},{8,0},{12,4},{16,24},{20,28},{24,16},{28,20},{1,9},{5... | collective-permute-start | bytes 1179656 | tf_op jit(solution)/shard_map/ppermute | solution.py:419
  30.7 1.5 %collective-permute-start.7 = (s16[3,64,1024]{2,1,0:T(8,128)(2,1)}, s16[3,64,1024]{2,1,0:T(8,128)(2,1)}, u32[]{:S(2)}, u32[]{:S(2)}) collective-permute-start(s16[3,64,1024]{2,1,0:T(8,128)(2,1)} %get-tuple-element.52), channel_id=1, source_target_pairs={{0,8},{4,12},{8,0},{12,4},{16,24},{20,28},{24,16},{28,20},{1,9},{5... | collective-permute-start | bytes 1179656 | tf_op jit(solution)/shard_map/ppermute | solution.py:419
  32.3 5.6 %collective-permute-done.3.after = f32[3,16,2,1024]{3,2,1,0:T(2,128)} collective-permute-done((f32[3,16,2,1024]{3,2,1,0:T(2,128)}, f32[3,16,2,1024]{3,2,1,0:T(2,128)}, u32[]{:S(2)}, u32[]{:S(2)}) %collective-permute-start.3) | collective-permute-done | bytes 393248 | tf_op jit(solution)/shard_map/ppermute | solution.py:415
  40.6 19.6 %shard_map.147 = (f32[2,5,2,256,1024]{4,3,2,1,0:T(8,128)}, s32[1]{0:T(128)}) custom-call(f32[1]{0:T(128)} %bitcast.9.viscosity, bf16[256,256]{1,0:T(8,128)(2,1)S(1)} %copy-done.5, bf16[384,160]{1,0:T(8,128)(2,1)S(1)} %copy-done.1, bf16[256,160]{1,0:T(8,128)(2,1)S(1)} %copy-done.3, f32[3,16,2,1024]{3,2,1,0:T(2,128)S(1)} %collective-permute-done.2.before, ...), custom_call_target="tpu_custom_call" | custom-call | bytes 33554432 | tf_op jit(solution)/shard_map/pallas_call | solution.py:243
  60.8 2.9 %broadcast_select_fusion.7 = (s16[3,64,1024]{2,1,0:T(8,128)(2,1)}, s16[3,64,1024]{2,1,0:T(8,128)(2,1)}, s16[3,64,1024]{2,1,0:T(8,128)(2,1)}, s16[3,64,1024]{2,1,0:T(8,128)(2,1)}) fusion(s16[3,64,1024]{2,1,0:T(8,128)(2,1)} %collective-permute-done.4, pred[]{:T(512)S(6)} %eq.44, s16[2,2,3,64,1024]{4,3,2,1,0:T(8,128)(2,1)} %collective-permute-done, ...), kind=kLoop, calls=%fused_computation.43 | loop fusion | flops 786432 | bytes 3932162 | tf_op jit(solution)/shard_map/jit(_where)/select_n | solution.py:447
  63.7 1.5 %collective-permute-start.9 = (s16[3,64,1024]{2,1,0:T(8,128)(2,1)}, s16[3,64,1024]{2,1,0:T(8,128)(2,1)S(1)}, u32[]{:S(2)}, u32[]{:S(2)}) collective-permute-start(s16[3,64,1024]{2,1,0:T(8,128)(2,1)} %get-tuple-element.57), channel_id=1, source_target_pairs={{0,8},{4,12},{8,0},{12,4},{16,24},{20,28},{24,16},{28,20},{1,9},{5... | collective-permute-start | bytes 1179656 | tf_op jit(solution)/shard_map/ppermute | solution.py:419
  65.2 1.3 collective-permute-start.8
  66.5 2.8 %broadcast_select_fusion.4 = (s16[3,64,1024]{2,1,0:T(8,128)(2,1)}, s16[3,64,1024]{2,1,0:T(8,128)(2,1)S(1)}, s16[3,64,1024]{2,1,0:T(8,128)(2,1)}, s16[3,64,1024]{2,1,0:T(8,128)(2,1)S(1)}) fusion(s16[3,64,1024]{2,1,0:T(8,128)(2,1)} %collective-permute-done.7, pred[]{:T(512)S(6)} %eq.45, s16[2,2,3,64,1024]{4,3,2,1,0:T(8,128)(2,1)} %collective-permute-done.1, ...), kind=kLoop, calls=%fused_computation.40 | loop fusion | flops 786432 | bytes 3932162 | tf_op jit(solution)/shard_map/jit(_where)/select_n | solution.py:448
  70.4 11.8 %shard_map.148 = (f32[1,5,2,256,1024]{4,3,2,1,0:T(8,128)}, s32[1]{0:T(128)}) custom-call(f32[1]{0:T(128)} %bitcast.9.viscosity, bf16[256,256]{1,0:T(8,128)(2,1)S(1)} %copy-done.6, bf16[384,160]{1,0:T(8,128)(2,1)S(1)} %copy-done.2, bf16[256,160]{1,0:T(8,128)(2,1)S(1)} %copy-done.4, f32[3,16,2,1024]{3,2,1,0:T(2,128)S(1)} %collective-permute-done.2.before, ...), custom_call_target="tpu_custom_call" | custom-call | bytes 16777216 | tf_op jit(solution)/shard_map/pallas_call | solution.py:243
  83.8 1.1 broadcast_select_fusion.3
  84.9 1.8 %collective-permute-start.12 = (s16[3,64,1024]{2,1,0:T(8,128)(2,1)S(1)}, s16[3,64,1024]{2,1,0:T(8,128)(2,1)}, u32[]{:S(2)}, u32[]{:S(2)}) collective-permute-start(s16[3,64,1024]{2,1,0:T(8,128)(2,1)S(1)} %broadcast_select_fusion.3), channel_id=1, source_target_pairs={{0,8},{4,12},{8,0},{12,4},{16,24},{20,28},{24,16},{28,20},{1,9},{5... | collective-permute-start | bytes 1179656 | tf_op jit(solution)/shard_map/ppermute | solution.py:419
  88.8 1.8 %collective-permute-start.17 = (s16[3,64,1024]{2,1,0:T(8,128)(2,1)}, s16[3,64,1024]{2,1,0:T(8,128)(2,1)}, u32[]{:S(2)}, u32[]{:S(2)}) collective-permute-start(s16[3,64,1024]{2,1,0:T(8,128)(2,1)} %broadcast_select_fusion.1), channel_id=1, source_target_pairs={{0,8},{4,12},{8,0},{12,4},{16,24},{20,28},{24,16},{28,20},{1,9},{5... | collective-permute-start | bytes 1179656 | tf_op jit(solution)/shard_map/ppermute | solution.py:419
  90.8 6.3 %collective-permute-done.12 = s16[3,64,1024]{2,1,0:T(8,128)(2,1)} collective-permute-done((s16[3,64,1024]{2,1,0:T(8,128)(2,1)S(1)}, s16[3,64,1024]{2,1,0:T(8,128)(2,1)}, u32[]{:S(2)}, u32[]{:S(2)}) %collective-permute-start.12) | collective-permute-done | bytes 393248 | tf_op jit(solution)/shard_map/ppermute | solution.py:419
  97.1 1.5 %select_bitcast_fusion.7 = (s16[1,3,64,1024]{3,2,1,0:T(8,128)(2,1)S(1)}, s16[1,3,64,1024]{3,2,1,0:T(8,128)(2,1)S(1)}) fusion(s16[3,64,1024]{2,1,0:T(8,128)(2,1)} %get-tuple-element.48, s16[3,64,1024]{2,1,0:T(8,128)(2,1)} %collective-permute-done.5, s16[3,64,1024]{2,1,0:T(8,128)(2,1)} %collective-permute-done.12, ...), kind=kLoop, calls=%fused_computation.35 | loop fusion | flops 983040 | bytes 2752515 | tf_op jit(solution)/shard_map/stack | solution.py:467
  99.1 1.4 select_bitcast_fusion.6
  100.5 3.0 %collective-permute-start.15 = (s16[2,3,16,1024]{3,2,1,0:T(8,128)(2,1)S(1)}, s16[2,3,16,1024]{3,2,1,0:T(8,128)(2,1)}, u32[]{:S(2)}, u32[]{:S(2)}) collective-permute-start(s16[2,3,16,1024]{3,2,1,0:T(8,128)(2,1)S(1)} %fusion.10), channel_id=1, source_target_pairs={{0,1},{1,2},{2,3},{3,0},{8,9},{9,10},{10,11},{11,8},{16,17},{17,18... | collective-permute-start | bytes 589832 | tf_op jit(solution)/shard_map/ppermute | solution.py:478
  103.5 4.6 %collective-permute-start.16 = (s16[2,3,16,1024]{3,2,1,0:T(8,128)(2,1)S(1)}, s16[2,3,16,1024]{3,2,1,0:T(8,128)(2,1)}, u32[]{:S(2)}, u32[]{:S(2)}) collective-permute-start(s16[2,3,16,1024]{3,2,1,0:T(8,128)(2,1)S(1)} %fusion.11), channel_id=1, source_target_pairs={{1,0},{2,1},{3,2},{0,3},{9,8},{10,9},{11,10},{8,11},{17,16},{18,17... | collective-permute-start | bytes 589832 | tf_op jit(solution)/shard_map/ppermute | solution.py:479
  108.6 1.4 collective-permute-done.15.before
  110.0 2.0 %collective-permute-done.16.after = s16[2,3,16,1024]{3,2,1,0:T(8,128)(2,1)} collective-permute-done((s16[2,3,16,1024]{3,2,1,0:T(8,128)(2,1)S(1)}, s16[2,3,16,1024]{3,2,1,0:T(8,128)(2,1)}, u32[]{:S(2)}, u32[]{:S(2)}) %collective-permute-start.16) | collective-permute-done | bytes 196640 | tf_op jit(solution)/shard_map/ppermute | solution.py:479
  112.0 1.5 %select_bitcast_fusion.2 = (s16[1,3,64,1024]{3,2,1,0:T(8,128)(2,1)S(1)}, s16[1,3,64,1024]{3,2,1,0:T(8,128)(2,1)S(1)}) fusion(s16[3,64,1024]{2,1,0:T(8,128)(2,1)S(1)} %copy-done.14, s16[3,64,1024]{2,1,0:T(8,128)(2,1)} %collective-permute-done.6, s16[3,64,1024]{2,1,0:T(8,128)(2,1)} %collective-permute-done.18, s16[3,64,1024]{2,1,0:T(8,128)(2,1)} %copy-done.15, ...), kind=kLoop, calls=%fused_computation.30 | loop fusion | flops 983040 | bytes 2752515 | tf_op jit(solution)/shard_map/stack | solution.py:467
  113.5 1.4 select_bitcast_fusion.3
  115.9 2.9 %collective-permute-done.20.before2 = s16[2,3,16,1024]{3,2,1,0:T(8,128)(2,1)S(1)} collective-permute-done((s16[2,3,16,1024]{3,2,1,0:T(8,128)(2,1)}, s16[2,3,16,1024]{3,2,1,0:T(8,128)(2,1)S(1)}, u32[]{:S(2)}, u32[]{:S(2)}) %collective-permute-start.20) | collective-permute-done | bytes 196640 | tf_op jit(solution)/shard_map/ppermute | solution.py:419
  120.5 24.0 %shard_map.149 = f32[1,3,256,2,1024]{4,3,2,1,0:T(2,128)} custom-call(s32[1]{0:T(128)} %bitcast.core, bf16[64,64]{1,0:T(8,128)(2,1)} %constant.65.clone.m_both, bf16[256,128]{1,0:T(8,128)(2,1)} %constant.66.clone.turn, s16[2,2,3,64,1024]{4,3,2,1,0:T(8,128)(2,1)} %copy-done.8, s16[2,2,3,64,1024]{4,3,2,1,0:T(8,128)(2,1)} %collective-permute-done.14.other0, ...), custom_call_target="tpu_custom_call" | custom-call | bytes 12582912 | tf_op jit(solution)/shard_map/pallas_call | solution.py:382
  (75 shorter events, 12.3 us)
Async XLA Ops:
  3.2 4.6 %copy-start = (bf16[1,3,256,8,1024]{4,3,2,1,0:T(8,128)(2,1)S(1)}, bf16[1,3,256,8,1024]{4,3,2,1,0:T(8,128)(2,1)}, u32[]{:S(2)}) copy-start(bf16[1,3,256,8,1024]{4,3,2,1,0:T(8,128)(2,1)} %param.16) | copy-start | bytes 37748740
  11.3 9.7 %collective-permute-start.1 = (s16[2,2,3,64,1024]{4,3,2,1,0:T(8,128)(2,1)}, s16[2,2,3,64,1024]{4,3,2,1,0:T(8,128)(2,1)}, u32[]{:S(2)}, u32[]{:S(2)}) collective-permute-start(s16[2,2,3,64,1024]{4,3,2,1,0:T(8,128)(2,1)} %get-tuple-element.42), channel_id=1, source_target_pairs={{0,4},{4,0},{8,12},{12,8},{16,20},{20,16},{24,28},{28,24},{1,5},{5... | collective-permute-start | bytes 4718600 | tf_op jit(solution)/shard_map/ppermute | solution.py:419
  15.2 8.1 %collective-permute-start = (s16[2,2,3,64,1024]{4,3,2,1,0:T(8,128)(2,1)}, s16[2,2,3,64,1024]{4,3,2,1,0:T(8,128)(2,1)}, u32[]{:S(2)}, u32[]{:S(2)}) collective-permute-start(s16[2,2,3,64,1024]{4,3,2,1,0:T(8,128)(2,1)} %get-tuple-element.40), channel_id=1, source_target_pairs={{0,4},{4,0},{8,12},{12,8},{16,20},{20,16},{24,28},{28,24},{1,5},{5... | collective-permute-start | bytes 4718600 | tf_op jit(solution)/shard_map/ppermute | solution.py:419
  15.3 15.4 %collective-permute-start.2 = (f32[3,16,2,1024]{3,2,1,0:T(2,128)}, f32[3,16,2,1024]{3,2,1,0:T(2,128)S(1)}, u32[]{:S(2)}, u32[]{:S(2)}) collective-permute-start(f32[3,16,2,1024]{3,2,1,0:T(2,128)} %get-tuple-element.44), channel_id=1, source_target_pairs={{0,1},{1,2},{2,3},{3,0},{4,5},{5,6},{6,7},{7,4},{8,9},{9,10},{10,1... | collective-permute-start | bytes 1179656 | tf_op jit(solution)/shard_map/ppermute | solution.py:415
  18.3 19.5 %collective-permute-start.3 = (f32[3,16,2,1024]{3,2,1,0:T(2,128)}, f32[3,16,2,1024]{3,2,1,0:T(2,128)}, u32[]{:S(2)}, u32[]{:S(2)}) collective-permute-start(f32[3,16,2,1024]{3,2,1,0:T(2,128)} %get-tuple-element.45), channel_id=1, source_target_pairs={{1,0},{2,1},{3,2},{0,3},{5,4},{6,5},{7,6},{4,7},{9,8},{10,9},{11,1... | collective-permute-start | bytes 1179656 | tf_op jit(solution)/shard_map/ppermute | solution.py:415
  23.3 6.2 %copy-start.18 = (f32[64]{0:T(128)S(1)}, f32[64]{0:T(128)}, u32[]{:S(2)}) copy-start(f32[64]{0:T(128)} %param.19) | copy-start | bytes 772
  25.7 35.1 %collective-permute-start.4 = (s16[3,64,1024]{2,1,0:T(8,128)(2,1)}, s16[3,64,1024]{2,1,0:T(8,128)(2,1)}, u32[]{:S(2)}, u32[]{:S(2)}) collective-permute-start(s16[3,64,1024]{2,1,0:T(8,128)(2,1)} %get-tuple-element.47), channel_id=1, source_target_pairs={{0,16},{4,20},{8,24},{12,28},{16,0},{20,4},{24,8},{28,12},{1,17},{... | collective-permute-start | bytes 1179656 | tf_op jit(solution)/shard_map/ppermute | solution.py:419
  27.4 33.4 %collective-permute-start.5 = (s16[3,64,1024]{2,1,0:T(8,128)(2,1)}, s16[3,64,1024]{2,1,0:T(8,128)(2,1)}, u32[]{:S(2)}, u32[]{:S(2)}) collective-permute-start(s16[3,64,1024]{2,1,0:T(8,128)(2,1)} %get-tuple-element.48), channel_id=1, source_target_pairs={{0,8},{4,12},{8,0},{12,4},{16,24},{20,28},{24,16},{28,20},{1,9},{5... | collective-permute-start | bytes 1179656 | tf_op jit(solution)/shard_map/ppermute | solution.py:419
  30.2 36.3 %collective-permute-start.6 = (s16[3,64,1024]{2,1,0:T(8,128)(2,1)}, s16[3,64,1024]{2,1,0:T(8,128)(2,1)}, u32[]{:S(2)}, u32[]{:S(2)}) collective-permute-start(s16[3,64,1024]{2,1,0:T(8,128)(2,1)} %get-tuple-element.51), channel_id=1, source_target_pairs={{0,16},{4,20},{8,24},{12,28},{16,0},{20,4},{24,8},{28,12},{1,17},{... | collective-permute-start | bytes 1179656 | tf_op jit(solution)/shard_map/ppermute | solution.py:419
  30.7 35.8 %collective-permute-start.7 = (s16[3,64,1024]{2,1,0:T(8,128)(2,1)}, s16[3,64,1024]{2,1,0:T(8,128)(2,1)}, u32[]{:S(2)}, u32[]{:S(2)}) collective-permute-start(s16[3,64,1024]{2,1,0:T(8,128)(2,1)} %get-tuple-element.52), channel_id=1, source_target_pairs={{0,8},{4,12},{8,0},{12,4},{16,24},{20,28},{24,16},{28,20},{1,9},{5... | collective-permute-start | bytes 1179656 | tf_op jit(solution)/shard_map/ppermute | solution.py:419
  63.7 19.1 %collective-permute-start.9 = (s16[3,64,1024]{2,1,0:T(8,128)(2,1)}, s16[3,64,1024]{2,1,0:T(8,128)(2,1)S(1)}, u32[]{:S(2)}, u32[]{:S(2)}) collective-permute-start(s16[3,64,1024]{2,1,0:T(8,128)(2,1)} %get-tuple-element.57), channel_id=1, source_target_pairs={{0,8},{4,12},{8,0},{12,4},{16,24},{20,28},{24,16},{28,20},{1,9},{5... | collective-permute-start | bytes 1179656 | tf_op jit(solution)/shard_map/ppermute | solution.py:419
  65.2 5.1 %copy-start.2 = (bf16[384,160]{1,0:T(8,128)(2,1)S(1)}, bf16[384,160]{1,0:T(8,128)(2,1)}, u32[]{:S(2)}) copy-start(bf16[384,160]{1,0:T(8,128)(2,1)} %constant.63.clone.m_all) | copy-start | bytes 368644
  65.2 5.1 %copy-start.4 = (bf16[256,160]{1,0:T(8,128)(2,1)S(1)}, bf16[256,160]{1,0:T(8,128)(2,1)}, u32[]{:S(2)}) copy-start(bf16[256,160]{1,0:T(8,128)(2,1)} %constant.64.clone.m_top) | copy-start | bytes 245764
  65.2 5.1 %copy-start.6 = (bf16[256,256]{1,0:T(8,128)(2,1)S(1)}, bf16[256,256]{1,0:T(8,128)(2,1)}, u32[]{:S(2)}) copy-start(bf16[256,256]{1,0:T(8,128)(2,1)} %constant.62.clone.turn) | copy-start | bytes 393220
  65.2 18.5 %collective-permute-start.8 = (s16[3,64,1024]{2,1,0:T(8,128)(2,1)}, s16[3,64,1024]{2,1,0:T(8,128)(2,1)}, u32[]{:S(2)}, u32[]{:S(2)}) collective-permute-start(s16[3,64,1024]{2,1,0:T(8,128)(2,1)} %get-tuple-element.56), channel_id=1, source_target_pairs={{0,16},{4,20},{8,24},{12,28},{16,0},{20,4},{24,8},{28,12},{1,17},{... | collective-permute-start | bytes 1179656 | tf_op jit(solution)/shard_map/ppermute | solution.py:419
  69.3 18.6 %collective-permute-start.10 = (s16[3,64,1024]{2,1,0:T(8,128)(2,1)}, s16[3,64,1024]{2,1,0:T(8,128)(2,1)S(1)}, u32[]{:S(2)}, u32[]{:S(2)}) collective-permute-start(s16[3,64,1024]{2,1,0:T(8,128)(2,1)} %get-tuple-element.59), channel_id=1, source_target_pairs={{0,16},{4,20},{8,24},{12,28},{16,0},{20,4},{24,8},{28,12},{1,17},{... | collective-permute-start | bytes 1179656 | tf_op jit(solution)/shard_map/ppermute | solution.py:419
  70.1 16.9 %collective-permute-start.11 = (s16[3,64,1024]{2,1,0:T(8,128)(2,1)}, s16[3,64,1024]{2,1,0:T(8,128)(2,1)S(1)}, u32[]{:S(2)}, u32[]{:S(2)}) collective-permute-start(s16[3,64,1024]{2,1,0:T(8,128)(2,1)} %get-tuple-element.60), channel_id=1, source_target_pairs={{0,8},{4,12},{8,0},{12,4},{16,24},{20,28},{24,16},{28,20},{1,9},{5... | collective-permute-start | bytes 1179656 | tf_op jit(solution)/shard_map/ppermute | solution.py:419
  70.4 12.5 %copy-start.10 = (s16[3,64,1024]{2,1,0:T(8,128)(2,1)S(1)}, s16[3,64,1024]{2,1,0:T(8,128)(2,1)}, u32[]{:S(2)}) copy-start(s16[3,64,1024]{2,1,0:T(8,128)(2,1)} %get-tuple-element.78) | copy-start | bytes 1179652
  70.4 13.4 %copy-start.11 = (s16[3,64,1024]{2,1,0:T(8,128)(2,1)S(1)}, s16[3,64,1024]{2,1,0:T(8,128)(2,1)}, u32[]{:S(2)}) copy-start(s16[3,64,1024]{2,1,0:T(8,128)(2,1)} %get-tuple-element.84) | copy-start | bytes 1179652
  84.9 12.2 %collective-permute-start.12 = (s16[3,64,1024]{2,1,0:T(8,128)(2,1)S(1)}, s16[3,64,1024]{2,1,0:T(8,128)(2,1)}, u32[]{:S(2)}, u32[]{:S(2)}) collective-permute-start(s16[3,64,1024]{2,1,0:T(8,128)(2,1)S(1)} %broadcast_select_fusion.3), channel_id=1, source_target_pairs={{0,8},{4,12},{8,0},{12,4},{16,24},{20,28},{24,16},{28,20},{1,9},{5... | collective-permute-start | bytes 1179656 | tf_op jit(solution)/shard_map/ppermute | solution.py:419
  86.7 12.4 %collective-permute-start.13 = (s16[3,64,1024]{2,1,0:T(8,128)(2,1)}, s16[3,64,1024]{2,1,0:T(8,128)(2,1)}, u32[]{:S(2)}, u32[]{:S(2)}) collective-permute-start(s16[3,64,1024]{2,1,0:T(8,128)(2,1)} %broadcast_select_fusion.2), channel_id=1, source_target_pairs={{0,16},{4,20},{8,24},{12,28},{16,0},{20,4},{24,8},{28,12},{1,17},{... | collective-permute-start | bytes 1179656 | tf_op jit(solution)/shard_map/ppermute | solution.py:419
  87.0 11.6 %copy-start.15 = (s16[3,64,1024]{2,1,0:T(8,128)(2,1)}, s16[3,64,1024]{2,1,0:T(8,128)(2,1)S(1)}, u32[]{:S(2)}) copy-start(s16[3,64,1024]{2,1,0:T(8,128)(2,1)S(1)} %collective-permute-done.11) | copy-start | bytes 1179652
  88.8 24.7 %collective-permute-start.17 = (s16[3,64,1024]{2,1,0:T(8,128)(2,1)}, s16[3,64,1024]{2,1,0:T(8,128)(2,1)}, u32[]{:S(2)}, u32[]{:S(2)}) collective-permute-start(s16[3,64,1024]{2,1,0:T(8,128)(2,1)} %broadcast_select_fusion.1), channel_id=1, source_target_pairs={{0,8},{4,12},{8,0},{12,4},{16,24},{20,28},{24,16},{28,20},{1,9},{5... | collective-permute-start | bytes 1179656 | tf_op jit(solution)/shard_map/ppermute | solution.py:419
  90.6 21.5 %collective-permute-start.18 = (s16[3,64,1024]{2,1,0:T(8,128)(2,1)}, s16[3,64,1024]{2,1,0:T(8,128)(2,1)}, u32[]{:S(2)}, u32[]{:S(2)}) collective-permute-start(s16[3,64,1024]{2,1,0:T(8,128)(2,1)} %broadcast_select_fusion), channel_id=1, source_target_pairs={{0,16},{4,20},{8,24},{12,28},{16,0},{20,4},{24,8},{28,12},{1,17},{... | collective-permute-start | bytes 1179656 | tf_op jit(solution)/shard_map/ppermute | solution.py:419
  100.5 9.6 %collective-permute-start.15 = (s16[2,3,16,1024]{3,2,1,0:T(8,128)(2,1)S(1)}, s16[2,3,16,1024]{3,2,1,0:T(8,128)(2,1)}, u32[]{:S(2)}, u32[]{:S(2)}) collective-permute-start(s16[2,3,16,1024]{3,2,1,0:T(8,128)(2,1)S(1)} %fusion.10), channel_id=1, source_target_pairs={{0,1},{1,2},{2,3},{3,0},{8,9},{9,10},{10,11},{11,8},{16,17},{17,18... | collective-permute-start | bytes 589832 | tf_op jit(solution)/shard_map/ppermute | solution.py:478
  103.5 8.5 %collective-permute-start.16 = (s16[2,3,16,1024]{3,2,1,0:T(8,128)(2,1)S(1)}, s16[2,3,16,1024]{3,2,1,0:T(8,128)(2,1)}, u32[]{:S(2)}, u32[]{:S(2)}) collective-permute-start(s16[2,3,16,1024]{3,2,1,0:T(8,128)(2,1)S(1)} %fusion.11), channel_id=1, source_target_pairs={{1,0},{2,1},{3,2},{0,3},{9,8},{10,9},{11,10},{8,11},{17,16},{18,17... | collective-permute-start | bytes 589832 | tf_op jit(solution)/shard_map/ppermute | solution.py:479
  108.5 6.4 %copy-start.8 = (s16[2,2,3,64,1024]{4,3,2,1,0:T(8,128)(2,1)}, s16[2,2,3,64,1024]{4,3,2,1,0:T(8,128)(2,1)S(1)}, u32[]{:S(2)}) copy-start(s16[2,2,3,64,1024]{4,3,2,1,0:T(8,128)(2,1)S(1)} %pad_add_fusion.held0) | copy-start | bytes 4718596
  108.5 5.0 %copy-start.13 = (s16[3,64,1024]{2,1,0:T(8,128)(2,1)S(1)}, s16[3,64,1024]{2,1,0:T(8,128)(2,1)}, u32[]{:S(2)}) copy-start(s16[3,64,1024]{2,1,0:T(8,128)(2,1)} %get-tuple-element.52) | copy-start | bytes 1179652
  108.5 10.6 %collective-permute-start.14 = (s16[2,2,3,64,1024]{4,3,2,1,0:T(8,128)(2,1)S(1)}, s16[2,2,3,64,1024]{4,3,2,1,0:T(8,128)(2,1)}, u32[]{:S(2)}, u32[]{:S(2)}) collective-permute-start(s16[2,2,3,64,1024]{4,3,2,1,0:T(8,128)(2,1)S(1)} %pad_add_fusion.held0), channel_id=1, source_target_pairs={{0,4},{4,0},{8,12},{12,8},{16,20},{20,16},{24,28},{28,24},{1,5},{5... | collective-permute-start | bytes 4718600 | tf_op jit(solution)/shard_map/ppermute | solution.py:419
  115.3 4.0 %collective-permute-start.19 = (s16[2,2,3,64,1024]{4,3,2,1,0:T(8,128)(2,1)S(1)}, s16[2,2,3,64,1024]{4,3,2,1,0:T(8,128)(2,1)S(1)}, u32[]{:S(2)}, u32[]{:S(2)}) collective-permute-start(s16[2,2,3,64,1024]{4,3,2,1,0:T(8,128)(2,1)S(1)} %pad_add_fusion.1.held1), channel_id=1, source_target_pairs={{0,4},{4,0},{8,12},{12,8},{16,20},{20,16},{24,28},{28,24},{1,5},{5... | collective-permute-start | bytes 4718600 | tf_op jit(solution)/shard_map/ppermute | solution.py:419
  115.4 3.5 %collective-permute-start.20 = (s16[2,3,16,1024]{3,2,1,0:T(8,128)(2,1)}, s16[2,3,16,1024]{3,2,1,0:T(8,128)(2,1)S(1)}, u32[]{:S(2)}, u32[]{:S(2)}) collective-permute-start(s16[2,3,16,1024]{3,2,1,0:T(8,128)(2,1)} %collective-permute-done.15.before), channel_id=1, source_target_pairs={{0,4},{4,0},{8,12},{12,8},{16,20},{20,16},{24,28},{28,24},{1,5},{5... | collective-permute-start | bytes 589832 | tf_op jit(solution)/shard_map/ppermute | solution.py:419
  115.9 3.3 %collective-permute-start.21 = (s16[2,3,16,1024]{3,2,1,0:T(8,128)(2,1)}, s16[2,3,16,1024]{3,2,1,0:T(8,128)(2,1)S(1)}, u32[]{:S(2)}, u32[]{:S(2)}) collective-permute-start(s16[2,3,16,1024]{3,2,1,0:T(8,128)(2,1)} %collective-permute-done.16.after), channel_id=1, source_target_pairs={{0,4},{4,0},{8,12},{12,8},{16,20},{20,16},{24,28},{28,24},{1,5},{5... | collective-permute-start | bytes 589832 | tf_op jit(solution)/shard_map/ppermute | solution.py:419
  (9 other events, 16.3 us)

commit v9 on v8

--- a/solution.py
+++ b/solution.py
@@ -14,7 +14,7 @@
 code_scale = 4096.0
 phases = 2
 streams = ((0, 3), (1, 2))
-shares = {(0, 1): ((0, 1), 44), (1, 1): ((2,), 52)}
+shares = {(0, 1): ((0,), 57), (1, 1): ((1, 2), 57)}
 
 
 def grant(mib):
@@ -370,7 +370,7 @@
     _, _, pair, slab, width = terms[0].shape
     comps = sum(t.shape[0] for t in terms)
     groups = tuple(comps_of for comps_of, _ in shares.values())
-    rows = min(slab, 32)
+    rows = min(slab, 64)
     turn = across_matrix([first_at(0)])
     high, low, _ = along_matrices(rows, length)
     both = np.concatenate([high, low], 0)

time: 145 us -> 141 us (0.972)
  local copies, waits for them, and re-layouts: 11.8 us -> 9.12 us
  Pallas kernels: 62.4 us -> 60.9 us
    unnamed x38 -> x34, local copies, waits for them, and re-layouts: 8.56 us -> 5.87 us
    pallas_call x1, Pallas kernels: 24 us -> 22.1 us  [final(): pl.pallas_call(functools.partial(final_kernel, groups), out_shape=jax.Sha...]
  transfers between devices with their start and end apart: 22 -> 22, of which waited for: 8 -> 7; matrix products, arithmetic and copies ran while one was open for 15% -> 15% of each run, Pallas kernels for 24% -> 25%
where the time goes in v9:
time: 141 us; the launch traced here: 140 us
  Pallas kernels  60.9 us (43%)
  starting transfers between devices  27.5 us (20%)
  other arithmetic  21.2 us (15%)
  waiting for transfers between devices  18.6 us (13%)
  local copies, waits for them, and re-layouts  9.12 us (6%)
  between operations  2.96 us (2%)
    pallas_call x2, Pallas kernels, field_terms(): pl.pallas_call(functools.partial(field_kernel, comps), out_shape=(shape,...  31.8 us
    pallas_call x1, Pallas kernels, final(): pl.pallas_call(functools.partial(final_kernel, groups), out_shape=jax.Sha...  22.1 us
    ppermute x18, starting transfers between devices, swap(): lax.ppermute(array, 'pert', [(i, i ^ bit) for i in range(lax.axis_size('p...  14.8 us
    ppermute x18, waiting for transfers between devices, swap(): lax.ppermute(array, 'pert', [(i, i ^ bit) for i in range(lax.axis_size('p...  9.7 us
    pallas_call x2, Pallas kernels, pack(): pl.pallas_call(pack_kernel, out_shape=(shape,) * 2, grid=(2, comps), in_s...  7.04 us
    another operation x6, other arithmetic, exchange(): parts.append(jnp.stack(row, 0))  5.93 us
    unnamed x34, local copies, waits for them, and re-layouts  5.87 us
    ppermute x2, waiting for transfers between devices, ring(): return (lax.ppermute(last, 'gx', up), lax.ppermute(first, 'gx', down))  5.57 us
  transfers between devices with their start and end apart: 22, of which 7 were waited for; matrix products, arithmetic and copies ran while one was open for 15% of the time, Pallas kernels for 25%

profile of v9, /device:TPU:0, one launch (start us, length us, event | category | flops | bytes accessed | tf_op | source)
XLA Modules:
  0.0 140.3 jit_solution(480707356716945754)
XLA Ops:
  0.0 3.3 %fusion.17 = (f32[3,16,2,1024]{3,2,1,0:T(2,128)}, f32[3,16,2,1024]{3,2,1,0:T(2,128)}) fusion(f32[3,256,8,1024]{3,2,1,0:T(8,128)} %bitcast.62), kind=kLoop, calls=%fused_computation.48 | loop fusion | bytes 1572864 | tf_op jit(solution)/shard_map/slice | solution.py:502
  3.3 4.6 %copy-done = bf16[1,3,256,8,1024]{4,3,2,1,0:T(8,128)(2,1)S(1)} copy-done((bf16[1,3,256,8,1024]{4,3,2,1,0:T(8,128)(2,1)S(1)}, bf16[1,3,256,8,1024]{4,3,2,1,0:T(8,128)(2,1)}, u32[]{:S(2)}) %copy-start) | copy-done | bytes 12582936
  7.8 3.5 %shard_map.146 = (s16[2,2,3,64,1024]{4,3,2,1,0:T(8,128)(2,1)S(1)}, s16[2,2,3,64,1024]{4,3,2,1,0:T(8,128)(2,1)}) custom-call(s32[1]{0:T(128)} %bitcast.core, bf16[128,256]{1,0:T(8,128)(2,1)S(1)} %copy-done.1, bf16[3,2048,1024]{2,1,0:T(8,128)(2,1)S(1)} %bitcast.60), custom_call_target="tpu_custom_call" | custom-call | bytes 12582912 | tf_op jit(solution)/shard_map/pallas_call | solution.py:124
  11.8 3.5 %shard_map.145 = (s16[2,2,3,64,1024]{4,3,2,1,0:T(8,128)(2,1)S(1)}, s16[2,2,3,64,1024]{4,3,2,1,0:T(8,128)(2,1)}) custom-call(s32[1]{0:T(128)} %bitcast.core, bf16[128,256]{1,0:T(8,128)(2,1)S(1)} %copy-done.1, bf16[3,2048,1024]{2,1,0:T(8,128)(2,1)S(1)} %bitcast.61), custom_call_target="tpu_custom_call" | custom-call | bytes 12582912 | tf_op jit(solution)/shard_map/pallas_call | solution.py:124
  15.4 3.0 %collective-permute-start.2 = (f32[3,16,2,1024]{3,2,1,0:T(2,128)}, f32[3,16,2,1024]{3,2,1,0:T(2,128)}, u32[]{:S(2)}, u32[]{:S(2)}) collective-permute-start(f32[3,16,2,1024]{3,2,1,0:T(2,128)} %get-tuple-element.44), channel_id=1, source_target_pairs={{0,1},{1,2},{2,3},{3,0},{4,5},{5,6},{6,7},{7,4},{8,9},{9,10},{10,1... | collective-permute-start | bytes 1179656 | tf_op jit(solution)/shard_map/ppermute | solution.py:415
  18.4 2.0 %collective-permute-start.3 = (f32[3,16,2,1024]{3,2,1,0:T(2,128)}, f32[3,16,2,1024]{3,2,1,0:T(2,128)}, u32[]{:S(2)}, u32[]{:S(2)}) collective-permute-start(f32[3,16,2,1024]{3,2,1,0:T(2,128)} %get-tuple-element.45), channel_id=1, source_target_pairs={{1,0},{2,1},{3,2},{0,3},{5,4},{6,5},{7,6},{4,7},{9,8},{10,9},{11,1... | collective-permute-start | bytes 1179656 | tf_op jit(solution)/shard_map/ppermute | solution.py:415
  21.1 2.3 %fusion.6 = (s16[3,64,1024]{2,1,0:T(8,128)(2,1)}, s16[3,64,1024]{2,1,0:T(8,128)(2,1)}) fusion(s16[2,2,3,64,1024]{4,3,2,1,0:T(8,128)(2,1)} %collective-permute-done.1, s16[2,2,3,64,1024]{4,3,2,1,0:T(8,128)(2,1)S(1)} %get-tuple-element.41, pred[]{:T(512)S(6)} %eq.41), kind=kLoop, calls=%fused_computation.21 | loop fusion | flops 393216 | bytes 2359297 | tf_op jit(solution)/shard_map/jit(_where)/select_n | solution.py:430
  23.4 2.2 %fusion.8 = (s16[3,64,1024]{2,1,0:T(8,128)(2,1)S(1)}, s16[3,64,1024]{2,1,0:T(8,128)(2,1)}) fusion(s16[2,2,3,64,1024]{4,3,2,1,0:T(8,128)(2,1)} %collective-permute-done, s16[2,2,3,64,1024]{4,3,2,1,0:T(8,128)(2,1)S(1)} %get-tuple-element.39, pred[]{:T(512)S(6)} %eq.41), kind=kLoop, calls=%fused_computation.25 | loop fusion | flops 393216 | bytes 2359297 | tf_op jit(solution)/shard_map/jit(_where)/select_n | solution.py:430
  25.6 1.7 %collective-permute-start.4 = (s16[3,64,1024]{2,1,0:T(8,128)(2,1)S(1)}, s16[3,64,1024]{2,1,0:T(8,128)(2,1)}, u32[]{:S(2)}, u32[]{:S(2)}) collective-permute-start(s16[3,64,1024]{2,1,0:T(8,128)(2,1)S(1)} %get-tuple-element.47), channel_id=1, source_target_pairs={{0,16},{4,20},{8,24},{12,28},{16,0},{20,4},{24,8},{28,12},{1,17},{... | collective-permute-start | bytes 1179656 | tf_op jit(solution)/shard_map/ppermute | solution.py:419
  27.3 1.5 %collective-permute-start.5 = (s16[3,64,1024]{2,1,0:T(8,128)(2,1)}, s16[3,64,1024]{2,1,0:T(8,128)(2,1)}, u32[]{:S(2)}, u32[]{:S(2)}) collective-permute-start(s16[3,64,1024]{2,1,0:T(8,128)(2,1)} %get-tuple-element.48), channel_id=1, source_target_pairs={{0,8},{4,12},{8,0},{12,4},{16,24},{20,28},{24,16},{28,20},{1,9},{5... | collective-permute-start | bytes 1179656 | tf_op jit(solution)/shard_map/ppermute | solution.py:419
  30.7 1.7 %collective-permute-start.7 = (s16[3,64,1024]{2,1,0:T(8,128)(2,1)}, s16[3,64,1024]{2,1,0:T(8,128)(2,1)}, u32[]{:S(2)}, u32[]{:S(2)}) collective-permute-start(s16[3,64,1024]{2,1,0:T(8,128)(2,1)} %get-tuple-element.52), channel_id=1, source_target_pairs={{0,8},{4,12},{8,0},{12,4},{16,24},{20,28},{24,16},{28,20},{1,9},{5... | collective-permute-start | bytes 1179656 | tf_op jit(solution)/shard_map/ppermute | solution.py:419
  32.4 5.5 %collective-permute-done.3.after = f32[3,16,2,1024]{3,2,1,0:T(2,128)} collective-permute-done((f32[3,16,2,1024]{3,2,1,0:T(2,128)}, f32[3,16,2,1024]{3,2,1,0:T(2,128)}, u32[]{:S(2)}, u32[]{:S(2)}) %collective-permute-start.3) | collective-permute-done | bytes 393248 | tf_op jit(solution)/shard_map/ppermute | solution.py:415
  37.9 11.8 %shard_map.147 = (f32[1,5,2,256,1024]{4,3,2,1,0:T(8,128)}, s32[1]{0:T(128)}) custom-call(f32[1]{0:T(128)} %bitcast.9.viscosity, bf16[256,256]{1,0:T(8,128)(2,1)} %constant.62.clone.turn, bf16[384,160]{1,0:T(8,128)(2,1)} %constant.63.clone.m_all, bf16[256,160]{1,0:T(8,128)(2,1)} %constant.64.clone.m_top, f32[3,16,2,1024]{3,2,1,0:T(2,128)} %collective-permute-done.2.before, ...), custom_call_target="tpu_custom_call" | custom-call | bytes 16777216 | tf_op jit(solution)/shard_map/pallas_call | solution.py:243
  50.3 2.7 %broadcast_select_fusion.7 = (s16[3,64,1024]{2,1,0:T(8,128)(2,1)}, s16[3,64,1024]{2,1,0:T(8,128)(2,1)S(1)}, s16[3,64,1024]{2,1,0:T(8,128)(2,1)}, s16[3,64,1024]{2,1,0:T(8,128)(2,1)}) fusion(s16[3,64,1024]{2,1,0:T(8,128)(2,1)} %collective-permute-done.4, pred[]{:T(512)S(6)} %eq.44, s16[2,2,3,64,1024]{4,3,2,1,0:T(8,128)(2,1)} %collective-permute-done, ...), kind=kLoop, calls=%fused_computation.43 | loop fusion | flops 786432 | bytes 3932162 | tf_op jit(solution)/shard_map/jit(_where)/select_n | solution.py:447
  53.0 1.3 collective-permute-start.9
  54.2 1.8 %collective-permute-start.8 = (s16[3,64,1024]{2,1,0:T(8,128)(2,1)}, s16[3,64,1024]{2,1,0:T(8,128)(2,1)}, u32[]{:S(2)}, u32[]{:S(2)}) collective-permute-start(s16[3,64,1024]{2,1,0:T(8,128)(2,1)} %get-tuple-element.56), channel_id=1, source_target_pairs={{0,16},{4,20},{8,24},{12,28},{16,0},{20,4},{24,8},{28,12},{1,17},{... | collective-permute-start | bytes 1179656 | tf_op jit(solution)/shard_map/ppermute | solution.py:419
  56.0 2.8 %broadcast_select_fusion.4 = (s16[3,64,1024]{2,1,0:T(8,128)(2,1)}, s16[3,64,1024]{2,1,0:T(8,128)(2,1)S(1)}, s16[3,64,1024]{2,1,0:T(8,128)(2,1)}, s16[3,64,1024]{2,1,0:T(8,128)(2,1)S(1)}) fusion(s16[3,64,1024]{2,1,0:T(8,128)(2,1)} %collective-permute-done.7, pred[]{:T(512)S(6)} %eq.45, s16[2,2,3,64,1024]{4,3,2,1,0:T(8,128)(2,1)} %collective-permute-done.1, ...), kind=kLoop, calls=%fused_computation.40 | loop fusion | flops 786432 | bytes 3932162 | tf_op jit(solution)/shard_map/jit(_where)/select_n | solution.py:448
  59.8 20.0 %shard_map.148 = (f32[2,5,2,256,1024]{4,3,2,1,0:T(8,128)}, s32[1]{0:T(128)}) custom-call(f32[1]{0:T(128)} %bitcast.9.viscosity, bf16[256,256]{1,0:T(8,128)(2,1)} %constant.62.clone.turn, bf16[384,160]{1,0:T(8,128)(2,1)} %constant.63.clone.m_all, bf16[256,160]{1,0:T(8,128)(2,1)} %constant.64.clone.m_top, f32[3,16,2,1024]{3,2,1,0:T(2,128)} %collective-permute-done.2.before, ...), custom_call_target="tpu_custom_call" | custom-call | bytes 33554432 | tf_op jit(solution)/shard_map/pallas_call | solution.py:243
  80.4 1.1 broadcast_select_fusion.2
  81.6 1.1 broadcast_select_fusion.3
  82.8 3.0 %collective-permute-start.13 = (s16[3,64,1024]{2,1,0:T(8,128)(2,1)S(1)}, s16[3,64,1024]{2,1,0:T(8,128)(2,1)S(1)}, u32[]{:S(2)}, u32[]{:S(2)}) collective-permute-start(s16[3,64,1024]{2,1,0:T(8,128)(2,1)S(1)} %broadcast_select_fusion.2), channel_id=1, source_target_pairs={{0,16},{4,20},{8,24},{12,28},{16,0},{20,4},{24,8},{28,12},{1,17},{... | collective-permute-start | bytes 1179656 | tf_op jit(solution)/shard_map/ppermute | solution.py:419
  88.7 6.3 %collective-permute-done.12 = s16[3,64,1024]{2,1,0:T(8,128)(2,1)} collective-permute-done((s16[3,64,1024]{2,1,0:T(8,128)(2,1)S(1)}, s16[3,64,1024]{2,1,0:T(8,128)(2,1)}, u32[]{:S(2)}, u32[]{:S(2)}) %collective-permute-start.12) | collective-permute-done | bytes 393248 | tf_op jit(solution)/shard_map/ppermute | solution.py:419
  95.0 1.6 %select_bitcast_fusion.7 = (s16[1,3,64,1024]{3,2,1,0:T(8,128)(2,1)S(1)}, s16[1,3,64,1024]{3,2,1,0:T(8,128)(2,1)S(1)}) fusion(s16[3,64,1024]{2,1,0:T(8,128)(2,1)} %get-tuple-element.48, s16[3,64,1024]{2,1,0:T(8,128)(2,1)} %collective-permute-done.5, s16[3,64,1024]{2,1,0:T(8,128)(2,1)} %collective-permute-done.12, ...), kind=kLoop, calls=%fused_computation.35 | loop fusion | flops 983040 | bytes 2752515 | tf_op jit(solution)/shard_map/stack | solution.py:467
  96.6 1.4 select_bitcast_fusion.6
  98.0 3.0 %collective-permute-start.15 = (s16[2,3,16,1024]{3,2,1,0:T(8,128)(2,1)S(1)}, s16[2,3,16,1024]{3,2,1,0:T(8,128)(2,1)S(1)}, u32[]{:S(2)}, u32[]{:S(2)}) collective-permute-start(s16[2,3,16,1024]{3,2,1,0:T(8,128)(2,1)S(1)} %fusion.10), channel_id=1, source_target_pairs={{0,1},{1,2},{2,3},{3,0},{8,9},{9,10},{10,11},{11,8},{16,17},{17,18... | collective-permute-start | bytes 589832 | tf_op jit(solution)/shard_map/ppermute | solution.py:478
  101.0 4.6 %collective-permute-start.16 = (s16[2,3,16,1024]{3,2,1,0:T(8,128)(2,1)S(1)}, s16[2,3,16,1024]{3,2,1,0:T(8,128)(2,1)S(1)}, u32[]{:S(2)}, u32[]{:S(2)}) collective-permute-start(s16[2,3,16,1024]{3,2,1,0:T(8,128)(2,1)S(1)} %fusion.11), channel_id=1, source_target_pairs={{1,0},{2,1},{3,2},{0,3},{9,8},{10,9},{11,10},{8,11},{17,16},{18,17... | collective-permute-start | bytes 589832 | tf_op jit(solution)/shard_map/ppermute | solution.py:479
  106.1 1.3 collective-permute-done.15.before
  107.4 2.0 %collective-permute-done.16.after = s16[2,3,16,1024]{3,2,1,0:T(8,128)(2,1)S(1)} collective-permute-done((s16[2,3,16,1024]{3,2,1,0:T(8,128)(2,1)S(1)}, s16[2,3,16,1024]{3,2,1,0:T(8,128)(2,1)S(1)}, u32[]{:S(2)}, u32[]{:S(2)}) %collective-permute-start.16) | collective-permute-done | bytes 196640 | tf_op jit(solution)/shard_map/ppermute | solution.py:479
  109.5 1.4 %select_bitcast_fusion.2 = (s16[1,3,64,1024]{3,2,1,0:T(8,128)(2,1)S(1)}, s16[1,3,64,1024]{3,2,1,0:T(8,128)(2,1)S(1)}) fusion(s16[3,64,1024]{2,1,0:T(8,128)(2,1)} %get-tuple-element.51, s16[3,64,1024]{2,1,0:T(8,128)(2,1)} %collective-permute-done.6, s16[3,64,1024]{2,1,0:T(8,128)(2,1)} %collective-permute-done.18, s16[3,64,1024]{2,1,0:T(8,128)(2,1)S(1)} %copy-done.11, ...), kind=kLoop, calls=%fused_computation.30 | loop fusion | flops 983040 | bytes 2752515 | tf_op jit(solution)/shard_map/stack | solution.py:467
  110.9 1.5 %select_bitcast_fusion.3 = (s16[1,3,64,1024]{3,2,1,0:T(8,128)(2,1)S(1)}, s16[1,3,64,1024]{3,2,1,0:T(8,128)(2,1)S(1)}) fusion(s16[3,64,1024]{2,1,0:T(8,128)(2,1)} %get-tuple-element.52, s16[3,64,1024]{2,1,0:T(8,128)(2,1)} %collective-permute-done.7, s16[3,64,1024]{2,1,0:T(8,128)(2,1)} %collective-permute-done.17, s16[3,64,1024]{2,1,0:T(8,128)(2,1)S(1)} %copy-done.9, ...), kind=kLoop, calls=%fused_computation.31 | loop fusion | flops 983040 | bytes 2752515 | tf_op jit(solution)/shard_map/stack | solution.py:467
  113.5 3.1 %collective-permute-done.20.before2 = s16[2,3,16,1024]{3,2,1,0:T(8,128)(2,1)S(1)} collective-permute-done((s16[2,3,16,1024]{3,2,1,0:T(8,128)(2,1)S(1)}, s16[2,3,16,1024]{3,2,1,0:T(8,128)(2,1)S(1)}, u32[]{:S(2)}, u32[]{:S(2)}) %collective-permute-start.20) | collective-permute-done | bytes 196640 | tf_op jit(solution)/shard_map/ppermute | solution.py:419
  118.1 22.1 %shard_map.149 = f32[1,3,256,2,1024]{4,3,2,1,0:T(2,128)} custom-call(s32[1]{0:T(128)} %bitcast.core, bf16[128,96]{1,0:T(8,128)(2,1)} %constant.65.clone.m_both, bf16[256,128]{1,0:T(8,128)(2,1)} %constant.66.clone.turn, s16[2,2,3,64,1024]{4,3,2,1,0:T(8,128)(2,1)} %copy-done.2, s16[2,2,3,64,1024]{4,3,2,1,0:T(8,128)(2,1)} %collective-permute-done.14.other0, ...), custom_call_target="tpu_custom_call" | custom-call | bytes 12582912 | tf_op jit(solution)/shard_map/pallas_call | solution.py:382
  (71 shorter events, 8.7 us)
Async XLA Ops:
  3.3 4.6 %copy-start = (bf16[1,3,256,8,1024]{4,3,2,1,0:T(8,128)(2,1)S(1)}, bf16[1,3,256,8,1024]{4,3,2,1,0:T(8,128)(2,1)}, u32[]{:S(2)}) copy-start(bf16[1,3,256,8,1024]{4,3,2,1,0:T(8,128)(2,1)} %param.16) | copy-start | bytes 37748740
  11.4 9.7 %collective-permute-start.1 = (s16[2,2,3,64,1024]{4,3,2,1,0:T(8,128)(2,1)}, s16[2,2,3,64,1024]{4,3,2,1,0:T(8,128)(2,1)}, u32[]{:S(2)}, u32[]{:S(2)}) collective-permute-start(s16[2,2,3,64,1024]{4,3,2,1,0:T(8,128)(2,1)} %get-tuple-element.42), channel_id=1, source_target_pairs={{0,4},{4,0},{8,12},{12,8},{16,20},{20,16},{24,28},{28,24},{1,5},{5... | collective-permute-start | bytes 4718600 | tf_op jit(solution)/shard_map/ppermute | solution.py:419
  15.3 8.1 %collective-permute-start = (s16[2,2,3,64,1024]{4,3,2,1,0:T(8,128)(2,1)}, s16[2,2,3,64,1024]{4,3,2,1,0:T(8,128)(2,1)}, u32[]{:S(2)}, u32[]{:S(2)}) collective-permute-start(s16[2,2,3,64,1024]{4,3,2,1,0:T(8,128)(2,1)} %get-tuple-element.40), channel_id=1, source_target_pairs={{0,4},{4,0},{8,12},{12,8},{16,20},{20,16},{24,28},{28,24},{1,5},{5... | collective-permute-start | bytes 4718600 | tf_op jit(solution)/shard_map/ppermute | solution.py:419
  15.4 15.3 %collective-permute-start.2 = (f32[3,16,2,1024]{3,2,1,0:T(2,128)}, f32[3,16,2,1024]{3,2,1,0:T(2,128)}, u32[]{:S(2)}, u32[]{:S(2)}) collective-permute-start(f32[3,16,2,1024]{3,2,1,0:T(2,128)} %get-tuple-element.44), channel_id=1, source_target_pairs={{0,1},{1,2},{2,3},{3,0},{4,5},{5,6},{6,7},{7,4},{8,9},{9,10},{10,1... | collective-permute-start | bytes 1179656 | tf_op jit(solution)/shard_map/ppermute | solution.py:415
  18.4 19.5 %collective-permute-start.3 = (f32[3,16,2,1024]{3,2,1,0:T(2,128)}, f32[3,16,2,1024]{3,2,1,0:T(2,128)}, u32[]{:S(2)}, u32[]{:S(2)}) collective-permute-start(f32[3,16,2,1024]{3,2,1,0:T(2,128)} %get-tuple-element.45), channel_id=1, source_target_pairs={{1,0},{2,1},{3,2},{0,3},{5,4},{6,5},{7,6},{4,7},{9,8},{10,9},{11,1... | collective-permute-start | bytes 1179656 | tf_op jit(solution)/shard_map/ppermute | solution.py:415
  23.4 6.1 %copy-start.16 = (f32[64]{0:T(128)S(1)}, f32[64]{0:T(128)}, u32[]{:S(2)}) copy-start(f32[64]{0:T(128)} %param.19) | copy-start | bytes 772
  25.6 24.2 %copy-start.6 = (s16[3,64,1024]{2,1,0:T(8,128)(2,1)}, s16[3,64,1024]{2,1,0:T(8,128)(2,1)S(1)}, u32[]{:S(2)}) copy-start(s16[3,64,1024]{2,1,0:T(8,128)(2,1)S(1)} %get-tuple-element.47) | copy-start | bytes 1179652
  25.6 24.7 %collective-permute-start.4 = (s16[3,64,1024]{2,1,0:T(8,128)(2,1)S(1)}, s16[3,64,1024]{2,1,0:T(8,128)(2,1)}, u32[]{:S(2)}, u32[]{:S(2)}) collective-permute-start(s16[3,64,1024]{2,1,0:T(8,128)(2,1)S(1)} %get-tuple-element.47), channel_id=1, source_target_pairs={{0,16},{4,20},{8,24},{12,28},{16,0},{20,4},{24,8},{28,12},{1,17},{... | collective-permute-start | bytes 1179656 | tf_op jit(solution)/shard_map/ppermute | solution.py:419
  27.3 23.0 %collective-permute-start.5 = (s16[3,64,1024]{2,1,0:T(8,128)(2,1)}, s16[3,64,1024]{2,1,0:T(8,128)(2,1)}, u32[]{:S(2)}, u32[]{:S(2)}) collective-permute-start(s16[3,64,1024]{2,1,0:T(8,128)(2,1)} %get-tuple-element.48), channel_id=1, source_target_pairs={{0,8},{4,12},{8,0},{12,4},{16,24},{20,28},{24,16},{28,20},{1,9},{5... | collective-permute-start | bytes 1179656 | tf_op jit(solution)/shard_map/ppermute | solution.py:419
  30.1 25.9 %collective-permute-start.6 = (s16[3,64,1024]{2,1,0:T(8,128)(2,1)}, s16[3,64,1024]{2,1,0:T(8,128)(2,1)}, u32[]{:S(2)}, u32[]{:S(2)}) collective-permute-start(s16[3,64,1024]{2,1,0:T(8,128)(2,1)} %get-tuple-element.51), channel_id=1, source_target_pairs={{0,16},{4,20},{8,24},{12,28},{16,0},{20,4},{24,8},{28,12},{1,17},{... | collective-permute-start | bytes 1179656 | tf_op jit(solution)/shard_map/ppermute | solution.py:419
  30.7 25.3 %collective-permute-start.7 = (s16[3,64,1024]{2,1,0:T(8,128)(2,1)}, s16[3,64,1024]{2,1,0:T(8,128)(2,1)}, u32[]{:S(2)}, u32[]{:S(2)}) collective-permute-start(s16[3,64,1024]{2,1,0:T(8,128)(2,1)} %get-tuple-element.52), channel_id=1, source_target_pairs={{0,8},{4,12},{8,0},{12,4},{16,24},{20,28},{24,16},{28,20},{1,9},{5... | collective-permute-start | bytes 1179656 | tf_op jit(solution)/shard_map/ppermute | solution.py:419
  53.0 27.4 %collective-permute-start.9 = (s16[3,64,1024]{2,1,0:T(8,128)(2,1)}, s16[3,64,1024]{2,1,0:T(8,128)(2,1)}, u32[]{:S(2)}, u32[]{:S(2)}) collective-permute-start(s16[3,64,1024]{2,1,0:T(8,128)(2,1)} %get-tuple-element.57), channel_id=1, source_target_pairs={{0,8},{4,12},{8,0},{12,4},{16,24},{20,28},{24,16},{28,20},{1,9},{5... | collective-permute-start | bytes 1179656 | tf_op jit(solution)/shard_map/ppermute | solution.py:419
  54.2 27.3 %collective-permute-start.8 = (s16[3,64,1024]{2,1,0:T(8,128)(2,1)}, s16[3,64,1024]{2,1,0:T(8,128)(2,1)}, u32[]{:S(2)}, u32[]{:S(2)}) collective-permute-start(s16[3,64,1024]{2,1,0:T(8,128)(2,1)} %get-tuple-element.56), channel_id=1, source_target_pairs={{0,16},{4,20},{8,24},{12,28},{16,0},{20,4},{24,8},{28,12},{1,17},{... | collective-permute-start | bytes 1179656 | tf_op jit(solution)/shard_map/ppermute | solution.py:419
  58.8 28.0 %collective-permute-start.10 = (s16[3,64,1024]{2,1,0:T(8,128)(2,1)}, s16[3,64,1024]{2,1,0:T(8,128)(2,1)S(1)}, u32[]{:S(2)}, u32[]{:S(2)}) collective-permute-start(s16[3,64,1024]{2,1,0:T(8,128)(2,1)} %get-tuple-element.59), channel_id=1, source_target_pairs={{0,16},{4,20},{8,24},{12,28},{16,0},{20,4},{24,8},{28,12},{1,17},{... | collective-permute-start | bytes 1179656 | tf_op jit(solution)/shard_map/ppermute | solution.py:419
  59.1 26.8 %collective-permute-start.11 = (s16[3,64,1024]{2,1,0:T(8,128)(2,1)}, s16[3,64,1024]{2,1,0:T(8,128)(2,1)S(1)}, u32[]{:S(2)}, u32[]{:S(2)}) collective-permute-start(s16[3,64,1024]{2,1,0:T(8,128)(2,1)} %get-tuple-element.60), channel_id=1, source_target_pairs={{0,8},{4,12},{8,0},{12,4},{16,24},{20,28},{24,16},{28,20},{1,9},{5... | collective-permute-start | bytes 1179656 | tf_op jit(solution)/shard_map/ppermute | solution.py:419
  59.8 21.8 %copy-start.4 = (s16[3,64,1024]{2,1,0:T(8,128)(2,1)S(1)}, s16[3,64,1024]{2,1,0:T(8,128)(2,1)}, u32[]{:S(2)}) copy-start(s16[3,64,1024]{2,1,0:T(8,128)(2,1)} %get-tuple-element.84) | copy-start | bytes 1179652
  82.7 12.2 %collective-permute-start.12 = (s16[3,64,1024]{2,1,0:T(8,128)(2,1)S(1)}, s16[3,64,1024]{2,1,0:T(8,128)(2,1)}, u32[]{:S(2)}, u32[]{:S(2)}) collective-permute-start(s16[3,64,1024]{2,1,0:T(8,128)(2,1)S(1)} %broadcast_select_fusion.3), channel_id=1, source_target_pairs={{0,8},{4,12},{8,0},{12,4},{16,24},{20,28},{24,16},{28,20},{1,9},{5... | collective-permute-start | bytes 1179656 | tf_op jit(solution)/shard_map/ppermute | solution.py:419
  82.8 13.7 %collective-permute-start.13 = (s16[3,64,1024]{2,1,0:T(8,128)(2,1)S(1)}, s16[3,64,1024]{2,1,0:T(8,128)(2,1)S(1)}, u32[]{:S(2)}, u32[]{:S(2)}) collective-permute-start(s16[3,64,1024]{2,1,0:T(8,128)(2,1)S(1)} %broadcast_select_fusion.2), channel_id=1, source_target_pairs={{0,16},{4,20},{8,24},{12,28},{16,0},{20,4},{24,8},{28,12},{1,17},{... | collective-permute-start | bytes 1179656 | tf_op jit(solution)/shard_map/ppermute | solution.py:419
  87.6 9.0 %copy-start.7 = (s16[3,64,1024]{2,1,0:T(8,128)(2,1)S(1)}, s16[3,64,1024]{2,1,0:T(8,128)(2,1)}, u32[]{:S(2)}) copy-start(s16[3,64,1024]{2,1,0:T(8,128)(2,1)} %copy-done.6) | copy-start | bytes 1179652
  87.6 23.3 %collective-permute-start.17 = (s16[3,64,1024]{2,1,0:T(8,128)(2,1)}, s16[3,64,1024]{2,1,0:T(8,128)(2,1)}, u32[]{:S(2)}, u32[]{:S(2)}) collective-permute-start(s16[3,64,1024]{2,1,0:T(8,128)(2,1)} %broadcast_select_fusion.1), channel_id=1, source_target_pairs={{0,8},{4,12},{8,0},{12,4},{16,24},{20,28},{24,16},{28,20},{1,9},{5... | collective-permute-start | bytes 1179656 | tf_op jit(solution)/shard_map/ppermute | solution.py:419
  87.9 21.5 %collective-permute-start.18 = (s16[3,64,1024]{2,1,0:T(8,128)(2,1)}, s16[3,64,1024]{2,1,0:T(8,128)(2,1)}, u32[]{:S(2)}, u32[]{:S(2)}) collective-permute-start(s16[3,64,1024]{2,1,0:T(8,128)(2,1)} %broadcast_select_fusion), channel_id=1, source_target_pairs={{0,16},{4,20},{8,24},{12,28},{16,0},{20,4},{24,8},{28,12},{1,17},{... | collective-permute-start | bytes 1179656 | tf_op jit(solution)/shard_map/ppermute | solution.py:419
  98.0 9.4 %collective-permute-start.15 = (s16[2,3,16,1024]{3,2,1,0:T(8,128)(2,1)S(1)}, s16[2,3,16,1024]{3,2,1,0:T(8,128)(2,1)S(1)}, u32[]{:S(2)}, u32[]{:S(2)}) collective-permute-start(s16[2,3,16,1024]{3,2,1,0:T(8,128)(2,1)S(1)} %fusion.10), channel_id=1, source_target_pairs={{0,1},{1,2},{2,3},{3,0},{8,9},{9,10},{10,11},{11,8},{16,17},{17,18... | collective-permute-start | bytes 589832 | tf_op jit(solution)/shard_map/ppermute | solution.py:478
  101.0 8.4 %collective-permute-start.16 = (s16[2,3,16,1024]{3,2,1,0:T(8,128)(2,1)S(1)}, s16[2,3,16,1024]{3,2,1,0:T(8,128)(2,1)S(1)}, u32[]{:S(2)}, u32[]{:S(2)}) collective-permute-start(s16[2,3,16,1024]{3,2,1,0:T(8,128)(2,1)S(1)} %fusion.11), channel_id=1, source_target_pairs={{1,0},{2,1},{3,2},{0,3},{9,8},{10,9},{11,10},{8,11},{17,16},{18,17... | collective-permute-start | bytes 589832 | tf_op jit(solution)/shard_map/ppermute | solution.py:479
  106.0 6.4 %copy-start.2 = (s16[2,2,3,64,1024]{4,3,2,1,0:T(8,128)(2,1)}, s16[2,2,3,64,1024]{4,3,2,1,0:T(8,128)(2,1)S(1)}, u32[]{:S(2)}) copy-start(s16[2,2,3,64,1024]{4,3,2,1,0:T(8,128)(2,1)S(1)} %pad_add_fusion.held0) | copy-start | bytes 4718596
  106.0 4.9 %copy-start.9 = (s16[3,64,1024]{2,1,0:T(8,128)(2,1)S(1)}, s16[3,64,1024]{2,1,0:T(8,128)(2,1)}, u32[]{:S(2)}) copy-start(s16[3,64,1024]{2,1,0:T(8,128)(2,1)} %copy-done.8) | copy-start | bytes 1179652
  106.1 10.8 %collective-permute-start.14 = (s16[2,2,3,64,1024]{4,3,2,1,0:T(8,128)(2,1)S(1)}, s16[2,2,3,64,1024]{4,3,2,1,0:T(8,128)(2,1)}, u32[]{:S(2)}, u32[]{:S(2)}) collective-permute-start(s16[2,2,3,64,1024]{4,3,2,1,0:T(8,128)(2,1)S(1)} %pad_add_fusion.held0), channel_id=1, source_target_pairs={{0,4},{4,0},{8,12},{12,8},{16,20},{20,16},{24,28},{28,24},{1,5},{5... | collective-permute-start | bytes 4718600 | tf_op jit(solution)/shard_map/ppermute | solution.py:419
  107.4 5.5 %copy-start.12 = (s16[2,3,16,1024]{3,2,1,0:T(8,128)(2,1)}, s16[2,3,16,1024]{3,2,1,0:T(8,128)(2,1)S(1)}, u32[]{:S(2)}) copy-start(s16[2,3,16,1024]{3,2,1,0:T(8,128)(2,1)S(1)} %collective-permute-done.15.before) | copy-start | bytes 589828
  109.5 3.9 %copy-start.13 = (s16[2,3,16,1024]{3,2,1,0:T(8,128)(2,1)}, s16[2,3,16,1024]{3,2,1,0:T(8,128)(2,1)S(1)}, u32[]{:S(2)}) copy-start(s16[2,3,16,1024]{3,2,1,0:T(8,128)(2,1)S(1)} %collective-permute-done.16.after) | copy-start | bytes 589828
  112.8 4.1 %copy-start.3 = (s16[2,2,3,64,1024]{4,3,2,1,0:T(8,128)(2,1)}, s16[2,2,3,64,1024]{4,3,2,1,0:T(8,128)(2,1)S(1)}, u32[]{:S(2)}) copy-start(s16[2,2,3,64,1024]{4,3,2,1,0:T(8,128)(2,1)S(1)} %pad_add_fusion.1.held1) | copy-start | bytes 4718596
  112.8 4.0 %collective-permute-start.19 = (s16[2,2,3,64,1024]{4,3,2,1,0:T(8,128)(2,1)S(1)}, s16[2,2,3,64,1024]{4,3,2,1,0:T(8,128)(2,1)S(1)}, u32[]{:S(2)}, u32[]{:S(2)}) collective-permute-start(s16[2,2,3,64,1024]{4,3,2,1,0:T(8,128)(2,1)S(1)} %pad_add_fusion.1.held1), channel_id=1, source_target_pairs={{0,4},{4,0},{8,12},{12,8},{16,20},{20,16},{24,28},{28,24},{1,5},{5... | collective-permute-start | bytes 4718600 | tf_op jit(solution)/shard_map/ppermute | solution.py:419
  112.9 3.7 %collective-permute-start.20 = (s16[2,3,16,1024]{3,2,1,0:T(8,128)(2,1)S(1)}, s16[2,3,16,1024]{3,2,1,0:T(8,128)(2,1)S(1)}, u32[]{:S(2)}, u32[]{:S(2)}) collective-permute-start(s16[2,3,16,1024]{3,2,1,0:T(8,128)(2,1)S(1)} %collective-permute-done.15.before), channel_id=1, source_target_pairs={{0,4},{4,0},{8,12},{12,8},{16,20},{20,16},{24,28},{28,24},{1,5},{5... | collective-permute-start | bytes 589832 | tf_op jit(solution)/shard_map/ppermute | solution.py:419
  113.4 3.5 %collective-permute-start.21 = (s16[2,3,16,1024]{3,2,1,0:T(8,128)(2,1)S(1)}, s16[2,3,16,1024]{3,2,1,0:T(8,128)(2,1)S(1)}, u32[]{:S(2)}, u32[]{:S(2)}) collective-permute-start(s16[2,3,16,1024]{3,2,1,0:T(8,128)(2,1)S(1)} %collective-permute-done.16.after), channel_id=1, source_target_pairs={{0,4},{4,0},{8,12},{12,8},{16,20},{20,16},{24,28},{28,24},{1,5},{5... | collective-permute-start | bytes 589832 | tf_op jit(solution)/shard_map/ppermute | solution.py:419
  (7 other events, 12.4 us)

commit v10 on v9

--- a/solution.py
+++ b/solution.py
@@ -413,6 +413,20 @@
     up = [(i, (i + 1) % size) for i in range(size)]
     down = [(j, i) for i, j in up]
     return lax.ppermute(last, "gx", up), lax.ppermute(first, "gx", down)
+
+
+def narrowed(rows, near):
+    high = lax.reduce_precision(rows, 8, 7)
+    low = (rows - high)[:, near]
+    return jnp.concatenate([high, low], 1).astype(jnp.bfloat16)
+
+
+def widened(sent, near):
+    rows = sent[:, :reach].astype(jnp.float32)
+    low = sent[:, reach:].astype(jnp.float32)
+    around = [(0, 0)] * rows.ndim
+    around[1] = (near.start, reach - near.stop)
+    return rows + jnp.pad(low, around)
 
 
 def swap(array, bit):
@@ -498,10 +512,11 @@
     in_pairs = lax.axis_size("pert") == 8
     core = (me % 2 if in_pairs else jnp.zeros_like(me)).astype(jnp.int32)[None]
     field = pert_field[0]
-    last, first, tile = lax.optimization_barrier(
-        (field[:, slab - reach :, 3:5], field[:, :reach, 3:5], tile)
-    )
+    last = narrowed(field[:, slab - reach :, 3:5], slice(reach - 4, reach))
+    first = narrowed(field[:, :reach, 3:5], slice(0, 4))
+    last, first, tile = lax.optimization_barrier((last, first, tile))
     before, after = ring(last, first)
+    before, after = widened(before, slice(reach - 4, reach)), widened(after, slice(0, 4))
     halves = [pack(tile, planes, core, u) for u in range(2)]
     done = {"field": field, "terms": []}
 

time: 141 us -> 148 us (1.050)
  other arithmetic: 21.2 us -> 28.3 us
  waiting for transfers between devices: 18.6 us -> 22.1 us
  local copies, waits for them, and re-layouts: 9.12 us -> 6.72 us
    ppermute x2, waiting for transfers between devices: 5.57 us -> 9.14 us  [ring(): return (lax.ppermute(last, 'gx', up), lax.ppermute(first, 'gx', down))]
    another operation x0 -> x3, other arithmetic: none -> 2.79 us
    add x0 -> x2, other arithmetic: none -> 2.79 us  [widened(): return rows + jnp.pad(low, around)]
    slice x1 -> x3, local copies, waits for them, and re-layouts: 3.26 us -> 0.84 us  [widened(): low = sent[:, reach:].astype(jnp.float32)]
    unnamed x34 -> x38, local copies, waits for them, and re-layouts: 5.87 us -> 5.88 us
  transfers between devices with their start and end apart: 22 -> 22, of which waited for: 7 -> 7; matrix products, arithmetic and copies ran while one was open for 15% -> 15% of each run, Pallas kernels for 25% -> 24%
where the time goes in v10:
time: 148 us; the launch traced here: 147 us
  Pallas kernels  61.1 us (41%)
  other arithmetic  28.3 us (19%)
  starting transfers between devices  26.1 us (18%)
  waiting for transfers between devices  22.1 us (15%)
  local copies, waits for them, and re-layouts  6.72 us (5%)
  between operations  3 us (2%)
    pallas_call x2, Pallas kernels, field_terms(): pl.pallas_call(functools.partial(field_kernel, comps), out_shape=(shape,...  32 us
    pallas_call x1, Pallas kernels, final(): pl.pallas_call(functools.partial(final_kernel, groups), out_shape=jax.Sha...  22.1 us
    ppermute x18, starting transfers between devices, swap(): lax.ppermute(array, 'pert', [(i, i ^ bit) for i in range(lax.axis_size('p...  13.4 us
    ppermute x18, waiting for transfers between devices, swap(): lax.ppermute(array, 'pert', [(i, i ^ bit) for i in range(lax.axis_size('p...  9.68 us
    ppermute x2, waiting for transfers between devices, ring(): return (lax.ppermute(last, 'gx', up), lax.ppermute(first, 'gx', down))  9.14 us
    pallas_call x2, Pallas kernels, pack(): pl.pallas_call(pack_kernel, out_shape=(shape,) * 2, grid=(2, comps), in_s...  7.09 us
    another operation x6, other arithmetic, exchange(): parts.append(jnp.stack(row, 0))  5.97 us
    unnamed x38, local copies, waits for them, and re-layouts  5.88 us
  transfers between devices with their start and end apart: 22, of which 7 were waited for; matrix products, arithmetic and copies ran while one was open for 15% of the time, Pallas kernels for 24%

profile of v10, /device:TPU:0, one launch (start us, length us, event | category | flops | bytes accessed | tf_op | source)
XLA Modules:
  0.0 147.4 jit_solution(9907905265852582948)
XLA Ops:
  0.0 2.7 %fusion.16 = (bf16[3,16,2,1024]{3,2,1,0:T(2,128)(2,1)S(1)}, bf16[3,16,2,1024]{3,2,1,0:T(2,128)(2,1)S(1)}, f32[3,16,2,1024]{3,2,1,0:T(2,128)S(1)}, f32[3,16,2,102...) fusion(f32[3,256,8,1024]{3,2,1,0:T(8,128)} %bitcast.62), kind=kLoop, calls=%fused_computation.59 | loop fusion | flops 393216 | bytes 2752512 | tf_op jit(solution)/shard_map/convert.4
  2.8 1.4 pad_maximum_fusion
  4.3 4.6 %copy-done = bf16[1,3,256,8,1024]{4,3,2,1,0:T(8,128)(2,1)S(1)} copy-done((bf16[1,3,256,8,1024]{4,3,2,1,0:T(8,128)(2,1)S(1)}, bf16[1,3,256,8,1024]{4,3,2,1,0:T(8,128)(2,1)}, u32[]{:S(2)}) %copy-start) | copy-done | bytes 12582936
  8.8 3.6 %shard_map.146 = (s16[2,2,3,64,1024]{4,3,2,1,0:T(8,128)(2,1)S(1)}, s16[2,2,3,64,1024]{4,3,2,1,0:T(8,128)(2,1)}) custom-call(s32[1]{0:T(128)} %bitcast.core, bf16[128,256]{1,0:T(8,128)(2,1)S(1)} %copy-done.1, bf16[3,2048,1024]{2,1,0:T(8,128)(2,1)S(1)} %bitcast.60), custom_call_target="tpu_custom_call" | custom-call | bytes 12582912 | tf_op jit(solution)/shard_map/pallas_call | solution.py:124
  12.8 3.5 %shard_map.145 = (s16[2,2,3,64,1024]{4,3,2,1,0:T(8,128)(2,1)S(1)}, s16[2,2,3,64,1024]{4,3,2,1,0:T(8,128)(2,1)}) custom-call(s32[1]{0:T(128)} %bitcast.core, bf16[128,256]{1,0:T(8,128)(2,1)S(1)} %copy-done.1, bf16[3,2048,1024]{2,1,0:T(8,128)(2,1)S(1)} %bitcast.61), custom_call_target="tpu_custom_call" | custom-call | bytes 12582912 | tf_op jit(solution)/shard_map/pallas_call | solution.py:124
  16.4 3.0 %collective-permute-start.2 = (bf16[3,20,2,1024]{3,2,1,0:T(2,128)(2,1)}, bf16[3,20,2,1024]{3,2,1,0:T(2,128)(2,1)S(1)}, u32[]{:S(2)}, u32[]{:S(2)}) collective-permute-start(bf16[3,20,2,1024]{3,2,1,0:T(2,128)(2,1)} %get-tuple-element.44), channel_id=1, source_target_pairs={{0,1},{1,2},{2,3},{3,0},{4,5},{5,6},{6,7},{7,4},{8,9},{9,10},{10,1... | collective-permute-start | bytes 737288 | tf_op jit(solution)/shard_map/ppermute | solution.py:415
  19.4 2.0 %collective-permute-start.3 = (bf16[3,20,2,1024]{3,2,1,0:T(2,128)(2,1)}, bf16[3,20,2,1024]{3,2,1,0:T(2,128)(2,1)}, u32[]{:S(2)}, u32[]{:S(2)}) collective-permute-start(bf16[3,20,2,1024]{3,2,1,0:T(2,128)(2,1)} %get-tuple-element.45), channel_id=1, source_target_pairs={{1,0},{2,1},{3,2},{0,3},{5,4},{6,5},{7,6},{4,7},{9,8},{10,9},{11,1... | collective-permute-start | bytes 737288 | tf_op jit(solution)/shard_map/ppermute | solution.py:415
  23.5 5.0 %collective-permute-done.2 = bf16[3,20,2,1024]{3,2,1,0:T(2,128)(2,1)S(1)} collective-permute-done((bf16[3,20,2,1024]{3,2,1,0:T(2,128)(2,1)}, bf16[3,20,2,1024]{3,2,1,0:T(2,128)(2,1)S(1)}, u32[]{:S(2)}, u32[]{:S(2)}) %collective-permute-start.2) | collective-permute-done | bytes 245792 | tf_op jit(solution)/shard_map/ppermute | solution.py:415
  28.5 4.2 %collective-permute-done.3 = bf16[3,20,2,1024]{3,2,1,0:T(2,128)(2,1)} collective-permute-done((bf16[3,20,2,1024]{3,2,1,0:T(2,128)(2,1)}, bf16[3,20,2,1024]{3,2,1,0:T(2,128)(2,1)}, u32[]{:S(2)}, u32[]{:S(2)}) %collective-permute-start.3) | collective-permute-done | bytes 245792 | tf_op jit(solution)/shard_map/ppermute | solution.py:415
  33.5 2.3 %fusion.6 = (s16[3,64,1024]{2,1,0:T(8,128)(2,1)}, s16[3,64,1024]{2,1,0:T(8,128)(2,1)}) fusion(s16[2,2,3,64,1024]{4,3,2,1,0:T(8,128)(2,1)} %collective-permute-done.1, s16[2,2,3,64,1024]{4,3,2,1,0:T(8,128)(2,1)S(1)} %get-tuple-element.41, pred[]{:T(512)S(6)} %eq.41), kind=kLoop, calls=%fused_computation.21 | loop fusion | flops 393216 | bytes 2359297 | tf_op jit(solution)/shard_map/jit(_where)/select_n | solution.py:444
  35.8 2.2 %fusion.8 = (s16[3,64,1024]{2,1,0:T(8,128)(2,1)S(1)}, s16[3,64,1024]{2,1,0:T(8,128)(2,1)}) fusion(s16[2,2,3,64,1024]{4,3,2,1,0:T(8,128)(2,1)} %collective-permute-done, s16[2,2,3,64,1024]{4,3,2,1,0:T(8,128)(2,1)S(1)} %get-tuple-element.39, pred[]{:T(512)S(6)} %eq.41), kind=kLoop, calls=%fused_computation.25 | loop fusion | flops 393216 | bytes 2359297 | tf_op jit(solution)/shard_map/jit(_where)/select_n | solution.py:444
  38.0 1.5 %collective-permute-start.4 = (s16[3,64,1024]{2,1,0:T(8,128)(2,1)S(1)}, s16[3,64,1024]{2,1,0:T(8,128)(2,1)}, u32[]{:S(2)}, u32[]{:S(2)}) collective-permute-start(s16[3,64,1024]{2,1,0:T(8,128)(2,1)S(1)} %get-tuple-element.47), channel_id=1, source_target_pairs={{0,16},{4,20},{8,24},{12,28},{16,0},{20,4},{24,8},{28,12},{1,17},{... | collective-permute-start | bytes 1179656 | tf_op jit(solution)/shard_map/ppermute | solution.py:433
  39.5 1.5 %collective-permute-start.5 = (s16[3,64,1024]{2,1,0:T(8,128)(2,1)}, s16[3,64,1024]{2,1,0:T(8,128)(2,1)}, u32[]{:S(2)}, u32[]{:S(2)}) collective-permute-start(s16[3,64,1024]{2,1,0:T(8,128)(2,1)} %get-tuple-element.48), channel_id=1, source_target_pairs={{0,8},{4,12},{8,0},{12,4},{16,24},{20,28},{24,16},{28,20},{1,9},{5... | collective-permute-start | bytes 1179656 | tf_op jit(solution)/shard_map/ppermute | solution.py:433
  42.0 1.8 %convert_add_fusion.after = f32[3,16,2,1024]{3,2,1,0:T(2,128)} fusion(bf16[3,20,2,1024]{3,2,1,0:T(2,128)(2,1)} %collective-permute-done.3, bf16[3,4,2,1024]{3,2,1,0:T(2,128)(2,1)S(1)} %slice.119), kind=kLoop, calls=%fused_computation.36 | loop fusion | flops 294912 | bytes 638976 | tf_op jit(solution)/shard_map/add | solution.py:429
  44.9 11.9 %shard_map.147 = (f32[1,5,2,256,1024]{4,3,2,1,0:T(8,128)}, s32[1]{0:T(128)}) custom-call(f32[1]{0:T(128)} %bitcast.9.viscosity, bf16[256,256]{1,0:T(8,128)(2,1)} %constant.65.clone.turn, bf16[384,160]{1,0:T(8,128)(2,1)} %constant.66.clone.m_all, bf16[256,160]{1,0:T(8,128)(2,1)} %constant.67.clone.m_top, f32[3,16,2,1024]{3,2,1,0:T(2,128)} %convert_add_fusion.1.before, ...), custom_call_target="tpu_custom_call" | custom-call | bytes 16777216 | tf_op jit(solution)/shard_map/pallas_call | solution.py:243
  57.3 2.7 %broadcast_select_fusion.7 = (s16[3,64,1024]{2,1,0:T(8,128)(2,1)}, s16[3,64,1024]{2,1,0:T(8,128)(2,1)S(1)}, s16[3,64,1024]{2,1,0:T(8,128)(2,1)}, s16[3,64,1024]{2,1,0:T(8,128)(2,1)}) fusion(s16[3,64,1024]{2,1,0:T(8,128)(2,1)} %collective-permute-done.4, pred[]{:T(512)S(6)} %eq.44, s16[2,2,3,64,1024]{4,3,2,1,0:T(8,128)(2,1)} %collective-permute-done, ...), kind=kLoop, calls=%fused_computation.45 | loop fusion | flops 786432 | bytes 3932162 | tf_op jit(solution)/shard_map/jit(_where)/select_n | solution.py:461
  60.0 1.5 %collective-permute-start.9 = (s16[3,64,1024]{2,1,0:T(8,128)(2,1)}, s16[3,64,1024]{2,1,0:T(8,128)(2,1)}, u32[]{:S(2)}, u32[]{:S(2)}) collective-permute-start(s16[3,64,1024]{2,1,0:T(8,128)(2,1)} %get-tuple-element.57), channel_id=1, source_target_pairs={{0,8},{4,12},{8,0},{12,4},{16,24},{20,28},{24,16},{28,20},{1,9},{5... | collective-permute-start | bytes 1179656 | tf_op jit(solution)/shard_map/ppermute | solution.py:433
  61.5 1.5 %collective-permute-start.8 = (s16[3,64,1024]{2,1,0:T(8,128)(2,1)}, s16[3,64,1024]{2,1,0:T(8,128)(2,1)}, u32[]{:S(2)}, u32[]{:S(2)}) collective-permute-start(s16[3,64,1024]{2,1,0:T(8,128)(2,1)} %get-tuple-element.56), channel_id=1, source_target_pairs={{0,16},{4,20},{8,24},{12,28},{16,0},{20,4},{24,8},{28,12},{1,17},{... | collective-permute-start | bytes 1179656 | tf_op jit(solution)/shard_map/ppermute | solution.py:433
  63.0 2.8 %broadcast_select_fusion.4 = (s16[3,64,1024]{2,1,0:T(8,128)(2,1)}, s16[3,64,1024]{2,1,0:T(8,128)(2,1)S(1)}, s16[3,64,1024]{2,1,0:T(8,128)(2,1)}, s16[3,64,1024]{2,1,0:T(8,128)(2,1)S(1)}) fusion(s16[3,64,1024]{2,1,0:T(8,128)(2,1)} %collective-permute-done.7, pred[]{:T(512)S(6)} %eq.45, s16[2,2,3,64,1024]{4,3,2,1,0:T(8,128)(2,1)} %collective-permute-done.1, ...), kind=kLoop, calls=%fused_computation.42 | loop fusion | flops 786432 | bytes 3932162 | tf_op jit(solution)/shard_map/jit(_where)/select_n | solution.py:462
  66.8 20.1 %shard_map.148 = (f32[2,5,2,256,1024]{4,3,2,1,0:T(8,128)}, s32[1]{0:T(128)}) custom-call(f32[1]{0:T(128)} %bitcast.9.viscosity, bf16[256,256]{1,0:T(8,128)(2,1)} %constant.65.clone.turn, bf16[384,160]{1,0:T(8,128)(2,1)} %constant.66.clone.m_all, bf16[256,160]{1,0:T(8,128)(2,1)} %constant.67.clone.m_top, f32[3,16,2,1024]{3,2,1,0:T(2,128)} %convert_add_fusion.1.before, ...), custom_call_target="tpu_custom_call" | custom-call | bytes 33554432 | tf_op jit(solution)/shard_map/pallas_call | solution.py:243
  89.8 1.3 collective-permute-start.12
  91.1 1.7 %collective-permute-start.13 = (s16[3,64,1024]{2,1,0:T(8,128)(2,1)S(1)}, s16[3,64,1024]{2,1,0:T(8,128)(2,1)S(1)}, u32[]{:S(2)}, u32[]{:S(2)}) collective-permute-start(s16[3,64,1024]{2,1,0:T(8,128)(2,1)S(1)} %broadcast_select_fusion.2), channel_id=1, source_target_pairs={{0,16},{4,20},{8,24},{12,28},{16,0},{20,4},{24,8},{28,12},{1,17},{... | collective-permute-start | bytes 1179656 | tf_op jit(solution)/shard_map/ppermute | solution.py:433
  95.8 6.3 %collective-permute-done.12 = s16[3,64,1024]{2,1,0:T(8,128)(2,1)} collective-permute-done((s16[3,64,1024]{2,1,0:T(8,128)(2,1)S(1)}, s16[3,64,1024]{2,1,0:T(8,128)(2,1)}, u32[]{:S(2)}, u32[]{:S(2)}) %collective-permute-start.12) | collective-permute-done | bytes 393248 | tf_op jit(solution)/shard_map/ppermute | solution.py:433
  102.0 1.5 %select_bitcast_fusion.7 = (s16[1,3,64,1024]{3,2,1,0:T(8,128)(2,1)S(1)}, s16[1,3,64,1024]{3,2,1,0:T(8,128)(2,1)S(1)}) fusion(s16[3,64,1024]{2,1,0:T(8,128)(2,1)} %get-tuple-element.48, s16[3,64,1024]{2,1,0:T(8,128)(2,1)} %collective-permute-done.5, s16[3,64,1024]{2,1,0:T(8,128)(2,1)} %collective-permute-done.12, ...), kind=kLoop, calls=%fused_computation.35 | loop fusion | flops 983040 | bytes 2752515 | tf_op jit(solution)/shard_map/stack | solution.py:481
  103.6 1.5 %select_bitcast_fusion.6 = (s16[1,3,64,1024]{3,2,1,0:T(8,128)(2,1)S(1)}, s16[1,3,64,1024]{3,2,1,0:T(8,128)(2,1)S(1)}) fusion(s16[3,64,1024]{2,1,0:T(8,128)(2,1)S(1)} %copy-done.7, s16[3,64,1024]{2,1,0:T(8,128)(2,1)} %collective-permute-done.4, s16[3,64,1024]{2,1,0:T(8,128)(2,1)S(1)} %collective-permute-done.13, ...), kind=kLoop, calls=%fused_computation.34 | loop fusion | flops 983040 | bytes 2752515 | tf_op jit(solution)/shard_map/stack | solution.py:481
  105.1 3.0 %collective-permute-start.15 = (s16[2,3,16,1024]{3,2,1,0:T(8,128)(2,1)S(1)}, s16[2,3,16,1024]{3,2,1,0:T(8,128)(2,1)S(1)}, u32[]{:S(2)}, u32[]{:S(2)}) collective-permute-start(s16[2,3,16,1024]{3,2,1,0:T(8,128)(2,1)S(1)} %fusion.10), channel_id=1, source_target_pairs={{0,1},{1,2},{2,3},{3,0},{8,9},{9,10},{10,11},{11,8},{16,17},{17,18... | collective-permute-start | bytes 589832 | tf_op jit(solution)/shard_map/ppermute | solution.py:492
  108.1 4.6 %collective-permute-start.16 = (s16[2,3,16,1024]{3,2,1,0:T(8,128)(2,1)S(1)}, s16[2,3,16,1024]{3,2,1,0:T(8,128)(2,1)S(1)}, u32[]{:S(2)}, u32[]{:S(2)}) collective-permute-start(s16[2,3,16,1024]{3,2,1,0:T(8,128)(2,1)S(1)} %fusion.11), channel_id=1, source_target_pairs={{1,0},{2,1},{3,2},{0,3},{9,8},{10,9},{11,10},{8,11},{17,16},{18,17... | collective-permute-start | bytes 589832 | tf_op jit(solution)/shard_map/ppermute | solution.py:493
  114.5 2.0 %collective-permute-done.16.after = s16[2,3,16,1024]{3,2,1,0:T(8,128)(2,1)S(1)} collective-permute-done((s16[2,3,16,1024]{3,2,1,0:T(8,128)(2,1)S(1)}, s16[2,3,16,1024]{3,2,1,0:T(8,128)(2,1)S(1)}, u32[]{:S(2)}, u32[]{:S(2)}) %collective-permute-start.16) | collective-permute-done | bytes 196640 | tf_op jit(solution)/shard_map/ppermute | solution.py:493
  116.6 1.6 %select_bitcast_fusion.2 = (s16[1,3,64,1024]{3,2,1,0:T(8,128)(2,1)S(1)}, s16[1,3,64,1024]{3,2,1,0:T(8,128)(2,1)S(1)}) fusion(s16[3,64,1024]{2,1,0:T(8,128)(2,1)} %get-tuple-element.51, s16[3,64,1024]{2,1,0:T(8,128)(2,1)} %collective-permute-done.6, s16[3,64,1024]{2,1,0:T(8,128)(2,1)} %collective-permute-done.18, s16[3,64,1024]{2,1,0:T(8,128)(2,1)S(1)} %copy-done.11, ...), kind=kLoop, calls=%fused_computation.30 | loop fusion | flops 983040 | bytes 2752515 | tf_op jit(solution)/shard_map/stack | solution.py:481
  118.2 1.4 select_bitcast_fusion.3
  120.6 3.1 %collective-permute-done.20.before2 = s16[2,3,16,1024]{3,2,1,0:T(8,128)(2,1)S(1)} collective-permute-done((s16[2,3,16,1024]{3,2,1,0:T(8,128)(2,1)S(1)}, s16[2,3,16,1024]{3,2,1,0:T(8,128)(2,1)S(1)}, u32[]{:S(2)}, u32[]{:S(2)}) %collective-permute-start.20) | collective-permute-done | bytes 196640 | tf_op jit(solution)/shard_map/ppermute | solution.py:433
  125.2 22.1 %shard_map.149 = f32[1,3,256,2,1024]{4,3,2,1,0:T(2,128)} custom-call(s32[1]{0:T(128)} %bitcast.core, bf16[128,96]{1,0:T(8,128)(2,1)} %constant.68.clone.m_both, bf16[256,128]{1,0:T(8,128)(2,1)} %constant.69.clone.turn, s16[2,2,3,64,1024]{4,3,2,1,0:T(8,128)(2,1)} %copy-done.2, s16[2,2,3,64,1024]{4,3,2,1,0:T(8,128)(2,1)} %collective-permute-done.14.other0, ...), custom_call_target="tpu_custom_call" | custom-call | bytes 12582912 | tf_op jit(solution)/shard_map/pallas_call | solution.py:382
  (85 shorter events, 14.6 us)
Async XLA Ops:
  12.4 10.4 %copy-start.18 = (f32[64]{0:T(128)S(1)}, f32[64]{0:T(128)}, u32[]{:S(2)}) copy-start(f32[64]{0:T(128)} %param.19) | copy-start | bytes 772
  12.4 21.1 %collective-permute-start.1 = (s16[2,2,3,64,1024]{4,3,2,1,0:T(8,128)(2,1)}, s16[2,2,3,64,1024]{4,3,2,1,0:T(8,128)(2,1)}, u32[]{:S(2)}, u32[]{:S(2)}) collective-permute-start(s16[2,2,3,64,1024]{4,3,2,1,0:T(8,128)(2,1)} %get-tuple-element.42), channel_id=1, source_target_pairs={{0,4},{4,0},{8,12},{12,8},{16,20},{20,16},{24,28},{28,24},{1,5},{5... | collective-permute-start | bytes 4718600 | tf_op jit(solution)/shard_map/ppermute | solution.py:433
  16.4 19.4 %collective-permute-start = (s16[2,2,3,64,1024]{4,3,2,1,0:T(8,128)(2,1)}, s16[2,2,3,64,1024]{4,3,2,1,0:T(8,128)(2,1)}, u32[]{:S(2)}, u32[]{:S(2)}) collective-permute-start(s16[2,2,3,64,1024]{4,3,2,1,0:T(8,128)(2,1)} %get-tuple-element.40), channel_id=1, source_target_pairs={{0,4},{4,0},{8,12},{12,8},{16,20},{20,16},{24,28},{28,24},{1,5},{5... | collective-permute-start | bytes 4718600 | tf_op jit(solution)/shard_map/ppermute | solution.py:433
  16.4 12.1 %collective-permute-start.2 = (bf16[3,20,2,1024]{3,2,1,0:T(2,128)(2,1)}, bf16[3,20,2,1024]{3,2,1,0:T(2,128)(2,1)S(1)}, u32[]{:S(2)}, u32[]{:S(2)}) collective-permute-start(bf16[3,20,2,1024]{3,2,1,0:T(2,128)(2,1)} %get-tuple-element.44), channel_id=1, source_target_pairs={{0,1},{1,2},{2,3},{3,0},{4,5},{5,6},{6,7},{7,4},{8,9},{9,10},{10,1... | collective-permute-start | bytes 737288 | tf_op jit(solution)/shard_map/ppermute | solution.py:415
  19.4 13.2 %collective-permute-start.3 = (bf16[3,20,2,1024]{3,2,1,0:T(2,128)(2,1)}, bf16[3,20,2,1024]{3,2,1,0:T(2,128)(2,1)}, u32[]{:S(2)}, u32[]{:S(2)}) collective-permute-start(bf16[3,20,2,1024]{3,2,1,0:T(2,128)(2,1)} %get-tuple-element.45), channel_id=1, source_target_pairs={{1,0},{2,1},{3,2},{0,3},{5,4},{6,5},{7,6},{4,7},{9,8},{10,9},{11,1... | collective-permute-start | bytes 737288 | tf_op jit(solution)/shard_map/ppermute | solution.py:415
  28.5 7.3 %copy-start.12 = (bf16[3,20,2,1024]{3,2,1,0:T(2,128)(2,1)}, bf16[3,20,2,1024]{3,2,1,0:T(2,128)(2,1)S(1)}, u32[]{:S(2)}) copy-start(bf16[3,20,2,1024]{3,2,1,0:T(2,128)(2,1)S(1)} %collective-permute-done.2) | copy-start | bytes 737284
  35.8 5.2 %copy-start.13 = (bf16[3,20,2,1024]{3,2,1,0:T(2,128)(2,1)S(1)}, bf16[3,20,2,1024]{3,2,1,0:T(2,128)(2,1)}, u32[]{:S(2)}) copy-start(bf16[3,20,2,1024]{3,2,1,0:T(2,128)(2,1)} %copy-done.12) | copy-start | bytes 737284
  35.8 5.2 %slice-start = ((bf16[3,20,2,1024]{3,2,1,0:T(2,128)(2,1)}), bf16[3,4,2,1024]{3,2,1,0:T(2,128)(2,1)S(1)}, s32[]{:S(2)}) async-start(bf16[3,20,2,1024]{3,2,1,0:T(2,128)(2,1)} %copy-done.12), calls=%async_computation | async-start | bytes 98304 | tf_op jit(solution)/shard_map/slice | solution.py:426
  38.0 18.7 %copy-start.6 = (s16[3,64,1024]{2,1,0:T(8,128)(2,1)}, s16[3,64,1024]{2,1,0:T(8,128)(2,1)S(1)}, u32[]{:S(2)}) copy-start(s16[3,64,1024]{2,1,0:T(8,128)(2,1)S(1)} %get-tuple-element.47) | copy-start | bytes 1179652
  38.0 19.3 %collective-permute-start.4 = (s16[3,64,1024]{2,1,0:T(8,128)(2,1)S(1)}, s16[3,64,1024]{2,1,0:T(8,128)(2,1)}, u32[]{:S(2)}, u32[]{:S(2)}) collective-permute-start(s16[3,64,1024]{2,1,0:T(8,128)(2,1)S(1)} %get-tuple-element.47), channel_id=1, source_target_pairs={{0,16},{4,20},{8,24},{12,28},{16,0},{20,4},{24,8},{28,12},{1,17},{... | collective-permute-start | bytes 1179656 | tf_op jit(solution)/shard_map/ppermute | solution.py:433
  39.5 17.8 %collective-permute-start.5 = (s16[3,64,1024]{2,1,0:T(8,128)(2,1)}, s16[3,64,1024]{2,1,0:T(8,128)(2,1)}, u32[]{:S(2)}, u32[]{:S(2)}) collective-permute-start(s16[3,64,1024]{2,1,0:T(8,128)(2,1)} %get-tuple-element.48), channel_id=1, source_target_pairs={{0,8},{4,12},{8,0},{12,4},{16,24},{20,28},{24,16},{28,20},{1,9},{5... | collective-permute-start | bytes 1179656 | tf_op jit(solution)/shard_map/ppermute | solution.py:433
  43.8 19.2 %collective-permute-start.6 = (s16[3,64,1024]{2,1,0:T(8,128)(2,1)}, s16[3,64,1024]{2,1,0:T(8,128)(2,1)}, u32[]{:S(2)}, u32[]{:S(2)}) collective-permute-start(s16[3,64,1024]{2,1,0:T(8,128)(2,1)} %get-tuple-element.51), channel_id=1, source_target_pairs={{0,16},{4,20},{8,24},{12,28},{16,0},{20,4},{24,8},{28,12},{1,17},{... | collective-permute-start | bytes 1179656 | tf_op jit(solution)/shard_map/ppermute | solution.py:433
  44.3 18.7 %collective-permute-start.7 = (s16[3,64,1024]{2,1,0:T(8,128)(2,1)}, s16[3,64,1024]{2,1,0:T(8,128)(2,1)}, u32[]{:S(2)}, u32[]{:S(2)}) collective-permute-start(s16[3,64,1024]{2,1,0:T(8,128)(2,1)} %get-tuple-element.52), channel_id=1, source_target_pairs={{0,8},{4,12},{8,0},{12,4},{16,24},{20,28},{24,16},{28,20},{1,9},{5... | collective-permute-start | bytes 1179656 | tf_op jit(solution)/shard_map/ppermute | solution.py:433
  60.0 27.5 %collective-permute-start.9 = (s16[3,64,1024]{2,1,0:T(8,128)(2,1)}, s16[3,64,1024]{2,1,0:T(8,128)(2,1)}, u32[]{:S(2)}, u32[]{:S(2)}) collective-permute-start(s16[3,64,1024]{2,1,0:T(8,128)(2,1)} %get-tuple-element.57), channel_id=1, source_target_pairs={{0,8},{4,12},{8,0},{12,4},{16,24},{20,28},{24,16},{28,20},{1,9},{5... | collective-permute-start | bytes 1179656 | tf_op jit(solution)/shard_map/ppermute | solution.py:433
  61.5 27.2 %collective-permute-start.8 = (s16[3,64,1024]{2,1,0:T(8,128)(2,1)}, s16[3,64,1024]{2,1,0:T(8,128)(2,1)}, u32[]{:S(2)}, u32[]{:S(2)}) collective-permute-start(s16[3,64,1024]{2,1,0:T(8,128)(2,1)} %get-tuple-element.56), channel_id=1, source_target_pairs={{0,16},{4,20},{8,24},{12,28},{16,0},{20,4},{24,8},{28,12},{1,17},{... | collective-permute-start | bytes 1179656 | tf_op jit(solution)/shard_map/ppermute | solution.py:433
  65.8 28.0 %collective-permute-start.10 = (s16[3,64,1024]{2,1,0:T(8,128)(2,1)}, s16[3,64,1024]{2,1,0:T(8,128)(2,1)S(1)}, u32[]{:S(2)}, u32[]{:S(2)}) collective-permute-start(s16[3,64,1024]{2,1,0:T(8,128)(2,1)} %get-tuple-element.59), channel_id=1, source_target_pairs={{0,16},{4,20},{8,24},{12,28},{16,0},{20,4},{24,8},{28,12},{1,17},{... | collective-permute-start | bytes 1179656 | tf_op jit(solution)/shard_map/ppermute | solution.py:433
  66.0 26.8 %collective-permute-start.11 = (s16[3,64,1024]{2,1,0:T(8,128)(2,1)}, s16[3,64,1024]{2,1,0:T(8,128)(2,1)S(1)}, u32[]{:S(2)}, u32[]{:S(2)}) collective-permute-start(s16[3,64,1024]{2,1,0:T(8,128)(2,1)} %get-tuple-element.60), channel_id=1, source_target_pairs={{0,8},{4,12},{8,0},{12,4},{16,24},{20,28},{24,16},{28,20},{1,9},{5... | collective-permute-start | bytes 1179656 | tf_op jit(solution)/shard_map/ppermute | solution.py:433
  66.8 21.8 %copy-start.4 = (s16[3,64,1024]{2,1,0:T(8,128)(2,1)S(1)}, s16[3,64,1024]{2,1,0:T(8,128)(2,1)}, u32[]{:S(2)}) copy-start(s16[3,64,1024]{2,1,0:T(8,128)(2,1)} %get-tuple-element.88) | copy-start | bytes 1179652
  89.8 12.2 %collective-permute-start.12 = (s16[3,64,1024]{2,1,0:T(8,128)(2,1)S(1)}, s16[3,64,1024]{2,1,0:T(8,128)(2,1)}, u32[]{:S(2)}, u32[]{:S(2)}) collective-permute-start(s16[3,64,1024]{2,1,0:T(8,128)(2,1)S(1)} %broadcast_select_fusion.3), channel_id=1, source_target_pairs={{0,8},{4,12},{8,0},{12,4},{16,24},{20,28},{24,16},{28,20},{1,9},{5... | collective-permute-start | bytes 1179656 | tf_op jit(solution)/shard_map/ppermute | solution.py:433
  91.1 12.4 %collective-permute-start.13 = (s16[3,64,1024]{2,1,0:T(8,128)(2,1)S(1)}, s16[3,64,1024]{2,1,0:T(8,128)(2,1)S(1)}, u32[]{:S(2)}, u32[]{:S(2)}) collective-permute-start(s16[3,64,1024]{2,1,0:T(8,128)(2,1)S(1)} %broadcast_select_fusion.2), channel_id=1, source_target_pairs={{0,16},{4,20},{8,24},{12,28},{16,0},{20,4},{24,8},{28,12},{1,17},{... | collective-permute-start | bytes 1179656 | tf_op jit(solution)/shard_map/ppermute | solution.py:433
  94.7 8.8 %copy-start.7 = (s16[3,64,1024]{2,1,0:T(8,128)(2,1)S(1)}, s16[3,64,1024]{2,1,0:T(8,128)(2,1)}, u32[]{:S(2)}) copy-start(s16[3,64,1024]{2,1,0:T(8,128)(2,1)} %copy-done.6) | copy-start | bytes 1179652
  94.7 23.4 %collective-permute-start.17 = (s16[3,64,1024]{2,1,0:T(8,128)(2,1)}, s16[3,64,1024]{2,1,0:T(8,128)(2,1)}, u32[]{:S(2)}, u32[]{:S(2)}) collective-permute-start(s16[3,64,1024]{2,1,0:T(8,128)(2,1)} %broadcast_select_fusion.1), channel_id=1, source_target_pairs={{0,8},{4,12},{8,0},{12,4},{16,24},{20,28},{24,16},{28,20},{1,9},{5... | collective-permute-start | bytes 1179656 | tf_op jit(solution)/shard_map/ppermute | solution.py:433
  94.8 21.8 %collective-permute-start.18 = (s16[3,64,1024]{2,1,0:T(8,128)(2,1)}, s16[3,64,1024]{2,1,0:T(8,128)(2,1)}, u32[]{:S(2)}, u32[]{:S(2)}) collective-permute-start(s16[3,64,1024]{2,1,0:T(8,128)(2,1)} %broadcast_select_fusion), channel_id=1, source_target_pairs={{0,16},{4,20},{8,24},{12,28},{16,0},{20,4},{24,8},{28,12},{1,17},{... | collective-permute-start | bytes 1179656 | tf_op jit(solution)/shard_map/ppermute | solution.py:433
  105.1 9.4 %collective-permute-start.15 = (s16[2,3,16,1024]{3,2,1,0:T(8,128)(2,1)S(1)}, s16[2,3,16,1024]{3,2,1,0:T(8,128)(2,1)S(1)}, u32[]{:S(2)}, u32[]{:S(2)}) collective-permute-start(s16[2,3,16,1024]{3,2,1,0:T(8,128)(2,1)S(1)} %fusion.10), channel_id=1, source_target_pairs={{0,1},{1,2},{2,3},{3,0},{8,9},{9,10},{10,11},{11,8},{16,17},{17,18... | collective-permute-start | bytes 589832 | tf_op jit(solution)/shard_map/ppermute | solution.py:492
  108.1 8.4 %collective-permute-start.16 = (s16[2,3,16,1024]{3,2,1,0:T(8,128)(2,1)S(1)}, s16[2,3,16,1024]{3,2,1,0:T(8,128)(2,1)S(1)}, u32[]{:S(2)}, u32[]{:S(2)}) collective-permute-start(s16[2,3,16,1024]{3,2,1,0:T(8,128)(2,1)S(1)} %fusion.11), channel_id=1, source_target_pairs={{1,0},{2,1},{3,2},{0,3},{9,8},{10,9},{11,10},{8,11},{17,16},{18,17... | collective-permute-start | bytes 589832 | tf_op jit(solution)/shard_map/ppermute | solution.py:493
  113.1 6.4 %copy-start.2 = (s16[2,2,3,64,1024]{4,3,2,1,0:T(8,128)(2,1)}, s16[2,2,3,64,1024]{4,3,2,1,0:T(8,128)(2,1)S(1)}, u32[]{:S(2)}) copy-start(s16[2,2,3,64,1024]{4,3,2,1,0:T(8,128)(2,1)S(1)} %pad_add_fusion.held0) | copy-start | bytes 4718596
  113.1 5.0 %copy-start.9 = (s16[3,64,1024]{2,1,0:T(8,128)(2,1)S(1)}, s16[3,64,1024]{2,1,0:T(8,128)(2,1)}, u32[]{:S(2)}) copy-start(s16[3,64,1024]{2,1,0:T(8,128)(2,1)} %copy-done.8) | copy-start | bytes 1179652
  113.2 10.8 %collective-permute-start.14 = (s16[2,2,3,64,1024]{4,3,2,1,0:T(8,128)(2,1)S(1)}, s16[2,2,3,64,1024]{4,3,2,1,0:T(8,128)(2,1)}, u32[]{:S(2)}, u32[]{:S(2)}) collective-permute-start(s16[2,2,3,64,1024]{4,3,2,1,0:T(8,128)(2,1)S(1)} %pad_add_fusion.held0), channel_id=1, source_target_pairs={{0,4},{4,0},{8,12},{12,8},{16,20},{20,16},{24,28},{28,24},{1,5},{5... | collective-permute-start | bytes 4718600 | tf_op jit(solution)/shard_map/ppermute | solution.py:433
  114.5 5.4 %copy-start.14 = (s16[2,3,16,1024]{3,2,1,0:T(8,128)(2,1)}, s16[2,3,16,1024]{3,2,1,0:T(8,128)(2,1)S(1)}, u32[]{:S(2)}) copy-start(s16[2,3,16,1024]{3,2,1,0:T(8,128)(2,1)S(1)} %collective-permute-done.15.before) | copy-start | bytes 589828
  119.9 4.0 %collective-permute-start.19 = (s16[2,2,3,64,1024]{4,3,2,1,0:T(8,128)(2,1)S(1)}, s16[2,2,3,64,1024]{4,3,2,1,0:T(8,128)(2,1)S(1)}, u32[]{:S(2)}, u32[]{:S(2)}) collective-permute-start(s16[2,2,3,64,1024]{4,3,2,1,0:T(8,128)(2,1)S(1)} %pad_add_fusion.1.held1), channel_id=1, source_target_pairs={{0,4},{4,0},{8,12},{12,8},{16,20},{20,16},{24,28},{28,24},{1,5},{5... | collective-permute-start | bytes 4718600 | tf_op jit(solution)/shard_map/ppermute | solution.py:433
  120.0 3.7 %collective-permute-start.20 = (s16[2,3,16,1024]{3,2,1,0:T(8,128)(2,1)S(1)}, s16[2,3,16,1024]{3,2,1,0:T(8,128)(2,1)S(1)}, u32[]{:S(2)}, u32[]{:S(2)}) collective-permute-start(s16[2,3,16,1024]{3,2,1,0:T(8,128)(2,1)S(1)} %collective-permute-done.15.before), channel_id=1, source_target_pairs={{0,4},{4,0},{8,12},{12,8},{16,20},{20,16},{24,28},{28,24},{1,5},{5... | collective-permute-start | bytes 589832 | tf_op jit(solution)/shard_map/ppermute | solution.py:433
  120.5 3.5 %collective-permute-start.21 = (s16[2,3,16,1024]{3,2,1,0:T(8,128)(2,1)S(1)}, s16[2,3,16,1024]{3,2,1,0:T(8,128)(2,1)S(1)}, u32[]{:S(2)}, u32[]{:S(2)}) collective-permute-start(s16[2,3,16,1024]{3,2,1,0:T(8,128)(2,1)S(1)} %collective-permute-done.16.after), channel_id=1, source_target_pairs={{0,4},{4,0},{8,12},{12,8},{16,20},{20,16},{24,28},{28,24},{1,5},{5... | collective-permute-start | bytes 589832 | tf_op jit(solution)/shard_map/ppermute | solution.py:433
  (10 other events, 25.9 us)

commit v11 on v9

--- a/solution.py
+++ b/solution.py
@@ -146,7 +146,7 @@
     inner, depth, along, across, sums = terms
 
     def send(i, n, p):
-        return pltpu.make_async_copy(terms[n].at[0, p], out.at[i, n, p], left.at[n, p])
+        return pltpu.make_async_copy(terms[n].at[i, p], out.at[i, n, p], left.at[i, n, p])
 
     slab, width = inner.shape[2:]
     planes = field.shape[1] // slab
@@ -174,9 +174,9 @@
                     d1, d2, d3 = plane[z - 1], plane[z - 2], plane[z - 3]
                     slope = 0.75 * (u1 - d1) - 0.15 * (u2 - d2) + (1.0 / 60.0) * (u3 - d3)
                     curve = 1.5 * (u1 + d1) - 0.15 * (u2 + d2) + (1.0 / 90.0) * (u3 + d3)
-                    inner[(0, p) + at] = centre
-                    depth[(0, p) + at] = slope
-                    sums[(0, p) + at] = centre + gain * (curve - (49.0 / 18.0) * centre)
+                    inner[(i, p) + at] = centre
+                    depth[(i, p) + at] = slope
+                    sums[(i, p) + at] = centre + gain * (curve - (49.0 / 18.0) * centre)
                 return carry
 
             lax.fori_loop(0, slab // 8, unpack, 0, unroll=4)
@@ -197,7 +197,7 @@
                 start = pl.multiple_of(r * 16, 16)
                 at = pl.ds(start, 16)
                 to = pl.ds(pl.multiple_of(start + reach, 16), 16)
-                high, low = split(inner[0, p, at, :])
+                high, low = split(inner[i, p, at, :])
                 high_x[to, :] = high
                 low_x[to, :] = low
                 high_s[at, :] = half_turned(high)
@@ -210,19 +210,20 @@
                 at = pl.ds(b * rows, rows)
                 one = product(m_all[...], high_x[window, :])
                 two = product(m_top[...], low_x[window, :])
-                along[0, p, at, :] = one[:rows] + one[2 * rows :] + two[:rows]
+                along[i, p, at, :] = one[:rows] + one[2 * rows :] + two[:rows]
                 curve = (gain / 180.0) * (one[rows : 2 * rows] + two[rows:])
-                sums[0, p, at, :] = sums[0, p, at, :] + curve
+                sums[i, p, at, :] = sums[i, p, at, :] + curve
             send(i, 2, p).start()
             for t in range(tiles):
                 side = pl.ds(t * lanes, lanes)
                 window = pl.ds(t * lanes, 2 * lanes)
                 both = product(high_s[:, window], turn[...]) + product(low_s[:, window], turn[...])
-                across[0, p, :, side] = both[:, :lanes] * (1.0 / 60.0)
+                across[i, p, :, side] = both[:, :lanes] * (1.0 / 60.0)
                 curve = both[:, lanes:] * (gain / 180.0)
-                sums[0, p, :, side] = sums[0, p, :, side] + curve
+                sums[i, p, :, side] = sums[i, p, :, side] + curve
             send(i, 3, p).start()
             send(i, 4, p).start()
+    for i in range(len(comps)):
         for n in range(5):
             for p in range(2):
                 send(i, n, p).wait()
@@ -248,7 +249,7 @@
         + [pl.BlockSpec(memory_space=pl.ANY)],
         out_specs=(spec, pl.BlockSpec(memory_space=pltpu.SMEM)),
         compiler_params=grant(room),
-        scratch_shapes=[pltpu.VMEM((1, 2, slab, width), jnp.float32)] * 5
+        scratch_shapes=[pltpu.VMEM((len(comps), 2, slab, width), jnp.float32)] * 5
         + [
             pltpu.VMEM((width // lanes, slab * planes, lanes), jnp.float32),
             pltpu.VMEM((slab, width + lanes), jnp.bfloat16),
@@ -256,7 +257,7 @@
             pltpu.VMEM((slab + 2 * reach, width), jnp.bfloat16),
             pltpu.VMEM((slab + 2 * reach, width), jnp.bfloat16),
             pltpu.SemaphoreType.DMA((width // lanes,)),
-            pltpu.SemaphoreType.DMA((5, 2)),
+            pltpu.SemaphoreType.DMA((len(comps), 5, 2)),
         ],
         cost_estimate=pl.CostEstimate(
             flops=0, bytes_accessed=4 * len(comps) * slab * planes * width * 2, transcendentals=0

time: 141 us -> 139 us (0.986)
  other arithmetic: 21.2 us -> 18.9 us
  starting transfers between devices: 27.5 us -> 29.5 us
    ppermute x18, starting transfers between devices: 14.8 us -> 16.8 us  [swap(): lax.ppermute(array, 'pert', [(i, i ^ bit) for i in range(lax.axis_size('p...]
  transfers between devices with their start and end apart: 22 -> 22, of which waited for: 7 -> 8; matrix products, arithmetic and copies ran while one was open for 15% -> 14% of each run, Pallas kernels for 25% -> 25%
where the time goes in v11:
time: 139 us
  Pallas kernels  59.6 us (43%)
  starting transfers between devices  29.5 us (21%)
  other arithmetic  18.9 us (14%)
  waiting for transfers between devices  18.8 us (14%)
  local copies, waits for them, and re-layouts  9.12 us (7%)
  between operations  2.93 us (2%)
    pallas_call x2, Pallas kernels, field_terms(): pl.pallas_call(functools.partial(field_kernel, comps), out_shape=(shape,...  30.5 us
    pallas_call x1, Pallas kernels, final(): pl.pallas_call(functools.partial(final_kernel, groups), out_shape=jax.Sha...  22 us
    ppermute x18, starting transfers between devices, swap(): lax.ppermute(array, 'pert', [(i, i ^ bit) for i in range(lax.axis_size('p...  16.8 us
    ppermute x18, waiting for transfers between devices, swap(): lax.ppermute(array, 'pert', [(i, i ^ bit) for i in range(lax.axis_size('p...  9.94 us
    pallas_call x2, Pallas kernels, pack(): pl.pallas_call(pack_kernel, out_shape=(shape,) * 2, grid=(2, comps), in_s...  7.04 us
    another operation x6, other arithmetic, exchange(): parts.append(jnp.stack(row, 0))  6.03 us
    unnamed x34, local copies, waits for them, and re-layouts  5.87 us
    ppermute x2, waiting for transfers between devices, ring(): return (lax.ppermute(last, 'gx', up), lax.ppermute(first, 'gx', down))  5.57 us
  transfers between devices with their start and end apart: 22, of which 8 were waited for; matrix products, arithmetic and copies ran while one was open for 14% of the time, Pallas kernels for 25%

profile of v11, /device:TPU:0, one launch (start us, length us, event | category | flops | bytes accessed | tf_op | source)
XLA Modules:
  0.0 138.9 jit_solution(1111247864105913686)
XLA Ops:
  0.0 3.3 %fusion.17 = (f32[3,16,2,1024]{3,2,1,0:T(2,128)}, f32[3,16,2,1024]{3,2,1,0:T(2,128)}) fusion(f32[3,256,8,1024]{3,2,1,0:T(8,128)} %bitcast.62), kind=kLoop, calls=%fused_computation.48 | loop fusion | bytes 1572864 | tf_op jit(solution)/shard_map/slice | solution.py:503
  3.3 4.6 %copy-done = bf16[1,3,256,8,1024]{4,3,2,1,0:T(8,128)(2,1)S(1)} copy-done((bf16[1,3,256,8,1024]{4,3,2,1,0:T(8,128)(2,1)S(1)}, bf16[1,3,256,8,1024]{4,3,2,1,0:T(8,128)(2,1)}, u32[]{:S(2)}) %copy-start) | copy-done | bytes 12582936
  7.8 3.5 %shard_map.146 = (s16[2,2,3,64,1024]{4,3,2,1,0:T(8,128)(2,1)S(1)}, s16[2,2,3,64,1024]{4,3,2,1,0:T(8,128)(2,1)}) custom-call(s32[1]{0:T(128)} %bitcast.core, bf16[128,256]{1,0:T(8,128)(2,1)S(1)} %copy-done.1, bf16[3,2048,1024]{2,1,0:T(8,128)(2,1)S(1)} %bitcast.60), custom_call_target="tpu_custom_call" | custom-call | bytes 12582912 | tf_op jit(solution)/shard_map/pallas_call | solution.py:124
  11.8 3.5 %shard_map.145 = (s16[2,2,3,64,1024]{4,3,2,1,0:T(8,128)(2,1)S(1)}, s16[2,2,3,64,1024]{4,3,2,1,0:T(8,128)(2,1)}) custom-call(s32[1]{0:T(128)} %bitcast.core, bf16[128,256]{1,0:T(8,128)(2,1)S(1)} %copy-done.1, bf16[3,2048,1024]{2,1,0:T(8,128)(2,1)S(1)} %bitcast.61), custom_call_target="tpu_custom_call" | custom-call | bytes 12582912 | tf_op jit(solution)/shard_map/pallas_call | solution.py:124
  15.4 3.0 %collective-permute-start.2 = (f32[3,16,2,1024]{3,2,1,0:T(2,128)}, f32[3,16,2,1024]{3,2,1,0:T(2,128)}, u32[]{:S(2)}, u32[]{:S(2)}) collective-permute-start(f32[3,16,2,1024]{3,2,1,0:T(2,128)} %get-tuple-element.44), channel_id=1, source_target_pairs={{0,1},{1,2},{2,3},{3,0},{4,5},{5,6},{6,7},{7,4},{8,9},{9,10},{10,1... | collective-permute-start | bytes 1179656 | tf_op jit(solution)/shard_map/ppermute | solution.py:416
  18.4 2.0 %collective-permute-start.3 = (f32[3,16,2,1024]{3,2,1,0:T(2,128)}, f32[3,16,2,1024]{3,2,1,0:T(2,128)}, u32[]{:S(2)}, u32[]{:S(2)}) collective-permute-start(f32[3,16,2,1024]{3,2,1,0:T(2,128)} %get-tuple-element.45), channel_id=1, source_target_pairs={{1,0},{2,1},{3,2},{0,3},{5,4},{6,5},{7,6},{4,7},{9,8},{10,9},{11,1... | collective-permute-start | bytes 1179656 | tf_op jit(solution)/shard_map/ppermute | solution.py:416
  21.1 2.3 %fusion.6 = (s16[3,64,1024]{2,1,0:T(8,128)(2,1)}, s16[3,64,1024]{2,1,0:T(8,128)(2,1)}) fusion(s16[2,2,3,64,1024]{4,3,2,1,0:T(8,128)(2,1)} %collective-permute-done.1, s16[2,2,3,64,1024]{4,3,2,1,0:T(8,128)(2,1)S(1)} %get-tuple-element.41, pred[]{:T(512)S(6)} %eq.41), kind=kLoop, calls=%fused_computation.21 | loop fusion | flops 393216 | bytes 2359297 | tf_op jit(solution)/shard_map/jit(_where)/select_n | solution.py:431
  23.4 2.2 %fusion.8 = (s16[3,64,1024]{2,1,0:T(8,128)(2,1)S(1)}, s16[3,64,1024]{2,1,0:T(8,128)(2,1)}) fusion(s16[2,2,3,64,1024]{4,3,2,1,0:T(8,128)(2,1)} %collective-permute-done, s16[2,2,3,64,1024]{4,3,2,1,0:T(8,128)(2,1)S(1)} %get-tuple-element.39, pred[]{:T(512)S(6)} %eq.41), kind=kLoop, calls=%fused_computation.25 | loop fusion | flops 393216 | bytes 2359297 | tf_op jit(solution)/shard_map/jit(_where)/select_n | solution.py:431
  25.6 1.7 %collective-permute-start.4 = (s16[3,64,1024]{2,1,0:T(8,128)(2,1)S(1)}, s16[3,64,1024]{2,1,0:T(8,128)(2,1)}, u32[]{:S(2)}, u32[]{:S(2)}) collective-permute-start(s16[3,64,1024]{2,1,0:T(8,128)(2,1)S(1)} %get-tuple-element.47), channel_id=1, source_target_pairs={{0,16},{4,20},{8,24},{12,28},{16,0},{20,4},{24,8},{28,12},{1,17},{... | collective-permute-start | bytes 1179656 | tf_op jit(solution)/shard_map/ppermute | solution.py:420
  27.3 1.5 %collective-permute-start.5 = (s16[3,64,1024]{2,1,0:T(8,128)(2,1)}, s16[3,64,1024]{2,1,0:T(8,128)(2,1)}, u32[]{:S(2)}, u32[]{:S(2)}) collective-permute-start(s16[3,64,1024]{2,1,0:T(8,128)(2,1)} %get-tuple-element.48), channel_id=1, source_target_pairs={{0,8},{4,12},{8,0},{12,4},{16,24},{20,28},{24,16},{28,20},{1,9},{5... | collective-permute-start | bytes 1179656 | tf_op jit(solution)/shard_map/ppermute | solution.py:420
  30.7 1.7 %collective-permute-start.7 = (s16[3,64,1024]{2,1,0:T(8,128)(2,1)}, s16[3,64,1024]{2,1,0:T(8,128)(2,1)}, u32[]{:S(2)}, u32[]{:S(2)}) collective-permute-start(s16[3,64,1024]{2,1,0:T(8,128)(2,1)} %get-tuple-element.52), channel_id=1, source_target_pairs={{0,8},{4,12},{8,0},{12,4},{16,24},{20,28},{24,16},{28,20},{1,9},{5... | collective-permute-start | bytes 1179656 | tf_op jit(solution)/shard_map/ppermute | solution.py:420
  32.4 5.5 %collective-permute-done.3.after = f32[3,16,2,1024]{3,2,1,0:T(2,128)} collective-permute-done((f32[3,16,2,1024]{3,2,1,0:T(2,128)}, f32[3,16,2,1024]{3,2,1,0:T(2,128)}, u32[]{:S(2)}, u32[]{:S(2)}) %collective-permute-start.3) | collective-permute-done | bytes 393248 | tf_op jit(solution)/shard_map/ppermute | solution.py:416
  37.9 11.8 %shard_map.147 = (f32[1,5,2,256,1024]{4,3,2,1,0:T(8,128)}, s32[1]{0:T(128)}) custom-call(f32[1]{0:T(128)} %bitcast.9.viscosity, bf16[256,256]{1,0:T(8,128)(2,1)} %constant.62.clone.turn, bf16[384,160]{1,0:T(8,128)(2,1)} %constant.63.clone.m_all, bf16[256,160]{1,0:T(8,128)(2,1)} %constant.64.clone.m_top, f32[3,16,2,1024]{3,2,1,0:T(2,128)} %collective-permute-done.2.before, ...), custom_call_target="tpu_custom_call" | custom-call | bytes 16777216 | tf_op jit(solution)/shard_map/pallas_call | solution.py:244
  50.3 2.4 %broadcast_select_fusion.7 = (s16[3,64,1024]{2,1,0:T(8,128)(2,1)}, s16[3,64,1024]{2,1,0:T(8,128)(2,1)S(1)}, s16[3,64,1024]{2,1,0:T(8,128)(2,1)}, s16[3,64,1024]{2,1,0:T(8,128)(2,1)}) fusion(s16[3,64,1024]{2,1,0:T(8,128)(2,1)} %collective-permute-done.4, pred[]{:T(512)S(6)} %eq.44, s16[2,2,3,64,1024]{4,3,2,1,0:T(8,128)(2,1)} %collective-permute-done, ...), kind=kLoop, calls=%fused_computation.43 | loop fusion | flops 786432 | bytes 3932162 | tf_op jit(solution)/shard_map/jit(_where)/select_n | solution.py:448
  52.8 1.7 %collective-permute-start.9 = (s16[3,64,1024]{2,1,0:T(8,128)(2,1)}, s16[3,64,1024]{2,1,0:T(8,128)(2,1)}, u32[]{:S(2)}, u32[]{:S(2)}) collective-permute-start(s16[3,64,1024]{2,1,0:T(8,128)(2,1)} %get-tuple-element.57), channel_id=1, source_target_pairs={{0,8},{4,12},{8,0},{12,4},{16,24},{20,28},{24,16},{28,20},{1,9},{5... | collective-permute-start | bytes 1179656 | tf_op jit(solution)/shard_map/ppermute | solution.py:420
  54.5 1.5 %collective-permute-start.8 = (s16[3,64,1024]{2,1,0:T(8,128)(2,1)}, s16[3,64,1024]{2,1,0:T(8,128)(2,1)}, u32[]{:S(2)}, u32[]{:S(2)}) collective-permute-start(s16[3,64,1024]{2,1,0:T(8,128)(2,1)} %get-tuple-element.56), channel_id=1, source_target_pairs={{0,16},{4,20},{8,24},{12,28},{16,0},{20,4},{24,8},{28,12},{1,17},{... | collective-permute-start | bytes 1179656 | tf_op jit(solution)/shard_map/ppermute | solution.py:420
  56.0 2.5 %broadcast_select_fusion.4 = (s16[3,64,1024]{2,1,0:T(8,128)(2,1)}, s16[3,64,1024]{2,1,0:T(8,128)(2,1)S(1)}, s16[3,64,1024]{2,1,0:T(8,128)(2,1)}, s16[3,64,1024]{2,1,0:T(8,128)(2,1)S(1)}) fusion(s16[3,64,1024]{2,1,0:T(8,128)(2,1)} %collective-permute-done.7, pred[]{:T(512)S(6)} %eq.45, s16[2,2,3,64,1024]{4,3,2,1,0:T(8,128)(2,1)} %collective-permute-done.1, ...), kind=kLoop, calls=%fused_computation.40 | loop fusion | flops 786432 | bytes 3932162 | tf_op jit(solution)/shard_map/jit(_where)/select_n | solution.py:449
  59.6 18.7 %shard_map.148 = (f32[2,5,2,256,1024]{4,3,2,1,0:T(8,128)}, s32[1]{0:T(128)}) custom-call(f32[1]{0:T(128)} %bitcast.9.viscosity, bf16[256,256]{1,0:T(8,128)(2,1)} %constant.62.clone.turn, bf16[384,160]{1,0:T(8,128)(2,1)} %constant.63.clone.m_all, bf16[256,160]{1,0:T(8,128)(2,1)} %constant.64.clone.m_top, f32[3,16,2,1024]{3,2,1,0:T(2,128)} %collective-permute-done.2.before, ...), custom_call_target="tpu_custom_call" | custom-call | bytes 33554432 | tf_op jit(solution)/shard_map/pallas_call | solution.py:244
  79.2 3.8 %collective-permute-start.12 = (s16[3,64,1024]{2,1,0:T(8,128)(2,1)S(1)}, s16[3,64,1024]{2,1,0:T(8,128)(2,1)}, u32[]{:S(2)}, u32[]{:S(2)}) collective-permute-start(s16[3,64,1024]{2,1,0:T(8,128)(2,1)S(1)} %broadcast_select_fusion.3), channel_id=1, source_target_pairs={{0,8},{4,12},{8,0},{12,4},{16,24},{20,28},{24,16},{28,20},{1,9},{5... | collective-permute-start | bytes 1179656 | tf_op jit(solution)/shard_map/ppermute | solution.py:420
  83.0 1.3 collective-permute-start.13
  84.3 0.9 broadcast_select_fusion
  86.9 6.2 %collective-permute-done.12 = s16[3,64,1024]{2,1,0:T(8,128)(2,1)} collective-permute-done((s16[3,64,1024]{2,1,0:T(8,128)(2,1)S(1)}, s16[3,64,1024]{2,1,0:T(8,128)(2,1)}, u32[]{:S(2)}, u32[]{:S(2)}) %collective-permute-start.12) | collective-permute-done | bytes 393248 | tf_op jit(solution)/shard_map/ppermute | solution.py:420
  93.2 1.6 %select_bitcast_fusion.7 = (s16[1,3,64,1024]{3,2,1,0:T(8,128)(2,1)S(1)}, s16[1,3,64,1024]{3,2,1,0:T(8,128)(2,1)S(1)}) fusion(s16[3,64,1024]{2,1,0:T(8,128)(2,1)} %get-tuple-element.48, s16[3,64,1024]{2,1,0:T(8,128)(2,1)} %collective-permute-done.5, s16[3,64,1024]{2,1,0:T(8,128)(2,1)} %collective-permute-done.12, ...), kind=kLoop, calls=%fused_computation.35 | loop fusion | flops 983040 | bytes 2752515 | tf_op jit(solution)/shard_map/stack | solution.py:468
  95.1 1.4 select_bitcast_fusion.6
  96.5 3.0 %collective-permute-start.15 = (s16[2,3,16,1024]{3,2,1,0:T(8,128)(2,1)S(1)}, s16[2,3,16,1024]{3,2,1,0:T(8,128)(2,1)S(1)}, u32[]{:S(2)}, u32[]{:S(2)}) collective-permute-start(s16[2,3,16,1024]{3,2,1,0:T(8,128)(2,1)S(1)} %fusion.10), channel_id=1, source_target_pairs={{0,1},{1,2},{2,3},{3,0},{8,9},{9,10},{10,11},{11,8},{16,17},{17,18... | collective-permute-start | bytes 589832 | tf_op jit(solution)/shard_map/ppermute | solution.py:479
  99.5 4.6 %collective-permute-start.16 = (s16[2,3,16,1024]{3,2,1,0:T(8,128)(2,1)S(1)}, s16[2,3,16,1024]{3,2,1,0:T(8,128)(2,1)S(1)}, u32[]{:S(2)}, u32[]{:S(2)}) collective-permute-start(s16[2,3,16,1024]{3,2,1,0:T(8,128)(2,1)S(1)} %fusion.11), channel_id=1, source_target_pairs={{1,0},{2,1},{3,2},{0,3},{9,8},{10,9},{11,10},{8,11},{17,16},{18,17... | collective-permute-start | bytes 589832 | tf_op jit(solution)/shard_map/ppermute | solution.py:480
  104.6 1.3 collective-permute-done.15.before
  105.9 2.0 %collective-permute-done.16.after = s16[2,3,16,1024]{3,2,1,0:T(8,128)(2,1)S(1)} collective-permute-done((s16[2,3,16,1024]{3,2,1,0:T(8,128)(2,1)S(1)}, s16[2,3,16,1024]{3,2,1,0:T(8,128)(2,1)S(1)}, u32[]{:S(2)}, u32[]{:S(2)}) %collective-permute-start.16) | collective-permute-done | bytes 196640 | tf_op jit(solution)/shard_map/ppermute | solution.py:480
  107.9 1.6 %select_bitcast_fusion.2 = (s16[1,3,64,1024]{3,2,1,0:T(8,128)(2,1)S(1)}, s16[1,3,64,1024]{3,2,1,0:T(8,128)(2,1)S(1)}) fusion(s16[3,64,1024]{2,1,0:T(8,128)(2,1)} %get-tuple-element.51, s16[3,64,1024]{2,1,0:T(8,128)(2,1)} %collective-permute-done.6, s16[3,64,1024]{2,1,0:T(8,128)(2,1)} %collective-permute-done.18, s16[3,64,1024]{2,1,0:T(8,128)(2,1)S(1)} %copy-done.11, ...), kind=kLoop, calls=%fused_computation.30 | loop fusion | flops 983040 | bytes 2752515 | tf_op jit(solution)/shard_map/stack | solution.py:468
  109.5 1.5 %select_bitcast_fusion.3 = (s16[1,3,64,1024]{3,2,1,0:T(8,128)(2,1)S(1)}, s16[1,3,64,1024]{3,2,1,0:T(8,128)(2,1)S(1)}) fusion(s16[3,64,1024]{2,1,0:T(8,128)(2,1)} %get-tuple-element.52, s16[3,64,1024]{2,1,0:T(8,128)(2,1)} %collective-permute-done.7, s16[3,64,1024]{2,1,0:T(8,128)(2,1)} %collective-permute-done.17, s16[3,64,1024]{2,1,0:T(8,128)(2,1)S(1)} %copy-done.9, ...), kind=kLoop, calls=%fused_computation.31 | loop fusion | flops 983040 | bytes 2752515 | tf_op jit(solution)/shard_map/stack | solution.py:468
  112.1 3.1 %collective-permute-done.20.before2 = s16[2,3,16,1024]{3,2,1,0:T(8,128)(2,1)S(1)} collective-permute-done((s16[2,3,16,1024]{3,2,1,0:T(8,128)(2,1)S(1)}, s16[2,3,16,1024]{3,2,1,0:T(8,128)(2,1)S(1)}, u32[]{:S(2)}, u32[]{:S(2)}) %collective-permute-start.20) | collective-permute-done | bytes 196640 | tf_op jit(solution)/shard_map/ppermute | solution.py:420
  116.7 22.0 %shard_map.149 = f32[1,3,256,2,1024]{4,3,2,1,0:T(2,128)} custom-call(s32[1]{0:T(128)} %bitcast.core, bf16[128,96]{1,0:T(8,128)(2,1)} %constant.65.clone.m_both, bf16[256,128]{1,0:T(8,128)(2,1)} %constant.66.clone.turn, s16[2,2,3,64,1024]{4,3,2,1,0:T(8,128)(2,1)} %copy-done.2, s16[2,2,3,64,1024]{4,3,2,1,0:T(8,128)(2,1)} %collective-permute-done.14.other0, ...), custom_call_target="tpu_custom_call" | custom-call | bytes 12582912 | tf_op jit(solution)/shard_map/pallas_call | solution.py:383
  (71 shorter events, 8.1 us)
Async XLA Ops:
  3.3 4.6 %copy-start = (bf16[1,3,256,8,1024]{4,3,2,1,0:T(8,128)(2,1)S(1)}, bf16[1,3,256,8,1024]{4,3,2,1,0:T(8,128)(2,1)}, u32[]{:S(2)}) copy-start(bf16[1,3,256,8,1024]{4,3,2,1,0:T(8,128)(2,1)} %param.16) | copy-start | bytes 37748740
  11.4 9.7 %collective-permute-start.1 = (s16[2,2,3,64,1024]{4,3,2,1,0:T(8,128)(2,1)}, s16[2,2,3,64,1024]{4,3,2,1,0:T(8,128)(2,1)}, u32[]{:S(2)}, u32[]{:S(2)}) collective-permute-start(s16[2,2,3,64,1024]{4,3,2,1,0:T(8,128)(2,1)} %get-tuple-element.42), channel_id=1, source_target_pairs={{0,4},{4,0},{8,12},{12,8},{16,20},{20,16},{24,28},{28,24},{1,5},{5... | collective-permute-start | bytes 4718600 | tf_op jit(solution)/shard_map/ppermute | solution.py:420
  15.3 8.1 %collective-permute-start = (s16[2,2,3,64,1024]{4,3,2,1,0:T(8,128)(2,1)}, s16[2,2,3,64,1024]{4,3,2,1,0:T(8,128)(2,1)}, u32[]{:S(2)}, u32[]{:S(2)}) collective-permute-start(s16[2,2,3,64,1024]{4,3,2,1,0:T(8,128)(2,1)} %get-tuple-element.40), channel_id=1, source_target_pairs={{0,4},{4,0},{8,12},{12,8},{16,20},{20,16},{24,28},{28,24},{1,5},{5... | collective-permute-start | bytes 4718600 | tf_op jit(solution)/shard_map/ppermute | solution.py:420
  15.4 15.3 %collective-permute-start.2 = (f32[3,16,2,1024]{3,2,1,0:T(2,128)}, f32[3,16,2,1024]{3,2,1,0:T(2,128)}, u32[]{:S(2)}, u32[]{:S(2)}) collective-permute-start(f32[3,16,2,1024]{3,2,1,0:T(2,128)} %get-tuple-element.44), channel_id=1, source_target_pairs={{0,1},{1,2},{2,3},{3,0},{4,5},{5,6},{6,7},{7,4},{8,9},{9,10},{10,1... | collective-permute-start | bytes 1179656 | tf_op jit(solution)/shard_map/ppermute | solution.py:416
  18.4 19.5 %collective-permute-start.3 = (f32[3,16,2,1024]{3,2,1,0:T(2,128)}, f32[3,16,2,1024]{3,2,1,0:T(2,128)}, u32[]{:S(2)}, u32[]{:S(2)}) collective-permute-start(f32[3,16,2,1024]{3,2,1,0:T(2,128)} %get-tuple-element.45), channel_id=1, source_target_pairs={{1,0},{2,1},{3,2},{0,3},{5,4},{6,5},{7,6},{4,7},{9,8},{10,9},{11,1... | collective-permute-start | bytes 1179656 | tf_op jit(solution)/shard_map/ppermute | solution.py:416
  23.4 6.1 %copy-start.16 = (f32[64]{0:T(128)S(1)}, f32[64]{0:T(128)}, u32[]{:S(2)}) copy-start(f32[64]{0:T(128)} %param.19) | copy-start | bytes 772
  25.6 24.2 %copy-start.6 = (s16[3,64,1024]{2,1,0:T(8,128)(2,1)}, s16[3,64,1024]{2,1,0:T(8,128)(2,1)S(1)}, u32[]{:S(2)}) copy-start(s16[3,64,1024]{2,1,0:T(8,128)(2,1)S(1)} %get-tuple-element.47) | copy-start | bytes 1179652
  25.6 24.7 %collective-permute-start.4 = (s16[3,64,1024]{2,1,0:T(8,128)(2,1)S(1)}, s16[3,64,1024]{2,1,0:T(8,128)(2,1)}, u32[]{:S(2)}, u32[]{:S(2)}) collective-permute-start(s16[3,64,1024]{2,1,0:T(8,128)(2,1)S(1)} %get-tuple-element.47), channel_id=1, source_target_pairs={{0,16},{4,20},{8,24},{12,28},{16,0},{20,4},{24,8},{28,12},{1,17},{... | collective-permute-start | bytes 1179656 | tf_op jit(solution)/shard_map/ppermute | solution.py:420
  27.3 23.0 %collective-permute-start.5 = (s16[3,64,1024]{2,1,0:T(8,128)(2,1)}, s16[3,64,1024]{2,1,0:T(8,128)(2,1)}, u32[]{:S(2)}, u32[]{:S(2)}) collective-permute-start(s16[3,64,1024]{2,1,0:T(8,128)(2,1)} %get-tuple-element.48), channel_id=1, source_target_pairs={{0,8},{4,12},{8,0},{12,4},{16,24},{20,28},{24,16},{28,20},{1,9},{5... | collective-permute-start | bytes 1179656 | tf_op jit(solution)/shard_map/ppermute | solution.py:420
  30.1 25.9 %collective-permute-start.6 = (s16[3,64,1024]{2,1,0:T(8,128)(2,1)}, s16[3,64,1024]{2,1,0:T(8,128)(2,1)}, u32[]{:S(2)}, u32[]{:S(2)}) collective-permute-start(s16[3,64,1024]{2,1,0:T(8,128)(2,1)} %get-tuple-element.51), channel_id=1, source_target_pairs={{0,16},{4,20},{8,24},{12,28},{16,0},{20,4},{24,8},{28,12},{1,17},{... | collective-permute-start | bytes 1179656 | tf_op jit(solution)/shard_map/ppermute | solution.py:420
  30.7 25.3 %collective-permute-start.7 = (s16[3,64,1024]{2,1,0:T(8,128)(2,1)}, s16[3,64,1024]{2,1,0:T(8,128)(2,1)}, u32[]{:S(2)}, u32[]{:S(2)}) collective-permute-start(s16[3,64,1024]{2,1,0:T(8,128)(2,1)} %get-tuple-element.52), channel_id=1, source_target_pairs={{0,8},{4,12},{8,0},{12,4},{16,24},{20,28},{24,16},{28,20},{1,9},{5... | collective-permute-start | bytes 1179656 | tf_op jit(solution)/shard_map/ppermute | solution.py:420
  52.8 26.2 %collective-permute-start.9 = (s16[3,64,1024]{2,1,0:T(8,128)(2,1)}, s16[3,64,1024]{2,1,0:T(8,128)(2,1)}, u32[]{:S(2)}, u32[]{:S(2)}) collective-permute-start(s16[3,64,1024]{2,1,0:T(8,128)(2,1)} %get-tuple-element.57), channel_id=1, source_target_pairs={{0,8},{4,12},{8,0},{12,4},{16,24},{20,28},{24,16},{28,20},{1,9},{5... | collective-permute-start | bytes 1179656 | tf_op jit(solution)/shard_map/ppermute | solution.py:420
  54.5 24.6 %collective-permute-start.8 = (s16[3,64,1024]{2,1,0:T(8,128)(2,1)}, s16[3,64,1024]{2,1,0:T(8,128)(2,1)}, u32[]{:S(2)}, u32[]{:S(2)}) collective-permute-start(s16[3,64,1024]{2,1,0:T(8,128)(2,1)} %get-tuple-element.56), channel_id=1, source_target_pairs={{0,16},{4,20},{8,24},{12,28},{16,0},{20,4},{24,8},{28,12},{1,17},{... | collective-permute-start | bytes 1179656 | tf_op jit(solution)/shard_map/ppermute | solution.py:420
  58.6 26.7 %collective-permute-start.10 = (s16[3,64,1024]{2,1,0:T(8,128)(2,1)}, s16[3,64,1024]{2,1,0:T(8,128)(2,1)S(1)}, u32[]{:S(2)}, u32[]{:S(2)}) collective-permute-start(s16[3,64,1024]{2,1,0:T(8,128)(2,1)} %get-tuple-element.59), channel_id=1, source_target_pairs={{0,16},{4,20},{8,24},{12,28},{16,0},{20,4},{24,8},{28,12},{1,17},{... | collective-permute-start | bytes 1179656 | tf_op jit(solution)/shard_map/ppermute | solution.py:420
  59.3 25.0 %collective-permute-start.11 = (s16[3,64,1024]{2,1,0:T(8,128)(2,1)}, s16[3,64,1024]{2,1,0:T(8,128)(2,1)S(1)}, u32[]{:S(2)}, u32[]{:S(2)}) collective-permute-start(s16[3,64,1024]{2,1,0:T(8,128)(2,1)} %get-tuple-element.60), channel_id=1, source_target_pairs={{0,8},{4,12},{8,0},{12,4},{16,24},{20,28},{24,16},{28,20},{1,9},{5... | collective-permute-start | bytes 1179656 | tf_op jit(solution)/shard_map/ppermute | solution.py:420
  59.6 19.5 %copy-start.4 = (s16[3,64,1024]{2,1,0:T(8,128)(2,1)S(1)}, s16[3,64,1024]{2,1,0:T(8,128)(2,1)}, u32[]{:S(2)}) copy-start(s16[3,64,1024]{2,1,0:T(8,128)(2,1)} %get-tuple-element.84) | copy-start | bytes 1179652
  79.2 13.9 %collective-permute-start.12 = (s16[3,64,1024]{2,1,0:T(8,128)(2,1)S(1)}, s16[3,64,1024]{2,1,0:T(8,128)(2,1)}, u32[]{:S(2)}, u32[]{:S(2)}) collective-permute-start(s16[3,64,1024]{2,1,0:T(8,128)(2,1)S(1)} %broadcast_select_fusion.3), channel_id=1, source_target_pairs={{0,8},{4,12},{8,0},{12,4},{16,24},{20,28},{24,16},{28,20},{1,9},{5... | collective-permute-start | bytes 1179656 | tf_op jit(solution)/shard_map/ppermute | solution.py:420
  83.0 12.1 %collective-permute-start.13 = (s16[3,64,1024]{2,1,0:T(8,128)(2,1)S(1)}, s16[3,64,1024]{2,1,0:T(8,128)(2,1)S(1)}, u32[]{:S(2)}, u32[]{:S(2)}) collective-permute-start(s16[3,64,1024]{2,1,0:T(8,128)(2,1)S(1)} %broadcast_select_fusion.2), channel_id=1, source_target_pairs={{0,16},{4,20},{8,24},{12,28},{16,0},{20,4},{24,8},{28,12},{1,17},{... | collective-permute-start | bytes 1179656 | tf_op jit(solution)/shard_map/ppermute | solution.py:420
  86.1 8.9 %copy-start.7 = (s16[3,64,1024]{2,1,0:T(8,128)(2,1)S(1)}, s16[3,64,1024]{2,1,0:T(8,128)(2,1)}, u32[]{:S(2)}) copy-start(s16[3,64,1024]{2,1,0:T(8,128)(2,1)} %copy-done.6) | copy-start | bytes 1179652
  86.1 23.4 %collective-permute-start.17 = (s16[3,64,1024]{2,1,0:T(8,128)(2,1)}, s16[3,64,1024]{2,1,0:T(8,128)(2,1)}, u32[]{:S(2)}, u32[]{:S(2)}) collective-permute-start(s16[3,64,1024]{2,1,0:T(8,128)(2,1)} %broadcast_select_fusion.1), channel_id=1, source_target_pairs={{0,8},{4,12},{8,0},{12,4},{16,24},{20,28},{24,16},{28,20},{1,9},{5... | collective-permute-start | bytes 1179656 | tf_op jit(solution)/shard_map/ppermute | solution.py:420
  86.9 21.1 %collective-permute-start.18 = (s16[3,64,1024]{2,1,0:T(8,128)(2,1)}, s16[3,64,1024]{2,1,0:T(8,128)(2,1)}, u32[]{:S(2)}, u32[]{:S(2)}) collective-permute-start(s16[3,64,1024]{2,1,0:T(8,128)(2,1)} %broadcast_select_fusion), channel_id=1, source_target_pairs={{0,16},{4,20},{8,24},{12,28},{16,0},{20,4},{24,8},{28,12},{1,17},{... | collective-permute-start | bytes 1179656 | tf_op jit(solution)/shard_map/ppermute | solution.py:420
  96.5 9.4 %collective-permute-start.15 = (s16[2,3,16,1024]{3,2,1,0:T(8,128)(2,1)S(1)}, s16[2,3,16,1024]{3,2,1,0:T(8,128)(2,1)S(1)}, u32[]{:S(2)}, u32[]{:S(2)}) collective-permute-start(s16[2,3,16,1024]{3,2,1,0:T(8,128)(2,1)S(1)} %fusion.10), channel_id=1, source_target_pairs={{0,1},{1,2},{2,3},{3,0},{8,9},{9,10},{10,11},{11,8},{16,17},{17,18... | collective-permute-start | bytes 589832 | tf_op jit(solution)/shard_map/ppermute | solution.py:479
  99.5 8.4 %collective-permute-start.16 = (s16[2,3,16,1024]{3,2,1,0:T(8,128)(2,1)S(1)}, s16[2,3,16,1024]{3,2,1,0:T(8,128)(2,1)S(1)}, u32[]{:S(2)}, u32[]{:S(2)}) collective-permute-start(s16[2,3,16,1024]{3,2,1,0:T(8,128)(2,1)S(1)} %fusion.11), channel_id=1, source_target_pairs={{1,0},{2,1},{3,2},{0,3},{9,8},{10,9},{11,10},{8,11},{17,16},{18,17... | collective-permute-start | bytes 589832 | tf_op jit(solution)/shard_map/ppermute | solution.py:480
  104.5 6.5 %copy-start.2 = (s16[2,2,3,64,1024]{4,3,2,1,0:T(8,128)(2,1)}, s16[2,2,3,64,1024]{4,3,2,1,0:T(8,128)(2,1)S(1)}, u32[]{:S(2)}) copy-start(s16[2,2,3,64,1024]{4,3,2,1,0:T(8,128)(2,1)S(1)} %pad_add_fusion.held0) | copy-start | bytes 4718596
  104.5 5.0 %copy-start.9 = (s16[3,64,1024]{2,1,0:T(8,128)(2,1)S(1)}, s16[3,64,1024]{2,1,0:T(8,128)(2,1)}, u32[]{:S(2)}) copy-start(s16[3,64,1024]{2,1,0:T(8,128)(2,1)} %copy-done.8) | copy-start | bytes 1179652
  104.5 10.9 %collective-permute-start.14 = (s16[2,2,3,64,1024]{4,3,2,1,0:T(8,128)(2,1)S(1)}, s16[2,2,3,64,1024]{4,3,2,1,0:T(8,128)(2,1)}, u32[]{:S(2)}, u32[]{:S(2)}) collective-permute-start(s16[2,2,3,64,1024]{4,3,2,1,0:T(8,128)(2,1)S(1)} %pad_add_fusion.held0), channel_id=1, source_target_pairs={{0,4},{4,0},{8,12},{12,8},{16,20},{20,16},{24,28},{28,24},{1,5},{5... | collective-permute-start | bytes 4718600 | tf_op jit(solution)/shard_map/ppermute | solution.py:420
  105.9 5.6 %copy-start.12 = (s16[2,3,16,1024]{3,2,1,0:T(8,128)(2,1)}, s16[2,3,16,1024]{3,2,1,0:T(8,128)(2,1)S(1)}, u32[]{:S(2)}) copy-start(s16[2,3,16,1024]{3,2,1,0:T(8,128)(2,1)S(1)} %collective-permute-done.15.before) | copy-start | bytes 589828
  107.9 4.0 %copy-start.13 = (s16[2,3,16,1024]{3,2,1,0:T(8,128)(2,1)}, s16[2,3,16,1024]{3,2,1,0:T(8,128)(2,1)S(1)}, u32[]{:S(2)}) copy-start(s16[2,3,16,1024]{3,2,1,0:T(8,128)(2,1)S(1)} %collective-permute-done.16.after) | copy-start | bytes 589828
  111.4 4.1 %copy-start.3 = (s16[2,2,3,64,1024]{4,3,2,1,0:T(8,128)(2,1)}, s16[2,2,3,64,1024]{4,3,2,1,0:T(8,128)(2,1)S(1)}, u32[]{:S(2)}) copy-start(s16[2,2,3,64,1024]{4,3,2,1,0:T(8,128)(2,1)S(1)} %pad_add_fusion.1.held1) | copy-start | bytes 4718596
  111.4 4.0 %collective-permute-start.19 = (s16[2,2,3,64,1024]{4,3,2,1,0:T(8,128)(2,1)S(1)}, s16[2,2,3,64,1024]{4,3,2,1,0:T(8,128)(2,1)S(1)}, u32[]{:S(2)}, u32[]{:S(2)}) collective-permute-start(s16[2,2,3,64,1024]{4,3,2,1,0:T(8,128)(2,1)S(1)} %pad_add_fusion.1.held1), channel_id=1, source_target_pairs={{0,4},{4,0},{8,12},{12,8},{16,20},{20,16},{24,28},{28,24},{1,5},{5... | collective-permute-start | bytes 4718600 | tf_op jit(solution)/shard_map/ppermute | solution.py:420
  111.5 3.7 %collective-permute-start.20 = (s16[2,3,16,1024]{3,2,1,0:T(8,128)(2,1)S(1)}, s16[2,3,16,1024]{3,2,1,0:T(8,128)(2,1)S(1)}, u32[]{:S(2)}, u32[]{:S(2)}) collective-permute-start(s16[2,3,16,1024]{3,2,1,0:T(8,128)(2,1)S(1)} %collective-permute-done.15.before), channel_id=1, source_target_pairs={{0,4},{4,0},{8,12},{12,8},{16,20},{20,16},{24,28},{28,24},{1,5},{5... | collective-permute-start | bytes 589832 | tf_op jit(solution)/shard_map/ppermute | solution.py:420
  112.0 3.5 %collective-permute-start.21 = (s16[2,3,16,1024]{3,2,1,0:T(8,128)(2,1)S(1)}, s16[2,3,16,1024]{3,2,1,0:T(8,128)(2,1)S(1)}, u32[]{:S(2)}, u32[]{:S(2)}) collective-permute-start(s16[2,3,16,1024]{3,2,1,0:T(8,128)(2,1)S(1)} %collective-permute-done.16.after), channel_id=1, source_target_pairs={{0,4},{4,0},{8,12},{12,8},{16,20},{20,16},{24,28},{28,24},{1,5},{5... | collective-permute-start | bytes 589832 | tf_op jit(solution)/shard_map/ppermute | solution.py:420
  (7 other events, 12.1 us)
